TPU v7x, 32 devices: a whole 2x2x4 slice. The times are simulated.
32 devices in a mesh: fsdp: 16 (over z, y, x), dp: 2 (over core).
Axes of the slice: x: 2, y: 2, z: 4, core: 2. Of those that a mesh axis runs over, the one named last changes fastest.
Arguments:
- tokens: bfloat16 [2, 2048, 2048], P('dp', 'fsdp'), may hold values from -6 to 6
- segment_ids: int32 [2, 2048], P('dp'), may hold values from 0 to 7, never falling along the last dimension, each value on 1 to 1280 neighbouring positions
- gain_attn: float32 [2048], replicated, may hold values from 0.5 to 1.5
- gain_mlp: float32 [2048], replicated, may hold values from 0.5 to 1.5
- query_matrix: bfloat16 [2048, 2048], P('fsdp'), may hold values from -0.125 to 0.125
- key_matrix: bfloat16 [2048, 256], P('fsdp'), may hold values from -0.125 to 0.125
- value_matrix: bfloat16 [2048, 256], P('fsdp'), may hold values from -0.125 to 0.125
- output_matrix: bfloat16 [2048, 2048], P('fsdp'), may hold values from -1 to 1
- gate_matrix: bfloat16 [16384, 2048], P('fsdp'), may hold values from -0.125 to 0.125
- upward_matrix: bfloat16 [16384, 2048], P('fsdp'), may hold values from -0.125 to 0.125
- down_matrix: bfloat16 [16384, 2048], P('fsdp'), may hold values from -0.046875 to 0.046875
- query_factor_first: bfloat16 [2048, 256], replicated, may hold values from -0.125 to 0.125
- query_factor_second: bfloat16 [256, 2048], replicated, may hold values from -0.1875 to 0.1875
- key_factor_first: bfloat16 [2048, 256], replicated, may hold values from -0.125 to 0.125
- key_factor_second: bfloat16 [256, 256], replicated, may hold values from -0.1875 to 0.1875
- value_factor_first: bfloat16 [2048, 256], replicated, may hold values from -0.125 to 0.125
- value_factor_second: bfloat16 [256, 256], replicated, may hold values from -0.1875 to 0.1875
- output_factor_first: bfloat16 [2048, 256], replicated, may hold values from -1 to 1
- output_factor_second: bfloat16 [256, 2048], replicated, may hold values from -0.1875 to 0.1875
- gate_factor_first: bfloat16 [2048, 256], replicated, may hold values from -0.125 to 0.125
- gate_factor_second: bfloat16 [256, 16384], replicated, may hold values from -0.1875 to 0.1875
- upward_factor_first: bfloat16 [2048, 256], replicated, may hold values from -0.125 to 0.125
- upward_factor_second: bfloat16 [256, 16384], replicated, may hold values from -0.1875 to 0.1875
- down_factor_first: bfloat16 [16384, 256], replicated, may hold values from -0.046875 to 0.046875
- down_factor_second: bfloat16 [256, 2048], replicated, may hold values from -0.1875 to 0.1875
- cotangent: bfloat16 [2, 2048, 2048], P('dp', 'fsdp'), may hold values from -6 to 6
Outputs:
- output: bfloat16 [2, 2048, 2048], P('dp', 'fsdp')
- grad_tokens: float32 [2, 2048, 2048], P('dp', 'fsdp')
- grad_gain_attn: float32 [2048], P('fsdp')
- grad_gain_mlp: float32 [2048], P('fsdp')
- grad_query_weight: float32 [2048, 2048], P('fsdp')
- grad_key_weight: float32 [2048, 256], P('fsdp')
- grad_value_weight: float32 [2048, 256], P('fsdp')
- grad_output_weight: float32 [2048, 2048], P('fsdp')
- grad_gate_weight: float32 [16384, 2048], P('fsdp')
- grad_up_weight: float32 [16384, 2048], P('fsdp')
- grad_down_weight: float32 [16384, 2048], P('fsdp')
- grad_query_in: float32 [2048, 256], P('fsdp')
- grad_query_out: float32 [256, 2048], P('fsdp')
- grad_key_in: float32 [2048, 256], P('fsdp')
- grad_key_out: float32 [256, 256], P('fsdp')
- grad_value_in: float32 [2048, 256], P('fsdp')
- grad_value_out: float32 [256, 256], P('fsdp')
- grad_output_in: float32 [2048, 256], P('fsdp')
- grad_output_out: float32 [256, 2048], P('fsdp')
- grad_gate_in: float32 [2048, 256], P('fsdp')
- grad_gate_out: float32 [256, 16384], P(None, 'fsdp')
- grad_up_in: float32 [2048, 256], P('fsdp')
- grad_up_out: float32 [256, 16384], P(None, 'fsdp')
- grad_down_in: float32 [16384, 256], P('fsdp')
- grad_down_out: float32 [256, 2048], P('fsdp')
Inputs may be any that keep to these rules, and one draw needn't show every extreme that they name: `segment_ids`: along each sequence the ids never fall; each of the 8 ids covers 1 to 1280 consecutive positions, and one covers exactly 1280.
All inputs are finite; a program needn't handle non-finite values.
Results may differ from a plain program's by a relative error of at most 0.017.
Values may be sent and summed in bfloat16 or wider, within the bound.
A program may use at most 448 MiB of HBM per device.

v0:
```python
import jax
import jax.numpy as jnp
from jax import lax
from jax.sharding import PartitionSpec as P

EPS = 1e-06


def matrix_product(left, right):
    return jnp.dot(left, right, preferred_element_type=jnp.float32)


def left_matrix_product(left, right):
    return lax.dot_general(
        left, right, (((0,), (0,)), ((), ())), preferred_element_type=jnp.float32
    )


def right_product(left, right):
    return lax.dot_general(
        left, right, (((1,), (1,)), ((), ())), preferred_element_type=jnp.float32
    )


def rms_norm(values, gain):
    factor = lax.rsqrt(jnp.mean(values * values, axis=-1, keepdims=True) + EPS)
    return values * factor * gain


def rotate(values, cosines, sines):
    half = values.shape[-1] // 2
    first = values[..., :half]
    second = values[..., half:]
    return jnp.concatenate(
        [first * cosines - second * sines, second * cosines + first * sines], axis=-1
    )


def doc_positions(segments):
    length = segments.shape[0]
    index = jnp.arange(length, dtype=jnp.int32)
    starts = jnp.concatenate([jnp.ones((1,), dtype=bool), segments[1:] != segments[:-1]])
    first = lax.cummax(jnp.where(starts, index, jnp.zeros_like(index)), axis=0)
    return index - first


def geglu(gate_activation, upper_bound):
    return jax.nn.gelu(gate_activation, approximate=True) * upper_bound


def local(
    tokens,
    segment_ids,
    gain_attn,
    gain_mlp,
    query_matrix,
    key_matrix,
    value_matrix,
    output_matrix,
    gate_matrix,
    upward_matrix,
    down_matrix,
    query_factor_first,
    query_factor_second,
    key_factor_first,
    key_factor_second,
    value_factor_first,
    value_factor_second,
    output_factor_first,
    output_factor_second,
    gate_factor_first,
    gate_factor_second,
    upward_factor_first,
    upward_factor_second,
    down_factor_first,
    down_factor_second,
    cotangent,
):
    compact_number_format = jnp.bfloat16
    tok_rows = tokens.shape[1]
    width = tokens.shape[2]
    length = segment_ids.shape[1]
    head_size = key_matrix.shape[1]
    heads = query_matrix.shape[1] // head_size
    unit_rows = gate_matrix.shape[0]
    offset = lax.axis_index("fsdp") * tok_rows
    input_rows = tokens[0].astype(jnp.float32)
    seg_all = segment_ids[0]
    seg_own = lax.dynamic_slice_in_dim(seg_all, offset, tok_rows, 0)
    positions = lax.dynamic_slice_in_dim(doc_positions(seg_all), offset, tok_rows, 0)
    half = head_size // 2
    inverse = 10000.0 ** (-(jnp.arange(half, dtype=jnp.float32) * 2.0 / head_size))
    angles = positions.astype(jnp.float32)[:, None] * inverse[None, :]
    cosines = jnp.cos(angles)
    sines = jnp.sin(angles)
    query_complete, key_complete, value_complete, output_complete = (
        lax.all_gather(query_matrix, "fsdp", axis=0, tiled=True),
        lax.all_gather(key_matrix, "fsdp", axis=0, tiled=True),
        lax.all_gather(value_matrix, "fsdp", axis=0, tiled=True),
        lax.all_gather(output_matrix, "fsdp", axis=0, tiled=True),
    )
    normed_attn, pull_attn = jax.vjp(rms_norm, input_rows, gain_attn)
    attention_input = normed_attn.astype(compact_number_format)
    query_adapter = matrix_product(attention_input, query_factor_first).astype(
        compact_number_format
    )
    key_adapter = matrix_product(attention_input, key_factor_first).astype(compact_number_format)
    value_adapter = matrix_product(attention_input, value_factor_first).astype(
        compact_number_format
    )
    query_linear = matrix_product(attention_input, query_complete) + matrix_product(
        query_adapter, query_factor_second
    )
    key_linear = matrix_product(attention_input, key_complete) + matrix_product(
        key_adapter, key_factor_second
    )
    value_reduced = (
        matrix_product(attention_input, value_complete)
        + matrix_product(value_adapter, value_factor_second)
    ).astype(compact_number_format)
    query_low = rotate(
        query_linear.reshape(tok_rows, heads, head_size), cosines[:, None, :], sines[:, None, :]
    ).astype(compact_number_format)
    key_low = rotate(key_linear, cosines, sines).astype(compact_number_format)
    keys_all, values_all = (
        lax.all_gather(key_low, "fsdp", axis=0, tiled=True),
        lax.all_gather(value_reduced, "fsdp", axis=0, tiled=True),
    )
    block = min(512, length)
    scale = head_size ** (-0.5)
    query_index = offset + jnp.arange(tok_rows, dtype=jnp.int32)
    needed = (offset + tok_rows + block - 1) // block
    first_block = (offset - positions[0]) // block

    def scores_of(start):
        key_block = lax.dynamic_slice_in_dim(keys_all, start, block, 0)
        value_block = lax.dynamic_slice_in_dim(values_all, start, block, 0)
        seg_block = lax.dynamic_slice_in_dim(seg_all, start, block, 0)
        key_index = start + jnp.arange(block, dtype=jnp.int32)
        allowed = (seg_own[:, None] == seg_block[None, :]) & (
            key_index[None, :] <= query_index[:, None]
        )
        allowed = allowed[:, None, :]
        raw = jnp.einsum("thd,kd->thk", query_low, key_block, preferred_element_type=jnp.float32)
        return (jnp.where(allowed, raw * scale, -1e30), allowed, key_block, value_block)

    def max_step(index, carry):
        top, total = carry
        logits, allowed, key_block, value_block = scores_of(index * block)
        new_top = jnp.maximum(top, jnp.max(logits, axis=-1, keepdims=True))
        weights = jnp.where(allowed, jnp.exp(logits - new_top), 0.0)
        return (new_top, total * jnp.exp(top - new_top) + jnp.sum(weights, axis=-1, keepdims=True))

    start_top = jnp.full((tok_rows, heads, 1), -1e30, jnp.float32)
    start_total = jnp.zeros((tok_rows, heads, 1), jnp.float32)
    top, total = lax.fori_loop(first_block, needed, max_step, (start_top, start_total))
    log_total = top + jnp.log(total)

    def probs_of(start):
        logits, allowed, key_block, value_block = scores_of(start)
        return (jnp.where(allowed, jnp.exp(logits - log_total), 0.0), key_block, value_block)

    def out_step(index, acc):
        probs, key_block, value_block = probs_of(index * block)
        return acc + jnp.einsum(
            "thk,kd->thd",
            probs.astype(compact_number_format),
            value_block,
            preferred_element_type=jnp.float32,
        )

    attn_raw = lax.fori_loop(
        first_block, needed, out_step, jnp.zeros((tok_rows, heads, head_size), jnp.float32)
    )
    attention_reduced = attn_raw.reshape(tok_rows, heads * head_size).astype(compact_number_format)
    output_adapter = matrix_product(attention_reduced, output_factor_first).astype(
        compact_number_format
    )
    residual_stream = (
        input_rows
        + matrix_product(attention_reduced, output_complete)
        + matrix_product(output_adapter, output_factor_second)
    )
    normed_mlp, pull_mlp = jax.vjp(rms_norm, residual_stream, gain_mlp)
    perceptron_input = normed_mlp.astype(compact_number_format)
    gate_adapter = matrix_product(perceptron_input, gate_factor_first).astype(compact_number_format)
    upward_adapter = matrix_product(perceptron_input, upward_factor_first).astype(
        compact_number_format
    )
    cot_full = cotangent[0].astype(jnp.float32)
    branch_gradient = cotangent[0]
    down_adapter_gradient = right_product(branch_gradient, down_factor_second).astype(
        compact_number_format
    )
    perceptron_total, lowrank_gate_total, lowrank_up_total = (
        lax.all_gather(perceptron_input, "fsdp", axis=0, tiled=True),
        lax.all_gather(gate_adapter, "fsdp", axis=0, tiled=True),
        lax.all_gather(upward_adapter, "fsdp", axis=0, tiled=True),
    )
    first_unit = lax.axis_index("fsdp") * unit_rows
    gate_column_count = lax.dynamic_slice_in_dim(gate_factor_second, first_unit, unit_rows, 1)
    upward_column_count = lax.dynamic_slice_in_dim(upward_factor_second, first_unit, unit_rows, 1)
    down_input_portion = lax.dynamic_slice_in_dim(down_factor_first, first_unit, unit_rows, 0)
    gate_preactivation = right_product(perceptron_total, gate_matrix) + matrix_product(
        lowrank_gate_total, gate_column_count
    )
    upward_preactivation = right_product(perceptron_total, upward_matrix) + matrix_product(
        lowrank_up_total, upward_column_count
    )
    hidden_full, pull_geglu = jax.vjp(geglu, gate_preactivation, upward_preactivation)
    hidden_activated_value = hidden_full.astype(compact_number_format)
    down_common_result, lowrank_down_sum = (
        lax.psum_scatter(
            matrix_product(hidden_activated_value, down_matrix),
            "fsdp",
            scatter_dimension=0,
            tiled=True,
        ),
        lax.psum_scatter(
            matrix_product(hidden_activated_value, down_input_portion),
            "fsdp",
            scatter_dimension=0,
            tiled=True,
        ),
    )
    down_lowrank_adapter = lowrank_down_sum.astype(compact_number_format)
    perceptron_branch = down_common_result + matrix_product(
        down_lowrank_adapter, down_factor_second
    )
    output_gradient_total, lowrank_down_gradient_total = (
        lax.all_gather(branch_gradient, "fsdp", axis=0, tiled=True),
        lax.all_gather(down_adapter_gradient, "fsdp", axis=0, tiled=True),
    )
    hidden_gradient = right_product(output_gradient_total, down_matrix) + right_product(
        lowrank_down_gradient_total, down_input_portion
    )
    grad_gate_full, grad_up_full = pull_geglu(hidden_gradient)
    gate_output_gradient = grad_gate_full.astype(compact_number_format)
    upward_output_gradient = grad_up_full.astype(compact_number_format)
    perceptron_entry_gradient, lowrank_gate_gradient_sum, lowrank_up_gradient_sum = (
        lax.psum_scatter(
            matrix_product(gate_output_gradient, gate_matrix)
            + matrix_product(upward_output_gradient, upward_matrix),
            "fsdp",
            scatter_dimension=0,
            tiled=True,
        ),
        lax.psum_scatter(
            right_product(gate_output_gradient, gate_column_count),
            "fsdp",
            scatter_dimension=0,
            tiled=True,
        ),
        lax.psum_scatter(
            right_product(upward_output_gradient, upward_column_count),
            "fsdp",
            scatter_dimension=0,
            tiled=True,
        ),
    )
    gate_lowrank_gradient = lowrank_gate_gradient_sum.astype(compact_number_format)
    upward_lowrank_gradient = lowrank_up_gradient_sum.astype(compact_number_format)
    gate_row_count = left_matrix_product(
        gate_output_gradient, jnp.concatenate([perceptron_total, lowrank_gate_total], axis=1)
    )
    upward_row_count = left_matrix_product(
        upward_output_gradient, jnp.concatenate([perceptron_total, lowrank_up_total], axis=1)
    )
    down_rows = left_matrix_product(
        hidden_activated_value,
        jnp.concatenate([output_gradient_total, lowrank_down_gradient_total], axis=1),
    )
    output = (residual_stream + perceptron_branch).astype(compact_number_format)
    perceptron_entry_gradient = (
        perceptron_entry_gradient
        + right_product(gate_lowrank_gradient, gate_factor_first)
        + right_product(upward_lowrank_gradient, upward_factor_first)
    )
    grad_resid_norm, grad_gain_mlp_term = pull_mlp(perceptron_entry_gradient)
    grad_resid = cot_full + grad_resid_norm
    gate_first_gradient_piece = left_matrix_product(perceptron_input, gate_lowrank_gradient)
    upward_first_gradient_piece = left_matrix_product(perceptron_input, upward_lowrank_gradient)
    down_second_gradient_piece = left_matrix_product(down_lowrank_adapter, branch_gradient)
    gradient_of_branch = grad_resid.astype(compact_number_format)
    output_adapter_gradient = right_product(gradient_of_branch, output_factor_second).astype(
        compact_number_format
    )
    grad_attn = (
        right_product(gradient_of_branch, output_complete)
        + right_product(output_adapter_gradient, output_factor_first)
    ).astype(compact_number_format)
    grad_output_weight_term = left_matrix_product(attention_reduced, gradient_of_branch)
    output_second_gradient_piece = left_matrix_product(output_adapter, gradient_of_branch)
    output_first_gradient_piece = left_matrix_product(attention_reduced, output_adapter_gradient)
    grad_attn_heads = grad_attn.reshape(tok_rows, heads, head_size)

    def delta_step(index, acc):
        probs, key_block, value_block = probs_of(index * block)
        grad_probs = jnp.einsum(
            "thd,kd->thk", grad_attn_heads, value_block, preferred_element_type=jnp.float32
        )
        return acc + jnp.sum(probs * grad_probs, axis=-1, keepdims=True)

    delta = lax.fori_loop(
        first_block, needed, delta_step, jnp.zeros((tok_rows, heads, 1), jnp.float32)
    )

    def grad_step(index, carry):
        grad_query_acc, key_terms, value_terms = carry
        start = index * block
        probs, key_block, value_block = probs_of(start)
        grad_probs = jnp.einsum(
            "thd,kd->thk", grad_attn_heads, value_block, preferred_element_type=jnp.float32
        )
        grad_scores = (scale * probs * (grad_probs - delta)).astype(compact_number_format)
        grad_query_acc = grad_query_acc + jnp.einsum(
            "thk,kd->thd", grad_scores, key_block, preferred_element_type=jnp.float32
        )
        key_part = jnp.einsum(
            "thk,thd->kd", grad_scores, query_low, preferred_element_type=jnp.float32
        )
        value_part = jnp.einsum(
            "thk,thd->kd",
            probs.astype(compact_number_format),
            grad_attn_heads,
            preferred_element_type=jnp.float32,
        )
        key_terms = lax.dynamic_update_slice_in_dim(key_terms, key_part, start, 0)
        value_terms = lax.dynamic_update_slice_in_dim(value_terms, value_part, start, 0)
        return (grad_query_acc, key_terms, value_terms)

    empty_keys = jnp.zeros((length, head_size), jnp.float32)
    grad_query_rot, key_terms, value_terms = lax.fori_loop(
        first_block,
        needed,
        grad_step,
        (jnp.zeros((tok_rows, heads, head_size), jnp.float32), empty_keys, empty_keys),
    )
    grad_key_rot, grad_value = (
        lax.psum_scatter(key_terms, "fsdp", scatter_dimension=0, tiled=True),
        lax.psum_scatter(value_terms, "fsdp", scatter_dimension=0, tiled=True),
    )
    query_linear_gradient = (
        rotate(grad_query_rot, cosines[:, None, :], -sines[:, None, :])
        .reshape(tok_rows, heads * head_size)
        .astype(compact_number_format)
    )
    key_linear_gradient = rotate(grad_key_rot, cosines, -sines).astype(compact_number_format)
    value_linear_gradient = grad_value.astype(compact_number_format)
    query_adapter_gradient = right_product(query_linear_gradient, query_factor_second).astype(
        compact_number_format
    )
    key_adapter_gradient = right_product(key_linear_gradient, key_factor_second).astype(
        compact_number_format
    )
    value_adapter_gradient = right_product(value_linear_gradient, value_factor_second).astype(
        compact_number_format
    )
    grad_attn_in = (
        right_product(query_linear_gradient, query_complete)
        + right_product(key_linear_gradient, key_complete)
        + right_product(value_linear_gradient, value_complete)
        + right_product(query_adapter_gradient, query_factor_first)
        + right_product(key_adapter_gradient, key_factor_first)
        + right_product(value_adapter_gradient, value_factor_first)
    )
    grad_inputs_norm, grad_gain_attn_term = pull_attn(grad_attn_in)
    grad_inputs = grad_resid + grad_inputs_norm
    shard_terms = (
        lax.psum_scatter(grad_gain_attn_term, "fsdp", scatter_dimension=0, tiled=True),
        lax.psum_scatter(grad_gain_mlp_term, "fsdp", scatter_dimension=0, tiled=True),
        lax.psum_scatter(
            left_matrix_product(attention_input, query_linear_gradient),
            "fsdp",
            scatter_dimension=0,
            tiled=True,
        ),
        lax.psum_scatter(
            left_matrix_product(attention_input, key_linear_gradient),
            "fsdp",
            scatter_dimension=0,
            tiled=True,
        ),
        lax.psum_scatter(
            left_matrix_product(attention_input, value_linear_gradient),
            "fsdp",
            scatter_dimension=0,
            tiled=True,
        ),
        lax.psum_scatter(grad_output_weight_term, "fsdp", scatter_dimension=0, tiled=True),
        lax.psum_scatter(
            left_matrix_product(attention_input, query_adapter_gradient),
            "fsdp",
            scatter_dimension=0,
            tiled=True,
        ),
        lax.psum_scatter(
            left_matrix_product(query_adapter, query_linear_gradient),
            "fsdp",
            scatter_dimension=0,
            tiled=True,
        ),
        lax.psum_scatter(
            left_matrix_product(attention_input, key_adapter_gradient),
            "fsdp",
            scatter_dimension=0,
            tiled=True,
        ),
        lax.psum_scatter(
            left_matrix_product(key_adapter, key_linear_gradient),
            "fsdp",
            scatter_dimension=0,
            tiled=True,
        ),
        lax.psum_scatter(
            left_matrix_product(attention_input, value_adapter_gradient),
            "fsdp",
            scatter_dimension=0,
            tiled=True,
        ),
        lax.psum_scatter(
            left_matrix_product(value_adapter, value_linear_gradient),
            "fsdp",
            scatter_dimension=0,
            tiled=True,
        ),
        lax.psum_scatter(output_first_gradient_piece, "fsdp", scatter_dimension=0, tiled=True),
        lax.psum_scatter(output_second_gradient_piece, "fsdp", scatter_dimension=0, tiled=True),
        lax.psum_scatter(gate_first_gradient_piece, "fsdp", scatter_dimension=0, tiled=True),
        lax.psum_scatter(upward_first_gradient_piece, "fsdp", scatter_dimension=0, tiled=True),
        lax.psum_scatter(down_second_gradient_piece, "fsdp", scatter_dimension=0, tiled=True),
    )
    (
        g_gain_attn,
        g_gain_mlp,
        g_query_weight,
        g_key_weight,
        g_value_weight,
        g_output_weight,
        g_query_in,
        g_query_out,
        g_key_in,
        g_key_out,
        g_value_in,
        g_value_out,
        g_output_in,
        g_output_out,
        g_gate_in,
        g_up_in,
        g_down_out,
        g_gate_rows,
        g_up_rows,
        g_down_rows,
    ) = lax.psum(
        (
            shard_terms[0],
            shard_terms[1],
            shard_terms[2],
            shard_terms[3],
            shard_terms[4],
            shard_terms[5],
            shard_terms[6],
            shard_terms[7],
            shard_terms[8],
            shard_terms[9],
            shard_terms[10],
            shard_terms[11],
            shard_terms[12],
            shard_terms[13],
            shard_terms[14],
            shard_terms[15],
            shard_terms[16],
            gate_row_count,
            upward_row_count,
            down_rows,
        ),
        "dp",
    )
    return (
        output[None],
        grad_inputs[None],
        g_gain_attn,
        g_gain_mlp,
        g_query_weight,
        g_key_weight,
        g_value_weight,
        g_output_weight,
        g_gate_rows[:, :width],
        g_up_rows[:, :width],
        g_down_rows[:, :width],
        g_query_in,
        g_query_out,
        g_key_in,
        g_key_out,
        g_value_in,
        g_value_out,
        g_output_in,
        g_output_out,
        g_gate_in,
        jnp.transpose(g_gate_rows[:, width:]),
        g_up_in,
        jnp.transpose(g_up_rows[:, width:]),
        g_down_rows[:, width:],
        g_down_out,
    )


def solution(mesh):
    in_specs = (
        P("dp", "fsdp", None),
        P("dp", None),
        P(),
        P(),
        P("fsdp", None),
        P("fsdp", None),
        P("fsdp", None),
        P("fsdp", None),
        P("fsdp", None),
        P("fsdp", None),
        P("fsdp", None),
        P(),
        P(),
        P(),
        P(),
        P(),
        P(),
        P(),
        P(),
        P(),
        P(),
        P(),
        P(),
        P(),
        P(),
        P("dp", "fsdp", None),
    )
    out_specs = (
        P("dp", "fsdp", None),
        P("dp", "fsdp", None),
        P("fsdp"),
        P("fsdp"),
        P("fsdp", None),
        P("fsdp", None),
        P("fsdp", None),
        P("fsdp", None),
        P("fsdp", None),
        P("fsdp", None),
        P("fsdp", None),
        P("fsdp", None),
        P("fsdp", None),
        P("fsdp", None),
        P("fsdp", None),
        P("fsdp", None),
        P("fsdp", None),
        P("fsdp", None),
        P("fsdp", None),
        P("fsdp", None),
        P(None, "fsdp"),
        P("fsdp", None),
        P(None, "fsdp"),
        P("fsdp", None),
        P("fsdp", None),
    )
    return jax.shard_map(local, mesh=mesh, in_specs=in_specs, out_specs=out_specs, check_vma=False)
```

profile of v0, /device:TPU:0, one launch (start us, length us, event | category | flops | bytes accessed | tf_op | source)
XLA Modules:
  0.0 3893.7 jit_solution(8080817231925765084)
XLA Ops:
  14.8 53.9 %all-gather.13.cloned.1.call-done = bf16[2048,256]{1,0:T(8,128)(2,1)} async-done(((bf16[128,256]{1,0:T(8,128)(2,1)}), bf16[2048,256]{1,0:T(8,128)(2,1)}) %all-gather.13.cloned.1.call-update) | async-done | bytes 1048592 | tf_op jit(solution)/shard_map/all_gather | solution.py:98
  73.3 52.1 %all-gather.19.cloned.1.call-done = bf16[2048,256]{1,0:T(8,128)(2,1)} async-done(((bf16[128,256]{1,0:T(8,128)(2,1)}), bf16[2048,256]{1,0:T(8,128)(2,1)}) %all-gather.19.cloned.1.call-update) | async-done | bytes 1048592 | tf_op jit(solution)/shard_map/all_gather | solution.py:99
  131.1 108.2 %all-gather.17.cloned.1.call-done = bf16[2048,2048]{1,0:T(8,128)(2,1)} async-done(((bf16[128,2048]{1,0:T(8,128)(2,1)}), bf16[2048,2048]{1,0:T(8,128)(2,1)}) %all-gather.17.cloned.1.call-update) | async-done | bytes 8388624 | tf_op jit(solution)/shard_map/all_gather | solution.py:97
  239.3 4.7 fusion.169
  247.3 48.5 %all-gather.15.cloned.1.call-done = bf16[2048,256]{1,0:T(8,128)(2,1)} async-done(((bf16[128,256]{1,0:T(8,128)(2,1)}), bf16[2048,256]{1,0:T(8,128)(2,1)}) %all-gather.15.cloned.1.call-update) | async-done | bytes 1048592 | tf_op jit(solution)/shard_map/all_gather | solution.py:126
  295.8 3.0 while.50
  298.8 54.1 %all-gather.21.cloned.1.call-done = bf16[2048,256]{1,0:T(8,128)(2,1)} async-done(((bf16[128,256]{1,0:T(8,128)(2,1)}), bf16[2048,256]{1,0:T(8,128)(2,1)}) %all-gather.21.cloned.1.call-update) | async-done | bytes 1048592 | tf_op jit(solution)/shard_map/all_gather | solution.py:127
  353.0 3.2 while.51
  360.7 106.0 %all-gather.23.cloned.1.call-done = bf16[2048,2048]{1,0:T(8,128)(2,1)} async-done(((bf16[128,2048]{1,0:T(8,128)(2,1)}), bf16[2048,2048]{1,0:T(8,128)(2,1)}) %all-gather.23.cloned.1.call-update) | async-done | bytes 8388624 | tf_op jit(solution)/shard_map/all_gather | solution.py:100
  466.7 4.8 convolution_add_fusion.17
  479.9 100.1 %all-gather.33.cloned.1.call-done = bf16[1,2048,2048]{2,1,0:T(8,128)(2,1)} async-done(((bf16[1,128,2048]{2,1,0:T(8,128)(2,1)}), bf16[1,2048,2048]{2,1,0:T(8,128)(2,1)}) %all-gather.33.cloned.1.call-update) | async-done | bytes 8388624 | tf_op jit(solution)/shard_map/all_gather | solution.py:231
  580.0 14.5 fusion.151
  594.5 99.3 %all-gather.25.cloned.1.call-done = bf16[2048,2048]{1,0:T(8,128)(2,1)} async-done(((bf16[128,2048]{1,0:T(8,128)(2,1)}), bf16[2048,2048]{1,0:T(8,128)(2,1)}) %all-gather.25.cloned.1.call-update) | async-done | bytes 8388624 | tf_op jit(solution)/shard_map/all_gather | solution.py:196
  693.8 14.7 fusion.176
  708.5 11.4 fusion.175
  719.9 30.6 all-gather.29.cloned.1.call-done
  750.5 8.5 convolution_add_fusion.4
  759.0 48.6 %all-gather.27.cloned.1.call-done = bf16[2048,256]{1,0:T(8,128)(2,1)} async-done(((bf16[128,256]{1,0:T(8,128)(2,1)}), bf16[2048,256]{1,0:T(8,128)(2,1)}) %all-gather.27.cloned.1.call-update) | async-done | bytes 1048592 | tf_op jit(solution)/shard_map/all_gather | solution.py:197
  807.6 8.5 convolution_add_fusion.5
  816.1 48.8 %all-gather.31.cloned.1.call-done = bf16[2048,256]{1,0:T(8,128)(2,1)} async-done(((bf16[128,256]{1,0:T(8,128)(2,1)}), bf16[2048,256]{1,0:T(8,128)(2,1)}) %all-gather.31.cloned.1.call-update) | async-done | bytes 1048592 | tf_op jit(solution)/shard_map/all_gather | solution.py:232
  864.9 15.7 multiply_convert_fusion
  882.7 3.7 fusion.113
  886.5 15.7 fusion.178
  902.2 17.2 convolution_add_fusion.2
  919.5 4.9 fusion.110
  924.5 4.9 fusion.108
  929.7 37.2 reduce-scatter.29.cloned.1.call-done
  966.9 345.3 %reduce-scatter.27.cloned.1.call-done = f32[128,2048]{1,0:T(8,128)} async-done(((f32[2048,2048]{1,0:T(8,128)}), f32[128,2048]{1,0:T(8,128)}) %reduce-scatter.27.cloned.1.call-update) | async-done | bytes 1048592 | tf_op jit(solution)/shard_map/reduce_scatter | solution.py:241
  1312.2 3.0 convolution_add_fusion.13
  1315.3 86.2 %reduce-scatter.31.cloned.1.call-done = f32[128,256]{1,0:T(8,128)} async-done(((f32[2048,256]{1,0:T(8,128)}), f32[128,256]{1,0:T(8,128)}) %reduce-scatter.31.cloned.1.call-update) | async-done | bytes 131088 | tf_op jit(solution)/shard_map/reduce_scatter | solution.py:254
  1405.6 6.5 fusion.179
  1412.6 3.5 while.52
  1419.2 7.5 while.53
  1431.5 50.7 %reduce-scatter.25.cloned.1.call-done = f32[128,256]{1,0:T(8,128)} async-done(((f32[2048,256]{1,0:T(8,128)}), f32[128,256]{1,0:T(8,128)}) %reduce-scatter.25.cloned.1.call-update) | async-done | bytes 131088 | tf_op jit(solution)/shard_map/reduce_scatter | solution.py:219
  1488.8 74.2 %reduce-scatter.33.cloned.1.call-done = f32[128,256]{1,0:T(8,128)} async-done(((f32[2048,256]{1,0:T(8,128)}), f32[128,256]{1,0:T(8,128)}) %reduce-scatter.33.cloned.1.call-update) | async-done | bytes 131088 | tf_op jit(solution)/shard_map/reduce_scatter | solution.py:340
  1577.2 66.2 %reduce-scatter.35.cloned.1.call-done = f32[128,256]{1,0:T(8,128)} async-done(((f32[2048,256]{1,0:T(8,128)}), f32[128,256]{1,0:T(8,128)}) %reduce-scatter.35.cloned.1.call-update) | async-done | bytes 131088 | tf_op jit(solution)/shard_map/reduce_scatter | solution.py:341
  1648.3 8.1 fusion.181
  1656.5 8.2 fusion.100
  1664.8 15.2 fusion.177
  1680.5 17.3 fusion.60
  1698.8 15.7 fusion.63
  1715.6 17.3 fusion.66
  1733.0 70.8 %reduce-scatter.63.cloned.1.call-done = f32[128,256]{1,0:T(8,128)} async-done(((f32[2048,256]{1,0:T(8,128)}), f32[128,256]{1,0:T(8,128)}) %reduce-scatter.63.cloned.1.call-update) | async-done | bytes 131088 | tf_op jit(solution)/shard_map/reduce_scatter | solution.py:430
  1803.8 80.2 %reduce-scatter.65.cloned.1.call-done = f32[16,2048]{1,0:T(8,128)} async-done(((f32[256,2048]{1,0:T(8,128)}), f32[16,2048]{1,0:T(8,128)}) %reduce-scatter.65.cloned.1.call-update) | async-done | bytes 131088 | tf_op jit(solution)/shard_map/reduce_scatter | solution.py:431
  1884.0 80.4 %reduce-scatter.57.cloned.1.call-done = f32[128,256]{1,0:T(8,128)} async-done(((f32[2048,256]{1,0:T(8,128)}), f32[128,256]{1,0:T(8,128)}) %reduce-scatter.57.cloned.1.call-update) | async-done | bytes 131088 | tf_op jit(solution)/shard_map/reduce_scatter | solution.py:427
  1964.3 80.4 %reduce-scatter.59.cloned.1.call-done = f32[16,2048]{1,0:T(8,128)} async-done(((f32[256,2048]{1,0:T(8,128)}), f32[16,2048]{1,0:T(8,128)}) %reduce-scatter.59.cloned.1.call-update) | async-done | bytes 131088 | tf_op jit(solution)/shard_map/reduce_scatter | solution.py:428
  2044.8 80.7 %reduce-scatter.39.cloned.1.call-done = f32[128,256]{1,0:T(8,128)} async-done(((f32[2048,256]{1,0:T(8,128)}), f32[128,256]{1,0:T(8,128)}) %reduce-scatter.39.cloned.1.call-update) | async-done | bytes 131088 | tf_op jit(solution)/shard_map/reduce_scatter | solution.py:378
  2125.5 80.3 %reduce-scatter.49.cloned.1.call-done = f32[128,256]{1,0:T(8,128)} async-done(((f32[2048,256]{1,0:T(8,128)}), f32[128,256]{1,0:T(8,128)}) %reduce-scatter.49.cloned.1.call-update) | async-done | bytes 131088 | tf_op jit(solution)/shard_map/reduce_scatter | solution.py:403
  2205.8 80.3 %reduce-scatter.45.cloned.1.call-done = f32[128,256]{1,0:T(8,128)} async-done(((f32[2048,256]{1,0:T(8,128)}), f32[128,256]{1,0:T(8,128)}) %reduce-scatter.45.cloned.1.call-update) | async-done | bytes 131088 | tf_op jit(solution)/shard_map/reduce_scatter | solution.py:391
  2286.1 80.3 %reduce-scatter.47.cloned.1.call-done = f32[16,2048]{1,0:T(8,128)} async-done(((f32[256,2048]{1,0:T(8,128)}), f32[16,2048]{1,0:T(8,128)}) %reduce-scatter.47.cloned.1.call-update) | async-done | bytes 131088 | tf_op jit(solution)/shard_map/reduce_scatter | solution.py:397
  2366.4 80.1 %reduce-scatter.53.cloned.1.call-done = f32[128,256]{1,0:T(8,128)} async-done(((f32[2048,256]{1,0:T(8,128)}), f32[128,256]{1,0:T(8,128)}) %reduce-scatter.53.cloned.1.call-update) | async-done | bytes 131088 | tf_op jit(solution)/shard_map/reduce_scatter | solution.py:415
  2446.5 81.0 %reduce-scatter.41.cloned.1.call-done = f32[128,256]{1,0:T(8,128)} async-done(((f32[2048,256]{1,0:T(8,128)}), f32[128,256]{1,0:T(8,128)}) %reduce-scatter.41.cloned.1.call-update) | async-done | bytes 131088 | tf_op jit(solution)/shard_map/reduce_scatter | solution.py:384
  2527.5 345.4 %reduce-scatter.43.cloned.1.call-done = f32[128,2048]{1,0:T(8,128)} async-done(((f32[2048,2048]{1,0:T(8,128)}), f32[128,2048]{1,0:T(8,128)}) %reduce-scatter.43.cloned.1.call-update) | async-done | bytes 1048592 | tf_op jit(solution)/shard_map/reduce_scatter | solution.py:390
  2872.9 354.2 %reduce-scatter.37.cloned.1.call-done = f32[128,2048]{1,0:T(8,128)} async-done(((f32[2048,2048]{1,0:T(8,128)}), f32[128,2048]{1,0:T(8,128)}) %reduce-scatter.37.cloned.1.call-update) | async-done | bytes 1048592 | tf_op jit(solution)/shard_map/reduce_scatter | solution.py:372
  3229.0 352.5 %reduce-scatter.23.cloned.1.call-done = f32[128,2048]{1,0:T(8,128)} async-done(((f32[2048,2048]{1,0:T(8,128)}), f32[128,2048]{1,0:T(8,128)}) %reduce-scatter.23.cloned.1.call-update) | async-done | bytes 1048592 | tf_op jit(solution)/shard_map/reduce_scatter | solution.py:213
  3584.2 6.4 fusion.180
  3594.5 79.4 %all-reduce.2 = (f32[2048]{0:T(1024)S(1)}, f32[2048]{0:T(1024)S(1)}) all-reduce(f32[2048]{0:T(1024)S(1)} %get-tuple-element.580, f32[2048]{0:T(1024)S(1)} %copy-done.70), channel_id=10, replica_groups=mesh['fsdp'=16,'dp'=2] {'fsdp'}, use_global_device_ids=true, to_apply=%region_25.26.clone | all-reduce | flops 4096 | bytes 32768
  3674.0 3.1 fusion.98
  3677.1 66.1 %reduce-scatter.55.cloned.1.call-done = f32[16,256]{1,0:T(8,128)} async-done(((f32[256,256]{1,0:T(8,128)}), f32[16,256]{1,0:T(8,128)}) %reduce-scatter.55.cloned.1.call-update) | async-done | bytes 16400 | tf_op jit(solution)/shard_map/reduce_scatter | solution.py:421
  3743.2 4.8 all-reduce.3
  3748.1 104.0 %all-reduce.7.cloned.1.call-done = (f32[128,2048]{1,0:T(8,128)}, f32[128,256]{1,0:T(8,128)}, f32[128,256]{1,0:T(8,128)}, f32[128,2048]{1,0:T(8,128)}, f32[1024,2...) async-done(((f32[128,2048]{1,0:T(8,128)}, ...) | async-done | bytes 31850512 | tf_op jit(solution)/shard_map/psum | solution.py:454
  3852.0 8.0 slice.89
  3861.6 4.4 slice.90
  3866.1 4.4 slice.91
  (390 shorter events, 118.7 us)
Async XLA Ops:
  7.2 466.8 %copy-start = (bf16[2048,256]{1,0:T(8,128)(2,1)S(1)}, bf16[2048,256]{1,0:T(8,128)(2,1)}, u32[]{:S(2)}) copy-start(bf16[2048,256]{1,0:T(8,128)(2,1)} %param.55) | copy-start | bytes 3145732
  7.3 61.4 %all-gather.13.cloned.1.call-start = ((), (), s32[]{:S(2)}) async-start(), calls=%async_computation.22 | async-start | bytes 1114112 | tf_op jit(solution)/shard_map/all_gather | solution.py:98
  8.0 117.4 %all-gather.19.cloned.1.call-start = ((), (), s32[]{:S(2)}) async-start(), calls=%async_computation.25 | async-start | bytes 1114112 | tf_op jit(solution)/shard_map/all_gather | solution.py:99
  8.7 230.6 %all-gather.17.cloned.1.call-start = ((), (), s32[]{:S(2)}) async-start(), calls=%async_computation.24 | async-start | bytes 8912896 | tf_op jit(solution)/shard_map/all_gather | solution.py:97
  9.5 286.3 %all-gather.15.cloned.1.call-start = ((), (), s32[]{:S(2)}) async-start(), calls=%async_computation.23 | async-start | bytes 1114112 | tf_op jit(solution)/shard_map/all_gather | solution.py:126
  10.9 116.1 %copy-start.78 = (f32[128]{0:T(128)}, f32[128]{0:T(128)S(1)}, u32[]{:S(2)}) copy-start(f32[128]{0:T(128)S(1)} %negate_power_fusion) | copy-start | bytes 1540
  11.2 115.8 %copy-start.74 = (f32[128]{0:T(128)}, f32[128]{0:T(128)S(1)}, u32[]{:S(2)}) copy-start(f32[128]{0:T(128)S(1)} %get-tuple-element.692) | copy-start | bytes 1540
  13.0 226.4 %copy-start.68 = (f32[128]{0:T(128)}, f32[128]{0:T(128)S(1)}, u32[]{:S(2)}) copy-start(f32[128]{0:T(128)S(1)} %fusion.146) | copy-start | bytes 1540
  13.0 114.0 %copy-start.42 = (bf16[256,256]{1,0:T(8,128)(2,1)S(1)}, bf16[256,256]{1,0:T(8,128)(2,1)}, u32[]{:S(2)}) copy-start(bf16[256,256]{1,0:T(8,128)(2,1)} %param.50) | copy-start | bytes 393220
  14.8 115.7 %copy-start.27 = (bf16[2048,256]{1,0:T(8,128)(2,1)S(1)}, bf16[2048,256]{1,0:T(8,128)(2,1)}, u32[]{:S(2)}) copy-start(bf16[2048,256]{1,0:T(8,128)(2,1)} %param.45) | copy-start | bytes 3145732
  71.6 281.3 %all-gather.21.cloned.1.call-start = ((), (), s32[]{:S(2)}) async-start(), calls=%async_computation.26 | async-start | bytes 1114112 | tf_op jit(solution)/shard_map/all_gather | solution.py:127
  127.8 338.9 %all-gather.23.cloned.1.call-start = ((), (), s32[]{:S(2)}) async-start(), calls=%async_computation.27 | async-start | bytes 8912896 | tf_op jit(solution)/shard_map/all_gather | solution.py:100
  128.4 451.6 %all-gather.33.cloned.1.call-start = ((), (), s32[]{:S(2)}) async-start(), calls=%async_computation.54 | async-start | bytes 8912896 | tf_op jit(solution)/shard_map/all_gather | solution.py:231
  129.1 564.7 %all-gather.25.cloned.1.call-start = ((), (), s32[]{:S(2)}) async-start(), calls=%async_computation.28 | async-start | bytes 8912896 | tf_op jit(solution)/shard_map/all_gather | solution.py:196
  130.9 113.1 %copy-start.52 = (bf16[128,256]{1,0:T(8,128)(2,1)}, bf16[128,256]{1,0:T(8,128)(2,1)S(1)}, u32[]{:S(2)}) copy-start(bf16[128,256]{1,0:T(8,128)(2,1)S(1)} %convolution_convert_fusion.7) | copy-start | bytes 196612
  131.0 115.9 %copy-start.38 = (f32[128,128]{0,1:T(8,128)}, f32[128,128]{0,1:T(8,128)S(1)}, u32[]{:S(2)}) copy-start(f32[128,128]{0,1:T(8,128)S(1)} %copy.83) | copy-start | bytes 196612
  131.1 112.9 %copy-start.18 = (bf16[256,2048]{1,0:T(8,128)(2,1)S(1)}, bf16[256,2048]{1,0:T(8,128)(2,1)}, u32[]{:S(2)}) copy-start(bf16[256,2048]{1,0:T(8,128)(2,1)} %param.46) | copy-start | bytes 3145732
  357.2 114.3 %copy-start.4 = (bf16[128,8,256]{2,0,1:T(8,128)(2,1)}, bf16[128,8,256]{2,0,1:T(8,128)(2,1)S(1)}, u32[]{:S(2)}) copy-start(bf16[128,8,256]{2,0,1:T(8,128)(2,1)S(1)} %get-tuple-element.1271) | copy-start | bytes 1572868
  357.2 114.3 %copy-start.54 = (s32[128]{0:T(128)}, s32[128]{0:T(128)S(1)}, u32[]{:S(2)}) copy-start(s32[128]{0:T(128)S(1)} %get-tuple-element.1366) | copy-start | bytes 1540
  357.2 114.3 %copy-start.76 = (f32[128,8,1]{0,1,2:T(8,128)}, f32[128,8,1]{0,1,2:T(8,128)S(1)}, u32[]{:S(2)}) copy-start(f32[128,8,1]{0,1,2:T(8,128)S(1)} %get-tuple-element.1409) | copy-start | bytes 12292
  358.9 112.6 %copy-start.10 = (bf16[128,8,256]{0,2,1:T(8,128)(2,1)}, bf16[128,8,256]{0,2,1:T(8,128)(2,1)S(1)}, u32[]{:S(2)}) copy-start(bf16[128,8,256]{0,2,1:T(8,128)(2,1)S(1)} %copy.89) | copy-start | bytes 1572868
  360.7 110.8 %copy-start.36 = (bf16[128,256]{1,0:T(8,128)(2,1)}, bf16[128,256]{1,0:T(8,128)(2,1)S(1)}, u32[]{:S(2)}) copy-start(bf16[128,256]{1,0:T(8,128)(2,1)S(1)} %convolution_convert_fusion.5) | copy-start | bytes 196612
  360.7 112.2 %copy-start.56 = (f32[2048]{0:T(1024)S(1)}, f32[2048]{0:T(1024)}, u32[]{:S(2)}) copy-start(f32[2048]{0:T(1024)} %param.37) | copy-start | bytes 24580
  472.0 122.6 %copy-start.84 = (f32[128]{0:T(128)}, f32[128]{0:T(128)S(1)}, u32[]{:S(2)}) copy-start(f32[128]{0:T(128)S(1)} %get-tuple-element.712) | copy-start | bytes 1540
  472.0 122.5 %copy-start.71 = (f32[128]{0:T(128)}, f32[128]{0:T(128)S(1)}, u32[]{:S(2)}) copy-start(f32[128]{0:T(128)S(1)} %fusion.147) | copy-start | bytes 1540
  473.9 276.5 %all-gather.29.cloned.1.call-start = ((), (), s32[]{:S(2)}) async-start(), calls=%async_computation.30 | async-start | bytes 1114112 | tf_op jit(solution)/shard_map/all_gather | solution.py:198
  476.0 331.6 %all-gather.27.cloned.1.call-start = ((), (), s32[]{:S(2)}) async-start(), calls=%async_computation.29 | async-start | bytes 1114112 | tf_op jit(solution)/shard_map/all_gather | solution.py:197
  478.4 386.5 %all-gather.31.cloned.1.call-start = ((), (), s32[]{:S(2)}) async-start(), calls=%async_computation.33 | async-start | bytes 1114112 | tf_op jit(solution)/shard_map/all_gather | solution.py:232
  479.7 487.3 %reduce-scatter.29.cloned.1.call-start = ((), (), s32[]{:S(2)}) async-start(), calls=%async_computation.35 | async-start | bytes 2228224 | tf_op jit(solution)/shard_map/reduce_scatter | solution.py:248
  886.4 425.8 %reduce-scatter.27.cloned.1.call-start = ((), (), s32[]{:S(2)}) async-start(), calls=%async_computation.34 | async-start | bytes 17825792 | tf_op jit(solution)/shard_map/reduce_scatter | solution.py:241
  919.5 482.0 %reduce-scatter.31.cloned.1.call-start = ((), (), s32[]{:S(2)}) async-start(), calls=%async_computation.36 | async-start | bytes 2228224 | tf_op jit(solution)/shard_map/reduce_scatter | solution.py:254
  924.5 557.8 %reduce-scatter.25.cloned.1.call-start = ((), (), s32[]{:S(2)}) async-start(), calls=%async_computation.32 | async-start | bytes 2228224 | tf_op jit(solution)/shard_map/reduce_scatter | solution.py:219
  929.4 472.0 %copy-start.7 = (f32[128,2048]{1,0:T(8,128)S(1)}, f32[128,2048]{1,0:T(8,128)}, u32[]{:S(2)}) copy-start(f32[128,2048]{1,0:T(8,128)} %copy-done.6) | copy-start | bytes 3145732
  929.4 472.0 %copy-start.57 = (f32[2048]{0:T(1024)S(1)}, f32[2048]{0:T(1024)}, u32[]{:S(2)}) copy-start(f32[2048]{0:T(1024)} %param.37) | copy-start | bytes 24580
  929.4 472.0 %copy-start.72 = (f32[128]{0:T(128)S(1)}, f32[128]{0:T(128)}, u32[]{:S(2)}) copy-start(f32[128]{0:T(128)} %copy-done.71) | copy-start | bytes 1540
  929.4 474.6 %copy-start.85 = (f32[128]{0:T(128)S(1)}, f32[128]{0:T(128)}, u32[]{:S(2)}) copy-start(f32[128]{0:T(128)} %copy-done.84) | copy-start | bytes 1540
  929.4 474.6 %copy-start.13 = (bf16[1,128,2048]{2,1,0:T(8,128)(2,1)S(1)}, bf16[1,128,2048]{2,1,0:T(8,128)(2,1)}, u32[]{:S(2)}) copy-start(bf16[1,128,2048]{2,1,0:T(8,128)(2,1)} %param.59) | copy-start | bytes 1572868
  929.5 633.6 %reduce-scatter.33.cloned.1.call-start = ((), (), s32[]{:S(2)}) async-start(), calls=%async_computation.37 | async-start | bytes 2228224 | tf_op jit(solution)/shard_map/reduce_scatter | solution.py:340
  1426.7 216.6 %reduce-scatter.35.cloned.1.call-start = ((), (), s32[]{:S(2)}) async-start(), calls=%async_computation.38 | async-start | bytes 2228224 | tf_op jit(solution)/shard_map/reduce_scatter | solution.py:341
  1427.3 305.7 %reduce-scatter.61.cloned.1.call-start = ((), (), s32[]{:S(2)}) async-start(), calls=%async_computation.51 | async-start | bytes 2228224 | tf_op jit(solution)/shard_map/reduce_scatter | solution.py:429
  1429.5 374.3 %reduce-scatter.63.cloned.1.call-start = ((), (), s32[]{:S(2)}) async-start(), calls=%async_computation.52 | async-start | bytes 2228224 | tf_op jit(solution)/shard_map/reduce_scatter | solution.py:430
  1431.5 452.5 %reduce-scatter.65.cloned.1.call-start = ((), (), s32[]{:S(2)}) async-start(), calls=%async_computation.53 | async-start | bytes 2228224 | tf_op jit(solution)/shard_map/reduce_scatter | solution.py:431
  1485.0 479.4 %reduce-scatter.57.cloned.1.call-start = ((), (), s32[]{:S(2)}) async-start(), calls=%async_computation.49 | async-start | bytes 2228224 | tf_op jit(solution)/shard_map/reduce_scatter | solution.py:427
  1486.8 558.0 %reduce-scatter.59.cloned.1.call-start = ((), (), s32[]{:S(2)}) async-start(), calls=%async_computation.50 | async-start | bytes 2228224 | tf_op jit(solution)/shard_map/reduce_scatter | solution.py:428
  1488.7 636.7 %reduce-scatter.39.cloned.1.call-start = ((), (), s32[]{:S(2)}) async-start(), calls=%async_computation.40 | async-start | bytes 2228224 | tf_op jit(solution)/shard_map/reduce_scatter | solution.py:378
  1566.1 639.7 %reduce-scatter.49.cloned.1.call-start = ((), (), s32[]{:S(2)}) async-start(), calls=%async_computation.45 | async-start | bytes 2228224 | tf_op jit(solution)/shard_map/reduce_scatter | solution.py:403
  1568.3 717.8 %reduce-scatter.45.cloned.1.call-start = ((), (), s32[]{:S(2)}) async-start(), calls=%async_computation.43 | async-start | bytes 2228224 | tf_op jit(solution)/shard_map/reduce_scatter | solution.py:391
  1571.4 85.0 %copy-start.14 = (bf16[128,8,256]{0,2,1:T(8,128)(2,1)}, bf16[128,8,256]{0,2,1:T(8,128)(2,1)S(1)}, u32[]{:S(2)}) copy-start(bf16[128,8,256]{0,2,1:T(8,128)(2,1)S(1)} %maximum_convert_fusion) | copy-start | bytes 1572868
  1575.2 791.2 %reduce-scatter.47.cloned.1.call-start = ((), (), s32[]{:S(2)}) async-start(), calls=%async_computation.44 | async-start | bytes 2228224 | tf_op jit(solution)/shard_map/reduce_scatter | solution.py:397
  1577.1 869.4 %reduce-scatter.53.cloned.1.call-start = ((), (), s32[]{:S(2)}) async-start(), calls=%async_computation.47 | async-start | bytes 2228224 | tf_op jit(solution)/shard_map/reduce_scatter | solution.py:415
  1646.3 881.2 %reduce-scatter.41.cloned.1.call-start = ((), (), s32[]{:S(2)}) async-start(), calls=%async_computation.41 | async-start | bytes 2228224 | tf_op jit(solution)/shard_map/reduce_scatter | solution.py:384
  1648.3 1224.6 %reduce-scatter.43.cloned.1.call-start = ((), (), s32[]{:S(2)}) async-start(), calls=%async_computation.42 | async-start | bytes 17825792 | tf_op jit(solution)/shard_map/reduce_scatter | solution.py:390
  1656.4 1570.7 %reduce-scatter.37.cloned.1.call-start = ((), (), s32[]{:S(2)}) async-start(), calls=%async_computation.39 | async-start | bytes 17825792 | tf_op jit(solution)/shard_map/reduce_scatter | solution.py:372
  1664.7 1916.8 %reduce-scatter.23.cloned.1.call-start = ((), (), s32[]{:S(2)}) async-start(), calls=%async_computation.31 | async-start | bytes 17825792 | tf_op jit(solution)/shard_map/reduce_scatter | solution.py:213
  1680.0 1997.1 %reduce-scatter.51.cloned.1.call-start = ((), (), s32[]{:S(2)}) async-start(), calls=%async_computation.46 | async-start | bytes 278528 | tf_op jit(solution)/shard_map/reduce_scatter | solution.py:409
  1698.8 2044.5 %reduce-scatter.55.cloned.1.call-start = ((), (), s32[]{:S(2)}) async-start(), calls=%async_computation.48 | async-start | bytes 278528 | tf_op jit(solution)/shard_map/reduce_scatter | solution.py:421
  1715.4 2136.6 %all-reduce.7.cloned.1.call-start = ((), (), s32[]{:S(2)}) async-start(), calls=%async_computation.55 | async-start | bytes 63700992 | tf_op jit(solution)/shard_map/psum | solution.py:454
  3227.1 354.4 %copy-start.8 = (f32[128,2048]{1,0:T(8,128)S(1)}, f32[128,2048]{1,0:T(8,128)}, u32[]{:S(2)}) copy-start(f32[128,2048]{1,0:T(8,128)} %copy-done.6) | copy-start | bytes 3145732
  3227.1 354.4 %copy-start.46 = (f32[128,256]{1,0:T(8,128)S(1)}, f32[128,256]{1,0:T(8,128)}, u32[]{:S(2)}) copy-start(f32[128,256]{1,0:T(8,128)} %reduce-scatter.25.cloned.1.call-done) | copy-start | bytes 393220
  3227.1 357.0 %copy-start.15 = (bf16[128,8,256]{0,2,1:T(8,128)(2,1)S(1)}, bf16[128,8,256]{0,2,1:T(8,128)(2,1)}, u32[]{:S(2)}) copy-start(bf16[128,8,256]{0,2,1:T(8,128)(2,1)} %copy-done.14) | copy-start | bytes 1572868
  3592.4 81.6 %copy-start.83 = (f32[128]{0:T(128)S(1)}, f32[128]{0:T(128)}, u32[]{:S(2)}) copy-start(f32[128]{0:T(128)} %copy-done.82) | copy-start | bytes 1540
  3592.4 81.6 %copy-start.58 = (f32[2048]{0:T(1024)S(1)}, f32[2048]{0:T(1024)}, u32[]{:S(2)}) copy-start(f32[2048]{0:T(1024)} %param.37) | copy-start | bytes 24580
  3592.4 81.6 %copy-start.73 = (f32[128]{0:T(128)S(1)}, f32[128]{0:T(128)}, u32[]{:S(2)}) copy-start(f32[128]{0:T(128)} %copy-done.71) | copy-start | bytes 1540
  3592.4 81.6 %copy-start.81 = (f32[128]{0:T(128)S(1)}, f32[128]{0:T(128)}, u32[]{:S(2)}) copy-start(f32[128]{0:T(128)} %copy-done.80) | copy-start | bytes 1540
  (65 other events, 1302.6 us)
Sparse Core Ops, SparseCore 0:
  10.8 57.7 all-gather.12
  71.4 53.9 all-gather.18
  128.2 111.1 all-gather.16
  242.5 53.2 all-gather.14
  299.0 53.9 all-gather.20
  355.6 111.1 all-gather.22
  469.5 110.4 all-gather.32
  583.3 110.4 all-gather.24
  697.2 53.2 all-gather.28
  753.6 53.9 all-gather.26
  810.9 53.9 all-gather.30
  886.5 80.3 reduce-scatter.28
  969.2 342.9 reduce-scatter.26
  1314.4 87.0 reduce-scatter.30
  1404.1 78.0 reduce-scatter.24
  1484.9 78.0 reduce-scatter.32
  1565.1 78.1 reduce-scatter.34
  1645.4 77.9 reduce-scatter.60
  1725.7 78.0 reduce-scatter.62
  1805.9 77.9 reduce-scatter.64
  1886.3 78.0 reduce-scatter.56
  1966.6 78.1 reduce-scatter.58
  2047.6 77.7 reduce-scatter.38
  2127.6 78.1 reduce-scatter.48
  2208.1 77.9 reduce-scatter.44
  2288.2 78.1 reduce-scatter.46
  2368.5 77.9 reduce-scatter.52
  2449.4 78.0 reduce-scatter.40
  2529.8 343.0 reduce-scatter.42
  2875.0 352.0 reduce-scatter.36
  3229.4 352.0 reduce-scatter.22
  3584.3 82.7 reduce-scatter.50
  3669.8 73.3 reduce-scatter.54
  3747.4 104.5 all-reduce.6
where the time goes:
time: 3900 us; the launch traced here: 3890 us
  waiting for transfers between devices  3430 us (88%)
  matrix products  293 us (8%)
  blocking collectives  84.2 us (2%)
  local copies, waits for them, and re-layouts  53.1 us (1%)
    reduce_scatter x1, waiting for transfers between devices, local(): lax.psum_scatter(left_matrix_product(attention_input, query_linear_gradie...  354 us
    reduce_scatter x1, waiting for transfers between devices, local(): lax.psum_scatter(matrix_product(hidden_activated_value, down_matrix), 'fs...  352 us
    reduce_scatter x1, waiting for transfers between devices, local(): lax.psum_scatter(grad_output_weight_term, 'fsdp', scatter_dimension=0, ti...  345 us
    reduce_scatter x1, waiting for transfers between devices, local(): lax.psum_scatter(matrix_product(gate_output_gradient, gate_matrix) + matr...  345 us
    all_gather x1, waiting for transfers between devices, local(): lax.all_gather(query_matrix, 'fsdp', axis=0, tiled=True)  108 us
    all_gather x1, waiting for transfers between devices, local(): lax.all_gather(output_matrix, 'fsdp', axis=0, tiled=True)  106 us
    psum x1, waiting for transfers between devices, local(): lax.psum((shard_terms[0], shard_terms[1], shard_terms[2], shard_terms[3],...  104 us
    all_gather x1, waiting for transfers between devices, local(): lax.all_gather(branch_gradient, 'fsdp', axis=0, tiled=True)  100 us
  transfers between devices with their start and end apart: 34, of which 32 were waited for; matrix products, arithmetic and copies ran while one was open for 8% of the time, Pallas kernels for 0%

commit v1 on v0

v1 whole, which is shorter than its diff:
```python
import jax
import jax.numpy as jnp
from jax import lax
from jax.sharding import PartitionSpec as P

EPS = 1e-06


def matrix_product(left, right):
    return jnp.dot(left, right, preferred_element_type=jnp.float32)


def left_matrix_product(left, right):
    return lax.dot_general(
        left, right, (((0,), (0,)), ((), ())), preferred_element_type=jnp.float32
    )


def right_product(left, right):
    return lax.dot_general(
        left, right, (((1,), (1,)), ((), ())), preferred_element_type=jnp.float32
    )


def rms_norm(values, gain):
    factor = lax.rsqrt(jnp.mean(values * values, axis=-1, keepdims=True) + EPS)
    return values * factor * gain


def rotate(values, cosines, sines):
    half = values.shape[-1] // 2
    first = values[..., :half]
    second = values[..., half:]
    return jnp.concatenate(
        [first * cosines - second * sines, second * cosines + first * sines], axis=-1
    )


def doc_positions(segments):
    length = segments.shape[0]
    index = jnp.arange(length, dtype=jnp.int32)
    starts = jnp.concatenate([jnp.ones((1,), dtype=bool), segments[1:] != segments[:-1]])
    first = lax.cummax(jnp.where(starts, index, jnp.zeros_like(index)), axis=0)
    return index - first


def geglu(gate, up):
    return jax.nn.gelu(gate, approximate=True) * up


def gather_shared(first, second, core):
    own = jnp.where(core == 0, first, second)
    gathered = lax.all_gather(own, "fsdp", axis=0, tiled=True)
    return gathered, lax.ppermute(gathered, "dp", [(0, 1), (1, 0)])


def scatter_shared(terms, core):
    half = terms.shape[2] // 2
    swap = [(0, 1), (1, 0)]
    own = lax.dynamic_slice_in_dim(terms, core * half, half, 2)
    away = lax.dynamic_slice_in_dim(terms, (1 - core) * half, half, 2)
    both = own + lax.ppermute(away, "dp", swap)
    mine = lax.psum_scatter(both, "fsdp", scatter_dimension=0, tiled=False)
    theirs = lax.ppermute(mine, "dp", swap)
    return jnp.where(
        core == 0,
        jnp.concatenate([mine, theirs], axis=1),
        jnp.concatenate([theirs, mine], axis=1),
    )


def local(
    tokens,
    segment_ids,
    gain_attn,
    gain_mlp,
    query_matrix,
    key_matrix,
    value_matrix,
    output_matrix,
    gate_matrix,
    upward_matrix,
    down_matrix,
    query_factor_first,
    query_factor_second,
    key_factor_first,
    key_factor_second,
    value_factor_first,
    value_factor_second,
    output_factor_first,
    output_factor_second,
    gate_factor_first,
    gate_factor_second,
    upward_factor_first,
    upward_factor_second,
    down_factor_first,
    down_factor_second,
    cotangent,
):
    bf16 = jnp.bfloat16
    f32 = jnp.float32
    tok_rows = tokens.shape[1]
    width = tokens.shape[2]
    length = segment_ids.shape[1]
    head_size = key_matrix.shape[1]
    heads = query_matrix.shape[1] // head_size
    unit_rows = gate_matrix.shape[0]
    in_rows = query_matrix.shape[0]
    shards = length // tok_rows
    rank = query_factor_first.shape[1]
    place = lax.axis_index("fsdp")
    core = lax.axis_index("dp")
    offset = place * tok_rows
    input_rows = tokens[0].astype(f32)
    seg_all = segment_ids[0]
    seg_own = lax.dynamic_slice_in_dim(seg_all, offset, tok_rows, 0)
    positions = lax.dynamic_slice_in_dim(doc_positions(seg_all), offset, tok_rows, 0)
    half = head_size // 2
    inverse = 10000.0 ** (-(jnp.arange(half, dtype=f32) * 2.0 / head_size))
    angles = positions.astype(f32)[:, None] * inverse[None, :]
    cosines = jnp.cos(angles)
    sines = jnp.sin(angles)

    def merged_rows(matrix, first, second):
        rows = lax.dynamic_slice_in_dim(first, place * in_rows, in_rows, 0)
        return (matrix.astype(f32) + matrix_product(rows, second)).astype(bf16)

    own_first = jnp.concatenate(
        [
            merged_rows(query_matrix, query_factor_first, query_factor_second),
            merged_rows(key_matrix, key_factor_first, key_factor_second),
        ],
        axis=1,
    )
    own_second = jnp.concatenate(
        [
            merged_rows(output_matrix, output_factor_first, output_factor_second),
            merged_rows(value_matrix, value_factor_first, value_factor_second),
        ],
        axis=1,
    )
    gathered, other = gather_shared(own_first, own_second, core)
    query_key = jnp.where(core == 0, gathered, other)
    output_value = jnp.where(core == 0, other, gathered)
    query_weight = query_key[:, : heads * head_size]
    key_weight = query_key[:, heads * head_size :]
    output_weight = output_value[:, :width]
    value_weight = output_value[:, width:]

    cot_own = cotangent[0]
    cot_all = lax.all_gather(cot_own, "fsdp", axis=0, tiled=True)

    normed_attn, pull_attn = jax.vjp(rms_norm, input_rows, gain_attn)
    attn_in = normed_attn.astype(bf16)
    query_lin = matrix_product(attn_in, query_weight)
    key_lin = matrix_product(attn_in, key_weight)
    value = matrix_product(attn_in, value_weight).astype(bf16)
    query = rotate(
        query_lin.reshape(tok_rows, heads, head_size), cosines[:, None, :], sines[:, None, :]
    ).astype(bf16)
    key = rotate(key_lin, cosines, sines).astype(bf16)
    key_value = lax.all_gather(
        jnp.concatenate([key, value], axis=1), "fsdp", axis=0, tiled=True
    )
    keys_all = key_value[:, :head_size]
    values_all = key_value[:, head_size:]
    block = min(512, length)
    scale = head_size ** (-0.5)
    query_index = offset + jnp.arange(tok_rows, dtype=jnp.int32)
    needed = (offset + tok_rows + block - 1) // block
    first_block = (offset - positions[0]) // block

    def scores_of(start):
        key_block = lax.dynamic_slice_in_dim(keys_all, start, block, 0)
        value_block = lax.dynamic_slice_in_dim(values_all, start, block, 0)
        seg_block = lax.dynamic_slice_in_dim(seg_all, start, block, 0)
        key_index = start + jnp.arange(block, dtype=jnp.int32)
        allowed = (seg_own[:, None] == seg_block[None, :]) & (
            key_index[None, :] <= query_index[:, None]
        )
        allowed = allowed[:, None, :]
        raw = jnp.einsum("thd,kd->thk", query, key_block, preferred_element_type=f32)
        return (jnp.where(allowed, raw * scale, -1e30), allowed, key_block, value_block)

    def max_step(index, carry):
        top, total = carry
        logits, allowed, key_block, value_block = scores_of(index * block)
        new_top = jnp.maximum(top, jnp.max(logits, axis=-1, keepdims=True))
        weights = jnp.where(allowed, jnp.exp(logits - new_top), 0.0)
        return (new_top, total * jnp.exp(top - new_top) + jnp.sum(weights, axis=-1, keepdims=True))

    start_top = jnp.full((tok_rows, heads, 1), -1e30, f32)
    start_total = jnp.zeros((tok_rows, heads, 1), f32)
    top, total = lax.fori_loop(first_block, needed, max_step, (start_top, start_total))
    log_total = top + jnp.log(total)

    def probs_of(start):
        logits, allowed, key_block, value_block = scores_of(start)
        return (jnp.where(allowed, jnp.exp(logits - log_total), 0.0), key_block, value_block)

    def out_step(index, acc):
        probs, key_block, value_block = probs_of(index * block)
        return acc + jnp.einsum(
            "thk,kd->thd", probs.astype(bf16), value_block, preferred_element_type=f32
        )

    attn_raw = lax.fori_loop(
        first_block, needed, out_step, jnp.zeros((tok_rows, heads, head_size), f32)
    )
    attn = attn_raw.reshape(tok_rows, heads * head_size).astype(bf16)
    resid = input_rows + matrix_product(attn, output_weight)
    normed_mlp, pull_mlp = jax.vjp(rms_norm, resid, gain_mlp)
    mlp_in = normed_mlp.astype(bf16)
    mlp_all = lax.all_gather(mlp_in, "fsdp", axis=0, tiled=True)

    first_unit = place * unit_rows
    gate_second = lax.dynamic_slice_in_dim(gate_factor_second, first_unit, unit_rows, 1)
    up_second = lax.dynamic_slice_in_dim(upward_factor_second, first_unit, unit_rows, 1)
    down_first = lax.dynamic_slice_in_dim(down_factor_first, first_unit, unit_rows, 0)

    def merged_units(matrix, first, second):
        low = lax.dot_general(
            second, first, (((0,), (1,)), ((), ())), preferred_element_type=f32
        )
        return (matrix.astype(f32) + low).astype(bf16)

    gate_weight = merged_units(gate_matrix, gate_factor_first, gate_second)
    up_weight = merged_units(upward_matrix, upward_factor_first, up_second)
    down_weight = (
        down_matrix.astype(f32) + matrix_product(down_first, down_factor_second)
    ).astype(bf16)

    gate = right_product(mlp_all, gate_weight)
    up = right_product(mlp_all, up_weight)
    hidden_full, pull_geglu = jax.vjp(geglu, gate, up)
    hidden = hidden_full.astype(bf16)
    down_sum = lax.psum_scatter(
        matrix_product(hidden, down_weight).astype(bf16), "fsdp", scatter_dimension=0, tiled=True
    )
    grad_hidden = right_product(cot_all, down_weight)
    grad_gate_full, grad_up_full = pull_geglu(grad_hidden)
    grad_gate = grad_gate_full.astype(bf16)
    grad_up = grad_up_full.astype(bf16)
    grad_mlp_in = lax.psum_scatter(
        (matrix_product(grad_gate, gate_weight) + matrix_product(grad_up, up_weight)).astype(bf16),
        "fsdp",
        scatter_dimension=0,
        tiled=True,
    ).astype(f32)
    gate_rows = left_matrix_product(grad_gate, mlp_all)
    up_rows = left_matrix_product(grad_up, mlp_all)
    down_rows = left_matrix_product(hidden, cot_all)
    gate_rows_low = gate_rows.astype(bf16)
    up_rows_low = up_rows.astype(bf16)
    down_rows_low = down_rows.astype(bf16)
    swap = [(0, 1), (1, 0)]
    g_gate_rows = gate_rows + lax.ppermute(gate_rows_low, "dp", swap).astype(f32)
    g_up_rows = up_rows + lax.ppermute(up_rows_low, "dp", swap).astype(f32)
    g_down_rows = down_rows + lax.ppermute(down_rows_low, "dp", swap).astype(f32)

    def columns_of(first, rows):
        return lax.dot_general(
            first, rows.astype(bf16), (((0,), (1,)), ((), ())), preferred_element_type=f32
        )

    g_gate_out = columns_of(gate_factor_first, g_gate_rows)
    g_up_out = columns_of(upward_factor_first, g_up_rows)
    g_down_in = right_product(g_down_rows.astype(bf16), down_factor_second)
    gate_in_term = lax.dot_general(
        gate_rows_low, gate_second, (((0,), (1,)), ((), ())), preferred_element_type=f32
    )
    up_in_term = lax.dot_general(
        up_rows_low, up_second, (((0,), (1,)), ((), ())), preferred_element_type=f32
    )
    down_out_term = left_matrix_product(down_first, down_rows_low)

    output = (resid + down_sum.astype(f32)).astype(bf16)
    grad_resid_norm, gain_mlp_term = pull_mlp(grad_mlp_in)
    grad_resid = cot_own.astype(f32) + grad_resid_norm
    grad_branch = grad_resid.astype(bf16)
    grad_attn = right_product(grad_branch, output_weight).astype(bf16)
    lora_output = matrix_product(attn, output_factor_first).astype(bf16)
    lora_query = matrix_product(attn_in, query_factor_first).astype(bf16)
    lora_key = matrix_product(attn_in, key_factor_first).astype(bf16)
    lora_value = matrix_product(attn_in, value_factor_first).astype(bf16)
    grad_attn_heads = grad_attn.reshape(tok_rows, heads, head_size)
    delta = jnp.sum(
        grad_attn_heads.astype(f32) * attn_raw, axis=-1, keepdims=True
    )

    def grad_step(index, carry):
        grad_query_acc, key_terms = carry
        start = index * block
        probs, key_block, value_block = probs_of(start)
        grad_probs = jnp.einsum(
            "thd,kd->thk", grad_attn_heads, value_block, preferred_element_type=f32
        )
        grad_scores = (scale * probs * (grad_probs - delta)).astype(bf16)
        grad_query_acc = grad_query_acc + jnp.einsum(
            "thk,kd->thd", grad_scores, key_block, preferred_element_type=f32
        )
        key_part = jnp.einsum("thk,thd->kd", grad_scores, query, preferred_element_type=f32)
        value_part = jnp.einsum(
            "thk,thd->kd", probs.astype(bf16), grad_attn_heads, preferred_element_type=f32
        )
        both = jnp.concatenate([key_part, value_part], axis=1).astype(bf16)
        key_terms = lax.dynamic_update_slice_in_dim(key_terms, both, start, 0)
        return (grad_query_acc, key_terms)

    grad_query_rot, key_terms = lax.fori_loop(
        first_block,
        needed,
        grad_step,
        (
            jnp.zeros((tok_rows, heads, head_size), f32),
            jnp.zeros((length, 2 * head_size), bf16),
        ),
    )
    key_sums = lax.psum_scatter(key_terms, "fsdp", scatter_dimension=0, tiled=True).astype(f32)
    grad_query_lin = (
        rotate(grad_query_rot, cosines[:, None, :], -sines[:, None, :])
        .reshape(tok_rows, heads * head_size)
        .astype(bf16)
    )
    grad_key_lin = rotate(key_sums[:, :head_size], cosines, -sines).astype(bf16)
    grad_value_lin = key_sums[:, head_size:].astype(bf16)
    grad_attn_in = (
        right_product(grad_query_lin, query_weight)
        + right_product(grad_key_lin, key_weight)
        + right_product(grad_value_lin, value_weight)
    )
    grad_inputs_norm, gain_attn_term = pull_attn(grad_attn_in)
    grad_inputs = grad_resid + grad_inputs_norm

    def low_term(left, right):
        return left_matrix_product(left, right).astype(bf16)

    per = in_rows
    few = rank // shards
    narrow = jnp.concatenate(
        [
            low_term(attn_in, grad_key_lin),
            low_term(attn_in, grad_value_lin),
            gate_in_term.astype(bf16),
            up_in_term.astype(bf16),
        ],
        axis=1,
    ).reshape(shards, 2, per // 2, 4 * head_size)
    tiny = jnp.concatenate(
        [
            low_term(lora_key, grad_key_lin).reshape(shards, few, head_size),
            low_term(lora_value, grad_value_lin).reshape(shards, few, head_size),
            gain_attn_term.astype(bf16).reshape(shards, few, -1),
            gain_mlp_term.astype(bf16).reshape(shards, few, -1),
        ],
        axis=2,
    )
    tiny = jnp.pad(tiny, ((0, 0), (0, 0), (0, width - tiny.shape[2])))
    terms = jnp.concatenate(
        [
            low_term(attn_in, grad_query_lin).reshape(shards, per, width),
            low_term(attn, grad_branch).reshape(shards, per, width),
            low_term(lora_query, grad_query_lin).reshape(shards, few, width),
            low_term(lora_output, grad_branch).reshape(shards, few, width),
            down_out_term.astype(bf16).reshape(shards, few, width),
            jnp.concatenate([narrow[:, 0], narrow[:, 1]], axis=2),
            tiny,
        ],
        axis=1,
    )
    sums = scatter_shared(terms, core).astype(f32)
    at = [0]

    def take(rows):
        at[0] += rows
        return sums[at[0] - rows : at[0]]

    g_query_weight = take(per)
    g_output_weight = take(per)
    g_query_out = take(few)
    g_output_out = take(few)
    g_down_out = take(few)
    pair = take(per // 2)
    pair = jnp.concatenate([pair[:, : width // 2], pair[:, width // 2 :]], axis=0)
    g_key_weight = pair[:, :head_size]
    g_value_weight = pair[:, head_size : 2 * head_size]
    g_gate_in = pair[:, 2 * head_size : 3 * head_size]
    g_up_in = pair[:, 3 * head_size :]
    last = take(few)
    g_key_out = last[:, :head_size]
    g_value_out = last[:, head_size : 2 * head_size]
    each = per // few
    g_gain_attn = last[:, 2 * head_size : 2 * head_size + each].reshape(per)
    g_gain_mlp = last[:, 2 * head_size + each : 2 * head_size + 2 * each].reshape(per)
    g_query_in = right_product(g_query_weight.astype(bf16), query_factor_second)
    g_output_in = right_product(g_output_weight.astype(bf16), output_factor_second)
    g_key_in = right_product(g_key_weight.astype(bf16), key_factor_second)
    g_value_in = right_product(g_value_weight.astype(bf16), value_factor_second)
    return (
        output[None],
        grad_inputs[None],
        g_gain_attn,
        g_gain_mlp,
        g_query_weight,
        g_key_weight,
        g_value_weight,
        g_output_weight,
        g_gate_rows,
        g_up_rows,
        g_down_rows,
        g_query_in,
        g_query_out,
        g_key_in,
        g_key_out,
        g_value_in,
        g_value_out,
        g_output_in,
        g_output_out,
        g_gate_in,
        g_gate_out,
        g_up_in,
        g_up_out,
        g_down_in,
        g_down_out,
    )


def solution(mesh):
    in_specs = (
        P("dp", "fsdp", None),
        P("dp", None),
        P(),
        P(),
        P("fsdp", None),
        P("fsdp", None),
        P("fsdp", None),
        P("fsdp", None),
        P("fsdp", None),
        P("fsdp", None),
        P("fsdp", None),
        P(),
        P(),
        P(),
        P(),
        P(),
        P(),
        P(),
        P(),
        P(),
        P(),
        P(),
        P(),
        P(),
        P(),
        P("dp", "fsdp", None),
    )
    out_specs = (
        P("dp", "fsdp", None),
        P("dp", "fsdp", None),
        P("fsdp"),
        P("fsdp"),
        P("fsdp", None),
        P("fsdp", None),
        P("fsdp", None),
        P("fsdp", None),
        P("fsdp", None),
        P("fsdp", None),
        P("fsdp", None),
        P("fsdp", None),
        P("fsdp", None),
        P("fsdp", None),
        P("fsdp", None),
        P("fsdp", None),
        P("fsdp", None),
        P("fsdp", None),
        P("fsdp", None),
        P("fsdp", None),
        P(None, "fsdp"),
        P("fsdp", None),
        P(None, "fsdp"),
        P("fsdp", None),
        P("fsdp", None),
    )
    return jax.shard_map(local, mesh=mesh, in_specs=in_specs, out_specs=out_specs, check_vma=False)
```

time: 3900 us -> 1360 us (0.35)
  waiting for transfers between devices: 3430 us -> 883 us
  blocking collectives: 84.2 us -> 0 us
  other arithmetic: 13.2 us -> 81.2 us
  local copies, waits for them, and re-layouts: 53.1 us -> 104 us
    reduce_scatter x21 -> x3, waiting for transfers between devices: 2500 us -> 448 us  [the longest x1 182 us: local(): lax.psum_scatter(matrix_product(hidden, down_weight).astype(bf16), 'fsdp'...]
    all_gather x11 -> x4, waiting for transfers between devices: 750 us -> 347 us  [the longest x1 125 us: gather_shared(): gathered = lax.all_gather(own, 'fsdp', axis=0, tiled=True)]
    psum x1 -> x0, waiting for transfers between devices: 104 us -> none  [local(): lax.psum((shard_terms[0], shard_terms[1], shard_terms[2], shard_terms[3],...]
    unnamed x1 -> x0, blocking collectives: 79.4 us -> none
    add x1 -> x5, other arithmetic: 0.01 us -> 45.6 us  [the longest x1 15.9 us: scatter_shared(): both = own + lax.ppermute(away, 'dp', swap)]
    dot_general x21 -> x12, matrix products: 98 us -> 65.9 us  [matrix_product(): return jnp.dot(left, right, preferred_element_type=jnp.float32)]
    dot_general x18 -> x12, matrix products: 89.5 us -> 70.6 us  [left_matrix_product(): lax.dot_general(left, right, (((0,), (0,)), ((), ())), preferred_element_...]
    dot_general x21 -> x12, matrix products: 91.4 us -> 82.5 us  [right_product(): lax.dot_general(left, right, (((1,), (1,)), ((), ())), preferred_element_...]
  transfers between devices with their start and end apart: 34 -> 14, of which waited for: 32 -> 11; matrix products, arithmetic and copies ran while one was open for 8% -> 18% of each run, Pallas kernels for 0% -> 0%
where the time goes in v1:
time: 1360 us; the launch traced here: 1340 us
  waiting for transfers between devices  883 us (65%)
  matrix products  257 us (19%)
  local copies, waits for them, and re-layouts  104 us (8%)
  other arithmetic  81.2 us (6%)
  between operations  15.4 us (1%)
    reduce_scatter x1, waiting for transfers between devices, local(): lax.psum_scatter(matrix_product(hidden, down_weight).astype(bf16), 'fsdp'...  182 us
    reduce_scatter x1, waiting for transfers between devices, scatter_shared(): mine = lax.psum_scatter(both, 'fsdp', scatter_dimension=0, tiled=False)  155 us
    all_gather x1, waiting for transfers between devices, gather_shared(): gathered = lax.all_gather(own, 'fsdp', axis=0, tiled=True)  125 us
    reduce_scatter x1, waiting for transfers between devices, local(): lax.psum_scatter((matrix_product(grad_gate, gate_weight) + matrix_product...  112 us
    all_gather x1, waiting for transfers between devices, local(): mlp_all = lax.all_gather(mlp_in, 'fsdp', axis=0, tiled=True)  105 us
    all_gather x1, waiting for transfers between devices, local(): cot_all = lax.all_gather(cot_own, 'fsdp', axis=0, tiled=True)  87.3 us
    dot_general x12, matrix products, right_product(): lax.dot_general(left, right, (((1,), (1,)), ((), ())), preferred_element_...  82.5 us
    dot_general x12, matrix products, left_matrix_product(): lax.dot_general(left, right, (((0,), (0,)), ((), ())), preferred_element_...  70.6 us
  transfers between devices with their start and end apart: 14, of which 11 were waited for; matrix products, arithmetic and copies ran while one was open for 18% of the time, Pallas kernels for 0%

profile of v1, /device:TPU:0, one launch (start us, length us, event | category | flops | bytes accessed | tf_op | source)
XLA Modules:
  0.0 1341.1 jit_solution(4143542020887000981)
XLA Ops:
  14.0 124.6 %all-gather.6.cloned.1.call-done = bf16[2048,2304]{1,0:T(8,128)(2,1)} async-done(((bf16[128,2304]{1,0:T(8,128)(2,1)}), bf16[2048,2304]{1,0:T(8,128)(2,1)}) %all-gather.6.cloned.1.call-update) | async-done | bytes 9437200 | tf_op jit(solution)/shard_map/all_gather | solution.py:53
  142.0 11.6 collective-permute-done
  153.6 7.4 broadcast_select_fusion.1
  161.4 3.1 copy-done.2
  164.9 2.5 copy-done.7
  169.8 8.4 slice_bitcast_fusion
  178.3 12.2 copy.92
  190.5 6.4 fusion.131
  198.2 29.5 %all-gather.8.cloned.1.call-done = bf16[2048,512]{1,0:T(8,128)(2,1)} async-done(((bf16[128,512]{1,0:T(8,128)(2,1)}), bf16[2048,512]{1,0:T(8,128)(2,1)}) %all-gather.8.cloned.1.call-update) | async-done | bytes 2097168 | tf_op jit(solution)/shard_map/all_gather | solution.py:162
  227.8 2.6 fusion.210
  233.6 3.0 while.38
  237.0 5.0 multiply_reduce_fusion.1
  244.9 5.8 add_convert_fusion.3
  250.7 4.7 add_convert_fusion.2
  255.4 4.3 add_convert_fusion.1
  259.7 105.3 %all-gather.10.cloned.1.call-done = bf16[2048,2048]{1,0:T(8,128)(2,1)} async-done(((bf16[128,2048]{1,0:T(8,128)(2,1)}), bf16[2048,2048]{1,0:T(8,128)(2,1)}) %all-gather.10.cloned.1.call-update) | async-done | bytes 8388624 | tf_op jit(solution)/shard_map/all_gather | solution.py:214
  365.0 14.7 %fusion.214 = f32[2048,1024]{1,0:T(8,128)} fusion(bf16[2048,2048]{1,0:T(8,128)(2,1)} %all-gather.10.cloned.1.call-done, bf16[1024,2048]{1,0:T(8,128)(2,1)} %add_convert_fusion.3), kind=kOutput, calls=%fused_computation.296 | convolution fusion | flops 8589934592 | bytes 20971520 | tf_op jit(solution)/shard_map/dot_general | solution.py:20
  379.7 11.2 fusion.215
  390.9 87.3 %all-gather.12.cloned.1.call-done = bf16[1,2048,2048]{2,1,0:T(8,128)(2,1)} async-done(((bf16[1,128,2048]{2,1,0:T(8,128)(2,1)}), bf16[1,2048,2048]{2,1,0:T(8,128)(2,1)}) %all-gather.12.cloned.1.call-update) | async-done | bytes 8388624 | tf_op jit(solution)/shard_map/all_gather | solution.py:151
  478.2 25.0 %fusion.56 = (bf16[2048,1024]{1,0:T(8,128)(2,1)}, bf16[2048,1024]{1,0:T(8,128)(2,1)}, bf16[2048,1024]{1,0:T(8,128)(2,1)}) fusion(f32[2048,1024]{1,0:T(8,128)} %fusion.214, f32[2048,1024]{1,0:T(8,128)} %fusion.215, bf16[1024,2048]{1,0:T(8,128)(2,1)} %add_convert_fusion.1, bf16[1,2048,2048]{2,1,0:T(8,128)(2,1)} %all-gather.12.cloned.1.call-done), kind=kOutput, calls=%fused_computation.79 | convolution fusion | flops 8644460544 | bytes 41943040 | tf_op jit(solution)/shard_map/dot_general | solution.py:20
  503.1 14.1 %fusion.216 = f32[2048,2048]{1,0:T(8,128)} fusion(bf16[2048,1024]{1,0:T(8,128)(2,1)} %get-tuple-element.448, bf16[1024,2048]{1,0:T(8,128)(2,1)S(1)} %copy-done.23), kind=kOutput, calls=%fused_computation.298 | convolution fusion | flops 8589934592 | bytes 25165824 | tf_op jit(solution)/shard_map/dot_general | solution.py:10
  517.2 15.8 %add_convert_fusion = bf16[2048,2048]{1,0:T(8,128)(2,1)} fusion(f32[2048,2048]{1,0:T(8,128)} %fusion.216, bf16[2048,1024]{1,0:T(8,128)(2,1)} %get-tuple-element.447, bf16[1024,2048]{1,0:T(8,128)(2,1)S(1)} %copy-done.22), kind=kOutput, calls=%fused_computation.64 | convolution fusion | flops 8598323200 | bytes 33554432 | tf_op jit(solution)/shard_map/dot_general | solution.py:10
  533.1 13.9 %convolution_convert_fusion = bf16[2048,2048]{1,0:T(8,128)(2,1)} fusion(bf16[2048,1024]{1,0:T(8,128)(2,1)} %get-tuple-element.449, bf16[1024,2048]{1,0:T(8,128)(2,1)} %add_convert_fusion.1), kind=kOutput, calls=%fused_computation.92 | convolution fusion | flops 8594128896 | bytes 16777216 | tf_op jit(solution)/shard_map/dot_general | solution.py:10
  549.1 15.1 %fusion.211 = (bf16[1024,2048]{1,0:T(8,128)(2,1)S(1)}, f32[1024,2048]{1,0:T(8,128)}) fusion(bf16[2048,1024]{1,0:T(8,128)(2,1)} %get-tuple-element.449, bf16[1,2048,2048]{2,1,0:T(8,128)(2,1)} %all-gather.12.cloned.1.call-done), kind=kOutput, calls=%fused_computation.293 | convolution fusion | flops 8592031744 | bytes 25165824 | tf_op jit(solution)/shard_map/dot_general | solution.py:14
  566.2 3.4 convolution_convert_fusion.9
  569.6 14.6 %fusion.212 = (bf16[1024,2048]{1,0:T(8,128)(2,1)}, f32[1024,2048]{1,0:T(8,128)}) fusion(bf16[2048,1024]{1,0:T(8,128)(2,1)S(1)} %copy-done.62, bf16[2048,2048]{1,0:T(8,128)(2,1)} %all-gather.10.cloned.1.call-done), kind=kOutput, calls=%fused_computation.294 | convolution fusion | flops 8592031744 | bytes 25165824 | tf_op jit(solution)/shard_map/dot_general | solution.py:14
  584.3 12.7 fusion.213
  597.0 112.3 %reduce-scatter.7.cloned.1.call-done = bf16[128,2048]{1,0:T(8,128)(2,1)} async-done(((bf16[2048,2048]{1,0:T(8,128)(2,1)}), bf16[128,2048]{1,0:T(8,128)(2,1)}) %reduce-scatter.7.cloned.1.call-update) | async-done | bytes 524304 | tf_op jit(solution)/shard_map/reduce_scatter | solution.py:244
  710.7 181.6 %reduce-scatter.5.cloned.1.call-done = bf16[128,2048]{1,0:T(8,128)(2,1)} async-done(((bf16[2048,2048]{1,0:T(8,128)(2,1)}), bf16[128,2048]{1,0:T(8,128)(2,1)}) %reduce-scatter.5.cloned.1.call-update) | async-done | bytes 524304 | tf_op jit(solution)/shard_map/reduce_scatter | solution.py:237
  892.3 2.5 fusion.116
  894.8 6.7 fusion.82
  906.6 9.1 while.39
  910.9 2.8 convolution_add_fusion.9
  916.0 4.6 convolution_convert_fusion.7
  920.6 4.6 convolution_convert_fusion.8
  927.1 3.3 convolution_convert_fusion.6
  930.3 5.8 convolution_convert_fusion.2
  936.2 8.5 constant_dynamic-update-slice_fusion.5
  944.7 5.7 convolution_convert_fusion.1
  950.4 8.5 constant_dynamic-update-slice_fusion.4
  960.0 3.2 convolution_convert_fusion.5
  967.9 49.3 %reduce-scatter.9.cloned.1.call-done = bf16[128,512]{1,0:T(8,128)(2,1)} async-done(((bf16[2048,512]{1,0:T(8,128)(2,1)}), bf16[128,512]{1,0:T(8,128)(2,1)}) %reduce-scatter.9.cloned.1.call-update) | async-done | bytes 131088 | tf_op jit(solution)/shard_map/reduce_scatter | solution.py:319
  1018.4 2.7 fusion.126
  1026.0 3.6 pad_maximum_fusion.1
  1029.5 6.5 copy.81
  1036.0 5.1 slice_bitcast_fusion.2
  1042.8 7.4 fusion.109
  1050.3 4.8 maximum_dynamic-update-slice_fusion
  1058.1 10.7 constant_dynamic-slice_fusion
  1068.8 19.5 %collective-permute-done.1 = bf16[16,384,1024]{2,1,0:T(8,128)(2,1)} collective-permute-done((bf16[16,384,1024]{2,1,0:T(8,128)(2,1)}, bf16[16,384,1024]{2,1,0:T(8,128)(2,1)}, u32[]{:S(2)}, u32[]{:S(2)}) %collective-permute-start.1) | collective-permute-done | bytes 12582944 | tf_op jit(solution)/shard_map/ppermute | solution.py:62
  1088.3 15.9 %dynamic-slice_add_fusion = bf16[16,384,1024]{2,1,0:T(8,128)(2,1)} fusion(bf16[16,384,1024]{2,1,0:T(8,128)(2,1)} %collective-permute-done.1, bf16[16,384,2048]{2,1,0:T(8,128)(2,1)} %fusion.122, s32[]{:T(128)S(6)} %select_n.105), kind=kLoop, calls=%fused_computation.65 | loop fusion | flops 25165824 | bytes 37748740 | tf_op jit(solution)/shard_map/add | solution.py:62
  1104.9 6.7 collective-permute-done.3
  1113.7 5.9 convert_add_fusion.2
  1119.6 2.7 fusion.92
  1122.3 11.0 convert_add_fusion.1
  1133.2 5.7 fusion.95
  1138.9 10.4 convert_add_fusion
  1149.2 154.5 %reduce-scatter.11.cloned.1.call-done = bf16[1,384,1024]{2,1,0:T(8,128)(2,1)} async-done(((bf16[16,384,1024]{2,1,0:T(8,128)(2,1)}), bf16[1,384,1024]{2,1,0:T(8,128)(2,1)}) %reduce-scatter.11.cloned.1.call-update) | async-done | bytes 786448 | tf_op jit(solution)/shard_map/reduce_scatter | solution.py:63
  1303.8 5.9 fusion.67
  1309.6 2.5 copy.83
  1312.2 2.5 copy.84
  1314.7 2.5 fusion.118
  1317.2 2.6 fusion.91
  1324.8 2.4 fusion.136
  (247 shorter events, 75.7 us)
Async XLA Ops:
  7.2 237.6 %copy-start = (bf16[2048,256]{1,0:T(8,128)(2,1)S(1)}, bf16[2048,256]{1,0:T(8,128)(2,1)}, u32[]{:S(2)}) copy-start(bf16[2048,256]{1,0:T(8,128)(2,1)} %param.51) | copy-start | bytes 3145732
  7.2 131.3 %all-gather.6.cloned.1.call-start = ((), (), s32[]{:S(2)}) async-start(), calls=%async_computation.4 | async-start | bytes 10027008 | tf_op jit(solution)/shard_map/all_gather | solution.py:53
  13.9 213.8 %all-gather.8.cloned.1.call-start = ((), (), s32[]{:S(2)}) async-start(), calls=%async_computation.5 | async-start | bytes 2228224 | tf_op jit(solution)/shard_map/all_gather | solution.py:162
  138.6 15.0 %collective-permute-start = (bf16[2048,2304]{1,0:T(8,128)(2,1)}, bf16[2048,2304]{1,0:T(8,128)(2,1)}, u32[]{:S(2)}, u32[]{:S(2)}) collective-permute-start(bf16[2048,2304]{1,0:T(8,128)(2,1)} %all-gather.6.cloned.1.call-done), channel_id=1, source_target_pairs={{0,1},{1,0},{2,3},{3,2},{4,5},{5,4},{6,7},{7,6},{8,9},{9,8},{10,11... | collective-permute-start | bytes 28311560 | tf_op jit(solution)/shard_map/ppermute | solution.py:54
  139.9 27.5 %copy-start.53 = (f32[128]{0:T(128)}, f32[128]{0:T(128)S(1)}, u32[]{:S(2)}) copy-start(f32[128]{0:T(128)S(1)} %negate_power_fusion) | copy-start | bytes 1540
  140.2 27.2 %copy-start.49 = (f32[128]{0:T(128)}, f32[128]{0:T(128)S(1)}, u32[]{:S(2)}) copy-start(f32[128]{0:T(128)S(1)} %get-tuple-element.441) | copy-start | bytes 1540
  142.0 48.6 %copy-start.45 = (f32[128]{0:T(128)}, f32[128]{0:T(128)S(1)}, u32[]{:S(2)}) copy-start(f32[128]{0:T(128)S(1)} %fusion.186) | copy-start | bytes 1540
  142.0 19.1 %copy-start.3 = (bf16[1,128,2048]{2,1,0:T(8,128)(2,1)S(1)}, bf16[1,128,2048]{2,1,0:T(8,128)(2,1)}, u32[]{:S(2)}) copy-start(bf16[1,128,2048]{2,1,0:T(8,128)(2,1)} %param.32) | copy-start | bytes 1572868
  142.0 19.1 %copy-start.38 = (f32[2048]{0:T(1024)S(1)}, f32[2048]{0:T(1024)}, u32[]{:S(2)}) copy-start(f32[2048]{0:T(1024)} %param.34) | copy-start | bytes 24580
  168.4 28.6 %copy-start.31 = (f32[128,128]{1,0:T(8,128)}, f32[128,128]{1,0:T(8,128)S(1)}, u32[]{:S(2)}) copy-start(f32[128,128]{1,0:T(8,128)S(1)} %get-tuple-element.483) | copy-start | bytes 196612
  169.1 196.0 %all-gather.10.cloned.1.call-start = ((), (), s32[]{:S(2)}) async-start(), calls=%async_computation.6 | async-start | bytes 8912896 | tf_op jit(solution)/shard_map/all_gather | solution.py:214
  236.7 14.0 %copy-start.10 = (f32[128,8,256]{2,0,1:T(8,128)}, f32[128,8,256]{2,0,1:T(8,128)S(1)}, u32[]{:S(2)}) copy-start(f32[128,8,256]{2,0,1:T(8,128)S(1)} %get-tuple-element.198) | copy-start | bytes 3145732
  236.7 14.0 %copy-start.41 = (s32[128]{0:T(128)}, s32[128]{0:T(128)S(1)}, u32[]{:S(2)}) copy-start(s32[128]{0:T(128)S(1)} %get-tuple-element.867) | copy-start | bytes 1540
  236.7 14.0 %copy-start.51 = (f32[128,8,1]{0,1,2:T(8,128)}, f32[128,8,1]{0,1,2:T(8,128)S(1)}, u32[]{:S(2)}) copy-start(f32[128,8,1]{0,1,2:T(8,128)S(1)} %get-tuple-element.868) | copy-start | bytes 12292
  237.0 13.7 %copy-start.12 = (bf16[128,8,256]{0,2,1:T(8,128)(2,1)}, bf16[128,8,256]{0,2,1:T(8,128)(2,1)S(1)}, u32[]{:S(2)}) copy-start(bf16[128,8,256]{0,2,1:T(8,128)(2,1)S(1)} %copy.74) | copy-start | bytes 1572868
  242.0 13.4 copy-start.59
  242.0 13.4 copy-start.47
  244.0 234.2 %all-gather.12.cloned.1.call-start = ((), (), s32[]{:S(2)}) async-start(), calls=%async_computation.11 | async-start | bytes 8912896 | tf_op jit(solution)/shard_map/all_gather | solution.py:151
  244.5 464.7 %reduce-scatter.7.cloned.1.call-start = ((), (), s32[]{:S(2)}) async-start(), calls=%async_computation.8 | async-start | bytes 8912896 | tf_op jit(solution)/shard_map/reduce_scatter | solution.py:244
  244.8 10.6 copy-start.20
  244.8 10.6 copy-start.25
  365.0 14.7 %copy-start.21 = (bf16[1024,2048]{1,0:T(8,128)(2,1)S(1)}, bf16[1024,2048]{1,0:T(8,128)(2,1)}, u32[]{:S(2)}) copy-start(bf16[1024,2048]{1,0:T(8,128)(2,1)} %add_convert_fusion.2) | copy-start | bytes 12582916
  365.0 14.7 %copy-start.57 = (bf16[2048,2048]{1,0:T(8,128)(2,1)S(1)}, bf16[2048,2048]{1,0:T(8,128)(2,1)}, u32[]{:S(2)}) copy-start(bf16[2048,2048]{1,0:T(8,128)(2,1)} %all-gather.10.cloned.1.call-done) | copy-start | bytes 25165828
  478.2 25.0 %copy-start.23 = (bf16[1024,2048]{1,0:T(8,128)(2,1)S(1)}, bf16[1024,2048]{1,0:T(8,128)(2,1)}, u32[]{:S(2)}) copy-start(bf16[1024,2048]{1,0:T(8,128)(2,1)} %add_convert_fusion.3) | copy-start | bytes 12582916
  503.1 14.1 %copy-start.22 = (bf16[1024,2048]{1,0:T(8,128)(2,1)S(1)}, bf16[1024,2048]{1,0:T(8,128)(2,1)}, u32[]{:S(2)}) copy-start(bf16[1024,2048]{1,0:T(8,128)(2,1)} %add_convert_fusion.2) | copy-start | bytes 12582916
  533.1 359.2 %reduce-scatter.5.cloned.1.call-start = ((), (), s32[]{:S(2)}) async-start(), calls=%async_computation.7 | async-start | bytes 8912896 | tf_op jit(solution)/shard_map/reduce_scatter | solution.py:237
  547.1 470.0 %reduce-scatter.9.cloned.1.call-start = ((), (), s32[]{:S(2)}) async-start(), calls=%async_computation.9 | async-start | bytes 2228224 | tf_op jit(solution)/shard_map/reduce_scatter | solution.py:319
  549.1 20.5 %copy-start.62 = (bf16[2048,1024]{1,0:T(8,128)(2,1)S(1)}, bf16[2048,1024]{1,0:T(8,128)(2,1)}, u32[]{:S(2)}) copy-start(bf16[2048,1024]{1,0:T(8,128)(2,1)} %get-tuple-element.447) | copy-start | bytes 12582916
  566.2 18.0 %slice-start = ((s8[8388608]{0:T(1024)(128)(4,1)}), s8[4194304]{0:T(1024)(128)(4,1)S(1)}, s32[]{:S(2)}) async-start(s8[8388608]{0:T(1024)(128)(4,1)} %bitcast.306), calls=%async_computation.12 | async-start | bytes 8388608
  569.6 14.6 %slice-start.1 = ((s8[8388608]{0:T(1024)(128)(4,1)}), s8[4194304]{0:T(1024)(128)(4,1)S(1)}, s32[]{:S(2)}) async-start(s8[8388608]{0:T(1024)(128)(4,1)} %bitcast.306), calls=%async_computation.13 | async-start | bytes 8388608
  569.6 14.6 %copy-start.61 = (bf16[2048,1024]{1,0:T(8,128)(2,1)S(1)}, bf16[2048,1024]{1,0:T(8,128)(2,1)}, u32[]{:S(2)}) copy-start(bf16[2048,1024]{1,0:T(8,128)(2,1)} %get-tuple-element.448) | copy-start | bytes 12582916
  584.2 125.0 %copy-start.9 = (f32[128,2048]{1,0:T(8,128)S(1)}, f32[128,2048]{1,0:T(8,128)}, u32[]{:S(2)}) copy-start(f32[128,2048]{1,0:T(8,128)} %copy-done.8) | copy-start | bytes 3145732
  584.2 125.0 %copy-start.44 = (f32[2048]{0:T(1024)S(1)}, f32[2048]{0:T(1024)}, u32[]{:S(2)}) copy-start(f32[2048]{0:T(1024)} %param.35) | copy-start | bytes 24580
  584.3 125.0 %copy-start.48 = (f32[128]{0:T(128)S(1)}, f32[128]{0:T(128)}, u32[]{:S(2)}) copy-start(f32[128]{0:T(128)} %copy-done.47) | copy-start | bytes 1540
  584.3 126.4 %copy-start.60 = (f32[128]{0:T(128)S(1)}, f32[128]{0:T(128)}, u32[]{:S(2)}) copy-start(f32[128]{0:T(128)} %copy-done.59) | copy-start | bytes 1540
  710.7 193.2 %copy-start.11 = (f32[128,8,256]{2,0,1:T(8,128)S(1)}, f32[128,8,256]{2,0,1:T(8,128)}, u32[]{:S(2)}) copy-start(f32[128,8,256]{2,0,1:T(8,128)} %copy-done.10) | copy-start | bytes 3145732
  894.8 7.6 copy-start.5
  894.8 11.8 copy-start.42
  894.8 11.8 copy-start.52
  915.7 9.5 copy-start.32
  915.7 9.5 copy-start.40
  915.7 388.0 %reduce-scatter.11.cloned.1.call-start = ((), (), s32[]{:S(2)}) async-start(), calls=%async_computation.10 | async-start | bytes 13369344 | tf_op jit(solution)/shard_map/reduce_scatter | solution.py:63
  916.0 11.1 copy-start.4
  916.0 11.1 copy-start.39
  916.0 11.1 copy-start.46
  926.9 9.3 copy-start.17
  936.2 8.5 copy-start.6
  936.2 8.5 copy-start.13
  950.4 8.5 copy-start.28
  958.9 59.1 %copy-start.50 = (f32[128]{0:T(128)S(1)}, f32[128]{0:T(128)}, u32[]{:S(2)}) copy-start(f32[128]{0:T(128)} %copy-done.49) | copy-start | bytes 1540
  959.0 59.1 %copy-start.54 = (f32[128]{0:T(128)S(1)}, f32[128]{0:T(128)}, u32[]{:S(2)}) copy-start(f32[128]{0:T(128)} %copy-done.53) | copy-start | bytes 1540
  1029.5 11.5 copy-start.34
  1029.5 13.2 copy-start.18
  1068.8 19.5 %collective-permute-start.1 = (bf16[16,384,1024]{2,1,0:T(8,128)(2,1)}, bf16[16,384,1024]{2,1,0:T(8,128)(2,1)}, u32[]{:S(2)}, u32[]{:S(2)}) collective-permute-start(bf16[16,384,1024]{2,1,0:T(8,128)(2,1)} %constant_dynamic-slice_fusion), channel_id=1, source_target_pairs={{0,1},{1,0},{2,3},{3,2},{4,5},{5,4},{6,7},{7,6},{8,9},{9,8},{10,11... | collective-permute-start | bytes 37748744 | tf_op jit(solution)/shard_map/ppermute | solution.py:62
  1104.2 7.4 collective-permute-start.3
  1104.4 17.8 %collective-permute-start.4 = (bf16[1024,2048]{1,0:T(8,128)(2,1)}, bf16[1024,2048]{1,0:T(8,128)(2,1)}, u32[]{:S(2)}, u32[]{:S(2)}) collective-permute-start(bf16[1024,2048]{1,0:T(8,128)(2,1)} %get-tuple-element.489), channel_id=1, source_target_pairs={{0,1},{1,0},{2,3},{3,2},{4,5},{5,4},{6,7},{7,6},{8,9},{9,8},{10,11... | collective-permute-start | bytes 12582920 | tf_op jit(solution)/shard_map/ppermute | solution.py:258
  1104.8 34.1 %collective-permute-start.5 = (bf16[1024,2048]{1,0:T(8,128)(2,1)}, bf16[1024,2048]{1,0:T(8,128)(2,1)}, u32[]{:S(2)}, u32[]{:S(2)}) collective-permute-start(bf16[1024,2048]{1,0:T(8,128)(2,1)} %copy-done.58), channel_id=1, source_target_pairs={{0,1},{1,0},{2,3},{3,2},{4,5},{5,4},{6,7},{7,6},{8,9},{9,8},{10,11... | collective-permute-start | bytes 12582920 | tf_op jit(solution)/shard_map/ppermute | solution.py:259
  1119.6 13.7 %copy-start.1 = (f32[1024,2048]{1,0:T(8,128)}, f32[1024,2048]{1,0:T(8,128)S(1)}, u32[]{:S(2)}) copy-start(f32[1024,2048]{1,0:T(8,128)S(1)} %convert_add_fusion.2) | copy-start | bytes 25165828
  1122.3 11.0 copy-start.29
  1303.7 10.9 copy-start.56
  1303.7 13.5 %collective-permute-start.2 = (bf16[384,1024]{1,0:T(8,128)(2,1)}, bf16[384,1024]{1,0:T(8,128)(2,1)}, u32[]{:S(2)}, u32[]{:S(2)}) collective-permute-start(bf16[384,1024]{1,0:T(8,128)(2,1)} %bitcast.296), channel_id=1, source_target_pairs={{0,1},{1,0},{2,3},{3,2},{4,5},{5,4},{6,7},{7,6},{8,9},{9,8},{10,11... | collective-permute-start | bytes 2359304 | tf_op jit(solution)/shard_map/ppermute | solution.py:64
  1314.7 14.1 %copy-start.33 = (bf16[256,256]{1,0:T(8,128)(2,1)S(1)}, bf16[256,256]{1,0:T(8,128)(2,1)}, u32[]{:S(2)}) copy-start(bf16[256,256]{1,0:T(8,128)(2,1)} %param.46) | copy-start | bytes 393220
  1317.2 7.5 copy-start.26
  1317.2 14.2 %copy-start.27 = (bf16[256,2048]{1,0:T(8,128)(2,1)S(1)}, bf16[256,2048]{1,0:T(8,128)(2,1)}, u32[]{:S(2)}) copy-start(bf16[256,2048]{1,0:T(8,128)(2,1)} %param.50) | copy-start | bytes 3145732
  (15 other events, 55.0 us)
Sparse Core Ops, SparseCore 0:
  14.1 124.4 all-gather.5
  169.2 58.5 all-gather.7
  244.1 120.9 all-gather.9
  367.7 110.4 all-gather.11
  533.2 176.0 reduce-scatter.6
  712.0 180.2 reduce-scatter.4
  915.9 101.1 reduce-scatter.8
  1104.3 199.3 reduce-scatter.10

commit v2 on v1

--- a/solution.py
+++ b/solution.py
@@ -1,9 +1,15 @@
+import functools
+
 import jax
 import jax.numpy as jnp
 from jax import lax
+from jax.experimental import pallas as pl
+from jax.experimental.pallas import tpu as pltpu
 from jax.sharding import PartitionSpec as P
 
 EPS = 1e-06
+MESH = pl.DeviceIdType.MESH
+LINE = 4
 
 
 def matrix_product(left, right):
@@ -48,25 +54,294 @@
     return jax.nn.gelu(gate, approximate=True) * up
 
 
-def gather_shared(first, second, core):
-    own = jnp.where(core == 0, first, second)
-    gathered = lax.all_gather(own, "fsdp", axis=0, tiled=True)
-    return gathered, lax.ppermute(gathered, "dp", [(0, 1), (1, 0)])
-
-
-def scatter_shared(terms, core):
-    half = terms.shape[2] // 2
+def place_of():
+    f = lax.axis_index("fsdp")
+    z, y, x = f // 4, (f // 2) % 2, f % 2
+    near_end = z // 2
+    inner = (z + near_end) % 2
+    visits = []
+    for k in range(LINE):
+        u = k + inner * (1 if k == 0 else -1 if k == 1 else 0)
+        visits.append(u + near_end * (3 - 2 * u))
+    return f, z, y, x, f + 1 - 2 * x, f + 2 - 4 * y, visits
+
+
+def greet(f, z, fx, fy, with_core):
+    barrier = pltpu.get_barrier_semaphore()
+
+    def signal(target):
+        pl.semaphore_signal(barrier, inc=1, device_id=target, device_id_type=MESH)
+
+    signal({"fsdp": fx})
+    signal({"fsdp": fy})
+    if with_core:
+        signal({"dp": 1 - lax.axis_index("dp")})
+
+    @pl.when(z > 0)
+    def _():
+        signal({"fsdp": f - 4})
+
+    @pl.when(z < LINE - 1)
+    def _():
+        signal({"fsdp": f + 4})
+
+    peers = 3 if with_core else 2
+    ends = jnp.where(z > 0, 1, 0) + jnp.where(z < LINE - 1, 1, 0)
+    pl.semaphore_wait(barrier, peers + ends)
+
+
+def send(source, target, send_sem, recv_sem, device):
+    copy = pltpu.make_async_remote_copy(
+        src_ref=source,
+        dst_ref=target,
+        send_sem=send_sem,
+        recv_sem=recv_sem,
+        device_id=device,
+        device_id_type=MESH,
+    )
+    copy.start()
+    return copy
+
+
+def arrived(ref, sem):
+    pltpu.make_async_copy(ref, ref, sem).wait()
+
+
+def gather_kernel(pieces, count, with_core, *refs):
+    ins, outs = refs[:count], refs[count : 2 * count]
+    z_send, z_recv, a_send, a_recv, b_send, b_recv, own_sem, c_send, c_recv = refs[2 * count :]
+    f, z, y, x, fx, fy, visits = place_of()
+    core = lax.axis_index("dp")
+    greet(f, z, fx, fy, with_core)
+
+    def at(index, where, rows):
+        ref = outs[index].at[where]
+        if with_core:
+            ref = ref.at[core]
+        return ref.at[pl.ds(*rows)]
+
+    own = []
+    for i in range(count):
+        target = outs[i].at[f, core] if with_core else outs[i].at[f]
+        copy = pltpu.make_async_copy(ins[i], target, own_sem.at[i])
+        copy.start()
+        own.append(copy)
+    sent = []
+
+    def spread_z(p, k):
+        index, rows, first = pieces[p]
+        v = visits[k]
+        where = v * 4 + y * 2 + x
+        target = at(index, where, rows)
+        if k > 0:
+            arrived(target, z_recv.at[p, v])
+        source = ins[index].at[pl.ds(*rows)] if k == 0 else target
+
+        @pl.when((v <= z) & (z < LINE - 1))
+        def _():
+            send(source, target, z_send.at[p, k, 0], z_recv.at[p, v], {"fsdp": f + 4})
+
+        @pl.when((v >= z) & (z > 0))
+        def _():
+            send(source, target, z_send.at[p, k, 1], z_recv.at[p, v], {"fsdp": f - 4})
+
+        fa, fb = (fy, fx) if first == "y" else (fx, fy)
+        sent.append(send(source, target, a_send.at[p, k], a_recv.at[p, k], {"fsdp": fa}))
+        sent.append(send(source, target, b_send.at[p, k, 0], b_recv.at[p, k, 0], {"fsdp": fb}))
+
+    def spread_a(p, k):
+        index, rows, first = pieces[p]
+        v = visits[k]
+        where = v * 4 + (1 - y) * 2 + x if first == "y" else v * 4 + y * 2 + (1 - x)
+        fb = fx if first == "y" else fy
+        target = at(index, where, rows)
+        arrived(target, a_recv.at[p, k])
+        sent.append(send(target, target, b_send.at[p, k, 1], b_recv.at[p, k, 1], {"fsdp": fb}))
+
+    def finish_b(p, k):
+        index, rows, first = pieces[p]
+        v = visits[k]
+        if first == "y":
+            spots = v * 4 + y * 2 + (1 - x), v * 4 + (1 - y) * 2 + (1 - x)
+        else:
+            spots = v * 4 + (1 - y) * 2 + x, v * 4 + (1 - y) * 2 + (1 - x)
+        for j in range(2):
+            arrived(at(index, spots[j], rows), b_recv.at[p, k, j])
+
+    def swap(k):
+        for i in range(count):
+            block = outs[i].at[pl.ds(visits[k] * 4, 4), core]
+            sent.append(
+                send(block, block, c_send.at[i, k], c_recv.at[i, k], {"dp": 1 - core})
+            )
+
+    def swapped(k):
+        for i in range(count):
+            arrived(outs[i].at[pl.ds(visits[k] * 4, 4), 1 - core], c_recv.at[i, k])
+
+    for k in range(LINE + 1):
+        if k < LINE:
+            for p in range(len(pieces)):
+                spread_z(p, k)
+        if k > 0:
+            for p in range(len(pieces)):
+                spread_a(p, k - 1)
+    for copy in own:
+        copy.wait()
+    for k in range(LINE):
+        for p in range(len(pieces)):
+            finish_b(p, k)
+        if with_core:
+            swap(k)
+    if with_core:
+        for k in range(LINE):
+            swapped(k)
+    for copy in sent:
+        copy.wait_send()
+    for p in range(len(pieces)):
+        index, rows, first = pieces[p]
+        for k in range(LINE):
+            v = visits[k]
+            block = at(index, f, rows)
+
+            @pl.when((v <= z) & (z < LINE - 1))
+            def _():
+                pltpu.make_async_copy(block, block, z_send.at[p, k, 0]).wait()
+
+            @pl.when((v >= z) & (z > 0))
+            def _():
+                pltpu.make_async_copy(block, block, z_send.at[p, k, 1]).wait()
+
+
+def gather_blocks(arrays, splits, with_core, number):
+    shards = 4 * LINE
+    pieces = []
+    for index, parts in enumerate(splits):
+        start = 0
+        for rows, first in parts:
+            pieces.append((index, (start, rows), first))
+            start += rows
+    lead = (shards, 2) if with_core else (shards,)
+    amount = len(pieces)
+    dma = pltpu.SemaphoreType.DMA
+    outs = pl.pallas_call(
+        functools.partial(gather_kernel, pieces, len(arrays), with_core),
+        out_shape=[jax.ShapeDtypeStruct(lead + a.shape, a.dtype) for a in arrays],
+        in_specs=[pl.BlockSpec(memory_space=pltpu.VMEM)] * len(arrays),
+        out_specs=[pl.BlockSpec(memory_space=pl.ANY)] * len(arrays),
+        scratch_shapes=[
+            dma((amount, LINE, 2)),
+            dma((amount, LINE)),
+            dma((amount, LINE)),
+            dma((amount, LINE)),
+            dma((amount, LINE, 2)),
+            dma((amount, LINE, 2)),
+            dma((len(arrays),)),
+            dma((len(arrays), LINE)),
+            dma((len(arrays), LINE)),
+        ],
+        compiler_params=pltpu.CompilerParams(collective_id=number, has_side_effects=True),
+        name="gather_blocks_%d" % number,
+    )(*arrays)
+    return [o.reshape((-1, o.shape[-1])) for o in outs]
+
+
+def bit_orders(bits):
+    rest = list(range(min(bits, 3), bits))
+    first = list(range(min(bits, 3)))
+    return [first[i % len(first) :] + first[: i % len(first)] + rest for i in range(3)]
+
+
+def halving_sum(terms, order, place, with_core=False):
+    shards = terms.shape[0]
+    bits = shards.bit_length() - 1
+    current = terms.reshape((2,) * bits + terms.shape[1:])
+    left = list(range(bits))[::-1]
+    steps = [("fsdp", b) for b in order]
+    if with_core:
+        steps = [("dp", None)] + steps
+    for axis, b in steps:
+        if axis == "dp":
+            where, mine = bits, lax.axis_index("dp")
+            pairs = [(0, 1), (1, 0)]
+        else:
+            where, mine = left.index(b), (place >> b) & 1
+            pairs = [(i, i ^ (1 << b)) for i in range(shards)]
+            left.remove(b)
+        away = lax.dynamic_index_in_dim(current, 1 - mine, where, keepdims=False)
+        keep = lax.dynamic_index_in_dim(current, mine, where, keepdims=False)
+        came = lax.ppermute(away, axis, pairs)
+        total = keep.astype(jnp.float32) + came.astype(jnp.float32)
+        current = total.astype(terms.dtype)
+    return total
+
+
+def scatter_rows(terms, place, shards):
+    blocks = terms.reshape(shards, terms.shape[0] // shards, terms.shape[1])
+    rows = blocks.shape[1]
+    third = (rows * 3 // 8) // 16 * 16
+    edges = [0, third, 2 * third, rows]
+    orders = bit_orders(shards.bit_length() - 1)
+    return jnp.concatenate(
+        [halving_sum(blocks[:, edges[i] : edges[i + 1]], orders[i], place) for i in range(3)],
+        axis=0,
+    )
+
+
+def scatter_both(big, small, place, core):
+    shards, rows, columns = big.shape
+    halves = big.reshape(shards, 2, 2, rows // 4, columns)
+    streams = [halves[:, 0], halves[:, 1], small.reshape(shards, 2, -1, columns)]
+    orders = bit_orders(shards.bit_length() - 1)
+    mine = jnp.stack(
+        [halving_sum(streams[i], orders[i], place, True).astype(big.dtype) for i in range(2)]
+    )
+    few = halving_sum(streams[2], orders[2], place, True).astype(big.dtype)
     swap = [(0, 1), (1, 0)]
-    own = lax.dynamic_slice_in_dim(terms, core * half, half, 2)
-    away = lax.dynamic_slice_in_dim(terms, (1 - core) * half, half, 2)
-    both = own + lax.ppermute(away, "dp", swap)
-    mine = lax.psum_scatter(both, "fsdp", scatter_dimension=0, tiled=False)
-    theirs = lax.ppermute(mine, "dp", swap)
-    return jnp.where(
-        core == 0,
-        jnp.concatenate([mine, theirs], axis=1),
-        jnp.concatenate([theirs, mine], axis=1),
-    )
+
+    def both(own):
+        other = lax.ppermute(own, "dp", swap)
+        low = jnp.where(core == 0, own, other)
+        high = jnp.where(core == 0, other, own)
+        return jnp.stack([low, high], axis=-3).astype(jnp.float32)
+
+    return both(mine).reshape(rows, columns), both(few).reshape(-1, columns)
+
+
+def pack_rows(terms, shards, width):
+    count = width // terms.shape[1]
+    parts = terms.reshape(shards, count, -1, terms.shape[1])
+    return jnp.concatenate([parts[:, i] for i in range(count)], axis=2)
+
+
+def unpack_rows(terms, columns):
+    count = terms.shape[1] // columns
+    return jnp.concatenate(
+        [terms[:, i * columns : (i + 1) * columns] for i in range(count)], axis=0
+    )
+
+
+def gather_weights(query, output, key_value, shards):
+    if shards == 4 * LINE:
+        rows = query.shape[0]
+        return gather_blocks(
+            [query, output, key_value],
+            [[(rows, "y")], [(rows, "x")], [(rows // 2, "y"), (rows // 2, "x")]],
+            True,
+            1,
+        )
+
+    def whole(own):
+        return lax.all_gather(own, ("fsdp", "dp"), axis=0, tiled=True)
+
+    return whole(query), whole(output), whole(key_value)
+
+
+def gather_rows(own, shards, number):
+    if shards == 4 * LINE:
+        half = own.shape[0] // 2
+        return gather_blocks([own], [[(half, "y"), (half, "x")]], False, number)[0]
+    return lax.all_gather(own, "fsdp", axis=0, tiled=True)
 
 
 def local(
@@ -121,47 +396,43 @@
     cosines = jnp.cos(angles)
     sines = jnp.sin(angles)
 
+    core_rows = in_rows // 2
+
+    def split_heads(values):
+        return values.reshape(tok_rows, heads, head_size).transpose(1, 0, 2)
+
+    def join_heads(values):
+        return values.transpose(1, 0, 2).reshape(tok_rows, heads * head_size)
+
     def merged_rows(matrix, first, second):
-        rows = lax.dynamic_slice_in_dim(first, place * in_rows, in_rows, 0)
-        return (matrix.astype(f32) + matrix_product(rows, second)).astype(bf16)
-
-    own_first = jnp.concatenate(
-        [
-            merged_rows(query_matrix, query_factor_first, query_factor_second),
-            merged_rows(key_matrix, key_factor_first, key_factor_second),
-        ],
-        axis=1,
-    )
-    own_second = jnp.concatenate(
-        [
-            merged_rows(output_matrix, output_factor_first, output_factor_second),
-            merged_rows(value_matrix, value_factor_first, value_factor_second),
-        ],
-        axis=1,
-    )
-    gathered, other = gather_shared(own_first, own_second, core)
-    query_key = jnp.where(core == 0, gathered, other)
-    output_value = jnp.where(core == 0, other, gathered)
-    query_weight = query_key[:, : heads * head_size]
-    key_weight = query_key[:, heads * head_size :]
-    output_weight = output_value[:, :width]
-    value_weight = output_value[:, width:]
-
+        own = lax.dynamic_slice_in_dim(matrix, core * core_rows, core_rows, 0)
+        rows = lax.dynamic_slice_in_dim(first, place * in_rows + core * core_rows, core_rows, 0)
+        return (own.astype(f32) + matrix_product(rows, second)).astype(bf16)
+
+    query_weight, output_weight, key_value_weight = gather_weights(
+        merged_rows(query_matrix, query_factor_first, query_factor_second),
+        merged_rows(output_matrix, output_factor_first, output_factor_second),
+        jnp.concatenate(
+            [
+                merged_rows(key_matrix, key_factor_first, key_factor_second),
+                merged_rows(value_matrix, value_factor_first, value_factor_second),
+            ],
+            axis=1,
+        ),
+        shards,
+    )
     cot_own = cotangent[0]
-    cot_all = lax.all_gather(cot_own, "fsdp", axis=0, tiled=True)
 
     normed_attn, pull_attn = jax.vjp(rms_norm, input_rows, gain_attn)
     attn_in = normed_attn.astype(bf16)
-    query_lin = matrix_product(attn_in, query_weight)
-    key_lin = matrix_product(attn_in, key_weight)
-    value = matrix_product(attn_in, value_weight).astype(bf16)
-    query = rotate(
-        query_lin.reshape(tok_rows, heads, head_size), cosines[:, None, :], sines[:, None, :]
-    ).astype(bf16)
-    key = rotate(key_lin, cosines, sines).astype(bf16)
+    key_value_lin = matrix_product(attn_in, key_value_weight)
+    key = rotate(key_value_lin[:, :head_size], cosines, sines).astype(bf16)
+    value = key_value_lin[:, head_size:].astype(bf16)
     key_value = lax.all_gather(
         jnp.concatenate([key, value], axis=1), "fsdp", axis=0, tiled=True
     )
+    query_lin = matrix_product(attn_in, query_weight)
+    query = rotate(split_heads(query_lin), cosines[None], sines[None]).astype(bf16)
     keys_all = key_value[:, :head_size]
     values_all = key_value[:, head_size:]
     block = min(512, length)
@@ -178,8 +449,8 @@
         allowed = (seg_own[:, None] == seg_block[None, :]) & (
             key_index[None, :] <= query_index[:, None]
         )
-        allowed = allowed[:, None, :]
-        raw = jnp.einsum("thd,kd->thk", query, key_block, preferred_element_type=f32)
+        allowed = allowed[None]
+        raw = jnp.einsum("htd,kd->htk", query, key_block, preferred_element_type=f32)
         return (jnp.where(allowed, raw * scale, -1e30), allowed, key_block, value_block)
 
     def max_step(index, carry):
@@ -189,8 +460,8 @@
         weights = jnp.where(allowed, jnp.exp(logits - new_top), 0.0)
         return (new_top, total * jnp.exp(top - new_top) + jnp.sum(weights, axis=-1, keepdims=True))
 
-    start_top = jnp.full((tok_rows, heads, 1), -1e30, f32)
-    start_total = jnp.zeros((tok_rows, heads, 1), f32)
+    start_top = jnp.full((heads, tok_rows, 1), -1e30, f32)
+    start_total = jnp.zeros((heads, tok_rows, 1), f32)
     top, total = lax.fori_loop(first_block, needed, max_step, (start_top, start_total))
     log_total = top + jnp.log(total)
 
@@ -201,17 +472,18 @@
     def out_step(index, acc):
         probs, key_block, value_block = probs_of(index * block)
         return acc + jnp.einsum(
-            "thk,kd->thd", probs.astype(bf16), value_block, preferred_element_type=f32
+            "htk,kd->htd", probs.astype(bf16), value_block, preferred_element_type=f32
         )
 
     attn_raw = lax.fori_loop(
-        first_block, needed, out_step, jnp.zeros((tok_rows, heads, head_size), f32)
-    )
-    attn = attn_raw.reshape(tok_rows, heads * head_size).astype(bf16)
+        first_block, needed, out_step, jnp.zeros((heads, tok_rows, head_size), f32)
+    )
+    attn = join_heads(attn_raw).astype(bf16)
     resid = input_rows + matrix_product(attn, output_weight)
     normed_mlp, pull_mlp = jax.vjp(rms_norm, resid, gain_mlp)
     mlp_in = normed_mlp.astype(bf16)
-    mlp_all = lax.all_gather(mlp_in, "fsdp", axis=0, tiled=True)
+    mlp_all = gather_rows(mlp_in, shards, 2)
+    cot_all = lax.all_gather(cot_own, "fsdp", axis=0, tiled=True)
 
     first_unit = place * unit_rows
     gate_second = lax.dynamic_slice_in_dim(gate_factor_second, first_unit, unit_rows, 1)
@@ -234,19 +506,16 @@
     up = right_product(mlp_all, up_weight)
     hidden_full, pull_geglu = jax.vjp(geglu, gate, up)
     hidden = hidden_full.astype(bf16)
-    down_sum = lax.psum_scatter(
-        matrix_product(hidden, down_weight).astype(bf16), "fsdp", scatter_dimension=0, tiled=True
-    )
+    down_sum = scatter_rows(matrix_product(hidden, down_weight).astype(bf16), place, shards)
     grad_hidden = right_product(cot_all, down_weight)
     grad_gate_full, grad_up_full = pull_geglu(grad_hidden)
     grad_gate = grad_gate_full.astype(bf16)
     grad_up = grad_up_full.astype(bf16)
-    grad_mlp_in = lax.psum_scatter(
+    grad_mlp_in = scatter_rows(
         (matrix_product(grad_gate, gate_weight) + matrix_product(grad_up, up_weight)).astype(bf16),
-        "fsdp",
-        scatter_dimension=0,
-        tiled=True,
-    ).astype(f32)
+        place,
+        shards,
+    )
     gate_rows = left_matrix_product(grad_gate, mlp_all)
     up_rows = left_matrix_product(grad_up, mlp_all)
     down_rows = left_matrix_product(hidden, cot_all)
@@ -274,7 +543,7 @@
     )
     down_out_term = left_matrix_product(down_first, down_rows_low)
 
-    output = (resid + down_sum.astype(f32)).astype(bf16)
+    output = (resid + down_sum).astype(bf16)
     grad_resid_norm, gain_mlp_term = pull_mlp(grad_mlp_in)
     grad_resid = cot_own.astype(f32) + grad_resid_norm
     grad_branch = grad_resid.astype(bf16)
@@ -283,7 +552,7 @@
     lora_query = matrix_product(attn_in, query_factor_first).astype(bf16)
     lora_key = matrix_product(attn_in, key_factor_first).astype(bf16)
     lora_value = matrix_product(attn_in, value_factor_first).astype(bf16)
-    grad_attn_heads = grad_attn.reshape(tok_rows, heads, head_size)
+    grad_attn_heads = split_heads(grad_attn)
     delta = jnp.sum(
         grad_attn_heads.astype(f32) * attn_raw, axis=-1, keepdims=True
     )
@@ -293,15 +562,15 @@
         start = index * block
         probs, key_block, value_block = probs_of(start)
         grad_probs = jnp.einsum(
-            "thd,kd->thk", grad_attn_heads, value_block, preferred_element_type=f32
+            "htd,kd->htk", grad_attn_heads, value_block, preferred_element_type=f32
         )
         grad_scores = (scale * probs * (grad_probs - delta)).astype(bf16)
         grad_query_acc = grad_query_acc + jnp.einsum(
-            "thk,kd->thd", grad_scores, key_block, preferred_element_type=f32
+            "htk,kd->htd", grad_scores, key_block, preferred_element_type=f32
         )
-        key_part = jnp.einsum("thk,thd->kd", grad_scores, query, preferred_element_type=f32)
+        key_part = jnp.einsum("htk,htd->kd", grad_scores, query, preferred_element_type=f32)
         value_part = jnp.einsum(
-            "thk,thd->kd", probs.astype(bf16), grad_attn_heads, preferred_element_type=f32
+            "htk,htd->kd", probs.astype(bf16), grad_attn_heads, preferred_element_type=f32
         )
         both = jnp.concatenate([key_part, value_part], axis=1).astype(bf16)
         key_terms = lax.dynamic_update_slice_in_dim(key_terms, both, start, 0)
@@ -312,22 +581,19 @@
         needed,
         grad_step,
         (
-            jnp.zeros((tok_rows, heads, head_size), f32),
+            jnp.zeros((heads, tok_rows, head_size), f32),
             jnp.zeros((length, 2 * head_size), bf16),
         ),
     )
-    key_sums = lax.psum_scatter(key_terms, "fsdp", scatter_dimension=0, tiled=True).astype(f32)
-    grad_query_lin = (
-        rotate(grad_query_rot, cosines[:, None, :], -sines[:, None, :])
-        .reshape(tok_rows, heads * head_size)
-        .astype(bf16)
-    )
-    grad_key_lin = rotate(key_sums[:, :head_size], cosines, -sines).astype(bf16)
-    grad_value_lin = key_sums[:, head_size:].astype(bf16)
-    grad_attn_in = (
-        right_product(grad_query_lin, query_weight)
-        + right_product(grad_key_lin, key_weight)
-        + right_product(grad_value_lin, value_weight)
+    key_sums = scatter_rows(key_terms, place, shards)
+    grad_query_lin = join_heads(
+        rotate(grad_query_rot, cosines[None], -sines[None]).astype(bf16)
+    )
+    grad_key_value_lin = jnp.concatenate(
+        [rotate(key_sums[:, :head_size], cosines, -sines), key_sums[:, head_size:]], axis=1
+    ).astype(bf16)
+    grad_attn_in = right_product(grad_query_lin, query_weight) + right_product(
+        grad_key_value_lin, key_value_weight
     )
     grad_inputs_norm, gain_attn_term = pull_attn(grad_attn_in)
     grad_inputs = grad_resid + grad_inputs_norm
@@ -337,56 +603,51 @@
 
     per = in_rows
     few = rank // shards
-    narrow = jnp.concatenate(
+    early = jnp.concatenate(
         [
-            low_term(attn_in, grad_key_lin),
-            low_term(attn_in, grad_value_lin),
-            gate_in_term.astype(bf16),
-            up_in_term.astype(bf16),
+            low_term(lora_output, grad_branch).reshape(shards, few, width),
+            down_out_term.astype(bf16).reshape(shards, few, width),
+            pack_rows(
+                jnp.concatenate([gate_in_term, up_in_term], axis=1).astype(bf16), shards, width
+            ),
         ],
         axis=1,
-    ).reshape(shards, 2, per // 2, 4 * head_size)
+    )
+    g_output_weight, early_sums = scatter_both(
+        low_term(attn, grad_branch).reshape(shards, per, width), early, place, core
+    )
+    g_output_out = early_sums[:few]
+    g_down_out = early_sums[few : 2 * few]
+    pair = unpack_rows(early_sums[2 * few :], 2 * head_size)
+    g_gate_in = pair[:, :head_size]
+    g_up_in = pair[:, head_size:]
+
     tiny = jnp.concatenate(
         [
-            low_term(lora_key, grad_key_lin).reshape(shards, few, head_size),
-            low_term(lora_value, grad_value_lin).reshape(shards, few, head_size),
+            low_term(lora_key, grad_key_value_lin[:, :head_size]).reshape(shards, few, head_size),
+            low_term(lora_value, grad_key_value_lin[:, head_size:]).reshape(shards, few, head_size),
             gain_attn_term.astype(bf16).reshape(shards, few, -1),
             gain_mlp_term.astype(bf16).reshape(shards, few, -1),
         ],
         axis=2,
     )
     tiny = jnp.pad(tiny, ((0, 0), (0, 0), (0, width - tiny.shape[2])))
-    terms = jnp.concatenate(
+    late = jnp.concatenate(
         [
-            low_term(attn_in, grad_query_lin).reshape(shards, per, width),
-            low_term(attn, grad_branch).reshape(shards, per, width),
             low_term(lora_query, grad_query_lin).reshape(shards, few, width),
-            low_term(lora_output, grad_branch).reshape(shards, few, width),
-            down_out_term.astype(bf16).reshape(shards, few, width),
-            jnp.concatenate([narrow[:, 0], narrow[:, 1]], axis=2),
+            pack_rows(low_term(attn_in, grad_key_value_lin), shards, width),
             tiny,
         ],
         axis=1,
     )
-    sums = scatter_shared(terms, core).astype(f32)
-    at = [0]
-
-    def take(rows):
-        at[0] += rows
-        return sums[at[0] - rows : at[0]]
-
-    g_query_weight = take(per)
-    g_output_weight = take(per)
-    g_query_out = take(few)
-    g_output_out = take(few)
-    g_down_out = take(few)
-    pair = take(per // 2)
-    pair = jnp.concatenate([pair[:, : width // 2], pair[:, width // 2 :]], axis=0)
+    g_query_weight, late_sums = scatter_both(
+        low_term(attn_in, grad_query_lin).reshape(shards, per, width), late, place, core
+    )
+    g_query_out = late_sums[:few]
+    pair = unpack_rows(late_sums[few : late_sums.shape[0] - few], 2 * head_size)
     g_key_weight = pair[:, :head_size]
-    g_value_weight = pair[:, head_size : 2 * head_size]
-    g_gate_in = pair[:, 2 * head_size : 3 * head_size]
-    g_up_in = pair[:, 3 * head_size :]
-    last = take(few)
+    g_value_weight = pair[:, head_size:]
+    last = late_sums[late_sums.shape[0] - few :]
     g_key_out = last[:, :head_size]
     g_value_out = last[:, head_size : 2 * head_size]
     each = per // few

time: 1360 us -> 1050 us (0.77)
  waiting for transfers between devices: 883 us -> 324 us
  Pallas kernels: 0 us -> 210 us
  starting transfers between devices: 1.43 us -> 90 us
  matrix products: 257 us -> 241 us
  other arithmetic: 81.2 us -> 67.3 us
    reduce_scatter x4 -> x0, waiting for transfers between devices: 498 us -> none  [the longest x1 182 us: local(): lax.psum_scatter(matrix_product(hidden, down_weight).astype(bf16), 'fsdp'...]
    ppermute x3 -> x70, waiting for transfers between devices: 31.1 us -> 298 us  [the longest x66 298 us: halving_sum(): came = lax.ppermute(away, axis, pairs)]
    all_gather x2 -> x0, waiting for transfers between devices: 230 us -> none  [the longest x1 125 us: gather_shared(): gathered = lax.all_gather(own, 'fsdp', axis=0, tiled=True)]
    pallas_call x0 -> x2, Pallas kernels: none -> 210 us  [gather_blocks(): pl.pallas_call(functools.partial(gather_kernel, pieces, len(arrays), with...]
    ppermute x3 -> x70, starting transfers between devices: 0.01 us -> 89.2 us  [the longest x66 88.9 us: halving_sum(): came = lax.ppermute(away, axis, pairs)]
    all_gather x1, waiting for transfers between devices: 87.3 us -> 0.01 us  [local(): cot_all = lax.all_gather(cot_own, 'fsdp', axis=0, tiled=True)]
    unnamed x139 -> x177, local copies, waits for them, and re-layouts: 45.6 us -> 12.1 us
    convert_element_type x3 -> x58, other arithmetic: 3.56 us -> 25.2 us  [the longest x51 22.7 us: halving_sum(): current = total.astype(terms.dtype)]
  transfers between devices with their start and end apart: 14 -> 75, of which waited for: 11 -> 42; matrix products, arithmetic and copies ran while one was open for 18% -> 26% of each run, Pallas kernels for 0% -> 12%
where the time goes in v2:
time: 1050 us; the launch traced here: 1040 us
  waiting for transfers between devices  324 us (31%)
  matrix products  241 us (23%)
  Pallas kernels  210 us (20%)
  local copies, waits for them, and re-layouts  93.2 us (9%)
  starting transfers between devices  90 us (9%)
  other arithmetic  67.3 us (6%)
  between operations  16.7 us (2%)
    ppermute x66, waiting for transfers between devices, halving_sum(): came = lax.ppermute(away, axis, pairs)  298 us
    pallas_call x2, Pallas kernels, gather_blocks(): pl.pallas_call(functools.partial(gather_kernel, pieces, len(arrays), with...  210 us
    ppermute x66, starting transfers between devices, halving_sum(): came = lax.ppermute(away, axis, pairs)  88.9 us
    dot_general x11, matrix products, right_product(): lax.dot_general(left, right, (((1,), (1,)), ((), ())), preferred_element_...  68.7 us
    dot_general x11, matrix products, left_matrix_product(): lax.dot_general(left, right, (((0,), (0,)), ((), ())), preferred_element_...  68 us
    dot_general x11, matrix products, matrix_product(): return jnp.dot(left, right, preferred_element_type=jnp.float32)  67.1 us
    all_gather x1, waiting for transfers between devices, local(): lax.all_gather(jnp.concatenate([key, value], axis=1), 'fsdp', axis=0, til...  24.9 us
    convert_element_type x51, other arithmetic, halving_sum(): current = total.astype(terms.dtype)  22.7 us
  transfers between devices with their start and end apart: 75, of which 42 were waited for; matrix products, arithmetic and copies ran while one was open for 26% of the time, Pallas kernels for 12%

profile of v2, /device:TPU:0, one launch (start us, length us, event | category | flops | bytes accessed | tf_op | source)
XLA Modules:
  0.0 1042.6 jit_solution(10993996259108033409)
XLA Ops:
  17.5 88.0 %gather_blocks_1.1 = (bf16[16,2,64,2048]{3,2,1,0:T(8,128)(2,1)}, bf16[16,2,64,2048]{3,2,1,0:T(8,128)(2,1)}, bf16[16,2,64,512]{3,2,1,0:T(8,128)(2,1)}) custom-call(bf16[64,2048]{1,0:T(8,128)(2,1)} %fusion.75.refs_0_, bf16[64,2048]{1,0:T(8,128)(2,1)} %fusion.76.refs_1_, bf16[64,512]{1,0:T(8,128)(2,1)} %pad_maximum_fusion.16.refs_2_), custom_call_target="tpu_custom_call" | custom-call | tf_op jit(solution)/shard_map/gather_blocks_1/pallas_call | solution.py:227
  110.2 12.2 %copy.84 = bf16[2048,2048]{1,0:T(8,128)(2,1)} copy(bf16[2048,2048]{0,1:T(8,128)(2,1)} %bitcast.759) | data formatting | bytes 16777216 | tf_op jit(solution)/shard_map/dot_general | solution.py:16
  122.5 6.3 convolution_bitcast_fusion.2
  130.0 5.8 add_convert_fusion.3
  135.9 4.5 add_convert_fusion.2
  140.4 4.3 add_convert_fusion.1
  144.8 24.9 %all-gather.4.cloned.1.call-done = bf16[2048,512]{1,0:T(8,128)(2,1)} async-done(((bf16[128,512]{1,0:T(8,128)(2,1)}), bf16[2048,512]{1,0:T(8,128)(2,1)}) %all-gather.4.cloned.1.call-update) | async-done | bytes 2097168 | tf_op jit(solution)/shard_map/all_gather | solution.py:431
  176.4 4.6 while.38
  183.6 5.3 multiply_reduce_fusion.3
  190.9 122.4 %gather_blocks_2.1 = bf16[16,128,2048]{2,1,0:T(8,128)(2,1)} custom-call(bf16[128,2048]{1,0:T(8,128)(2,1)} %multiply_convert_fusion.1.refs_0_), custom_call_target="tpu_custom_call" | custom-call | tf_op jit(solution)/shard_map/gather_blocks_2/pallas_call | solution.py:227
  313.3 14.7 %fusion.246 = f32[2048,1024]{1,0:T(8,128)} fusion(bf16[2048,2048]{1,0:T(8,128)(2,1)} %bitcast.787, bf16[1024,2048]{1,0:T(8,128)(2,1)} %add_convert_fusion.3), kind=kOutput, calls=%fused_computation.537 | convolution fusion | flops 8589934592 | bytes 20971520 | tf_op jit(solution)/shard_map/dot_general | solution.py:26
  328.0 11.2 %fusion.247 = f32[2048,1024]{1,0:T(8,128)} fusion(bf16[2048,2048]{1,0:T(8,128)(2,1)S(1)} %bitcast.790, bf16[1024,2048]{1,0:T(8,128)(2,1)S(1)} %copy-done.27), kind=kOutput, calls=%fused_computation.538 | convolution fusion | flops 8589934592 | bytes 20971520 | tf_op jit(solution)/shard_map/dot_general | solution.py:26
  339.2 24.7 %fusion.54 = (bf16[2048,1024]{1,0:T(8,128)(2,1)}, bf16[2048,1024]{1,0:T(8,128)(2,1)}, bf16[2048,1024]{1,0:T(8,128)(2,1)}) fusion(f32[2048,1024]{1,0:T(8,128)} %fusion.246, f32[2048,1024]{1,0:T(8,128)} %fusion.247, bf16[1024,2048]{1,0:T(8,128)(2,1)} %add_convert_fusion.1, bf16[1,2048,2048]{2,1,0:T(8,128)(2,1)} %all-gather.6.cloned.1.call-done), kind=kOutput, calls=%fused_computation.75 | convolution fusion | flops 8644460544 | bytes 41943040 | tf_op jit(solution)/shard_map/dot_general | solution.py:26
  363.9 14.0 %fusion.248 = f32[2048,2048]{1,0:T(8,128)} fusion(bf16[2048,1024]{1,0:T(8,128)(2,1)} %get-tuple-element.432, bf16[1024,2048]{1,0:T(8,128)(2,1)S(1)} %copy-done.28), kind=kOutput, calls=%fused_computation.539 | convolution fusion | flops 8589934592 | bytes 25165824 | tf_op jit(solution)/shard_map/dot_general | solution.py:16
  377.9 14.5 %add_convert_fusion = bf16[2048,2048]{1,0:T(8,128)(2,1)S(1)} fusion(f32[2048,2048]{1,0:T(8,128)} %fusion.248, bf16[2048,1024]{1,0:T(8,128)(2,1)} %get-tuple-element.431, bf16[1024,2048]{1,0:T(8,128)(2,1)} %add_convert_fusion.2), kind=kOutput, calls=%fused_computation.63 | convolution fusion | flops 8598323200 | bytes 33554432 | tf_op jit(solution)/shard_map/dot_general | solution.py:16
  393.8 13.9 %convolution_convert_fusion = bf16[2048,2048]{1,0:T(8,128)(2,1)} fusion(bf16[2048,1024]{1,0:T(8,128)(2,1)} %get-tuple-element.433, bf16[1024,2048]{1,0:T(8,128)(2,1)} %add_convert_fusion.1), kind=kOutput, calls=%fused_computation.88 | convolution fusion | flops 8594128896 | bytes 16777216 | tf_op jit(solution)/shard_map/dot_general | solution.py:16
  409.4 3.4 fusion.232
  412.9 15.7 %fusion.242 = (bf16[1024,2048]{1,0:T(8,128)(2,1)}, f32[1024,2048]{1,0:T(8,128)}) fusion(bf16[2048,1024]{1,0:T(8,128)(2,1)} %get-tuple-element.432, bf16[2048,2048]{1,0:T(8,128)(2,1)} %bitcast.788), kind=kOutput, calls=%fused_computation.533 | convolution fusion | flops 8592031744 | bytes 25165824 | tf_op jit(solution)/shard_map/dot_general | solution.py:20
  428.6 14.5 %fusion.243 = (bf16[1024,2048]{1,0:T(8,128)(2,1)}, f32[1024,2048]{1,0:T(8,128)}) fusion(bf16[2048,1024]{1,0:T(8,128)(2,1)S(1)} %copy-done.84, bf16[2048,2048]{1,0:T(8,128)(2,1)} %bitcast.789), kind=kOutput, calls=%fused_computation.534 | convolution fusion | flops 8592031744 | bytes 25165824 | tf_op jit(solution)/shard_map/dot_general | solution.py:20
  443.2 4.6 convolution_convert_fusion.7
  448.3 4.6 convolution_convert_fusion.6
  458.8 14.1 %fusion.244 = (bf16[1024,2048]{1,0:T(8,128)(2,1)}, f32[1024,2048]{1,0:T(8,128)}) fusion(bf16[2048,1024]{1,0:T(8,128)(2,1)S(1)} %copy-done.83, bf16[1,2048,2048]{2,1,0:T(8,128)(2,1)} %all-gather.6.cloned.1.call-done), kind=kOutput, calls=%fused_computation.535 | convolution fusion | flops 8592031744 | bytes 25165824 | tf_op jit(solution)/shard_map/dot_general | solution.py:20
  472.9 4.6 convolution_convert_fusion.8
  482.9 18.5 %collective-permute-done.8 = bf16[2,2,2,32,2048]{4,3,0,1,2:T(8,128)(2,1)S(1)} collective-permute-done((bf16[2,2,2,32,2048]{4,3,0,1,2:T(8,128)(2,1)S(1)}, bf16[2,2,2,32,2048]{4,3,0,1,2:T(8,128)(2,1)S(1)}, u32[]{:S(2)}, u32[]{:S(2)}) %collective-permute-start.8) | collective-permute-done | bytes 1048608 | tf_op jit(solution)/shard_map/ppermute | solution.py:273
  503.4 14.3 %collective-permute-done.12 = bf16[2,2,2,48,2048]{4,3,0,1,2:T(8,128)(2,1)S(1)} collective-permute-done((bf16[2,2,2,48,2048]{4,3,0,1,2:T(8,128)(2,1)S(1)}, bf16[2,2,2,48,2048]{4,3,0,1,2:T(8,128)(2,1)S(1)}, u32[]{:S(2)}, u32[]{:S(2)}) %collective-permute-start.12) | collective-permute-done | bytes 1572896 | tf_op jit(solution)/shard_map/ppermute | solution.py:273
  519.1 18.1 %collective-permute-done.4 = bf16[2,2,2,48,2048]{4,3,0,2,1:T(8,128)(2,1)S(1)} collective-permute-done((bf16[2,2,2,48,2048]{4,3,0,2,1:T(8,128)(2,1)S(1)}, bf16[2,2,2,48,2048]{4,3,0,2,1:T(8,128)(2,1)S(1)}, u32[]{:S(2)}, u32[]{:S(2)}) %collective-permute-start.4) | collective-permute-done | bytes 1572896 | tf_op jit(solution)/shard_map/ppermute | solution.py:273
  539.1 25.1 %collective-permute-done.21 = bf16[2,2,32,2048]{3,2,0,1:T(8,128)(2,1)S(1)} collective-permute-done((bf16[2,2,32,2048]{3,2,0,1:T(8,128)(2,1)S(1)}, bf16[2,2,32,2048]{3,2,0,1:T(8,128)(2,1)S(1)}, u32[]{:S(2)}, u32[]{:S(2)}) %collective-permute-start.21) | collective-permute-done | bytes 524320 | tf_op jit(solution)/shard_map/ppermute | solution.py:273
  565.3 10.8 %collective-permute-done.9 = bf16[2,2,32,2048]{3,2,0,1:T(8,128)(2,1)S(1)} collective-permute-done((bf16[2,2,32,2048]{3,2,0,1:T(8,128)(2,1)S(1)}, bf16[2,2,32,2048]{3,2,0,1:T(8,128)(2,1)S(1)}, u32[]{:S(2)}, u32[]{:S(2)}) %collective-permute-start.9) | collective-permute-done | bytes 524320 | tf_op jit(solution)/shard_map/ppermute | solution.py:273
  577.7 6.1 collective-permute-done.22
  584.6 5.5 collective-permute-done.10
  590.1 3.9 collective-permute-start.23
  594.1 4.5 collective-permute-done.23
  601.1 3.4 collective-permute-done.11
  604.4 5.3 collective-permute-start.13
  610.2 15.3 %collective-permute-done.13 = bf16[2,2,48,2048]{3,2,0,1:T(8,128)(2,1)S(1)} collective-permute-done((bf16[2,2,48,2048]{3,2,0,1:T(8,128)(2,1)S(1)}, bf16[2,2,48,2048]{3,2,0,1:T(8,128)(2,1)S(1)}, u32[]{:S(2)}, u32[]{:S(2)}) %collective-permute-start.13) | collective-permute-done | bytes 786464 | tf_op jit(solution)/shard_map/ppermute | solution.py:273
  628.7 8.9 collective-permute-done.1
  640.0 9.4 collective-permute-done.14
  650.9 3.3 collective-permute-start.19
  654.3 7.0 collective-permute-done.2
  666.3 8.3 collective-permute-done.15
  677.0 5.7 collective-permute-done.3
  691.0 8.9 while.39
  704.2 5.7 convolution_convert_fusion.1
  714.3 7.5 collective-permute-start.32
  724.9 4.0 fusion.229
  742.0 3.3 copy.220
  751.8 4.4 collective-permute-done.24
  760.5 9.6 collective-permute-start.35
  774.4 3.6 collective-permute-done.29
  779.6 4.1 collective-permute-done.25
  784.8 3.5 collective-permute-done.30
  808.7 6.4 fusion.249
  840.4 5.8 convert_add_fusion.2
  846.3 13.0 %convert_add_fusion.1 = f32[1024,2048]{1,0:T(8,128)} fusion(f32[1024,2048]{1,0:T(8,128)} %get-tuple-element.530, bf16[1024,2048]{1,0:T(8,128)(2,1)} %collective-permute-done.65), kind=kLoop, calls=%fused_computation.81 | loop fusion | flops 4194304 | bytes 20971520 | tf_op jit(solution)/shard_map/add | solution.py:527
  861.9 4.6 fusion.96
  867.9 5.9 convert_add_fusion
  897.5 10.4 collective-permute-done.59
  917.1 32.1 %collective-permute-done.60 = bf16[2,2,32,2048]{3,2,0,1:T(8,128)(2,1)S(1)} collective-permute-done((bf16[2,2,32,2048]{3,2,0,1:T(8,128)(2,1)S(1)}, bf16[2,2,32,2048]{3,2,0,1:T(8,128)(2,1)S(1)}, u32[]{:S(2)}, u32[]{:S(2)}) %collective-permute-start.60) | collective-permute-done | bytes 524320 | tf_op jit(solution)/shard_map/ppermute | solution.py:273
  951.6 12.4 %collective-permute-done.69 = bf16[2,2,32,2048]{3,2,0,1:T(8,128)(2,1)S(1)} collective-permute-done((bf16[2,2,32,2048]{3,2,0,1:T(8,128)(2,1)S(1)}, bf16[2,2,32,2048]{3,2,0,1:T(8,128)(2,1)S(1)}, u32[]{:S(2)}, u32[]{:S(2)}) %collective-permute-start.69) | collective-permute-done | bytes 524320 | tf_op jit(solution)/shard_map/ppermute | solution.py:273
  970.9 4.2 collective-permute-done.70
  978.3 11.4 %collective-permute-done.71 = bf16[32,2048]{1,0:T(8,128)(2,1)S(1)} collective-permute-done((bf16[32,2048]{1,0:T(8,128)(2,1)S(1)}, bf16[32,2048]{1,0:T(8,128)(2,1)S(1)}, u32[]{:S(2)}, u32[]{:S(2)}) %collective-permute-start.71) | collective-permute-done | bytes 131104 | tf_op jit(solution)/shard_map/ppermute | solution.py:273
  990.0 6.5 collective-permute-done.57
  1002.1 7.5 collective-permute-done.39
  1013.1 9.8 collective-permute-done.40
  (567 shorter events, 250.7 us)
Async XLA Ops:
  7.2 162.4 %all-gather.4.cloned.1.call-start = ((), (), s32[]{:S(2)}) async-start(), calls=%async_computation | async-start | bytes 2228224 | tf_op jit(solution)/shard_map/all_gather | solution.py:431
  108.8 230.4 %all-gather.6.cloned.1.call-start = ((), (), s32[]{:S(2)}) async-start(), calls=%async_computation.1 | async-start | bytes 8912896 | tf_op jit(solution)/shard_map/all_gather | solution.py:486
  443.1 396.8 %collective-permute-start.64 = (bf16[1024,2048]{1,0:T(8,128)(2,1)}, bf16[1024,2048]{1,0:T(8,128)(2,1)}, u32[]{:S(2)}, u32[]{:S(2)}) collective-permute-start(bf16[1024,2048]{1,0:T(8,128)(2,1)} %get-tuple-element.527), channel_id=1, source_target_pairs={{0,1},{1,0},{2,3},{3,2},{4,5},{5,4},{6,7},{7,6},{8,9},{9,8},{10,11... | collective-permute-start | bytes 12582920 | tf_op jit(solution)/shard_map/ppermute | solution.py:526
  447.8 398.4 %collective-permute-start.65 = (bf16[1024,2048]{1,0:T(8,128)(2,1)}, bf16[1024,2048]{1,0:T(8,128)(2,1)}, u32[]{:S(2)}, u32[]{:S(2)}) collective-permute-start(bf16[1024,2048]{1,0:T(8,128)(2,1)} %get-tuple-element.529), channel_id=1, source_target_pairs={{0,1},{1,0},{2,3},{3,2},{4,5},{5,4},{6,7},{7,6},{8,9},{9,8},{10,11... | collective-permute-start | bytes 12582920 | tf_op jit(solution)/shard_map/ppermute | solution.py:527
  453.5 28.1 %collective-permute-start.20 = (bf16[2,2,2,32,2048]{4,3,0,1,2:T(8,128)(2,1)S(1)}, bf16[2,2,2,32,2048]{4,3,0,1,2:T(8,128)(2,1)S(1)}, u32[]{:S(2)}, u32[]{:S(2)}) collective-permute-start(bf16[2,2,2,32,2048]{4,3,0,1,2:T(8,128)(2,1)S(1)} %bitcast.808), channel_id=1, source_target_pairs={{0,8},{2,10},{4,12},{6,14},{8,0},{10,2},{12,4},{14,6},{16,24},{18,... | collective-permute-start | bytes 3145736 | tf_op jit(solution)/shard_map/ppermute | solution.py:273
  456.8 45.9 %collective-permute-start.16 = (bf16[2,2,2,48,2048]{4,3,0,2,1:T(8,128)(2,1)S(1)}, bf16[2,2,2,48,2048]{4,3,0,2,1:T(8,128)(2,1)S(1)}, u32[]{:S(2)}, u32[]{:S(2)}) collective-permute-start(bf16[2,2,2,48,2048]{4,3,0,2,1:T(8,128)(2,1)S(1)} %bitcast.805), channel_id=1, source_target_pairs={{0,4},{2,6},{4,0},{6,2},{8,12},{10,14},{12,8},{14,10},{16,20},{18,... | collective-permute-start | bytes 4718600 | tf_op jit(solution)/shard_map/ppermute | solution.py:273
  457.7 43.8 %collective-permute-start.8 = (bf16[2,2,2,32,2048]{4,3,0,1,2:T(8,128)(2,1)S(1)}, bf16[2,2,2,32,2048]{4,3,0,1,2:T(8,128)(2,1)S(1)}, u32[]{:S(2)}, u32[]{:S(2)}) collective-permute-start(bf16[2,2,2,32,2048]{4,3,0,1,2:T(8,128)(2,1)S(1)} %bitcast.809), channel_id=1, source_target_pairs={{0,8},{2,10},{4,12},{6,14},{8,0},{10,2},{12,4},{14,6},{16,24},{18,... | collective-permute-start | bytes 3145736 | tf_op jit(solution)/shard_map/ppermute | solution.py:273
  481.6 36.1 %collective-permute-start.12 = (bf16[2,2,2,48,2048]{4,3,0,1,2:T(8,128)(2,1)S(1)}, bf16[2,2,2,48,2048]{4,3,0,1,2:T(8,128)(2,1)S(1)}, u32[]{:S(2)}, u32[]{:S(2)}) collective-permute-start(bf16[2,2,2,48,2048]{4,3,0,1,2:T(8,128)(2,1)S(1)} %bitcast.807), channel_id=1, source_target_pairs={{0,2},{2,0},{4,6},{6,4},{8,10},{10,8},{12,14},{14,12},{16,18},{18,... | collective-permute-start | bytes 4718600 | tf_op jit(solution)/shard_map/ppermute | solution.py:273
  501.5 35.7 %collective-permute-start.4 = (bf16[2,2,2,48,2048]{4,3,0,2,1:T(8,128)(2,1)S(1)}, bf16[2,2,2,48,2048]{4,3,0,2,1:T(8,128)(2,1)S(1)}, u32[]{:S(2)}, u32[]{:S(2)}) collective-permute-start(bf16[2,2,2,48,2048]{4,3,0,2,1:T(8,128)(2,1)S(1)} %bitcast.806), channel_id=1, source_target_pairs={{0,4},{2,6},{4,0},{6,2},{8,12},{10,14},{12,8},{14,10},{16,20},{18,... | collective-permute-start | bytes 4718600 | tf_op jit(solution)/shard_map/ppermute | solution.py:273
  502.7 365.2 %collective-permute-start.66 = (bf16[1024,2048]{1,0:T(8,128)(2,1)}, bf16[1024,2048]{1,0:T(8,128)(2,1)}, u32[]{:S(2)}, u32[]{:S(2)}) collective-permute-start(bf16[1024,2048]{1,0:T(8,128)(2,1)} %get-tuple-element.531), channel_id=1, source_target_pairs={{0,1},{1,0},{2,3},{3,2},{4,5},{5,4},{6,7},{7,6},{8,9},{9,8},{10,11... | collective-permute-start | bytes 12582920 | tf_op jit(solution)/shard_map/ppermute | solution.py:528
  517.7 59.2 %collective-permute-start = (bf16[2,2,2,48,2048]{4,3,0,1,2:T(8,128)(2,1)S(1)}, bf16[2,2,2,48,2048]{4,3,0,1,2:T(8,128)(2,1)S(1)}, u32[]{:S(2)}, u32[]{:S(2)}) collective-permute-start(bf16[2,2,2,48,2048]{4,3,0,1,2:T(8,128)(2,1)S(1)} %bitcast.804), channel_id=1, source_target_pairs={{0,2},{2,0},{4,6},{6,4},{8,10},{10,8},{12,14},{14,12},{16,18},{18,... | collective-permute-start | bytes 4718600 | tf_op jit(solution)/shard_map/ppermute | solution.py:273
  537.2 27.0 %collective-permute-start.21 = (bf16[2,2,32,2048]{3,2,0,1:T(8,128)(2,1)S(1)}, bf16[2,2,32,2048]{3,2,0,1:T(8,128)(2,1)S(1)}, u32[]{:S(2)}, u32[]{:S(2)}) collective-permute-start(bf16[2,2,32,2048]{3,2,0,1:T(8,128)(2,1)S(1)} %dynamic-slice_bitcast_fusion.17), channel_id=1, source_target_pairs={{0,2},{2,0},{4,6},{6,4},{8,10},{10,8},{12,14},{14,12},{16,18},{18,... | collective-permute-start | bytes 1572872 | tf_op jit(solution)/shard_map/ppermute | solution.py:273
  564.2 11.9 %collective-permute-start.9 = (bf16[2,2,32,2048]{3,2,0,1:T(8,128)(2,1)S(1)}, bf16[2,2,32,2048]{3,2,0,1:T(8,128)(2,1)S(1)}, u32[]{:S(2)}, u32[]{:S(2)}) collective-permute-start(bf16[2,2,32,2048]{3,2,0,1:T(8,128)(2,1)S(1)} %dynamic-slice_bitcast_fusion.18), channel_id=1, source_target_pairs={{0,2},{2,0},{4,6},{6,4},{8,10},{10,8},{12,14},{14,12},{16,18},{18,... | collective-permute-start | bytes 1572872 | tf_op jit(solution)/shard_map/ppermute | solution.py:273
  576.0 7.7 collective-permute-start.22
  576.9 32.9 %collective-permute-start.17 = (bf16[2,2,48,2048]{3,2,0,1:T(8,128)(2,1)S(1)}, bf16[2,2,48,2048]{3,2,0,1:T(8,128)(2,1)S(1)}, u32[]{:S(2)}, u32[]{:S(2)}) collective-permute-start(bf16[2,2,48,2048]{3,2,0,1:T(8,128)(2,1)S(1)} %dynamic-slice_bitcast_fusion.7), channel_id=1, source_target_pairs={{0,8},{2,10},{4,12},{6,14},{8,0},{10,2},{12,4},{14,6},{16,24},{18,... | collective-permute-start | bytes 2359304 | tf_op jit(solution)/shard_map/ppermute | solution.py:273
  583.8 6.4 collective-permute-start.10
  590.1 8.4 collective-permute-start.23
  604.4 21.0 %collective-permute-start.13 = (bf16[2,2,48,2048]{3,2,0,1:T(8,128)(2,1)S(1)}, bf16[2,2,48,2048]{3,2,0,1:T(8,128)(2,1)S(1)}, u32[]{:S(2)}, u32[]{:S(2)}) collective-permute-start(bf16[2,2,48,2048]{3,2,0,1:T(8,128)(2,1)S(1)} %dynamic-slice_bitcast_fusion.8), channel_id=1, source_target_pairs={{0,4},{2,6},{4,0},{6,2},{8,12},{10,14},{12,8},{14,10},{16,20},{18,... | collective-permute-start | bytes 2359304 | tf_op jit(solution)/shard_map/ppermute | solution.py:273
  609.8 18.0 %collective-permute-start.5 = (bf16[2,2,48,2048]{3,2,0,1:T(8,128)(2,1)S(1)}, bf16[2,2,48,2048]{3,2,0,1:T(8,128)(2,1)S(1)}, u32[]{:S(2)}, u32[]{:S(2)}) collective-permute-start(bf16[2,2,48,2048]{3,2,0,1:T(8,128)(2,1)S(1)} %dynamic-slice_bitcast_fusion.9), channel_id=1, source_target_pairs={{0,8},{2,10},{4,12},{6,14},{8,0},{10,2},{12,4},{14,6},{16,24},{18,... | collective-permute-start | bytes 2359304 | tf_op jit(solution)/shard_map/ppermute | solution.py:273
  625.5 12.1 %collective-permute-start.1 = (bf16[2,2,48,2048]{3,2,0,1:T(8,128)(2,1)S(1)}, bf16[2,2,48,2048]{3,2,0,1:T(8,128)(2,1)S(1)}, u32[]{:S(2)}, u32[]{:S(2)}) collective-permute-start(bf16[2,2,48,2048]{3,2,0,1:T(8,128)(2,1)S(1)} %dynamic-slice_bitcast_fusion.10), channel_id=1, source_target_pairs={{0,4},{2,6},{4,0},{6,2},{8,12},{10,14},{12,8},{14,10},{16,20},{18,... | collective-permute-start | bytes 2359304 | tf_op jit(solution)/shard_map/ppermute | solution.py:273
  627.9 11.3 %collective-permute-start.18 = (bf16[2,48,2048]{2,1,0:T(8,128)(2,1)S(1)}, bf16[2,48,2048]{2,1,0:T(8,128)(2,1)S(1)}, u32[]{:S(2)}, u32[]{:S(2)}) collective-permute-start(bf16[2,48,2048]{2,1,0:T(8,128)(2,1)S(1)} %dynamic-slice_bitcast_fusion.19), channel_id=1, source_target_pairs={{0,2},{2,0},{4,6},{6,4},{8,10},{10,8},{12,14},{14,12},{16,18},{18,... | collective-permute-start | bytes 1179656 | tf_op jit(solution)/shard_map/ppermute | solution.py:273
  637.6 11.8 %collective-permute-start.14 = (bf16[2,48,2048]{2,1,0:T(8,128)(2,1)S(1)}, bf16[2,48,2048]{2,1,0:T(8,128)(2,1)S(1)}, u32[]{:S(2)}, u32[]{:S(2)}) collective-permute-start(bf16[2,48,2048]{2,1,0:T(8,128)(2,1)S(1)} %dynamic-slice_bitcast_fusion.20), channel_id=1, source_target_pairs={{0,8},{2,10},{4,12},{6,14},{8,0},{10,2},{12,4},{14,6},{16,24},{18,... | collective-permute-start | bytes 1179656 | tf_op jit(solution)/shard_map/ppermute | solution.py:273
  639.2 11.7 %collective-permute-start.6 = (bf16[2,48,2048]{2,1,0:T(8,128)(2,1)S(1)}, bf16[2,48,2048]{2,1,0:T(8,128)(2,1)S(1)}, u32[]{:S(2)}, u32[]{:S(2)}) collective-permute-start(bf16[2,48,2048]{2,1,0:T(8,128)(2,1)S(1)} %dynamic-slice_bitcast_fusion.21), channel_id=1, source_target_pairs={{0,2},{2,0},{4,6},{6,4},{8,10},{10,8},{12,14},{14,12},{16,18},{18,... | collective-permute-start | bytes 1179656 | tf_op jit(solution)/shard_map/ppermute | solution.py:273
  649.4 11.9 %collective-permute-start.2 = (bf16[2,48,2048]{2,1,0:T(8,128)(2,1)S(1)}, bf16[2,48,2048]{2,1,0:T(8,128)(2,1)S(1)}, u32[]{:S(2)}, u32[]{:S(2)}) collective-permute-start(bf16[2,48,2048]{2,1,0:T(8,128)(2,1)S(1)} %dynamic-slice_bitcast_fusion.22), channel_id=1, source_target_pairs={{0,8},{2,10},{4,12},{6,14},{8,0},{10,2},{12,4},{14,6},{16,24},{18,... | collective-permute-start | bytes 1179656 | tf_op jit(solution)/shard_map/ppermute | solution.py:273
  650.9 15.2 %collective-permute-start.19 = (bf16[48,2048]{1,0:T(8,128)(2,1)S(1)}, bf16[48,2048]{1,0:T(8,128)(2,1)S(1)}, u32[]{:S(2)}, u32[]{:S(2)}) collective-permute-start(bf16[48,2048]{1,0:T(8,128)(2,1)S(1)} %dynamic-slice_bitcast_fusion.33), channel_id=1, source_target_pairs={{0,16},{2,18},{4,20},{6,22},{8,24},{10,26},{12,28},{14,30},{16,0},... | collective-permute-start | bytes 589832 | tf_op jit(solution)/shard_map/ppermute | solution.py:273
  661.3 13.2 %collective-permute-start.15 = (bf16[48,2048]{1,0:T(8,128)(2,1)S(1)}, bf16[48,2048]{1,0:T(8,128)(2,1)S(1)}, u32[]{:S(2)}, u32[]{:S(2)}) collective-permute-start(bf16[48,2048]{1,0:T(8,128)(2,1)S(1)} %dynamic-slice_bitcast_fusion.34), channel_id=1, source_target_pairs={{0,16},{2,18},{4,20},{6,22},{8,24},{10,26},{12,28},{14,30},{16,0},... | collective-permute-start | bytes 589832 | tf_op jit(solution)/shard_map/ppermute | solution.py:273
  666.1 10.8 %collective-permute-start.7 = (bf16[48,2048]{1,0:T(8,128)(2,1)S(1)}, bf16[48,2048]{1,0:T(8,128)(2,1)S(1)}, u32[]{:S(2)}, u32[]{:S(2)}) collective-permute-start(bf16[48,2048]{1,0:T(8,128)(2,1)S(1)} %dynamic-slice_bitcast_fusion.35), channel_id=1, source_target_pairs={{0,16},{2,18},{4,20},{6,22},{8,24},{10,26},{12,28},{14,30},{16,0},... | collective-permute-start | bytes 589832 | tf_op jit(solution)/shard_map/ppermute | solution.py:273
  674.5 8.1 collective-permute-start.3
  714.3 24.5 %collective-permute-start.32 = (bf16[2,2,2,32,512]{4,3,0,1,2:T(8,128)(2,1)S(1)}, bf16[2,2,2,32,512]{4,3,0,1,2:T(8,128)(2,1)S(1)}, u32[]{:S(2)}, u32[]{:S(2)}) collective-permute-start(bf16[2,2,2,32,512]{4,3,0,1,2:T(8,128)(2,1)S(1)} %bitcast.815), channel_id=1, source_target_pairs={{0,8},{2,10},{4,12},{6,14},{8,0},{10,2},{12,4},{14,6},{16,24},{18,... | collective-permute-start | bytes 786440 | tf_op jit(solution)/shard_map/ppermute | solution.py:273
  724.5 26.1 %collective-permute-start.28 = (bf16[2,2,2,48,512]{4,3,0,2,1:T(8,128)(2,1)}, bf16[2,2,2,48,512]{4,3,0,2,1:T(8,128)(2,1)}, u32[]{:S(2)}, u32[]{:S(2)}) collective-permute-start(bf16[2,2,2,48,512]{4,3,0,2,1:T(8,128)(2,1)} %bitcast.694), channel_id=1, source_target_pairs={{0,4},{2,6},{4,0},{6,2},{8,12},{10,14},{12,8},{14,10},{16,20},{18,... | collective-permute-start | bytes 1179656 | tf_op jit(solution)/shard_map/ppermute | solution.py:273
  739.6 8.8 collective-permute-start.33
  748.4 7.8 collective-permute-start.24
  750.6 127.8 %collective-permute-start.58 = (bf16[2,2,2,2,32,2048]{5,4,0,3,1,2:T(8,128)(2,1)}, bf16[2,2,2,2,32,2048]{5,4,0,3,1,2:T(8,128)(2,1)}, u32[]{:S(2)}, u32[]{:S(2)}) collective-permute-start(bf16[2,2,2,2,32,2048]{5,4,0,3,1,2:T(8,128)(2,1)} %bitcast.684), channel_id=1, source_target_pairs={{0,1},{1,0},{2,3},{3,2},{4,5},{5,4},{6,7},{7,6},{8,9},{9,8},{10,11... | collective-permute-start | bytes 6291464 | tf_op jit(solution)/shard_map/ppermute | solution.py:273
  760.5 11.5 %collective-permute-start.35 = (bf16[32,512]{1,0:T(8,128)(2,1)S(1)}, bf16[32,512]{1,0:T(8,128)(2,1)S(1)}, u32[]{:S(2)}, u32[]{:S(2)}) collective-permute-start(bf16[32,512]{1,0:T(8,128)(2,1)S(1)} %fusion.208), channel_id=1, source_target_pairs={{0,16},{2,18},{4,20},{6,22},{8,24},{10,26},{12,28},{14,30},{16,0},... | collective-permute-start | bytes 98312 | tf_op jit(solution)/shard_map/ppermute | solution.py:273
  802.9 78.9 %collective-permute-start.53 = (bf16[2,2,2,2,32,2048]{5,4,0,1,2,3:T(8,128)(2,1)}, bf16[2,2,2,2,32,2048]{5,4,0,1,2,3:T(8,128)(2,1)}, u32[]{:S(2)}, u32[]{:S(2)}) collective-permute-start(bf16[2,2,2,2,32,2048]{5,4,0,1,2,3:T(8,128)(2,1)} %bitcast.685), channel_id=1, source_target_pairs={{0,1},{1,0},{2,3},{3,2},{4,5},{5,4},{6,7},{7,6},{8,9},{9,8},{10,11... | collective-permute-start | bytes 6291464 | tf_op jit(solution)/shard_map/ppermute | solution.py:273
  839.9 46.2 %collective-permute-start.67 = (bf16[2,2,2,2,32,2048]{5,4,0,2,3,1:T(8,128)(2,1)}, bf16[2,2,2,2,32,2048]{5,4,0,2,3,1:T(8,128)(2,1)}, u32[]{:S(2)}, u32[]{:S(2)}) collective-permute-start(bf16[2,2,2,2,32,2048]{5,4,0,2,3,1:T(8,128)(2,1)} %bitcast.683), channel_id=1, source_target_pairs={{0,1},{1,0},{2,3},{3,2},{4,5},{5,4},{6,7},{7,6},{8,9},{9,8},{10,11... | collective-permute-start | bytes 6291464 | tf_op jit(solution)/shard_map/ppermute | solution.py:273
  846.2 43.9 %collective-permute-start.36 = (bf16[2,2,2,2,32,2048]{5,4,3,2,1,0:T(8,128)(2,1)}, bf16[2,2,2,2,32,2048]{5,4,3,2,1,0:T(8,128)(2,1)}, u32[]{:S(2)}, u32[]{:S(2)}) collective-permute-start(bf16[2,2,2,2,32,2048]{5,4,3,2,1,0:T(8,128)(2,1)} %dynamic-slice_bitcast_fusion), channel_id=1, source_target_pairs={{0,1},{1,0},{2,3},{3,2},{4,5},{5,4},{6,7},{7,6},{8,9},{9,8},{10,11... | collective-permute-start | bytes 6291464 | tf_op jit(solution)/shard_map/ppermute | solution.py:273
  867.9 26.8 %collective-permute-start.47 = (bf16[2,2,2,2,32,2048]{5,4,0,3,1,2:T(8,128)(2,1)}, bf16[2,2,2,2,32,2048]{5,4,0,3,1,2:T(8,128)(2,1)S(1)}, u32[]{:S(2)}, u32[]{:S(2)}) collective-permute-start(bf16[2,2,2,2,32,2048]{5,4,0,3,1,2:T(8,128)(2,1)} %bitcast.802), channel_id=1, source_target_pairs={{0,1},{1,0},{2,3},{3,2},{4,5},{5,4},{6,7},{7,6},{8,9},{9,8},{10,11... | collective-permute-start | bytes 6291464 | tf_op jit(solution)/shard_map/ppermute | solution.py:273
  878.5 17.5 %collective-permute-start.42 = (bf16[2,2,2,2,32,2048]{5,4,0,1,2,3:T(8,128)(2,1)S(1)}, bf16[2,2,2,2,32,2048]{5,4,0,1,2,3:T(8,128)(2,1)S(1)}, u32[]{:S(2)}, u32[]{:S(2)}) collective-permute-start(bf16[2,2,2,2,32,2048]{5,4,0,1,2,3:T(8,128)(2,1)S(1)} %bitcast.801), channel_id=1, source_target_pairs={{0,1},{1,0},{2,3},{3,2},{4,5},{5,4},{6,7},{7,6},{8,9},{9,8},{10,11... | collective-permute-start | bytes 6291464 | tf_op jit(solution)/shard_map/ppermute | solution.py:273
  881.8 26.1 %collective-permute-start.59 = (bf16[2,2,2,32,2048]{4,3,0,2,1:T(8,128)(2,1)S(1)}, bf16[2,2,2,32,2048]{4,3,0,2,1:T(8,128)(2,1)S(1)}, u32[]{:S(2)}, u32[]{:S(2)}) collective-permute-start(bf16[2,2,2,32,2048]{4,3,0,2,1:T(8,128)(2,1)S(1)} %dynamic-slice_bitcast_fusion.2), channel_id=1, source_target_pairs={{0,4},{2,6},{4,0},{6,2},{8,12},{10,14},{12,8},{14,10},{16,20},{18,... | collective-permute-start | bytes 3145736 | tf_op jit(solution)/shard_map/ppermute | solution.py:273
  886.0 26.1 %collective-permute-start.54 = (bf16[2,2,2,32,2048]{4,3,0,1,2:T(8,128)(2,1)S(1)}, bf16[2,2,2,32,2048]{4,3,0,1,2:T(8,128)(2,1)S(1)}, u32[]{:S(2)}, u32[]{:S(2)}) collective-permute-start(bf16[2,2,2,32,2048]{4,3,0,1,2:T(8,128)(2,1)S(1)} %dynamic-slice_bitcast_fusion.3), channel_id=1, source_target_pairs={{0,2},{2,0},{4,6},{6,4},{8,10},{10,8},{12,14},{14,12},{16,18},{18,... | collective-permute-start | bytes 3145736 | tf_op jit(solution)/shard_map/ppermute | solution.py:273
  890.1 26.1 %collective-permute-start.68 = (bf16[2,2,2,32,2048]{4,3,0,1,2:T(8,128)(2,1)S(1)}, bf16[2,2,2,32,2048]{4,3,0,1,2:T(8,128)(2,1)S(1)}, u32[]{:S(2)}, u32[]{:S(2)}) collective-permute-start(bf16[2,2,2,32,2048]{4,3,0,1,2:T(8,128)(2,1)S(1)} %dynamic-slice_bitcast_fusion.1), channel_id=1, source_target_pairs={{0,8},{2,10},{4,12},{6,14},{8,0},{10,2},{12,4},{14,6},{16,24},{18,... | collective-permute-start | bytes 3145736 | tf_op jit(solution)/shard_map/ppermute | solution.py:273
  894.7 71.2 %collective-permute-start.37 = (bf16[2,2,2,32,2048]{4,3,2,1,0:T(8,128)(2,1)S(1)}, bf16[2,2,2,32,2048]{4,3,2,1,0:T(8,128)(2,1)S(1)}, u32[]{:S(2)}, u32[]{:S(2)}) collective-permute-start(bf16[2,2,2,32,2048]{4,3,2,1,0:T(8,128)(2,1)S(1)} %dynamic-slice_bitcast_fusion.6), channel_id=1, source_target_pairs={{0,8},{2,10},{4,12},{6,14},{8,0},{10,2},{12,4},{14,6},{16,24},{18,... | collective-permute-start | bytes 3145736 | tf_op jit(solution)/shard_map/ppermute | solution.py:273
  896.0 70.8 %collective-permute-start.48 = (bf16[2,2,2,32,2048]{4,3,0,2,1:T(8,128)(2,1)S(1)}, bf16[2,2,2,32,2048]{4,3,0,2,1:T(8,128)(2,1)S(1)}, u32[]{:S(2)}, u32[]{:S(2)}) collective-permute-start(bf16[2,2,2,32,2048]{4,3,0,2,1:T(8,128)(2,1)S(1)} %dynamic-slice_bitcast_fusion.4), channel_id=1, source_target_pairs={{0,4},{2,6},{4,0},{6,2},{8,12},{10,14},{12,8},{14,10},{16,20},{18,... | collective-permute-start | bytes 3145736 | tf_op jit(solution)/shard_map/ppermute | solution.py:273
  907.9 60.5 %collective-permute-start.43 = (bf16[2,2,2,32,2048]{4,3,0,1,2:T(8,128)(2,1)S(1)}, bf16[2,2,2,32,2048]{4,3,0,1,2:T(8,128)(2,1)S(1)}, u32[]{:S(2)}, u32[]{:S(2)}) collective-permute-start(bf16[2,2,2,32,2048]{4,3,0,1,2:T(8,128)(2,1)S(1)} %dynamic-slice_bitcast_fusion.5), channel_id=1, source_target_pairs={{0,2},{2,0},{4,6},{6,4},{8,10},{10,8},{12,14},{14,12},{16,18},{18,... | collective-permute-start | bytes 3145736 | tf_op jit(solution)/shard_map/ppermute | solution.py:273
  912.1 37.0 %collective-permute-start.60 = (bf16[2,2,32,2048]{3,2,0,1:T(8,128)(2,1)S(1)}, bf16[2,2,32,2048]{3,2,0,1:T(8,128)(2,1)S(1)}, u32[]{:S(2)}, u32[]{:S(2)}) collective-permute-start(bf16[2,2,32,2048]{3,2,0,1:T(8,128)(2,1)S(1)} %dynamic-slice_bitcast_fusion.12), channel_id=1, source_target_pairs={{0,8},{2,10},{4,12},{6,14},{8,0},{10,2},{12,4},{14,6},{16,24},{18,... | collective-permute-start | bytes 1572872 | tf_op jit(solution)/shard_map/ppermute | solution.py:273
  916.2 34.0 %collective-permute-start.55 = (bf16[2,2,32,2048]{3,2,0,1:T(8,128)(2,1)S(1)}, bf16[2,2,32,2048]{3,2,0,1:T(8,128)(2,1)S(1)}, u32[]{:S(2)}, u32[]{:S(2)}) collective-permute-start(bf16[2,2,32,2048]{3,2,0,1:T(8,128)(2,1)S(1)} %dynamic-slice_bitcast_fusion.13), channel_id=1, source_target_pairs={{0,4},{2,6},{4,0},{6,2},{8,12},{10,14},{12,8},{14,10},{16,20},{18,... | collective-permute-start | bytes 1572872 | tf_op jit(solution)/shard_map/ppermute | solution.py:273
  949.2 14.8 %collective-permute-start.69 = (bf16[2,2,32,2048]{3,2,0,1:T(8,128)(2,1)S(1)}, bf16[2,2,32,2048]{3,2,0,1:T(8,128)(2,1)S(1)}, u32[]{:S(2)}, u32[]{:S(2)}) collective-permute-start(bf16[2,2,32,2048]{3,2,0,1:T(8,128)(2,1)S(1)} %dynamic-slice_bitcast_fusion.11), channel_id=1, source_target_pairs={{0,2},{2,0},{4,6},{6,4},{8,10},{10,8},{12,14},{14,12},{16,18},{18,... | collective-permute-start | bytes 1572872 | tf_op jit(solution)/shard_map/ppermute | solution.py:273
  950.3 19.3 %collective-permute-start.61 = (bf16[2,32,2048]{2,1,0:T(8,128)(2,1)S(1)}, bf16[2,32,2048]{2,1,0:T(8,128)(2,1)S(1)}, u32[]{:S(2)}, u32[]{:S(2)}) collective-permute-start(bf16[2,32,2048]{2,1,0:T(8,128)(2,1)S(1)} %dynamic-slice_bitcast_fusion.24), channel_id=1, source_target_pairs={{0,2},{2,0},{4,6},{6,4},{8,10},{10,8},{12,14},{14,12},{16,18},{18,... | collective-permute-start | bytes 786440 | tf_op jit(solution)/shard_map/ppermute | solution.py:273
  964.0 14.2 %collective-permute-start.56 = (bf16[2,32,2048]{2,1,0:T(8,128)(2,1)S(1)}, bf16[2,32,2048]{2,1,0:T(8,128)(2,1)S(1)}, u32[]{:S(2)}, u32[]{:S(2)}) collective-permute-start(bf16[2,32,2048]{2,1,0:T(8,128)(2,1)S(1)} %dynamic-slice_bitcast_fusion.25), channel_id=1, source_target_pairs={{0,8},{2,10},{4,12},{6,14},{8,0},{10,2},{12,4},{14,6},{16,24},{18,... | collective-permute-start | bytes 786440 | tf_op jit(solution)/shard_map/ppermute | solution.py:273
  965.9 9.2 collective-permute-start.70
  966.8 33.8 %collective-permute-start.38 = (bf16[2,2,32,2048]{3,2,1,0:T(8,128)(2,1)S(1)}, bf16[2,2,32,2048]{3,2,1,0:T(8,128)(2,1)S(1)}, u32[]{:S(2)}, u32[]{:S(2)}) collective-permute-start(bf16[2,2,32,2048]{3,2,1,0:T(8,128)(2,1)S(1)} %dynamic-slice_bitcast_fusion.16), channel_id=1, source_target_pairs={{0,2},{2,0},{4,6},{6,4},{8,10},{10,8},{12,14},{14,12},{16,18},{18,... | collective-permute-start | bytes 1572872 | tf_op jit(solution)/shard_map/ppermute | solution.py:273
  968.4 32.5 %collective-permute-start.49 = (bf16[2,2,32,2048]{3,2,0,1:T(8,128)(2,1)S(1)}, bf16[2,2,32,2048]{3,2,0,1:T(8,128)(2,1)S(1)}, u32[]{:S(2)}, u32[]{:S(2)}) collective-permute-start(bf16[2,2,32,2048]{3,2,0,1:T(8,128)(2,1)S(1)} %dynamic-slice_bitcast_fusion.14), channel_id=1, source_target_pairs={{0,8},{2,10},{4,12},{6,14},{8,0},{10,2},{12,4},{14,6},{16,24},{18,... | collective-permute-start | bytes 1572872 | tf_op jit(solution)/shard_map/ppermute | solution.py:273
  969.6 31.6 %collective-permute-start.44 = (bf16[2,2,32,2048]{3,2,0,1:T(8,128)(2,1)S(1)}, bf16[2,2,32,2048]{3,2,0,1:T(8,128)(2,1)S(1)}, u32[]{:S(2)}, u32[]{:S(2)}) collective-permute-start(bf16[2,2,32,2048]{3,2,0,1:T(8,128)(2,1)S(1)} %dynamic-slice_bitcast_fusion.15), channel_id=1, source_target_pairs={{0,4},{2,6},{4,0},{6,2},{8,12},{10,14},{12,8},{14,10},{16,20},{18,... | collective-permute-start | bytes 1572872 | tf_op jit(solution)/shard_map/ppermute | solution.py:273
  975.1 14.7 %collective-permute-start.62 = (bf16[32,2048]{1,0:T(8,128)(2,1)S(1)}, bf16[32,2048]{1,0:T(8,128)(2,1)S(1)}, u32[]{:S(2)}, u32[]{:S(2)}) collective-permute-start(bf16[32,2048]{1,0:T(8,128)(2,1)S(1)} %dynamic-slice_bitcast_fusion.38), channel_id=1, source_target_pairs={{0,16},{2,18},{4,20},{6,22},{8,24},{10,26},{12,28},{14,30},{16,0},... | collective-permute-start | bytes 393224 | tf_op jit(solution)/shard_map/ppermute | solution.py:273
  978.1 11.6 %collective-permute-start.71 = (bf16[32,2048]{1,0:T(8,128)(2,1)S(1)}, bf16[32,2048]{1,0:T(8,128)(2,1)S(1)}, u32[]{:S(2)}, u32[]{:S(2)}) collective-permute-start(bf16[32,2048]{1,0:T(8,128)(2,1)S(1)} %dynamic-slice_bitcast_fusion.37), channel_id=1, source_target_pairs={{0,16},{2,18},{4,20},{6,22},{8,24},{10,26},{12,28},{14,30},{16,0},... | collective-permute-start | bytes 393224 | tf_op jit(solution)/shard_map/ppermute | solution.py:273
  989.8 6.7 collective-permute-start.57
  989.8 6.8 collective-permute-start.72
  1000.8 8.8 collective-permute-start.39
  1001.1 8.8 collective-permute-start.50
  1001.3 11.5 %collective-permute-start.45 = (bf16[2,32,2048]{2,1,0:T(8,128)(2,1)S(1)}, bf16[2,32,2048]{2,1,0:T(8,128)(2,1)S(1)}, u32[]{:S(2)}, u32[]{:S(2)}) collective-permute-start(bf16[2,32,2048]{2,1,0:T(8,128)(2,1)S(1)} %dynamic-slice_bitcast_fusion.27), channel_id=1, source_target_pairs={{0,8},{2,10},{4,12},{6,14},{8,0},{10,2},{12,4},{14,6},{16,24},{18,... | collective-permute-start | bytes 786440 | tf_op jit(solution)/shard_map/ppermute | solution.py:273
  1009.7 13.2 %collective-permute-start.40 = (bf16[32,2048]{1,0:T(8,128)(2,1)S(1)}, bf16[32,2048]{1,0:T(8,128)(2,1)S(1)}, u32[]{:S(2)}, u32[]{:S(2)}) collective-permute-start(bf16[32,2048]{1,0:T(8,128)(2,1)S(1)} %dynamic-slice_bitcast_fusion.42), channel_id=1, source_target_pairs={{0,16},{2,18},{4,20},{6,22},{8,24},{10,26},{12,28},{14,30},{16,0},... | collective-permute-start | bytes 393224 | tf_op jit(solution)/shard_map/ppermute | solution.py:273
  1009.9 15.8 %collective-permute-start.51 = (bf16[32,2048]{1,0:T(8,128)(2,1)S(1)}, bf16[32,2048]{1,0:T(8,128)(2,1)S(1)}, u32[]{:S(2)}, u32[]{:S(2)}) collective-permute-start(bf16[32,2048]{1,0:T(8,128)(2,1)S(1)} %dynamic-slice_bitcast_fusion.40), channel_id=1, source_target_pairs={{0,16},{2,18},{4,20},{6,22},{8,24},{10,26},{12,28},{14,30},{16,0},... | collective-permute-start | bytes 393224 | tf_op jit(solution)/shard_map/ppermute | solution.py:273
  1012.9 15.5 %collective-permute-start.46 = (bf16[32,2048]{1,0:T(8,128)(2,1)S(1)}, bf16[32,2048]{1,0:T(8,128)(2,1)S(1)}, u32[]{:S(2)}, u32[]{:S(2)}) collective-permute-start(bf16[32,2048]{1,0:T(8,128)(2,1)S(1)} %dynamic-slice_bitcast_fusion.41), channel_id=1, source_target_pairs={{0,16},{2,18},{4,20},{6,22},{8,24},{10,26},{12,28},{14,30},{16,0},... | collective-permute-start | bytes 393224 | tf_op jit(solution)/shard_map/ppermute | solution.py:273
  (98 other events, 1768.9 us)
Sparse Core Ops, SparseCore 0:
  108.9 60.6 all-gather.3
  172.4 156.9 all-gather.5

commit v3 on v2

--- a/solution.py
+++ b/solution.py
@@ -252,60 +252,249 @@
     return [first[i % len(first) :] + first[: i % len(first)] + rest for i in range(3)]
 
 
-def halving_sum(terms, order, place, with_core=False):
-    shards = terms.shape[0]
-    bits = shards.bit_length() - 1
-    current = terms.reshape((2,) * bits + terms.shape[1:])
-    left = list(range(bits))[::-1]
-    steps = [("fsdp", b) for b in order]
-    if with_core:
-        steps = [("dp", None)] + steps
-    for axis, b in steps:
-        if axis == "dp":
-            where, mine = bits, lax.axis_index("dp")
-            pairs = [(0, 1), (1, 0)]
+def add_rows(target, other):
+    rows = target.shape[0]
+    step = 16
+
+    @pl.loop(0, rows // step)
+    def _(i):
+        part = pl.ds(pl.multiple_of(i * step, step), step)
+        total = target[part].astype(jnp.float32) + other[part].astype(jnp.float32)
+        target[part] = total.astype(target.dtype)
+
+
+def scatter_kernel(terms_ref, out_ref, *refs):
+    held, c_buf, a_buf, b_buf, z_buf = refs[:5]
+    h_sem, c_send, c_recv, a_send, a_recv, b_send, b_recv, z_send, z_recv, o_send, o_recv = refs[5:]
+    f, z, y, x, fx, fy, visits = place_of()
+    core = lax.axis_index("dp")
+    visits = visits[::-1]
+    rows = out_ref.shape[0] // 2
+    base = pl.multiple_of(core * rows, 16)
+    away = pl.multiple_of((1 - core) * rows, 16)
+    part = rows // 2
+    loads = []
+    for k in range(LINE):
+        four = pl.ds(visits[k] * 4, 4)
+        copy = pltpu.make_async_copy(
+            terms_ref.at[four, pl.ds(base, rows)], held.at[four], h_sem.at[k]
+        )
+        copy.start()
+        loads.append(copy)
+    greet(f, z, fx, fy, True)
+
+    def spots(p, v):
+        piece = pl.ds(p * part, part)
+        both = held.at[v * 4 + (1 - y) * 2 + (1 - x), piece]
+        only_x = held.at[v * 4 + y * 2 + (1 - x), piece]
+        only_y = held.at[v * 4 + (1 - y) * 2 + x, piece]
+        own = held.at[v * 4 + y * 2 + x, piece]
+        return (both, only_x, only_y, own) if p == 0 else (both, only_y, only_x, own)
+
+    sent = []
+    near = ((fx, fy), (fy, fx))
+    for k in range(LINE):
+        source = terms_ref.at[pl.ds(visits[k] * 4, 4), pl.ds(away, rows)]
+        sent.append(send(source, c_buf.at[k], c_send.at[k], c_recv.at[k], {"dp": 1 - core}))
+
+    def start_a(k):
+        loads[k].wait()
+        arrived(c_buf.at[k], c_recv.at[k])
+        for j in range(4):
+            add_rows(held.at[visits[k] * 4 + j], c_buf.at[k, j])
+        for j in range(2):
+            for p in range(2):
+                sent.append(
+                    send(
+                        spots(p, visits[k])[j],
+                        a_buf.at[p, k, j],
+                        a_send.at[p, k, j],
+                        a_recv.at[p, k, j],
+                        {"fsdp": near[p][0]},
+                    )
+                )
+
+    def start_b(p, k):
+        flipped = spots(p, visits[k])[2]
+        arrived(a_buf.at[p, k, 0], a_recv.at[p, k, 0])
+        add_rows(flipped, a_buf.at[p, k, 0])
+        sent.append(
+            send(flipped, b_buf.at[p, k], b_send.at[p, k], b_recv.at[p, k], {"fsdp": near[p][1]})
+        )
+        arrived(a_buf.at[p, k, 1], a_recv.at[p, k, 1])
+        add_rows(spots(p, visits[k])[3], a_buf.at[p, k, 1])
+
+    def take(p, own, slot):
+        arrived(z_buf.at[p, slot], z_recv.at[p, slot])
+        add_rows(own, z_buf.at[p, slot])
+
+    def start_z(p, k):
+        v = visits[k]
+        own = spots(p, v)[3]
+        arrived(b_buf.at[p, k], b_recv.at[p, k])
+        add_rows(own, b_buf.at[p, k])
+        if k == LINE - 1:
+
+            @pl.when(z > 0)
+            def _():
+                take(p, own, z)
+
+            @pl.when(z < LINE - 1)
+            def _():
+                take(p, own, LINE)
+
+            return
+
+        @pl.when(v > z)
+        def _():
+            @pl.when(z > 0)
+            def _():
+                take(p, own, v)
+
+            send(own, z_buf.at[p, v], z_send.at[p, k], z_recv.at[p, v], {"fsdp": f + 4})
+
+        @pl.when(v < z)
+        def _():
+            @pl.when(z < LINE - 1)
+            def _():
+                take(p, own, v)
+
+            @pl.when(v == z - 1)
+            def _():
+                send(own, z_buf.at[p, LINE], z_send.at[p, k], z_recv.at[p, LINE], {"fsdp": f - 4})
+
+            @pl.when(v < z - 1)
+            def _():
+                send(own, z_buf.at[p, v], z_send.at[p, k], z_recv.at[p, v], {"fsdp": f - 4})
+
+    start_a(0)
+    start_a(1)
+    for k in range(LINE + 1):
+        if k + 2 < LINE:
+            start_a(k + 2)
+        if k < LINE:
+            for p in range(2):
+                start_b(p, k)
+        if k > 0:
+            for p in range(2):
+                start_z(p, k - 1)
+    step = 16
+
+    @pl.loop(0, rows // step)
+    def _(i):
+        offset = pl.multiple_of(i * step, step)
+        out_ref[pl.ds(pl.multiple_of(base + offset, step), step)] = held[f, pl.ds(offset, step)]
+
+    final = out_ref.at[pl.ds(base, rows)]
+    sent.append(send(final, final, o_send.at[0], o_recv.at[0], {"dp": 1 - core}))
+    arrived(out_ref.at[pl.ds(away, rows)], o_recv.at[0])
+    for copy in sent:
+        copy.wait_send()
+    for p in range(2):
+        for k in range(LINE - 1):
+            pltpu.make_async_copy(b_buf.at[p, k], b_buf.at[p, k], z_send.at[p, k]).wait()
+
+
+def scatter_blocks(terms, number):
+    shards, rows, columns = terms.shape
+    dma = pltpu.SemaphoreType.DMA
+    own = rows // 2
+    part = own // 2
+    return pl.pallas_call(
+        scatter_kernel,
+        out_shape=jax.ShapeDtypeStruct((rows, columns), terms.dtype),
+        in_specs=[pl.BlockSpec(memory_space=pl.ANY)],
+        out_specs=pl.BlockSpec(memory_space=pltpu.VMEM),
+        scratch_shapes=[
+            pltpu.VMEM((shards, own, columns), terms.dtype),
+            pltpu.VMEM((LINE, 4, own, columns), terms.dtype),
+            pltpu.VMEM((2, LINE, 2, part, columns), terms.dtype),
+            pltpu.VMEM((2, LINE, part, columns), terms.dtype),
+            pltpu.VMEM((2, LINE + 1, part, columns), terms.dtype),
+            dma((LINE,)),
+            dma((LINE,)),
+            dma((LINE,)),
+            dma((2, LINE, 2)),
+            dma((2, LINE, 2)),
+            dma((2, LINE)),
+            dma((2, LINE)),
+            dma((2, LINE)),
+            dma((2, LINE + 1)),
+            dma((1,)),
+            dma((1,)),
+        ],
+        compiler_params=pltpu.CompilerParams(
+            collective_id=number, has_side_effects=True, vmem_limit_bytes=40 * 1024 * 1024
+        ),
+        name="scatter_blocks_%d" % number,
+    )(terms)
+
+
+class HalvingSum:
+    def __init__(self, terms, place, shards, edges):
+        blocks = terms.reshape(shards, terms.shape[0] // shards, terms.shape[1])
+        self.place, self.shards, self.kind = place, shards, terms.dtype
+        self.bits = shards.bit_length() - 1
+        self.orders = bit_orders(self.bits)
+        self.held = [
+            blocks[:, low:high].reshape((2,) * self.bits + (high - low, terms.shape[1]))
+            for low, high in zip(edges[:-1], edges[1:])
+        ]
+        self.left = [list(range(self.bits))[::-1] for _ in self.held]
+        self.step = 0
+        self.came = []
+
+    def start(self):
+        self.keep, self.came = [], []
+        for i, current in enumerate(self.held):
+            b = self.orders[i][self.step]
+            where, mine = self.left[i].index(b), (self.place >> b) & 1
+            self.left[i].remove(b)
+            away = lax.dynamic_index_in_dim(current, 1 - mine, where, keepdims=False)
+            self.keep.append(lax.dynamic_index_in_dim(current, mine, where, keepdims=False))
+            pairs = [(j, j ^ (1 << b)) for j in range(self.shards)]
+            self.came.append(lax.ppermute(away, "fsdp", pairs))
+        self.step += 1
+
+    def finish(self, came):
+        totals = [k.astype(jnp.float32) + c.astype(jnp.float32) for k, c in zip(self.keep, came)]
+        if self.step == self.bits:
+            self.sum = jnp.concatenate(totals, axis=0)
         else:
-            where, mine = left.index(b), (place >> b) & 1
-            pairs = [(i, i ^ (1 << b)) for i in range(shards)]
-            left.remove(b)
-        away = lax.dynamic_index_in_dim(current, 1 - mine, where, keepdims=False)
-        keep = lax.dynamic_index_in_dim(current, mine, where, keepdims=False)
-        came = lax.ppermute(away, axis, pairs)
-        total = keep.astype(jnp.float32) + came.astype(jnp.float32)
-        current = total.astype(terms.dtype)
-    return total
-
-
-def scatter_rows(terms, place, shards):
-    blocks = terms.reshape(shards, terms.shape[0] // shards, terms.shape[1])
-    rows = blocks.shape[1]
+            self.held = [t.astype(self.kind) for t in totals]
+
+    def rest(self):
+        while self.step < self.bits:
+            self.start()
+            self.finish(self.came)
+        return self.sum
+
+
+def together(sums, work):
+    came, work = lax.optimization_barrier(([s.came for s in sums], work))
+    for one, own in zip(sums, came):
+        one.finish(own)
+    return work
+
+
+def row_edges(rows):
     third = (rows * 3 // 8) // 16 * 16
-    edges = [0, third, 2 * third, rows]
-    orders = bit_orders(shards.bit_length() - 1)
-    return jnp.concatenate(
-        [halving_sum(blocks[:, edges[i] : edges[i + 1]], orders[i], place) for i in range(3)],
-        axis=0,
-    )
-
-
-def scatter_both(big, small, place, core):
-    shards, rows, columns = big.shape
-    halves = big.reshape(shards, 2, 2, rows // 4, columns)
-    streams = [halves[:, 0], halves[:, 1], small.reshape(shards, 2, -1, columns)]
-    orders = bit_orders(shards.bit_length() - 1)
-    mine = jnp.stack(
-        [halving_sum(streams[i], orders[i], place, True).astype(big.dtype) for i in range(2)]
-    )
-    few = halving_sum(streams[2], orders[2], place, True).astype(big.dtype)
+    return [0, third, 2 * third, rows]
+
+
+def scatter_shared(terms, core):
+    half = terms.shape[2] // 2
     swap = [(0, 1), (1, 0)]
-
-    def both(own):
-        other = lax.ppermute(own, "dp", swap)
-        low = jnp.where(core == 0, own, other)
-        high = jnp.where(core == 0, other, own)
-        return jnp.stack([low, high], axis=-3).astype(jnp.float32)
-
-    return both(mine).reshape(rows, columns), both(few).reshape(-1, columns)
+    own = lax.dynamic_slice_in_dim(terms, core * half, half, 2)
+    away = lax.dynamic_slice_in_dim(terms, (1 - core) * half, half, 2)
+    both = own + lax.ppermute(away, "dp", swap)
+    mine = lax.psum_scatter(both, "fsdp", scatter_dimension=0, tiled=False)
+    theirs = lax.ppermute(mine, "dp", swap)
+    return jnp.where(
+        core == 0,
+        jnp.concatenate([mine, theirs], axis=1),
+        jnp.concatenate([theirs, mine], axis=1),
+    )
 
 
 def pack_rows(terms, shards, width):
@@ -399,10 +588,12 @@
     core_rows = in_rows // 2
 
     def split_heads(values):
-        return values.reshape(tok_rows, heads, head_size).transpose(1, 0, 2)
+        return jnp.stack(
+            [values[:, h * head_size : (h + 1) * head_size] for h in range(heads)]
+        )
 
     def join_heads(values):
-        return values.transpose(1, 0, 2).reshape(tok_rows, heads * head_size)
+        return jnp.concatenate([values[h] for h in range(heads)], axis=1)
 
     def merged_rows(matrix, first, second):
         own = lax.dynamic_slice_in_dim(matrix, core * core_rows, core_rows, 0)
@@ -421,16 +612,15 @@
         ),
         shards,
     )
-    cot_own = cotangent[0]
+    cot_own, key_value_weight = lax.optimization_barrier((cotangent[0], key_value_weight))
+    cot_all = lax.all_gather(cot_own, "fsdp", axis=0, tiled=True)
 
     normed_attn, pull_attn = jax.vjp(rms_norm, input_rows, gain_attn)
     attn_in = normed_attn.astype(bf16)
     key_value_lin = matrix_product(attn_in, key_value_weight)
     key = rotate(key_value_lin[:, :head_size], cosines, sines).astype(bf16)
     value = key_value_lin[:, head_size:].astype(bf16)
-    key_value = lax.all_gather(
-        jnp.concatenate([key, value], axis=1), "fsdp", axis=0, tiled=True
-    )
+    key_value = gather_rows(jnp.concatenate([key, value], axis=1), shards, 3)
     query_lin = matrix_product(attn_in, query_weight)
     query = rotate(split_heads(query_lin), cosines[None], sines[None]).astype(bf16)
     keys_all = key_value[:, :head_size]
@@ -483,7 +673,6 @@
     normed_mlp, pull_mlp = jax.vjp(rms_norm, resid, gain_mlp)
     mlp_in = normed_mlp.astype(bf16)
     mlp_all = gather_rows(mlp_in, shards, 2)
-    cot_all = lax.all_gather(cot_own, "fsdp", axis=0, tiled=True)
 
     first_unit = place * unit_rows
     gate_second = lax.dynamic_slice_in_dim(gate_factor_second, first_unit, unit_rows, 1)
@@ -506,103 +695,73 @@
     up = right_product(mlp_all, up_weight)
     hidden_full, pull_geglu = jax.vjp(geglu, gate, up)
     hidden = hidden_full.astype(bf16)
-    down_sum = scatter_rows(matrix_product(hidden, down_weight).astype(bf16), place, shards)
+    edges = row_edges(tok_rows)
+    down_terms = HalvingSum(
+        matrix_product(hidden, down_weight).astype(bf16), place, shards, edges
+    )
+    down_terms.start()
     grad_hidden = right_product(cot_all, down_weight)
     grad_gate_full, grad_up_full = pull_geglu(grad_hidden)
-    grad_gate = grad_gate_full.astype(bf16)
-    grad_up = grad_up_full.astype(bf16)
-    grad_mlp_in = scatter_rows(
-        (matrix_product(grad_gate, gate_weight) + matrix_product(grad_up, up_weight)).astype(bf16),
-        place,
-        shards,
-    )
+    grad_gate, grad_up = together(
+        [down_terms], (grad_gate_full.astype(bf16), grad_up_full.astype(bf16))
+    )
+    down_terms.start()
+    in_terms = matrix_product(grad_gate, gate_weight)
+    in_terms, grad_gate, grad_up = together([down_terms], (in_terms, grad_gate, grad_up))
+    down_terms.start()
+    in_terms = (in_terms + matrix_product(grad_up, up_weight)).astype(bf16)
+    in_terms, grad_gate, grad_up = together([down_terms], (in_terms, grad_gate, grad_up))
+    mlp_terms = HalvingSum(in_terms, place, shards, edges)
+    down_terms.start()
+    mlp_terms.start()
     gate_rows = left_matrix_product(grad_gate, mlp_all)
     up_rows = left_matrix_product(grad_up, mlp_all)
+    gate_rows, up_rows, hidden = together([down_terms, mlp_terms], (gate_rows, up_rows, hidden))
+    mlp_terms.start()
     down_rows = left_matrix_product(hidden, cot_all)
     gate_rows_low = gate_rows.astype(bf16)
+    down_rows, gate_rows_low = together([mlp_terms], (down_rows, gate_rows_low))
+    mlp_terms.start()
+    gate_in_term = lax.dot_general(
+        gate_rows_low, gate_second, (((0,), (1,)), ((), ())), preferred_element_type=f32
+    )
     up_rows_low = up_rows.astype(bf16)
     down_rows_low = down_rows.astype(bf16)
+    gate_in_term, up_rows_low, down_rows_low = together(
+        [mlp_terms], (gate_in_term, up_rows_low, down_rows_low)
+    )
+    mlp_terms.start()
+    up_in_term = lax.dot_general(
+        up_rows_low, up_second, (((0,), (1,)), ((), ())), preferred_element_type=f32
+    )
+    down_out_term = left_matrix_product(down_first, down_rows_low)
+    up_in_term, down_out_term = together([mlp_terms], (up_in_term, down_out_term))
+    grad_mlp_in = mlp_terms.rest()
+    down_sum = down_terms.rest()
     swap = [(0, 1), (1, 0)]
-    g_gate_rows = gate_rows + lax.ppermute(gate_rows_low, "dp", swap).astype(f32)
-    g_up_rows = up_rows + lax.ppermute(up_rows_low, "dp", swap).astype(f32)
-    g_down_rows = down_rows + lax.ppermute(down_rows_low, "dp", swap).astype(f32)
+
+    def over_cores(rows, low):
+        return rows + lax.ppermute(low, "dp", swap).astype(f32)
 
     def columns_of(first, rows):
         return lax.dot_general(
             first, rows.astype(bf16), (((0,), (1,)), ((), ())), preferred_element_type=f32
         )
-
-    g_gate_out = columns_of(gate_factor_first, g_gate_rows)
-    g_up_out = columns_of(upward_factor_first, g_up_rows)
-    g_down_in = right_product(g_down_rows.astype(bf16), down_factor_second)
-    gate_in_term = lax.dot_general(
-        gate_rows_low, gate_second, (((0,), (1,)), ((), ())), preferred_element_type=f32
-    )
-    up_in_term = lax.dot_general(
-        up_rows_low, up_second, (((0,), (1,)), ((), ())), preferred_element_type=f32
-    )
-    down_out_term = left_matrix_product(down_first, down_rows_low)
 
     output = (resid + down_sum).astype(bf16)
     grad_resid_norm, gain_mlp_term = pull_mlp(grad_mlp_in)
     grad_resid = cot_own.astype(f32) + grad_resid_norm
     grad_branch = grad_resid.astype(bf16)
+    def low_term(left, right):
+        return left_matrix_product(left, right).astype(bf16)
+
+    per = in_rows
+    few = rank // shards
     grad_attn = right_product(grad_branch, output_weight).astype(bf16)
     lora_output = matrix_product(attn, output_factor_first).astype(bf16)
     lora_query = matrix_product(attn_in, query_factor_first).astype(bf16)
     lora_key = matrix_product(attn_in, key_factor_first).astype(bf16)
     lora_value = matrix_product(attn_in, value_factor_first).astype(bf16)
-    grad_attn_heads = split_heads(grad_attn)
-    delta = jnp.sum(
-        grad_attn_heads.astype(f32) * attn_raw, axis=-1, keepdims=True
-    )
-
-    def grad_step(index, carry):
-        grad_query_acc, key_terms = carry
-        start = index * block
-        probs, key_block, value_block = probs_of(start)
-        grad_probs = jnp.einsum(
-            "htd,kd->htk", grad_attn_heads, value_block, preferred_element_type=f32
-        )
-        grad_scores = (scale * probs * (grad_probs - delta)).astype(bf16)
-        grad_query_acc = grad_query_acc + jnp.einsum(
-            "htk,kd->htd", grad_scores, key_block, preferred_element_type=f32
-        )
-        key_part = jnp.einsum("htk,htd->kd", grad_scores, query, preferred_element_type=f32)
-        value_part = jnp.einsum(
-            "htk,htd->kd", probs.astype(bf16), grad_attn_heads, preferred_element_type=f32
-        )
-        both = jnp.concatenate([key_part, value_part], axis=1).astype(bf16)
-        key_terms = lax.dynamic_update_slice_in_dim(key_terms, both, start, 0)
-        return (grad_query_acc, key_terms)
-
-    grad_query_rot, key_terms = lax.fori_loop(
-        first_block,
-        needed,
-        grad_step,
-        (
-            jnp.zeros((heads, tok_rows, head_size), f32),
-            jnp.zeros((length, 2 * head_size), bf16),
-        ),
-    )
-    key_sums = scatter_rows(key_terms, place, shards)
-    grad_query_lin = join_heads(
-        rotate(grad_query_rot, cosines[None], -sines[None]).astype(bf16)
-    )
-    grad_key_value_lin = jnp.concatenate(
-        [rotate(key_sums[:, :head_size], cosines, -sines), key_sums[:, head_size:]], axis=1
-    ).astype(bf16)
-    grad_attn_in = right_product(grad_query_lin, query_weight) + right_product(
-        grad_key_value_lin, key_value_weight
-    )
-    grad_inputs_norm, gain_attn_term = pull_attn(grad_attn_in)
-    grad_inputs = grad_resid + grad_inputs_norm
-
-    def low_term(left, right):
-        return left_matrix_product(left, right).astype(bf16)
-
-    per = in_rows
-    few = rank // shards
     early = jnp.concatenate(
         [
             low_term(lora_output, grad_branch).reshape(shards, few, width),
@@ -613,14 +772,88 @@
         ],
         axis=1,
     )
-    g_output_weight, early_sums = scatter_both(
-        low_term(attn, grad_branch).reshape(shards, per, width), early, place, core
-    )
+    early_sums = scatter_shared(
+        jnp.concatenate(
+            [low_term(attn, grad_branch).reshape(shards, per, width), early], axis=1
+        ),
+        core,
+    ).astype(f32)
+    g_output_weight = early_sums[:per]
+    early_sums = early_sums[per:]
     g_output_out = early_sums[:few]
     g_down_out = early_sums[few : 2 * few]
     pair = unpack_rows(early_sums[2 * few :], 2 * head_size)
     g_gate_in = pair[:, :head_size]
     g_up_in = pair[:, head_size:]
+
+    grad_attn_heads = split_heads(grad_attn)
+    delta = jnp.sum(
+        grad_attn_heads.astype(f32) * attn_raw, axis=-1, keepdims=True
+    )
+
+    def grad_step(index, carry):
+        grad_query_acc, key_terms = carry
+        start = index * block
+        probs, key_block, value_block = probs_of(start)
+        grad_probs = jnp.einsum(
+            "htd,kd->htk", grad_attn_heads, value_block, preferred_element_type=f32
+        )
+        grad_scores = (scale * probs * (grad_probs - delta)).astype(bf16)
+        grad_query_acc = grad_query_acc + jnp.einsum(
+            "htk,kd->htd", grad_scores, key_block, preferred_element_type=f32
+        )
+        key_part = jnp.einsum("htk,htd->kd", grad_scores, query, preferred_element_type=f32)
+        value_part = jnp.einsum(
+            "htk,htd->kd", probs.astype(bf16), grad_attn_heads, preferred_element_type=f32
+        )
+        both = jnp.concatenate([key_part, value_part], axis=1).astype(bf16)
+        key_terms = lax.dynamic_update_slice_in_dim(key_terms, both, start, 0)
+        return (grad_query_acc, key_terms)
+
+    grad_query_rot, key_terms = lax.fori_loop(
+        first_block,
+        needed,
+        grad_step,
+        (
+            jnp.zeros((heads, tok_rows, head_size), f32),
+            jnp.zeros((length, 2 * head_size), bf16),
+        ),
+    )
+    grad_query_lin = join_heads(
+        rotate(grad_query_rot, cosines[None], -sines[None]).astype(bf16)
+    )
+    key_halves = HalvingSum(key_terms, place, shards, [0, tok_rows // 2, tok_rows])
+    key_halves.start()
+    g_gate_rows = over_cores(gate_rows, gate_rows_low)
+    g_gate_rows, up_rows, up_rows_low = together(
+        [key_halves], (g_gate_rows, up_rows, up_rows_low)
+    )
+    key_halves.start()
+    g_up_rows = over_cores(up_rows, up_rows_low)
+    g_up_rows, down_rows, down_rows_low = together(
+        [key_halves], (g_up_rows, down_rows, down_rows_low)
+    )
+    key_halves.start()
+    g_down_rows = over_cores(down_rows, down_rows_low)
+    g_gate_out = columns_of(gate_factor_first, g_gate_rows)
+    g_down_rows, g_gate_out, g_up_rows, grad_query_lin = together(
+        [key_halves], (g_down_rows, g_gate_out, g_up_rows, grad_query_lin)
+    )
+    key_halves.start()
+    g_up_out = columns_of(upward_factor_first, g_up_rows)
+    g_down_in = right_product(g_down_rows.astype(bf16), down_factor_second)
+    query_terms = low_term(attn_in, grad_query_lin)
+    query_grad = right_product(grad_query_lin, query_weight)
+    g_up_out, g_down_in, query_terms, query_grad = together(
+        [key_halves], (g_up_out, g_down_in, query_terms, query_grad)
+    )
+    key_sums = key_halves.rest()
+    grad_key_value_lin = jnp.concatenate(
+        [rotate(key_sums[:, :head_size], cosines, -sines), key_sums[:, head_size:]], axis=1
+    ).astype(bf16)
+    grad_attn_in = query_grad + right_product(grad_key_value_lin, key_value_weight)
+    grad_inputs_norm, gain_attn_term = pull_attn(grad_attn_in)
+    grad_inputs = grad_resid + grad_inputs_norm
 
     tiny = jnp.concatenate(
         [
@@ -640,9 +873,13 @@
         ],
         axis=1,
     )
-    g_query_weight, late_sums = scatter_both(
-        low_term(attn_in, grad_query_lin).reshape(shards, per, width), late, place, core
-    )
+    late = jnp.concatenate([query_terms.reshape(shards, per, width), late], axis=1)
+    if shards == 4 * LINE:
+        late_sums = scatter_blocks(late, 4).astype(f32)
+    else:
+        late_sums = scatter_shared(late, core).astype(f32)
+    g_query_weight = late_sums[:per]
+    late_sums = late_sums[per:]
     g_query_out = late_sums[:few]
     pair = unpack_rows(late_sums[few : late_sums.shape[0] - few], 2 * head_size)
     g_key_weight = pair[:, :head_size]

time: 1050 us -> 868 us (0.83)
  waiting for transfers between devices: 324 us -> 55.5 us
  Pallas kernels: 210 us -> 317 us
  other arithmetic: 67.3 us -> 118 us
  local copies, waits for them, and re-layouts: 93.2 us -> 66.8 us
  starting transfers between devices: 90 us -> 64.3 us
  matrix products: 241 us -> 222 us
    ppermute x73 -> x37, waiting for transfers between devices: 298 us -> 51.3 us  [the longest x32 51.3 us: start(): self.came.append(lax.ppermute(away, 'fsdp', pairs))]
    pallas_call x0 -> x1, Pallas kernels: none -> 95.2 us  [scatter_blocks(): pl.pallas_call(scatter_kernel, out_shape=jax.ShapeDtypeStruct((rows, colu...]
    ppermute x73 -> x37, starting transfers between devices: 89.9 us -> 64.3 us  [the longest x32 63.8 us: start(): self.came.append(lax.ppermute(away, 'fsdp', pairs))]
    all_gather x1 -> x0, waiting for transfers between devices: 24.9 us -> none  [local(): lax.all_gather(jnp.concatenate([key, value], axis=1), 'fsdp', axis=0, til...]
    concatenate x4, other arithmetic: 2.41 us -> 20.4 us  [the longest x1 13.4 us: local(): jnp.concatenate([low_term(attn, grad_branch).reshape(shards, per, width),...]
    convert_element_type x58 -> x29, other arithmetic: 25.2 us -> 42.1 us  [the longest x24 15.3 us: finish(): self.held = [t.astype(self.kind) for t in totals]]
    add x12 -> x10, other arithmetic: 25.1 us -> 40.8 us  [the longest x3 26.2 us: over_cores(): return rows + lax.ppermute(low, 'dp', swap).astype(f32)]
    dot_general x1 -> x0, local copies, waits for them, and re-layouts: 12.2 us -> none  [matrix_product(): return jnp.dot(left, right, preferred_element_type=jnp.float32)]
  transfers between devices with their start and end apart: 75 -> 39, of which waited for: 42 -> 7; matrix products, arithmetic and copies ran while one was open for 26% -> 39% of each run, Pallas kernels for 12% -> 27%
where the time goes in v3:
time: 868 us; the launch traced here: 862 us
  Pallas kernels  317 us (37%)
  matrix products  222 us (26%)
  other arithmetic  118 us (14%)
  local copies, waits for them, and re-layouts  66.8 us (8%)
  starting transfers between devices  64.3 us (7%)
  waiting for transfers between devices  55.5 us (6%)
  between operations  16.4 us (2%)
    pallas_call x3, Pallas kernels, gather_blocks(): pl.pallas_call(functools.partial(gather_kernel, pieces, len(arrays), with...  222 us
    pallas_call x1, Pallas kernels, scatter_blocks(): pl.pallas_call(scatter_kernel, out_shape=jax.ShapeDtypeStruct((rows, colu...  95.2 us
    dot_general x11, matrix products, right_product(): lax.dot_general(left, right, (((1,), (1,)), ((), ())), preferred_element_...  67.9 us
    ppermute x32, starting transfers between devices, start(): self.came.append(lax.ppermute(away, 'fsdp', pairs))  63.8 us
    dot_general x11, matrix products, matrix_product(): return jnp.dot(left, right, preferred_element_type=jnp.float32)  59.9 us
    dot_general x11, matrix products, left_matrix_product(): lax.dot_general(left, right, (((0,), (0,)), ((), ())), preferred_element_...  58.1 us
    ppermute x32, waiting for transfers between devices, start(): self.came.append(lax.ppermute(away, 'fsdp', pairs))  51.3 us
    add x3, other arithmetic, over_cores(): return rows + lax.ppermute(low, 'dp', swap).astype(f32)  26.2 us
  transfers between devices with their start and end apart: 39, of which 7 were waited for; matrix products, arithmetic and copies ran while one was open for 39% of the time, Pallas kernels for 27%

profile of v3, /device:TPU:0, one launch (start us, length us, event | category | flops | bytes accessed | tf_op | source)
XLA Modules:
  0.0 861.6 jit_solution(9411545404525211645)
XLA Ops:
  10.2 2.3 fusion.64.refs_0_
  12.5 2.3 fusion.65.refs_1_
  14.7 88.0 %gather_blocks_1.1 = (bf16[16,2,64,2048]{3,2,1,0:T(8,128)(2,1)}, bf16[16,2,64,2048]{3,2,1,0:T(8,128)(2,1)}, bf16[16,2,64,512]{3,2,1,0:T(8,128)(2,1)}) custom-call(bf16[64,2048]{1,0:T(8,128)(2,1)} %fusion.64.refs_0_, bf16[64,2048]{1,0:T(8,128)(2,1)} %fusion.65.refs_1_, bf16[64,512]{1,0:T(8,128)(2,1)} %pad_maximum_fusion.11.refs_2_), custom_call_target="tpu_custom_call" | custom-call | tf_op jit(solution)/shard_map/gather_blocks_1/pallas_call | solution.py:227
  107.8 35.0 %gather_blocks_3.1 = bf16[16,128,512]{2,1,0:T(8,128)(2,1)} custom-call(bf16[128,512]{1,0:T(8,128)(2,1)} %pad_maximum_fusion.8.refs_0_), custom_call_target="tpu_custom_call" | custom-call | tf_op jit(solution)/shard_map/gather_blocks_3/pallas_call | solution.py:227
  142.8 2.7 fusion.223
  145.5 4.7 fusion.114
  161.9 5.2 multiply_reduce_fusion.3
  169.1 99.2 %gather_blocks_2.1 = bf16[16,128,2048]{2,1,0:T(8,128)(2,1)} custom-call(bf16[128,2048]{1,0:T(8,128)(2,1)} %multiply_convert_fusion.2.refs_0_), custom_call_target="tpu_custom_call" | custom-call | tf_op jit(solution)/shard_map/gather_blocks_2/pallas_call | solution.py:227
  268.3 3.8 add_convert_fusion.3
  272.2 2.9 add_convert_fusion.2
  276.3 5.7 add_convert_fusion.1
  282.1 11.2 %fusion.231 = f32[2048,1024]{1,0:T(8,128)} fusion(bf16[2048,2048]{1,0:T(8,128)(2,1)S(1)} %bitcast.622, bf16[1024,2048]{1,0:T(8,128)(2,1)S(1)} %add_convert_fusion.3), kind=kOutput, calls=%fused_computation.473 | convolution fusion | flops 8589934592 | bytes 20971520 | tf_op jit(solution)/shard_map/dot_general | solution.py:26
  293.2 11.2 %fusion.232 = f32[2048,1024]{1,0:T(8,128)} fusion(bf16[2048,2048]{1,0:T(8,128)(2,1)S(1)} %bitcast.623, bf16[1024,2048]{1,0:T(8,128)(2,1)S(1)} %add_convert_fusion.2), kind=kOutput, calls=%fused_computation.474 | convolution fusion | flops 8589934592 | bytes 20971520 | tf_op jit(solution)/shard_map/dot_general | solution.py:26
  304.4 25.9 %multiply_convert_fusion = (bf16[2048,1024]{1,0:T(8,128)(2,1)}, bf16[2048,1024]{1,0:T(8,128)(2,1)}, bf16[2048,1024]{1,0:T(8,128)(2,1)}) fusion(f32[2048,1024]{1,0:T(8,128)} %fusion.231, f32[2048,1024]{1,0:T(8,128)} %fusion.232, bf16[2048,2048]{1,0:T(8,128)(2,1)} %all-gather.2.cloned.1.call-done, bf16[1024,2048]{1,0:T(8,128)(2,1)} %add_convert_fusion.1), kind=kOutput, calls=%fused_computation.78 | convolution fusion | flops 8644460544 | bytes 41943040 | tf_op jit(solution)/shard_map/dot_general | solution.py:26
  330.3 12.1 %convolution_convert_fusion = bf16[2048,2048]{1,0:T(8,128)(2,1)S(1)} fusion(bf16[2048,1024]{1,0:T(8,128)(2,1)} %get-tuple-element.296, bf16[1024,2048]{1,0:T(8,128)(2,1)} %add_convert_fusion.1), kind=kOutput, calls=%fused_computation.84 | convolution fusion | flops 8594128896 | bytes 16777216 | tf_op jit(solution)/shard_map/dot_general | solution.py:16
  343.6 2.5 copy-done.14
  358.4 19.9 %collective-permute-done.2 = bf16[2,2,2,32,2048]{4,3,0,1,2:T(8,128)(2,1)} collective-permute-done((bf16[2,2,2,32,2048]{4,3,0,1,2:T(8,128)(2,1)}, bf16[2,2,2,32,2048]{4,3,0,1,2:T(8,128)(2,1)}, u32[]{:S(2)}, u32[]{:S(2)}) %collective-permute-start.2) | collective-permute-done | bytes 1048608 | tf_op jit(solution)/shard_map/ppermute | solution.py:456
  378.3 3.0 collective-permute-done
  381.3 4.0 collective-permute-done.1
  394.6 11.7 %fusion.233 = f32[2048,2048]{1,0:T(8,128)} fusion(bf16[2048,1024]{1,0:T(8,128)(2,1)S(1)} %copy-done.83, bf16[1024,2048]{1,0:T(8,128)(2,1)S(1)} %copy-done.23), kind=kOutput, calls=%fused_computation.475 | convolution fusion | flops 8589934592 | bytes 25165824 | tf_op jit(solution)/shard_map/dot_general | solution.py:16
  407.4 2.3 collective-permute-start.6
  412.5 11.7 %fusion.234 = f32[2048,2048]{1,0:T(8,128)} fusion(bf16[2048,1024]{1,0:T(8,128)(2,1)S(1)} %copy-done.82, bf16[1024,2048]{1,0:T(8,128)(2,1)S(1)} %copy-done.21), kind=kOutput, calls=%fused_computation.476 | convolution fusion | flops 8589934592 | bytes 25165824 | tf_op jit(solution)/shard_map/dot_general | solution.py:16
  424.2 11.9 %add_convert_fusion = bf16[2048,2048]{1,0:T(8,128)(2,1)S(1)} fusion(f32[2048,2048]{1,0:T(8,128)} %fusion.233, f32[2048,2048]{1,0:T(8,128)} %fusion.234), kind=kLoop, calls=%fused_computation.63 | loop fusion | flops 8388608 | bytes 41943040 | tf_op jit(solution)/shard_map/convert_element_type | solution.py:712
  438.2 6.8 collective-permute-start.9
  446.0 3.0 collective-permute-start.11
  454.2 11.3 %fusion.235 = f32[1024,2048]{1,0:T(8,128)} fusion(bf16[2048,1024]{1,0:T(8,128)(2,1)S(1)} %copy-done.84, bf16[2048,2048]{1,0:T(8,128)(2,1)S(1)} %bitcast.626), kind=kOutput, calls=%fused_computation.477 | convolution fusion | flops 8589934592 | bytes 20971520 | tf_op jit(solution)/shard_map/dot_general | solution.py:20
  466.7 11.5 %fusion.236 = f32[1024,2048]{1,0:T(8,128)S(1)} fusion(bf16[2048,1024]{1,0:T(8,128)(2,1)} %get-tuple-element.289, bf16[2048,2048]{1,0:T(8,128)(2,1)S(1)} %bitcast.627), kind=kOutput, calls=%fused_computation.478 | convolution fusion | flops 8589934592 | bytes 20971520 | tf_op jit(solution)/shard_map/dot_general | solution.py:20
  478.3 11.3 %collective-permute-done.14 = bf16[2,2,2,32,2048]{4,3,0,1,2:T(8,128)(2,1)S(1)} collective-permute-done((bf16[2,2,2,32,2048]{4,3,0,1,2:T(8,128)(2,1)S(1)}, bf16[2,2,2,32,2048]{4,3,0,1,2:T(8,128)(2,1)S(1)}, u32[]{:S(2)}, u32[]{:S(2)}) %collective-permute-start.14) | collective-permute-done | bytes 1048608 | tf_op jit(solution)/shard_map/ppermute | solution.py:456
  497.9 11.3 %fusion.237 = f32[1024,2048]{1,0:T(8,128)S(1)} fusion(bf16[2048,1024]{1,0:T(8,128)(2,1)} %get-tuple-element.296, bf16[2048,2048]{1,0:T(8,128)(2,1)S(1)} %bitcast.657), kind=kOutput, calls=%fused_computation.479 | convolution fusion | flops 8589934592 | bytes 20971520 | tf_op jit(solution)/shard_map/dot_general | solution.py:20
  510.2 8.2 convert_element_type.658
  518.4 2.7 convert_element_type.671
  528.9 2.6 convert_element_type.672
  531.5 4.8 fusion.139
  536.4 3.5 collective-permute-start.21
  540.2 3.0 collective-permute-start.23
  543.2 3.4 fusion.136
  546.6 4.8 fusion.133
  551.4 12.2 %collective-permute-done.23 = bf16[32,2048]{1,0:T(8,128)(2,1)S(1)} collective-permute-done((bf16[32,2048]{1,0:T(8,128)(2,1)S(1)}, bf16[32,2048]{1,0:T(8,128)(2,1)S(1)}, u32[]{:S(2)}, u32[]{:S(2)}) %collective-permute-start.23) | collective-permute-done | bytes 131104 | tf_op jit(solution)/shard_map/ppermute | solution.py:456
  566.0 2.9 convolution_convert_fusion.6
  572.1 9.5 %while.39 = (s32[]{:T(128)}, f32[8,128,256]{2,1,0:T(8,128)}, bf16[2048,512]{1,0:T(8,128)(2,1)}, s32[]{:T(128)}, s32[128]{0:T(128)S(1)}, /*index=5*/s32[2048]{0:T...) while((s32[]{:T(128)}, f32[8,128,256]{2,1,0:T(8,128)}, ...), condition=%wide.region_13.14_spmd.clone, body=%wide.region_12.13_spmd.clone.sunk | while | flops 1348665984 | bytes 20336396 | solution.py:813
  576.3 2.8 convolution_add_fusion.10
  589.5 3.2 convolution_convert_fusion.4
  592.7 2.4 convolution_convert_fusion.1
  595.1 10.2 %convert_add_fusion.2 = f32[1024,2048]{1,0:T(8,128)} fusion(f32[1024,2048]{1,0:T(8,128)} %fusion.235, bf16[1024,2048]{1,0:T(8,128)(2,1)} %collective-permute-done.26), kind=kLoop, calls=%fused_computation.77 | loop fusion | flops 4194304 | bytes 20971520 | tf_op jit(solution)/shard_map/add | solution.py:744
  605.4 13.4 %maximum_maximum_fusion = bf16[16,192,2048]{2,1,0:T(8,128)(2,1)} fusion(bf16[16,32,512]{2,1,0:T(8,128)(2,1)S(1)} %copy-done.41, bf16[16,32,512]{2,1,0:T(8,128)(2,1)S(1)} %copy-done.42, bf16[16,32,512]{2,1,0:T(8,128)(2,1)S(1)} %copy-done.40, bf16[16,32,512]{2,1,0:T(8,128)(2,1)S(1)} %copy-done.39, bf16[16,16,2048]{2,1,0:T(8,128)(2,1)} %bitcast.642, ...), kind=kLoop, calls=%fused_computation.65 | loop fusion | flops 88080384 | bytes 25165824 | tf_op jit(solution)/shard_map/concatenate | solution.py:776
  618.8 6.5 constant_dynamic-slice_fusion
  630.5 9.9 %collective-permute-start.28 = (bf16[2,2,64,512]{3,2,0,1:T(8,128)(2,1)S(1)}, bf16[2,2,64,512]{3,2,0,1:T(8,128)(2,1)S(1)}, u32[]{:S(2)}, u32[]{:S(2)}) collective-permute-start(bf16[2,2,64,512]{3,2,0,1:T(8,128)(2,1)S(1)} %dynamic-slice_bitcast_fusion.10), channel_id=1, source_target_pairs={{0,8},{2,10},{4,12},{6,14},{8,0},{10,2},{12,4},{14,6},{16,24},{18,... | collective-permute-start | bytes 786440 | tf_op jit(solution)/shard_map/ppermute | solution.py:456
  640.4 10.1 %convert_add_fusion.1 = f32[1024,2048]{1,0:T(8,128)} fusion(f32[1024,2048]{1,0:T(8,128)} %copy-done.5, bf16[1024,2048]{1,0:T(8,128)(2,1)} %collective-permute-done.29), kind=kLoop, calls=%fused_computation.76 | loop fusion | flops 4194304 | bytes 20971520 | tf_op jit(solution)/shard_map/add | solution.py:744
  654.1 10.7 %dynamic-slice_add_fusion = bf16[16,192,1024]{2,1,0:T(8,128)(2,1)} fusion(bf16[16,192,1024]{2,1,0:T(8,128)(2,1)} %collective-permute-done.35, bf16[16,192,2048]{2,1,0:T(8,128)(2,1)} %maximum_maximum_fusion, s32[]{:T(128)S(6)} %select_n.194), kind=kLoop, calls=%fused_computation.87 | loop fusion | flops 12582912 | bytes 18874372 | tf_op jit(solution)/shard_map/add | solution.py:490
  664.9 5.7 fusion.76
  672.4 5.9 convert_add_fusion
  678.4 12.9 %collective-permute-start.33 = (bf16[64,512]{1,0:T(8,128)(2,1)S(1)}, bf16[64,512]{1,0:T(8,128)(2,1)}, u32[]{:S(2)}, u32[]{:S(2)}) collective-permute-start(bf16[64,512]{1,0:T(8,128)(2,1)S(1)} %dynamic-slice_bitcast_fusion.23), channel_id=1, source_target_pairs={{0,16},{2,18},{4,20},{6,22},{8,24},{10,26},{12,28},{14,30},{16,0},... | collective-permute-start | bytes 196616 | tf_op jit(solution)/shard_map/ppermute | solution.py:456
  691.5 5.8 convolution_convert_fusion.2
  697.3 6.1 fusion.79
  705.7 3.9 fusion.238
  709.6 3.3 convolution_convert_fusion.5
  712.9 2.5 copy.92
  718.2 4.3 fusion.91
  727.5 6.3 pad_maximum_fusion.1.terms_ref
  733.8 95.2 %scatter_blocks_4.1 = bf16[192,2048]{1,0:T(8,128)(2,1)S(1)} custom-call(bf16[16,192,2048]{2,1,0:T(8,128)(2,1)S(1)} %pad_maximum_fusion.1.terms_ref), custom_call_target="tpu_custom_call" | custom-call | tf_op jit(solution)/shard_map/scatter_blocks_4/pallas_call | solution.py:403
  834.0 2.5 copy.93
  840.0 2.9 fusion.98
  842.8 4.2 reduce-scatter.2.cloned.1.call-done
  847.7 2.7 fusion.129
  (462 shorter events, 132.8 us)
Async XLA Ops:
  7.2 261.0 %copy-start = (bf16[2048,256]{1,0:T(8,128)(2,1)S(1)}, bf16[2048,256]{1,0:T(8,128)(2,1)}, u32[]{:S(2)}) copy-start(bf16[2048,256]{1,0:T(8,128)(2,1)} %param.51) | copy-start | bytes 3145732
  7.2 95.6 %copy-start.57 = (s32[1,2048]{1,0:T(1,128)S(1)}, s32[1,2048]{1,0:T(1,128)}, u32[]{:S(2)}) copy-start(s32[1,2048]{1,0:T(1,128)} %param.33) | copy-start | bytes 24580
  7.2 96.6 %copy-start.2 = (bf16[1,128,2048]{2,1,0:T(8,128)(2,1)S(1)}, bf16[1,128,2048]{2,1,0:T(8,128)(2,1)}, u32[]{:S(2)}) copy-start(bf16[1,128,2048]{2,1,0:T(8,128)(2,1)} %param.32) | copy-start | bytes 1572868
  7.2 96.8 %copy-start.49 = (f32[2048]{0:T(1024)S(1)}, f32[2048]{0:T(1024)}, u32[]{:S(2)}) copy-start(f32[2048]{0:T(1024)} %param.34) | copy-start | bytes 24580
  7.3 297.1 %all-gather.2.cloned.1.call-start = ((), (), s32[]{:S(2)}) async-start(), calls=%async_computation.1 | async-start | bytes 8912896 | tf_op jit(solution)/shard_map/all_gather | solution.py:616
  102.8 744.3 %reduce-scatter.2.cloned.1.call-start = ((), (), s32[]{:S(2)}) async-start(), calls=%async_computation.2 | async-start | bytes 6684672 | tf_op jit(solution)/shard_map/reduce_scatter | solution.py:491
  103.7 41.8 %copy-start.71 = (f32[128]{0:T(128)}, f32[128]{0:T(128)S(1)}, u32[]{:S(2)}) copy-start(f32[128]{0:T(128)S(1)} %get-tuple-element.559) | copy-start | bytes 1540
  103.8 41.7 %copy-start.77 = (f32[128]{0:T(128)}, f32[128]{0:T(128)S(1)}, u32[]{:S(2)}) copy-start(f32[128]{0:T(128)S(1)} %negate_power_fusion) | copy-start | bytes 1540
  104.0 41.5 %copy-start.69 = (f32[128]{0:T(128)}, f32[128]{0:T(128)S(1)}, u32[]{:S(2)}) copy-start(f32[128]{0:T(128)S(1)} %fusion.201) | copy-start | bytes 1540
  107.1 48.4 %copy-start.51 = (f32[128,128]{1,0:T(8,128)}, f32[128,128]{1,0:T(8,128)S(1)}, u32[]{:S(2)}) copy-start(f32[128,128]{1,0:T(8,128)S(1)} %get-tuple-element.630) | copy-start | bytes 196612
  167.1 101.1 %copy-start.78 = (f32[128]{0:T(128)}, f32[128]{0:T(128)S(1)}, u32[]{:S(2)}) copy-start(f32[128]{0:T(128)S(1)} %get-tuple-element.631) | copy-start | bytes 1540
  347.7 33.5 %collective-permute-start = (bf16[2,2,2,48,2048]{4,3,0,1,2:T(8,128)(2,1)}, bf16[2,2,2,48,2048]{4,3,0,1,2:T(8,128)(2,1)}, u32[]{:S(2)}, u32[]{:S(2)}) collective-permute-start(bf16[2,2,2,48,2048]{4,3,0,1,2:T(8,128)(2,1)} %bitcast.540), channel_id=1, source_target_pairs={{0,2},{2,0},{4,6},{6,4},{8,10},{10,8},{12,14},{14,12},{16,18},{18,... | collective-permute-start | bytes 4718600 | tf_op jit(solution)/shard_map/ppermute | solution.py:456
  351.6 33.7 %collective-permute-start.1 = (bf16[2,2,2,48,2048]{4,3,0,2,1:T(8,128)(2,1)}, bf16[2,2,2,48,2048]{4,3,0,2,1:T(8,128)(2,1)}, u32[]{:S(2)}, u32[]{:S(2)}) collective-permute-start(bf16[2,2,2,48,2048]{4,3,0,2,1:T(8,128)(2,1)} %bitcast.539), channel_id=1, source_target_pairs={{0,4},{2,6},{4,0},{6,2},{8,12},{10,14},{12,8},{14,10},{16,20},{18,... | collective-permute-start | bytes 4718600 | tf_op jit(solution)/shard_map/ppermute | solution.py:456
  356.3 22.0 %collective-permute-start.2 = (bf16[2,2,2,32,2048]{4,3,0,1,2:T(8,128)(2,1)}, bf16[2,2,2,32,2048]{4,3,0,1,2:T(8,128)(2,1)}, u32[]{:S(2)}, u32[]{:S(2)}) collective-permute-start(bf16[2,2,2,32,2048]{4,3,0,1,2:T(8,128)(2,1)} %bitcast.542), channel_id=1, source_target_pairs={{0,8},{2,10},{4,12},{6,14},{8,0},{10,2},{12,4},{14,6},{16,24},{18,... | collective-permute-start | bytes 3145736 | tf_op jit(solution)/shard_map/ppermute | solution.py:456
  358.4 29.7 %copy-start.15 = (bf16[2,2,1,2,48,2048]{5,4,3,2,1,0:T(8,128)(2,1)S(1)}, bf16[2,2,1,2,48,2048]{5,4,3,2,1,0:T(8,128)(2,1)}, u32[]{:S(2)}) copy-start(bf16[2,2,1,2,48,2048]{5,4,3,2,1,0:T(8,128)(2,1)} %get-tuple-element.574) | copy-start | bytes 4718596
  387.4 18.9 %collective-permute-start.3 = (bf16[2,2,48,2048]{3,2,0,1:T(8,128)(2,1)S(1)}, bf16[2,2,48,2048]{3,2,0,1:T(8,128)(2,1)S(1)}, u32[]{:S(2)}, u32[]{:S(2)}) collective-permute-start(bf16[2,2,48,2048]{3,2,0,1:T(8,128)(2,1)S(1)} %dynamic-slice_bitcast_fusion.3), channel_id=1, source_target_pairs={{0,4},{2,6},{4,0},{6,2},{8,12},{10,14},{12,8},{14,10},{16,20},{18,... | collective-permute-start | bytes 2359304 | tf_op jit(solution)/shard_map/ppermute | solution.py:456
  390.3 16.8 %collective-permute-start.4 = (bf16[2,2,48,2048]{3,2,0,1:T(8,128)(2,1)S(1)}, bf16[2,2,48,2048]{3,2,0,1:T(8,128)(2,1)S(1)}, u32[]{:S(2)}, u32[]{:S(2)}) collective-permute-start(bf16[2,2,48,2048]{3,2,0,1:T(8,128)(2,1)S(1)} %dynamic-slice_bitcast_fusion.2), channel_id=1, source_target_pairs={{0,8},{2,10},{4,12},{6,14},{8,0},{10,2},{12,4},{14,6},{16,24},{18,... | collective-permute-start | bytes 2359304 | tf_op jit(solution)/shard_map/ppermute | solution.py:456
  393.7 12.6 %collective-permute-start.5 = (bf16[2,2,32,2048]{3,2,0,1:T(8,128)(2,1)S(1)}, bf16[2,2,32,2048]{3,2,0,1:T(8,128)(2,1)S(1)}, u32[]{:S(2)}, u32[]{:S(2)}) collective-permute-start(bf16[2,2,32,2048]{3,2,0,1:T(8,128)(2,1)S(1)} %dynamic-slice_bitcast_fusion.5), channel_id=1, source_target_pairs={{0,2},{2,0},{4,6},{6,4},{8,10},{10,8},{12,14},{14,12},{16,18},{18,... | collective-permute-start | bytes 1572872 | tf_op jit(solution)/shard_map/ppermute | solution.py:456
  407.4 28.7 %collective-permute-start.6 = (bf16[2,48,2048]{2,1,0:T(8,128)(2,1)S(1)}, bf16[2,48,2048]{2,1,0:T(8,128)(2,1)S(1)}, u32[]{:S(2)}, u32[]{:S(2)}) collective-permute-start(bf16[2,48,2048]{2,1,0:T(8,128)(2,1)S(1)} %dynamic-slice_bitcast_fusion.9), channel_id=1, source_target_pairs={{0,8},{2,10},{4,12},{6,14},{8,0},{10,2},{12,4},{14,6},{16,24},{18,... | collective-permute-start | bytes 1179656 | tf_op jit(solution)/shard_map/ppermute | solution.py:456
  410.0 26.1 %collective-permute-start.7 = (bf16[2,48,2048]{2,1,0:T(8,128)(2,1)S(1)}, bf16[2,48,2048]{2,1,0:T(8,128)(2,1)S(1)}, u32[]{:S(2)}, u32[]{:S(2)}) collective-permute-start(bf16[2,48,2048]{2,1,0:T(8,128)(2,1)S(1)} %dynamic-slice_bitcast_fusion.8), channel_id=1, source_target_pairs={{0,2},{2,0},{4,6},{6,4},{8,10},{10,8},{12,14},{14,12},{16,18},{18,... | collective-permute-start | bytes 1179656 | tf_op jit(solution)/shard_map/ppermute | solution.py:456
  410.7 25.4 %collective-permute-start.8 = (bf16[2,32,2048]{2,1,0:T(8,128)(2,1)S(1)}, bf16[2,32,2048]{2,1,0:T(8,128)(2,1)S(1)}, u32[]{:S(2)}, u32[]{:S(2)}) collective-permute-start(bf16[2,32,2048]{2,1,0:T(8,128)(2,1)S(1)} %dynamic-slice_bitcast_fusion.13), channel_id=1, source_target_pairs={{0,4},{2,6},{4,0},{6,2},{8,12},{10,14},{12,8},{14,10},{16,20},{18,... | collective-permute-start | bytes 786440 | tf_op jit(solution)/shard_map/ppermute | solution.py:456
  438.2 40.0 %collective-permute-start.9 = (bf16[48,2048]{1,0:T(8,128)(2,1)}, bf16[48,2048]{1,0:T(8,128)(2,1)}, u32[]{:S(2)}, u32[]{:S(2)}) collective-permute-start(bf16[48,2048]{1,0:T(8,128)(2,1)} %dynamic-slice_bitcast_fusion.17), channel_id=1, source_target_pairs={{0,16},{2,18},{4,20},{6,22},{8,24},{10,26},{12,28},{14,30},{16,0},... | collective-permute-start | bytes 589832 | tf_op jit(solution)/shard_map/ppermute | solution.py:456
  445.9 32.3 %collective-permute-start.10 = (bf16[48,2048]{1,0:T(8,128)(2,1)}, bf16[48,2048]{1,0:T(8,128)(2,1)}, u32[]{:S(2)}, u32[]{:S(2)}) collective-permute-start(bf16[48,2048]{1,0:T(8,128)(2,1)} %dynamic-slice_bitcast_fusion.16), channel_id=1, source_target_pairs={{0,16},{2,18},{4,20},{6,22},{8,24},{10,26},{12,28},{14,30},{16,0},... | collective-permute-start | bytes 589832 | tf_op jit(solution)/shard_map/ppermute | solution.py:456
  446.0 19.8 %collective-permute-start.11 = (bf16[32,2048]{1,0:T(8,128)(2,1)S(1)}, bf16[32,2048]{1,0:T(8,128)(2,1)S(1)}, u32[]{:S(2)}, u32[]{:S(2)}) collective-permute-start(bf16[32,2048]{1,0:T(8,128)(2,1)S(1)} %dynamic-slice_bitcast_fusion.21), channel_id=1, source_target_pairs={{0,16},{2,18},{4,20},{6,22},{8,24},{10,26},{12,28},{14,30},{16,0},... | collective-permute-start | bytes 393224 | tf_op jit(solution)/shard_map/ppermute | solution.py:456
  449.4 40.2 %collective-permute-start.12 = (bf16[2,2,2,48,2048]{4,3,0,1,2:T(8,128)(2,1)S(1)}, bf16[2,2,2,48,2048]{4,3,0,1,2:T(8,128)(2,1)S(1)}, u32[]{:S(2)}, u32[]{:S(2)}) collective-permute-start(bf16[2,2,2,48,2048]{4,3,0,1,2:T(8,128)(2,1)S(1)} %bitcast.640), channel_id=1, source_target_pairs={{0,2},{2,0},{4,6},{6,4},{8,10},{10,8},{12,14},{14,12},{16,18},{18,... | collective-permute-start | bytes 4718600 | tf_op jit(solution)/shard_map/ppermute | solution.py:456
  451.1 38.5 %collective-permute-start.13 = (bf16[2,2,2,48,2048]{4,3,0,2,1:T(8,128)(2,1)S(1)}, bf16[2,2,2,48,2048]{4,3,0,2,1:T(8,128)(2,1)S(1)}, u32[]{:S(2)}, u32[]{:S(2)}) collective-permute-start(bf16[2,2,2,48,2048]{4,3,0,2,1:T(8,128)(2,1)S(1)} %bitcast.641), channel_id=1, source_target_pairs={{0,4},{2,6},{4,0},{6,2},{8,12},{10,14},{12,8},{14,10},{16,20},{18,... | collective-permute-start | bytes 4718600 | tf_op jit(solution)/shard_map/ppermute | solution.py:456
  465.8 23.8 %collective-permute-start.14 = (bf16[2,2,2,32,2048]{4,3,0,1,2:T(8,128)(2,1)S(1)}, bf16[2,2,2,32,2048]{4,3,0,1,2:T(8,128)(2,1)S(1)}, u32[]{:S(2)}, u32[]{:S(2)}) collective-permute-start(bf16[2,2,2,32,2048]{4,3,0,1,2:T(8,128)(2,1)S(1)} %bitcast.643), channel_id=1, source_target_pairs={{0,8},{2,10},{4,12},{6,14},{8,0},{10,2},{12,4},{14,6},{16,24},{18,... | collective-permute-start | bytes 3145736 | tf_op jit(solution)/shard_map/ppermute | solution.py:456
  478.2 40.2 %copy-start.5 = (f32[1024,2048]{1,0:T(8,128)}, f32[1024,2048]{1,0:T(8,128)S(1)}, u32[]{:S(2)}) copy-start(f32[1024,2048]{1,0:T(8,128)S(1)} %fusion.236) | copy-start | bytes 25165828
  491.1 31.2 %collective-permute-start.15 = (bf16[2,2,48,2048]{3,2,0,1:T(8,128)(2,1)}, bf16[2,2,48,2048]{3,2,0,1:T(8,128)(2,1)}, u32[]{:S(2)}, u32[]{:S(2)}) collective-permute-start(bf16[2,2,48,2048]{3,2,0,1:T(8,128)(2,1)} %dynamic-slice_bitcast_fusion.1), channel_id=1, source_target_pairs={{0,4},{2,6},{4,0},{6,2},{8,12},{10,14},{12,8},{14,10},{16,20},{18,... | collective-permute-start | bytes 2359304 | tf_op jit(solution)/shard_map/ppermute | solution.py:456
  493.9 28.4 %collective-permute-start.16 = (bf16[2,2,48,2048]{3,2,0,1:T(8,128)(2,1)}, bf16[2,2,48,2048]{3,2,0,1:T(8,128)(2,1)}, u32[]{:S(2)}, u32[]{:S(2)}) collective-permute-start(bf16[2,2,48,2048]{3,2,0,1:T(8,128)(2,1)} %dynamic-slice_bitcast_fusion), channel_id=1, source_target_pairs={{0,8},{2,10},{4,12},{6,14},{8,0},{10,2},{12,4},{14,6},{16,24},{18,... | collective-permute-start | bytes 2359304 | tf_op jit(solution)/shard_map/ppermute | solution.py:456
  496.7 25.6 %collective-permute-start.17 = (bf16[2,2,32,2048]{3,2,0,1:T(8,128)(2,1)}, bf16[2,2,32,2048]{3,2,0,1:T(8,128)(2,1)}, u32[]{:S(2)}, u32[]{:S(2)}) collective-permute-start(bf16[2,2,32,2048]{3,2,0,1:T(8,128)(2,1)} %dynamic-slice_bitcast_fusion.4), channel_id=1, source_target_pairs={{0,2},{2,0},{4,6},{6,4},{8,10},{10,8},{12,14},{14,12},{16,18},{18,... | collective-permute-start | bytes 1572872 | tf_op jit(solution)/shard_map/ppermute | solution.py:456
  509.3 19.6 %copy-start.4 = (f32[1024,2048]{1,0:T(8,128)}, f32[1024,2048]{1,0:T(8,128)S(1)}, u32[]{:S(2)}) copy-start(f32[1024,2048]{1,0:T(8,128)S(1)} %fusion.237) | copy-start | bytes 25165828
  523.8 12.5 %collective-permute-start.18 = (bf16[2,48,2048]{2,1,0:T(8,128)(2,1)S(1)}, bf16[2,48,2048]{2,1,0:T(8,128)(2,1)S(1)}, u32[]{:S(2)}, u32[]{:S(2)}) collective-permute-start(bf16[2,48,2048]{2,1,0:T(8,128)(2,1)S(1)} %dynamic-slice_bitcast_fusion.7), channel_id=1, source_target_pairs={{0,8},{2,10},{4,12},{6,14},{8,0},{10,2},{12,4},{14,6},{16,24},{18,... | collective-permute-start | bytes 1179656 | tf_op jit(solution)/shard_map/ppermute | solution.py:456
  525.6 10.7 %collective-permute-start.19 = (bf16[2,48,2048]{2,1,0:T(8,128)(2,1)S(1)}, bf16[2,48,2048]{2,1,0:T(8,128)(2,1)S(1)}, u32[]{:S(2)}, u32[]{:S(2)}) collective-permute-start(bf16[2,48,2048]{2,1,0:T(8,128)(2,1)S(1)} %dynamic-slice_bitcast_fusion.6), channel_id=1, source_target_pairs={{0,2},{2,0},{4,6},{6,4},{8,10},{10,8},{12,14},{14,12},{16,18},{18,... | collective-permute-start | bytes 1179656 | tf_op jit(solution)/shard_map/ppermute | solution.py:456
  527.9 8.3 collective-permute-start.20
  531.5 63.6 %collective-permute-start.26 = (bf16[1024,2048]{1,0:T(8,128)(2,1)}, bf16[1024,2048]{1,0:T(8,128)(2,1)}, u32[]{:S(2)}, u32[]{:S(2)}) collective-permute-start(bf16[1024,2048]{1,0:T(8,128)(2,1)} %convert_element_type.658), channel_id=1, source_target_pairs={{0,1},{1,0},{2,3},{3,2},{4,5},{5,4},{6,7},{7,6},{8,9},{9,8},{10,11... | collective-permute-start | bytes 12582920 | tf_op jit(solution)/shard_map/ppermute | solution.py:744
  536.4 27.1 %collective-permute-start.21 = (bf16[48,2048]{1,0:T(8,128)(2,1)S(1)}, bf16[48,2048]{1,0:T(8,128)(2,1)S(1)}, u32[]{:S(2)}, u32[]{:S(2)}) collective-permute-start(bf16[48,2048]{1,0:T(8,128)(2,1)S(1)} %dynamic-slice_bitcast_fusion.15), channel_id=1, source_target_pairs={{0,16},{2,18},{4,20},{6,22},{8,24},{10,26},{12,28},{14,30},{16,0},... | collective-permute-start | bytes 589832 | tf_op jit(solution)/shard_map/ppermute | solution.py:456
  540.0 23.5 %collective-permute-start.22 = (bf16[48,2048]{1,0:T(8,128)(2,1)S(1)}, bf16[48,2048]{1,0:T(8,128)(2,1)S(1)}, u32[]{:S(2)}, u32[]{:S(2)}) collective-permute-start(bf16[48,2048]{1,0:T(8,128)(2,1)S(1)} %dynamic-slice_bitcast_fusion.14), channel_id=1, source_target_pairs={{0,16},{2,18},{4,20},{6,22},{8,24},{10,26},{12,28},{14,30},{16,0},... | collective-permute-start | bytes 589832 | tf_op jit(solution)/shard_map/ppermute | solution.py:456
  540.2 23.4 %collective-permute-start.23 = (bf16[32,2048]{1,0:T(8,128)(2,1)S(1)}, bf16[32,2048]{1,0:T(8,128)(2,1)S(1)}, u32[]{:S(2)}, u32[]{:S(2)}) collective-permute-start(bf16[32,2048]{1,0:T(8,128)(2,1)S(1)} %dynamic-slice_bitcast_fusion.20), channel_id=1, source_target_pairs={{0,16},{2,18},{4,20},{6,22},{8,24},{10,26},{12,28},{14,30},{16,0},... | collective-permute-start | bytes 393224 | tf_op jit(solution)/shard_map/ppermute | solution.py:456
  546.6 17.1 %copy-start.9 = (f32[128,2048]{1,0:T(8,128)S(1)}, f32[128,2048]{1,0:T(8,128)}, u32[]{:S(2)}) copy-start(f32[128,2048]{1,0:T(8,128)} %copy-done.8) | copy-start | bytes 3145732
  546.6 17.1 %copy-start.68 = (f32[2048]{0:T(1024)S(1)}, f32[2048]{0:T(1024)}, u32[]{:S(2)}) copy-start(f32[2048]{0:T(1024)} %param.35) | copy-start | bytes 24580
  546.6 17.1 %copy-start.74 = (f32[128]{0:T(128)S(1)}, f32[128]{0:T(128)}, u32[]{:S(2)}) copy-start(f32[128]{0:T(128)} %copy-done.73) | copy-start | bytes 1540
  546.6 17.4 %copy-start.79 = (f32[128]{0:T(128)S(1)}, f32[128]{0:T(128)}, u32[]{:S(2)}) copy-start(f32[128]{0:T(128)} %copy-done.78) | copy-start | bytes 1540
  546.6 17.4 %copy-start.33 = (bf16[1,128,2048]{2,1,0:T(8,128)(2,1)S(1)}, bf16[1,128,2048]{2,1,0:T(8,128)(2,1)}, u32[]{:S(2)}) copy-start(bf16[1,128,2048]{2,1,0:T(8,128)(2,1)} %param.57) | copy-start | bytes 1572868
  546.6 17.4 %copy-start.44 = (f32[32,2048]{1,0:T(8,128)S(1)}, f32[32,2048]{1,0:T(8,128)}, u32[]{:S(2)}) copy-start(f32[32,2048]{1,0:T(8,128)} %convert_add_fusion.32) | copy-start | bytes 786436
  546.6 18.6 %slice-start.2 = ((s8[8388608]{0:T(1024)(128)(4,1)}), s8[4194304]{0:T(1024)(128)(4,1)S(1)}, s32[]{:S(2)}) async-start(s8[8388608]{0:T(1024)(128)(4,1)} %bitcast.605), calls=%async_computation.5 | async-start | bytes 8388608
  584.3 21.1 %collective-permute-start.24 = (bf16[2,2,2,64,512]{4,3,0,1,2:T(8,128)(2,1)}, bf16[2,2,2,64,512]{4,3,0,1,2:T(8,128)(2,1)}, u32[]{:S(2)}, u32[]{:S(2)}) collective-permute-start(bf16[2,2,2,64,512]{4,3,0,1,2:T(8,128)(2,1)} %bitcast.544), channel_id=1, source_target_pairs={{0,2},{2,0},{4,6},{6,4},{8,10},{10,8},{12,14},{14,12},{16,18},{18,... | collective-permute-start | bytes 1572872 | tf_op jit(solution)/shard_map/ppermute | solution.py:456
  586.7 18.7 %collective-permute-start.25 = (bf16[2,2,2,64,512]{4,3,0,2,1:T(8,128)(2,1)}, bf16[2,2,2,64,512]{4,3,0,2,1:T(8,128)(2,1)}, u32[]{:S(2)}, u32[]{:S(2)}) collective-permute-start(bf16[2,2,2,64,512]{4,3,0,2,1:T(8,128)(2,1)} %bitcast.543), channel_id=1, source_target_pairs={{0,4},{2,6},{4,0},{6,2},{8,12},{10,14},{12,8},{14,10},{16,20},{18,... | collective-permute-start | bytes 1572872 | tf_op jit(solution)/shard_map/ppermute | solution.py:456
  605.4 35.0 %collective-permute-start.29 = (bf16[1024,2048]{1,0:T(8,128)(2,1)}, bf16[1024,2048]{1,0:T(8,128)(2,1)}, u32[]{:S(2)}, u32[]{:S(2)}) collective-permute-start(bf16[1024,2048]{1,0:T(8,128)(2,1)} %convert_element_type.671), channel_id=1, source_target_pairs={{0,1},{1,0},{2,3},{3,2},{4,5},{5,4},{6,7},{7,6},{8,9},{9,8},{10,11... | collective-permute-start | bytes 12582920 | tf_op jit(solution)/shard_map/ppermute | solution.py:744
  625.4 28.7 %collective-permute-start.35 = (bf16[16,192,1024]{2,1,0:T(8,128)(2,1)}, bf16[16,192,1024]{2,1,0:T(8,128)(2,1)}, u32[]{:S(2)}, u32[]{:S(2)}) collective-permute-start(bf16[16,192,1024]{2,1,0:T(8,128)(2,1)} %constant_dynamic-slice_fusion), channel_id=1, source_target_pairs={{0,1},{1,0},{2,3},{3,2},{4,5},{5,4},{6,7},{7,6},{8,9},{9,8},{10,11... | collective-permute-start | bytes 18874376 | tf_op jit(solution)/shard_map/ppermute | solution.py:490
  627.8 22.7 %collective-permute-start.27 = (bf16[2,2,64,512]{3,2,0,1:T(8,128)(2,1)S(1)}, bf16[2,2,64,512]{3,2,0,1:T(8,128)(2,1)S(1)}, u32[]{:S(2)}, u32[]{:S(2)}) collective-permute-start(bf16[2,2,64,512]{3,2,0,1:T(8,128)(2,1)S(1)} %dynamic-slice_bitcast_fusion.11), channel_id=1, source_target_pairs={{0,4},{2,6},{4,0},{6,2},{8,12},{10,14},{12,8},{14,10},{16,20},{18,... | collective-permute-start | bytes 786440 | tf_op jit(solution)/shard_map/ppermute | solution.py:456
  630.5 22.2 %copy-start.52 = (f32[128,128]{1,0:T(8,128)S(1)}, f32[128,128]{1,0:T(8,128)}, u32[]{:S(2)}) copy-start(f32[128,128]{1,0:T(8,128)} %copy-done.51) | copy-start | bytes 196612
  630.5 22.2 %copy-start.64 = (f32[128,128]{1,0:T(8,128)S(1)}, f32[128,128]{1,0:T(8,128)}, u32[]{:S(2)}) copy-start(f32[128,128]{1,0:T(8,128)} %get-tuple-element.626) | copy-start | bytes 196612
  630.5 20.0 %collective-permute-start.28 = (bf16[2,2,64,512]{3,2,0,1:T(8,128)(2,1)S(1)}, bf16[2,2,64,512]{3,2,0,1:T(8,128)(2,1)S(1)}, u32[]{:S(2)}, u32[]{:S(2)}) collective-permute-start(bf16[2,2,64,512]{3,2,0,1:T(8,128)(2,1)S(1)} %dynamic-slice_bitcast_fusion.10), channel_id=1, source_target_pairs={{0,8},{2,10},{4,12},{6,14},{8,0},{10,2},{12,4},{14,6},{16,24},{18,... | collective-permute-start | bytes 786440 | tf_op jit(solution)/shard_map/ppermute | solution.py:456
  651.9 20.5 %collective-permute-start.32 = (bf16[1024,2048]{1,0:T(8,128)(2,1)}, bf16[1024,2048]{1,0:T(8,128)(2,1)}, u32[]{:S(2)}, u32[]{:S(2)}) collective-permute-start(bf16[1024,2048]{1,0:T(8,128)(2,1)} %convert_element_type.672), channel_id=1, source_target_pairs={{0,1},{1,0},{2,3},{3,2},{4,5},{5,4},{6,7},{7,6},{8,9},{9,8},{10,11... | collective-permute-start | bytes 12582920 | tf_op jit(solution)/shard_map/ppermute | solution.py:744
  670.7 7.6 collective-permute-start.30
  671.0 20.5 %copy-start.3 = (bf16[1,128,2048]{2,1,0:T(8,128)(2,1)S(1)}, bf16[1,128,2048]{2,1,0:T(8,128)(2,1)}, u32[]{:S(2)}) copy-start(bf16[1,128,2048]{2,1,0:T(8,128)(2,1)} %param.32) | copy-start | bytes 1572868
  671.0 20.5 %copy-start.50 = (f32[2048]{0:T(1024)S(1)}, f32[2048]{0:T(1024)}, u32[]{:S(2)}) copy-start(f32[2048]{0:T(1024)} %param.34) | copy-start | bytes 24580
  671.0 20.5 %copy-start.70 = (f32[128]{0:T(128)S(1)}, f32[128]{0:T(128)}, u32[]{:S(2)}) copy-start(f32[128]{0:T(128)} %copy-done.69) | copy-start | bytes 1540
  671.0 7.4 collective-permute-start.31
  678.3 25.1 %copy-start.1 = (f32[1024,2048]{1,0:T(8,128)}, f32[1024,2048]{1,0:T(8,128)S(1)}, u32[]{:S(2)}) copy-start(f32[1024,2048]{1,0:T(8,128)S(1)} %convert_add_fusion) | copy-start | bytes 25165828
  678.4 37.0 %collective-permute-start.33 = (bf16[64,512]{1,0:T(8,128)(2,1)S(1)}, bf16[64,512]{1,0:T(8,128)(2,1)}, u32[]{:S(2)}, u32[]{:S(2)}) collective-permute-start(bf16[64,512]{1,0:T(8,128)(2,1)S(1)} %dynamic-slice_bitcast_fusion.23), channel_id=1, source_target_pairs={{0,16},{2,18},{4,20},{6,22},{8,24},{10,26},{12,28},{14,30},{16,0},... | collective-permute-start | bytes 196616 | tf_op jit(solution)/shard_map/ppermute | solution.py:456
  691.4 24.0 %collective-permute-start.34 = (bf16[64,512]{1,0:T(8,128)(2,1)S(1)}, bf16[64,512]{1,0:T(8,128)(2,1)}, u32[]{:S(2)}, u32[]{:S(2)}) collective-permute-start(bf16[64,512]{1,0:T(8,128)(2,1)S(1)} %dynamic-slice_bitcast_fusion.22), channel_id=1, source_target_pairs={{0,16},{2,18},{4,20},{6,22},{8,24},{10,26},{12,28},{14,30},{16,0},... | collective-permute-start | bytes 196616 | tf_op jit(solution)/shard_map/ppermute | solution.py:456
  847.1 3.3 collective-permute-start.36
  (70 other events, 386.2 us)
Sparse Core Ops, SparseCore 0:
  102.9 146.1 all-gather.1
  664.9 182.1 reduce-scatter.1

commit v4 on v3

--- a/solution.py
+++ b/solution.py
@@ -487,7 +487,11 @@
     swap = [(0, 1), (1, 0)]
     own = lax.dynamic_slice_in_dim(terms, core * half, half, 2)
     away = lax.dynamic_slice_in_dim(terms, (1 - core) * half, half, 2)
-    both = own + lax.ppermute(away, "dp", swap)
+    return scatter_half(own + lax.ppermute(away, "dp", swap), core)
+
+
+def scatter_half(both, core):
+    swap = [(0, 1), (1, 0)]
     mine = lax.psum_scatter(both, "fsdp", scatter_dimension=0, tiled=False)
     theirs = lax.ppermute(mine, "dp", swap)
     return jnp.where(
@@ -696,11 +700,12 @@
     hidden_full, pull_geglu = jax.vjp(geglu, gate, up)
     hidden = hidden_full.astype(bf16)
     edges = row_edges(tok_rows)
-    down_terms = HalvingSum(
-        matrix_product(hidden, down_weight).astype(bf16), place, shards, edges
-    )
+    down_product, hidden, cot_late = lax.optimization_barrier(
+        (matrix_product(hidden, down_weight).astype(bf16), hidden, cot_all)
+    )
+    down_terms = HalvingSum(down_product, place, shards, edges)
     down_terms.start()
-    grad_hidden = right_product(cot_all, down_weight)
+    grad_hidden = right_product(cot_late, down_weight)
     grad_gate_full, grad_up_full = pull_geglu(grad_hidden)
     grad_gate, grad_up = together(
         [down_terms], (grad_gate_full.astype(bf16), grad_up_full.astype(bf16))
@@ -714,34 +719,36 @@
     mlp_terms = HalvingSum(in_terms, place, shards, edges)
     down_terms.start()
     mlp_terms.start()
-    gate_rows = left_matrix_product(grad_gate, mlp_all)
-    up_rows = left_matrix_product(grad_up, mlp_all)
+    gate_rows = left_matrix_product(grad_gate, mlp_all).astype(bf16)
+    up_rows = left_matrix_product(grad_up, mlp_all).astype(bf16)
     gate_rows, up_rows, hidden = together([down_terms, mlp_terms], (gate_rows, up_rows, hidden))
     mlp_terms.start()
-    down_rows = left_matrix_product(hidden, cot_all)
-    gate_rows_low = gate_rows.astype(bf16)
-    down_rows, gate_rows_low = together([mlp_terms], (down_rows, gate_rows_low))
+    down_rows = left_matrix_product(hidden, cot_all).astype(bf16)
+    down_rows, gate_rows = together([mlp_terms], (down_rows, gate_rows))
     mlp_terms.start()
     gate_in_term = lax.dot_general(
-        gate_rows_low, gate_second, (((0,), (1,)), ((), ())), preferred_element_type=f32
-    )
-    up_rows_low = up_rows.astype(bf16)
-    down_rows_low = down_rows.astype(bf16)
-    gate_in_term, up_rows_low, down_rows_low = together(
-        [mlp_terms], (gate_in_term, up_rows_low, down_rows_low)
-    )
+        gate_rows, gate_second, (((0,), (1,)), ((), ())), preferred_element_type=f32
+    ).astype(bf16)
+    gate_in_term, up_rows, down_rows = together([mlp_terms], (gate_in_term, up_rows, down_rows))
     mlp_terms.start()
     up_in_term = lax.dot_general(
-        up_rows_low, up_second, (((0,), (1,)), ((), ())), preferred_element_type=f32
-    )
-    down_out_term = left_matrix_product(down_first, down_rows_low)
-    up_in_term, down_out_term = together([mlp_terms], (up_in_term, down_out_term))
+        up_rows, up_second, (((0,), (1,)), ((), ())), preferred_element_type=f32
+    ).astype(bf16)
+    few = rank // shards
+    early = jnp.concatenate(
+        [
+            left_matrix_product(down_first, down_rows).astype(bf16).reshape(shards, few, width),
+            pack_rows(jnp.concatenate([gate_in_term, up_in_term], axis=1), shards, width),
+        ],
+        axis=1,
+    )
+    early = together([mlp_terms], early)
     grad_mlp_in = mlp_terms.rest()
     down_sum = down_terms.rest()
     swap = [(0, 1), (1, 0)]
 
-    def over_cores(rows, low):
-        return rows + lax.ppermute(low, "dp", swap).astype(f32)
+    def over_cores(rows):
+        return rows.astype(f32) + lax.ppermute(rows, "dp", swap).astype(f32)
 
     def columns_of(first, rows):
         return lax.dot_general(
@@ -756,28 +763,33 @@
         return left_matrix_product(left, right).astype(bf16)
 
     per = in_rows
-    few = rank // shards
     grad_attn = right_product(grad_branch, output_weight).astype(bf16)
     lora_output = matrix_product(attn, output_factor_first).astype(bf16)
     lora_query = matrix_product(attn_in, query_factor_first).astype(bf16)
     lora_key = matrix_product(attn_in, key_factor_first).astype(bf16)
     lora_value = matrix_product(attn_in, value_factor_first).astype(bf16)
-    early = jnp.concatenate(
+    columns = width // 2
+
+    def half_of(values, which):
+        return lax.dynamic_slice_in_dim(values, which * columns, columns, values.ndim - 1)
+
+    def early_parts(which):
+        branch = half_of(grad_branch, which)
+        return [
+            low_term(attn, branch).reshape(shards, per, columns),
+            low_term(lora_output, branch).reshape(shards, few, columns),
+            half_of(early, which),
+        ]
+
+    early_half = jnp.concatenate(
         [
-            low_term(lora_output, grad_branch).reshape(shards, few, width),
-            down_out_term.astype(bf16).reshape(shards, few, width),
-            pack_rows(
-                jnp.concatenate([gate_in_term, up_in_term], axis=1).astype(bf16), shards, width
-            ),
+            own + lax.ppermute(away, "dp", swap)
+            for own, away in zip(early_parts(core), early_parts(1 - core))
         ],
         axis=1,
     )
-    early_sums = scatter_shared(
-        jnp.concatenate(
-            [low_term(attn, grad_branch).reshape(shards, per, width), early], axis=1
-        ),
-        core,
-    ).astype(f32)
+    early_half, grad_attn = lax.optimization_barrier((early_half, grad_attn))
+    early_sums = scatter_half(early_half, core).astype(f32)
     g_output_weight = early_sums[:per]
     early_sums = early_sums[per:]
     g_output_out = early_sums[:few]
@@ -824,17 +836,13 @@
     )
     key_halves = HalvingSum(key_terms, place, shards, [0, tok_rows // 2, tok_rows])
     key_halves.start()
-    g_gate_rows = over_cores(gate_rows, gate_rows_low)
-    g_gate_rows, up_rows, up_rows_low = together(
-        [key_halves], (g_gate_rows, up_rows, up_rows_low)
-    )
+    g_gate_rows = over_cores(gate_rows)
+    g_gate_rows, up_rows = together([key_halves], (g_gate_rows, up_rows))
     key_halves.start()
-    g_up_rows = over_cores(up_rows, up_rows_low)
-    g_up_rows, down_rows, down_rows_low = together(
-        [key_halves], (g_up_rows, down_rows, down_rows_low)
-    )
+    g_up_rows = over_cores(up_rows)
+    g_up_rows, down_rows = together([key_halves], (g_up_rows, down_rows))
     key_halves.start()
-    g_down_rows = over_cores(down_rows, down_rows_low)
+    g_down_rows = over_cores(down_rows)
     g_gate_out = columns_of(gate_factor_first, g_gate_rows)
     g_down_rows, g_gate_out, g_up_rows, grad_query_lin = together(
         [key_halves], (g_down_rows, g_gate_out, g_up_rows, grad_query_lin)

time: 868 us -> 815 us (0.939)
  other arithmetic: 118 us -> 78.5 us
  local copies, waits for them, and re-layouts: 66.8 us -> 49.5 us
  waiting for transfers between devices: 55.5 us -> 43.4 us
  matrix products: 222 us -> 231 us
    ppermute x32, waiting for transfers between devices: 51.3 us -> 35.3 us  [start(): self.came.append(lax.ppermute(away, 'fsdp', pairs))]
    add x5 -> x6, other arithmetic: 38.1 us -> 24.8 us  [the longest x3 19.6 us: over_cores(): return rows.astype(f32) + lax.ppermute(rows, 'dp', swap).astype(f32)]
    convert_element_type x4 -> x2, other arithmetic: 14.9 us -> 2.89 us  [the longest x1 1.56 us: local(): grad_branch = grad_resid.astype(bf16)]
    unnamed x213 -> x159, local copies, waits for them, and re-layouts: 23.1 us -> 15.9 us
    dot_general x11 -> x12, matrix products: 59.9 us -> 64.2 us  [matrix_product(): return jnp.dot(left, right, preferred_element_type=jnp.float32)]
    dot_general x11 -> x13, matrix products: 58.1 us -> 59.4 us  [left_matrix_product(): lax.dot_general(left, right, (((0,), (0,)), ((), ())), preferred_element_...]
  transfers between devices with their start and end apart: 39 -> 41, of which waited for: 7 -> 13; matrix products, arithmetic and copies ran while one was open for 39% -> 41% of each run, Pallas kernels for 27% -> 29%
where the time goes in v4:
time: 815 us; the launch traced here: 802 us
  Pallas kernels  317 us (39%)
  matrix products  231 us (28%)
  other arithmetic  78.5 us (10%)
  starting transfers between devices  66.2 us (8%)
  local copies, waits for them, and re-layouts  49.5 us (6%)
  waiting for transfers between devices  43.4 us (5%)
  between operations  16.3 us (2%)
    pallas_call x3, Pallas kernels, gather_blocks(): pl.pallas_call(functools.partial(gather_kernel, pieces, len(arrays), with...  222 us
    pallas_call x1, Pallas kernels, scatter_blocks(): pl.pallas_call(scatter_kernel, out_shape=jax.ShapeDtypeStruct((rows, colu...  94.5 us
    dot_general x11, matrix products, right_product(): lax.dot_general(left, right, (((1,), (1,)), ((), ())), preferred_element_...  74 us
    ppermute x32, starting transfers between devices, start(): self.came.append(lax.ppermute(away, 'fsdp', pairs))  64.9 us
    dot_general x12, matrix products, matrix_product(): return jnp.dot(left, right, preferred_element_type=jnp.float32)  64.2 us
    dot_general x13, matrix products, left_matrix_product(): lax.dot_general(left, right, (((0,), (0,)), ((), ())), preferred_element_...  59.4 us
    ppermute x32, waiting for transfers between devices, start(): self.came.append(lax.ppermute(away, 'fsdp', pairs))  35.3 us
    add x3, other arithmetic, over_cores(): return rows.astype(f32) + lax.ppermute(rows, 'dp', swap).astype(f32)  19.6 us
  transfers between devices with their start and end apart: 41, of which 13 were waited for; matrix products, arithmetic and copies ran while one was open for 41% of the time, Pallas kernels for 29%

profile of v4, /device:TPU:0, one launch (start us, length us, event | category | flops | bytes accessed | tf_op | source)
XLA Modules:
  0.0 802.3 jit_solution(6599703972549064244)
XLA Ops:
  10.2 2.3 fusion.64.refs_0_
  12.5 2.3 fusion.65.refs_1_
  14.7 88.0 %gather_blocks_1.1 = (bf16[16,2,64,2048]{3,2,1,0:T(8,128)(2,1)}, bf16[16,2,64,2048]{3,2,1,0:T(8,128)(2,1)}, bf16[16,2,64,512]{3,2,1,0:T(8,128)(2,1)}) custom-call(bf16[64,2048]{1,0:T(8,128)(2,1)} %fusion.64.refs_0_, bf16[64,2048]{1,0:T(8,128)(2,1)} %fusion.65.refs_1_, bf16[64,512]{1,0:T(8,128)(2,1)} %pad_maximum_fusion.12.refs_2_), custom_call_target="tpu_custom_call" | custom-call | tf_op jit(solution)/shard_map/gather_blocks_1/pallas_call | solution.py:227
  107.8 35.0 %gather_blocks_3.1 = bf16[16,128,512]{2,1,0:T(8,128)(2,1)} custom-call(bf16[128,512]{1,0:T(8,128)(2,1)} %pad_maximum_fusion.9.refs_0_), custom_call_target="tpu_custom_call" | custom-call | tf_op jit(solution)/shard_map/gather_blocks_3/pallas_call | solution.py:227
  142.8 2.7 fusion.220
  145.5 4.7 fusion.114
  159.4 2.2 while.38
  161.9 5.3 multiply_reduce_fusion.3
  169.3 99.2 %gather_blocks_2.1 = bf16[16,128,2048]{2,1,0:T(8,128)(2,1)} custom-call(bf16[128,2048]{1,0:T(8,128)(2,1)} %multiply_convert_fusion.2.refs_0_), custom_call_target="tpu_custom_call" | custom-call | tf_op jit(solution)/shard_map/gather_blocks_2/pallas_call | solution.py:227
  268.5 3.8 add_convert_fusion.3
  272.4 2.9 add_convert_fusion.2
  276.5 5.8 add_convert_fusion.1
  282.3 11.6 %fusion.228 = f32[2048,1024]{1,0:T(8,128)} fusion(bf16[2048,2048]{1,0:T(8,128)(2,1)S(1)} %bitcast.609, bf16[1024,2048]{1,0:T(8,128)(2,1)S(1)} %add_convert_fusion.3), kind=kOutput, calls=%fused_computation.468 | convolution fusion | flops 8589934592 | bytes 20971520 | tf_op jit(solution)/shard_map/dot_general | solution.py:26
  293.9 15.5 %multiply_convert_fusion.1 = (bf16[2048,1024]{1,0:T(8,128)(2,1)}, f32[2048,1024]{1,0:T(8,128)}) fusion(f32[2048,1024]{1,0:T(8,128)} %fusion.228, bf16[2048,2048]{1,0:T(8,128)(2,1)S(1)} %bitcast.610, bf16[1024,2048]{1,0:T(8,128)(2,1)S(1)} %add_convert_fusion.2), kind=kOutput, calls=%fused_computation.79 | convolution fusion | flops 8610906112 | bytes 33554432 | tf_op jit(solution)/shard_map/dot_general | solution.py:26
  309.5 14.1 %convolution_convert_fusion = bf16[2048,2048]{1,0:T(8,128)(2,1)} fusion(bf16[2048,1024]{1,0:T(8,128)(2,1)} %get-tuple-element.301, bf16[1024,2048]{1,0:T(8,128)(2,1)} %add_convert_fusion.1), kind=kOutput, calls=%fused_computation.83 | convolution fusion | flops 8594128896 | bytes 16777216 | tf_op jit(solution)/shard_map/dot_general | solution.py:16
  323.6 3.4 fusion.218
  337.2 24.6 %multiply_convert_fusion = (bf16[2048,1024]{1,0:T(8,128)(2,1)}, bf16[2048,1024]{1,0:T(8,128)(2,1)}) fusion(f32[2048,1024]{1,0:T(8,128)} %fusion.228, f32[2048,1024]{1,0:T(8,128)} %get-tuple-element.638, bf16[2048,2048]{1,0:T(8,128)(2,1)} %all-gather.2.cloned.1.call-done, bf16[1024,2048]{1,0:T(8,128)(2,1)} %add_convert_fusion.1), kind=kOutput, calls=%fused_computation.77 | convolution fusion | flops 8640266240 | bytes 37748736 | tf_op jit(solution)/shard_map/dot_general | solution.py:26
  361.9 2.2 collective-permute-done
  364.1 3.0 collective-permute-done.1
  376.3 12.1 %fusion.229 = f32[2048,2048]{1,0:T(8,128)} fusion(bf16[2048,1024]{1,0:T(8,128)(2,1)S(1)} %copy-done.61, bf16[1024,2048]{1,0:T(8,128)(2,1)S(1)} %copy-done.17), kind=kOutput, calls=%fused_computation.469 | convolution fusion | flops 8589934592 | bytes 25165824 | tf_op jit(solution)/shard_map/dot_general | solution.py:16
  388.8 2.5 collective-permute-start.6
  394.2 11.7 %fusion.230 = f32[2048,2048]{1,0:T(8,128)} fusion(bf16[2048,1024]{1,0:T(8,128)(2,1)S(1)} %copy-done.60, bf16[1024,2048]{1,0:T(8,128)(2,1)S(1)} %copy-done.15), kind=kOutput, calls=%fused_computation.470 | convolution fusion | flops 8589934592 | bytes 25165824 | tf_op jit(solution)/shard_map/dot_general | solution.py:16
  405.9 11.5 %add_convert_fusion = bf16[2048,2048]{1,0:T(8,128)(2,1)S(1)} fusion(f32[2048,2048]{1,0:T(8,128)} %fusion.229, f32[2048,2048]{1,0:T(8,128)} %fusion.230), kind=kLoop, calls=%fused_computation.63 | loop fusion | flops 8388608 | bytes 41943040 | tf_op jit(solution)/shard_map/convert_element_type | solution.py:717
  418.9 6.4 collective-permute-start.9
  425.6 3.0 collective-permute-start.11
  432.7 12.6 %convolution_convert_fusion.4 = bf16[1024,2048]{1,0:T(8,128)(2,1)} fusion(bf16[2048,1024]{1,0:T(8,128)(2,1)} %get-tuple-element.292, bf16[2048,2048]{1,0:T(8,128)(2,1)S(1)} %bitcast.613), kind=kOutput, calls=%fused_computation.94 | convolution fusion | flops 8592031744 | bytes 16777216 | tf_op jit(solution)/shard_map/dot_general | solution.py:20
  446.5 11.1 %convolution_convert_fusion.3 = bf16[1024,2048]{1,0:T(8,128)(2,1)S(1)} fusion(bf16[2048,1024]{1,0:T(8,128)(2,1)} %get-tuple-element.293, bf16[2048,2048]{1,0:T(8,128)(2,1)S(1)} %bitcast.614), kind=kOutput, calls=%fused_computation.93 | convolution fusion | flops 8592031744 | bytes 16777216 | tf_op jit(solution)/shard_map/dot_general | solution.py:20
  457.6 12.0 %collective-permute-done.14 = bf16[2,2,2,32,2048]{4,3,0,1,2:T(8,128)(2,1)S(1)} collective-permute-done((bf16[2,2,2,32,2048]{4,3,0,1,2:T(8,128)(2,1)S(1)}, bf16[2,2,2,32,2048]{4,3,0,1,2:T(8,128)(2,1)S(1)}, u32[]{:S(2)}, u32[]{:S(2)}) %collective-permute-start.14) | collective-permute-done | bytes 1048608 | tf_op jit(solution)/shard_map/ppermute | solution.py:456
  475.4 13.3 %convolution_convert_fusion.2 = bf16[1024,2048]{1,0:T(8,128)(2,1)} fusion(bf16[2048,1024]{1,0:T(8,128)(2,1)S(1)} %copy-done.59, bf16[2048,2048]{1,0:T(8,128)(2,1)} %all-gather.2.cloned.1.call-done), kind=kOutput, calls=%fused_computation.92 | convolution fusion | flops 8592031744 | bytes 16777216 | tf_op jit(solution)/shard_map/dot_general | solution.py:20
  494.7 3.6 convolution_convert_fusion.11
  501.3 3.4 collective-permute-start.21
  505.0 3.0 collective-permute-start.23
  508.0 2.4 convolution_convert_fusion.9
  510.8 3.6 convolution_convert_fusion.10
  514.4 2.3 maximum_maximum_fusion
  516.8 7.8 collective-permute-done.23
  526.6 3.3 convolution_convert_fusion.5
  537.2 6.4 convolution_convert_fusion.12
  543.6 2.7 collective-permute-done.25
  547.2 4.3 add.472
  551.5 5.5 pad_maximum_fusion.2
  560.2 9.2 %while.39 = (s32[]{:T(128)}, f32[8,128,256]{2,1,0:T(8,128)}, bf16[2048,512]{1,0:T(8,128)(2,1)}, s32[]{:T(128)}, s32[128]{0:T(128)S(1)}, /*index=5*/s32[2048]{0:T...) while((s32[]{:T(128)}, f32[8,128,256]{2,1,0:T(8,128)}, ...), condition=%wide.region_13.14_spmd.clone, body=%wide.region_12.13_spmd.clone.sunk | while | flops 1348665984 | bytes 20336396 | solution.py:825
  564.5 2.8 convolution_add_fusion.10
  573.7 8.9 %convert_add_fusion.2 = f32[1024,2048]{1,0:T(8,128)} fusion(bf16[1024,2048]{1,0:T(8,128)(2,1)} %collective-permute-done.29, bf16[1024,2048]{1,0:T(8,128)(2,1)} %convolution_convert_fusion.4), kind=kLoop, calls=%fused_computation.76 | loop fusion | flops 6291456 | bytes 16777216 | tf_op jit(solution)/shard_map/add | solution.py:751
  582.6 3.0 collective-permute-done.27
  588.1 7.8 collective-permute-start.31
  595.9 5.3 convert_add_fusion.1
  604.3 5.6 fusion.76
  610.0 5.7 collective-permute-start.33
  617.7 5.4 convert_add_fusion
  623.2 8.9 %collective-permute-start.36 = (bf16[64,512]{1,0:T(8,128)(2,1)S(1)}, bf16[64,512]{1,0:T(8,128)(2,1)}, u32[]{:S(2)}, u32[]{:S(2)}) collective-permute-start(bf16[64,512]{1,0:T(8,128)(2,1)S(1)} %dynamic-slice_bitcast_fusion.23), channel_id=1, source_target_pairs={{0,16},{2,18},{4,20},{6,22},{8,24},{10,26},{12,28},{14,30},{16,0},... | collective-permute-start | bytes 196616 | tf_op jit(solution)/shard_map/ppermute | solution.py:456
  633.0 5.8 convolution_convert_fusion.1
  638.8 5.9 fusion.79
  644.7 2.5 fusion.54
  647.2 2.9 fusion.231
  650.2 3.2 convolution_convert_fusion.8
  653.4 2.5 copy.98
  658.7 4.0 fusion.91
  667.8 6.3 pad_maximum_fusion.1.terms_ref
  674.1 94.5 %scatter_blocks_4.1 = bf16[192,2048]{1,0:T(8,128)(2,1)S(1)} custom-call(bf16[16,192,2048]{2,1,0:T(8,128)(2,1)S(1)} %pad_maximum_fusion.1.terms_ref), custom_call_target="tpu_custom_call" | custom-call | tf_op jit(solution)/shard_map/scatter_blocks_4/pallas_call | solution.py:403
  773.7 2.5 copy.99
  779.6 2.8 fusion.98
  782.5 5.3 reduce-scatter.2.cloned.1.call-done
  788.4 2.7 fusion.122
  (414 shorter events, 121.3 us)
Async XLA Ops:
  7.2 261.2 %copy-start = (bf16[2048,256]{1,0:T(8,128)(2,1)S(1)}, bf16[2048,256]{1,0:T(8,128)(2,1)}, u32[]{:S(2)}) copy-start(bf16[2048,256]{1,0:T(8,128)(2,1)} %param.51) | copy-start | bytes 3145732
  7.2 95.6 %copy-start.39 = (s32[1,2048]{1,0:T(1,128)S(1)}, s32[1,2048]{1,0:T(1,128)}, u32[]{:S(2)}) copy-start(s32[1,2048]{1,0:T(1,128)} %param.33) | copy-start | bytes 24580
  7.2 96.6 %copy-start.2 = (bf16[1,128,2048]{2,1,0:T(8,128)(2,1)S(1)}, bf16[1,128,2048]{2,1,0:T(8,128)(2,1)}, u32[]{:S(2)}) copy-start(bf16[1,128,2048]{2,1,0:T(8,128)(2,1)} %param.32) | copy-start | bytes 1572868
  7.2 96.8 %copy-start.31 = (f32[2048]{0:T(1024)S(1)}, f32[2048]{0:T(1024)}, u32[]{:S(2)}) copy-start(f32[2048]{0:T(1024)} %param.34) | copy-start | bytes 24580
  7.3 316.3 %all-gather.2.cloned.1.call-start = ((), (), s32[]{:S(2)}) async-start(), calls=%async_computation.1 | async-start | bytes 8912896 | tf_op jit(solution)/shard_map/all_gather | solution.py:620
  102.8 685.0 %reduce-scatter.2.cloned.1.call-start = ((), (), s32[]{:S(2)}) async-start(), calls=%async_computation.2 | async-start | bytes 6684672 | tf_op jit(solution)/shard_map/reduce_scatter | solution.py:495
  103.7 41.8 %copy-start.48 = (f32[128]{0:T(128)}, f32[128]{0:T(128)S(1)}, u32[]{:S(2)}) copy-start(f32[128]{0:T(128)S(1)} %get-tuple-element.565) | copy-start | bytes 1540
  103.8 41.7 %copy-start.54 = (f32[128]{0:T(128)}, f32[128]{0:T(128)S(1)}, u32[]{:S(2)}) copy-start(f32[128]{0:T(128)S(1)} %negate_power_fusion) | copy-start | bytes 1540
  104.0 41.5 %copy-start.46 = (f32[128]{0:T(128)}, f32[128]{0:T(128)S(1)}, u32[]{:S(2)}) copy-start(f32[128]{0:T(128)S(1)} %fusion.199) | copy-start | bytes 1540
  107.1 48.4 %copy-start.33 = (f32[128,128]{1,0:T(8,128)}, f32[128,128]{1,0:T(8,128)S(1)}, u32[]{:S(2)}) copy-start(f32[128,128]{1,0:T(8,128)S(1)} %get-tuple-element.634) | copy-start | bytes 196612
  167.3 101.1 %copy-start.55 = (f32[128]{0:T(128)}, f32[128]{0:T(128)S(1)}, u32[]{:S(2)}) copy-start(f32[128]{0:T(128)S(1)} %get-tuple-element.635) | copy-start | bytes 1540
  272.4 9.9 %copy-start.16 = (bf16[1024,2048]{1,0:T(8,128)(2,1)}, bf16[1024,2048]{1,0:T(8,128)(2,1)S(1)}, u32[]{:S(2)}) copy-start(bf16[1024,2048]{1,0:T(8,128)(2,1)S(1)} %add_convert_fusion.3) | copy-start | bytes 12582916
  276.5 17.4 %copy-start.14 = (bf16[1024,2048]{1,0:T(8,128)(2,1)}, bf16[1024,2048]{1,0:T(8,128)(2,1)S(1)}, u32[]{:S(2)}) copy-start(bf16[1024,2048]{1,0:T(8,128)(2,1)S(1)} %add_convert_fusion.2) | copy-start | bytes 12582916
  330.4 33.6 %collective-permute-start = (bf16[2,2,2,48,2048]{4,3,0,1,2:T(8,128)(2,1)}, bf16[2,2,2,48,2048]{4,3,0,1,2:T(8,128)(2,1)}, u32[]{:S(2)}, u32[]{:S(2)}) collective-permute-start(bf16[2,2,2,48,2048]{4,3,0,1,2:T(8,128)(2,1)} %bitcast.529), channel_id=1, source_target_pairs={{0,2},{2,0},{4,6},{6,4},{8,10},{10,8},{12,14},{14,12},{16,18},{18,... | collective-permute-start | bytes 4718600 | tf_op jit(solution)/shard_map/ppermute | solution.py:456
  333.2 33.8 %collective-permute-start.1 = (bf16[2,2,2,48,2048]{4,3,0,2,1:T(8,128)(2,1)}, bf16[2,2,2,48,2048]{4,3,0,2,1:T(8,128)(2,1)}, u32[]{:S(2)}, u32[]{:S(2)}) collective-permute-start(bf16[2,2,2,48,2048]{4,3,0,2,1:T(8,128)(2,1)} %bitcast.528), channel_id=1, source_target_pairs={{0,4},{2,6},{4,0},{6,2},{8,12},{10,14},{12,8},{14,10},{16,20},{18,... | collective-permute-start | bytes 4718600 | tf_op jit(solution)/shard_map/ppermute | solution.py:456
  336.2 25.6 %collective-permute-start.2 = (bf16[2,2,2,32,2048]{4,3,0,1,2:T(8,128)(2,1)}, bf16[2,2,2,32,2048]{4,3,0,1,2:T(8,128)(2,1)}, u32[]{:S(2)}, u32[]{:S(2)}) collective-permute-start(bf16[2,2,2,32,2048]{4,3,0,1,2:T(8,128)(2,1)} %bitcast.531), channel_id=1, source_target_pairs={{0,8},{2,10},{4,12},{6,14},{8,0},{10,2},{12,4},{14,6},{16,24},{18,... | collective-permute-start | bytes 3145736 | tf_op jit(solution)/shard_map/ppermute | solution.py:456
  369.1 19.3 %collective-permute-start.3 = (bf16[2,2,48,2048]{3,2,0,1:T(8,128)(2,1)S(1)}, bf16[2,2,48,2048]{3,2,0,1:T(8,128)(2,1)S(1)}, u32[]{:S(2)}, u32[]{:S(2)}) collective-permute-start(bf16[2,2,48,2048]{3,2,0,1:T(8,128)(2,1)S(1)} %dynamic-slice_bitcast_fusion.3), channel_id=1, source_target_pairs={{0,4},{2,6},{4,0},{6,2},{8,12},{10,14},{12,8},{14,10},{16,20},{18,... | collective-permute-start | bytes 2359304 | tf_op jit(solution)/shard_map/ppermute | solution.py:456
  371.9 16.6 %collective-permute-start.4 = (bf16[2,2,48,2048]{3,2,0,1:T(8,128)(2,1)S(1)}, bf16[2,2,48,2048]{3,2,0,1:T(8,128)(2,1)S(1)}, u32[]{:S(2)}, u32[]{:S(2)}) collective-permute-start(bf16[2,2,48,2048]{3,2,0,1:T(8,128)(2,1)S(1)} %dynamic-slice_bitcast_fusion.2), channel_id=1, source_target_pairs={{0,8},{2,10},{4,12},{6,14},{8,0},{10,2},{12,4},{14,6},{16,24},{18,... | collective-permute-start | bytes 2359304 | tf_op jit(solution)/shard_map/ppermute | solution.py:456
  375.4 13.1 %collective-permute-start.5 = (bf16[2,2,32,2048]{3,2,0,1:T(8,128)(2,1)S(1)}, bf16[2,2,32,2048]{3,2,0,1:T(8,128)(2,1)S(1)}, u32[]{:S(2)}, u32[]{:S(2)}) collective-permute-start(bf16[2,2,32,2048]{3,2,0,1:T(8,128)(2,1)S(1)} %dynamic-slice_bitcast_fusion.5), channel_id=1, source_target_pairs={{0,2},{2,0},{4,6},{6,4},{8,10},{10,8},{12,14},{14,12},{16,18},{18,... | collective-permute-start | bytes 1572872 | tf_op jit(solution)/shard_map/ppermute | solution.py:456
  388.8 28.6 %collective-permute-start.6 = (bf16[2,48,2048]{2,1,0:T(8,128)(2,1)S(1)}, bf16[2,48,2048]{2,1,0:T(8,128)(2,1)S(1)}, u32[]{:S(2)}, u32[]{:S(2)}) collective-permute-start(bf16[2,48,2048]{2,1,0:T(8,128)(2,1)S(1)} %dynamic-slice_bitcast_fusion.9), channel_id=1, source_target_pairs={{0,8},{2,10},{4,12},{6,14},{8,0},{10,2},{12,4},{14,6},{16,24},{18,... | collective-permute-start | bytes 1179656 | tf_op jit(solution)/shard_map/ppermute | solution.py:456
  391.7 25.7 %collective-permute-start.7 = (bf16[2,48,2048]{2,1,0:T(8,128)(2,1)S(1)}, bf16[2,48,2048]{2,1,0:T(8,128)(2,1)S(1)}, u32[]{:S(2)}, u32[]{:S(2)}) collective-permute-start(bf16[2,48,2048]{2,1,0:T(8,128)(2,1)S(1)} %dynamic-slice_bitcast_fusion.8), channel_id=1, source_target_pairs={{0,2},{2,0},{4,6},{6,4},{8,10},{10,8},{12,14},{14,12},{16,18},{18,... | collective-permute-start | bytes 1179656 | tf_op jit(solution)/shard_map/ppermute | solution.py:456
  392.1 25.3 %collective-permute-start.8 = (bf16[2,32,2048]{2,1,0:T(8,128)(2,1)S(1)}, bf16[2,32,2048]{2,1,0:T(8,128)(2,1)S(1)}, u32[]{:S(2)}, u32[]{:S(2)}) collective-permute-start(bf16[2,32,2048]{2,1,0:T(8,128)(2,1)S(1)} %dynamic-slice_bitcast_fusion.13), channel_id=1, source_target_pairs={{0,4},{2,6},{4,0},{6,2},{8,12},{10,14},{12,8},{14,10},{16,20},{18,... | collective-permute-start | bytes 786440 | tf_op jit(solution)/shard_map/ppermute | solution.py:456
  418.9 38.7 %collective-permute-start.9 = (bf16[48,2048]{1,0:T(8,128)(2,1)S(1)}, bf16[48,2048]{1,0:T(8,128)(2,1)S(1)}, u32[]{:S(2)}, u32[]{:S(2)}) collective-permute-start(bf16[48,2048]{1,0:T(8,128)(2,1)S(1)} %dynamic-slice_bitcast_fusion.17), channel_id=1, source_target_pairs={{0,16},{2,18},{4,20},{6,22},{8,24},{10,26},{12,28},{14,30},{16,0},... | collective-permute-start | bytes 589832 | tf_op jit(solution)/shard_map/ppermute | solution.py:456
  425.4 32.2 %collective-permute-start.10 = (bf16[48,2048]{1,0:T(8,128)(2,1)S(1)}, bf16[48,2048]{1,0:T(8,128)(2,1)S(1)}, u32[]{:S(2)}, u32[]{:S(2)}) collective-permute-start(bf16[48,2048]{1,0:T(8,128)(2,1)S(1)} %dynamic-slice_bitcast_fusion.16), channel_id=1, source_target_pairs={{0,16},{2,18},{4,20},{6,22},{8,24},{10,26},{12,28},{14,30},{16,0},... | collective-permute-start | bytes 589832 | tf_op jit(solution)/shard_map/ppermute | solution.py:456
  425.6 20.0 %collective-permute-start.11 = (bf16[32,2048]{1,0:T(8,128)(2,1)S(1)}, bf16[32,2048]{1,0:T(8,128)(2,1)S(1)}, u32[]{:S(2)}, u32[]{:S(2)}) collective-permute-start(bf16[32,2048]{1,0:T(8,128)(2,1)S(1)} %dynamic-slice_bitcast_fusion.21), channel_id=1, source_target_pairs={{0,16},{2,18},{4,20},{6,22},{8,24},{10,26},{12,28},{14,30},{16,0},... | collective-permute-start | bytes 393224 | tf_op jit(solution)/shard_map/ppermute | solution.py:456
  428.9 40.7 %collective-permute-start.12 = (bf16[2,2,2,48,2048]{4,3,0,1,2:T(8,128)(2,1)S(1)}, bf16[2,2,2,48,2048]{4,3,0,1,2:T(8,128)(2,1)S(1)}, u32[]{:S(2)}, u32[]{:S(2)}) collective-permute-start(bf16[2,2,2,48,2048]{4,3,0,1,2:T(8,128)(2,1)S(1)} %bitcast.628), channel_id=1, source_target_pairs={{0,2},{2,0},{4,6},{6,4},{8,10},{10,8},{12,14},{14,12},{16,18},{18,... | collective-permute-start | bytes 4718600 | tf_op jit(solution)/shard_map/ppermute | solution.py:456
  430.7 38.8 %collective-permute-start.13 = (bf16[2,2,2,48,2048]{4,3,0,2,1:T(8,128)(2,1)S(1)}, bf16[2,2,2,48,2048]{4,3,0,2,1:T(8,128)(2,1)S(1)}, u32[]{:S(2)}, u32[]{:S(2)}) collective-permute-start(bf16[2,2,2,48,2048]{4,3,0,2,1:T(8,128)(2,1)S(1)} %bitcast.629), channel_id=1, source_target_pairs={{0,4},{2,6},{4,0},{6,2},{8,12},{10,14},{12,8},{14,10},{16,20},{18,... | collective-permute-start | bytes 4718600 | tf_op jit(solution)/shard_map/ppermute | solution.py:456
  445.5 24.1 %collective-permute-start.14 = (bf16[2,2,2,32,2048]{4,3,0,1,2:T(8,128)(2,1)S(1)}, bf16[2,2,2,32,2048]{4,3,0,1,2:T(8,128)(2,1)S(1)}, u32[]{:S(2)}, u32[]{:S(2)}) collective-permute-start(bf16[2,2,2,32,2048]{4,3,0,1,2:T(8,128)(2,1)S(1)} %bitcast.630), channel_id=1, source_target_pairs={{0,8},{2,10},{4,12},{6,14},{8,0},{10,2},{12,4},{14,6},{16,24},{18,... | collective-permute-start | bytes 3145736 | tf_op jit(solution)/shard_map/ppermute | solution.py:456
  457.6 50.4 %copy-start.24 = (bf16[1024,2048]{1,0:T(8,128)(2,1)}, bf16[1024,2048]{1,0:T(8,128)(2,1)S(1)}, u32[]{:S(2)}) copy-start(bf16[1024,2048]{1,0:T(8,128)(2,1)S(1)} %convolution_convert_fusion.3) | copy-start | bytes 12582916
  470.3 18.5 %collective-permute-start.15 = (bf16[2,2,48,2048]{3,2,0,1:T(8,128)(2,1)S(1)}, bf16[2,2,48,2048]{3,2,0,1:T(8,128)(2,1)S(1)}, u32[]{:S(2)}, u32[]{:S(2)}) collective-permute-start(bf16[2,2,48,2048]{3,2,0,1:T(8,128)(2,1)S(1)} %dynamic-slice_bitcast_fusion.1), channel_id=1, source_target_pairs={{0,4},{2,6},{4,0},{6,2},{8,12},{10,14},{12,8},{14,10},{16,20},{18,... | collective-permute-start | bytes 2359304 | tf_op jit(solution)/shard_map/ppermute | solution.py:456
  472.8 17.4 %collective-permute-start.16 = (bf16[2,2,48,2048]{3,2,0,1:T(8,128)(2,1)S(1)}, bf16[2,2,48,2048]{3,2,0,1:T(8,128)(2,1)S(1)}, u32[]{:S(2)}, u32[]{:S(2)}) collective-permute-start(bf16[2,2,48,2048]{3,2,0,1:T(8,128)(2,1)S(1)} %dynamic-slice_bitcast_fusion), channel_id=1, source_target_pairs={{0,8},{2,10},{4,12},{6,14},{8,0},{10,2},{12,4},{14,6},{16,24},{18,... | collective-permute-start | bytes 2359304 | tf_op jit(solution)/shard_map/ppermute | solution.py:456
  474.3 14.5 %collective-permute-start.17 = (bf16[2,2,32,2048]{3,2,0,1:T(8,128)(2,1)S(1)}, bf16[2,2,32,2048]{3,2,0,1:T(8,128)(2,1)S(1)}, u32[]{:S(2)}, u32[]{:S(2)}) collective-permute-start(bf16[2,2,32,2048]{3,2,0,1:T(8,128)(2,1)S(1)} %dynamic-slice_bitcast_fusion.4), channel_id=1, source_target_pairs={{0,2},{2,0},{4,6},{6,4},{8,10},{10,8},{12,14},{14,12},{16,18},{18,... | collective-permute-start | bytes 1572872 | tf_op jit(solution)/shard_map/ppermute | solution.py:456
  490.6 9.6 %collective-permute-start.18 = (bf16[2,48,2048]{2,1,0:T(8,128)(2,1)S(1)}, bf16[2,48,2048]{2,1,0:T(8,128)(2,1)S(1)}, u32[]{:S(2)}, u32[]{:S(2)}) collective-permute-start(bf16[2,48,2048]{2,1,0:T(8,128)(2,1)S(1)} %dynamic-slice_bitcast_fusion.7), channel_id=1, source_target_pairs={{0,8},{2,10},{4,12},{6,14},{8,0},{10,2},{12,4},{14,6},{16,24},{18,... | collective-permute-start | bytes 1179656 | tf_op jit(solution)/shard_map/ppermute | solution.py:456
  492.6 8.5 %collective-permute-start.19 = (bf16[2,48,2048]{2,1,0:T(8,128)(2,1)S(1)}, bf16[2,48,2048]{2,1,0:T(8,128)(2,1)S(1)}, u32[]{:S(2)}, u32[]{:S(2)}) collective-permute-start(bf16[2,48,2048]{2,1,0:T(8,128)(2,1)S(1)} %dynamic-slice_bitcast_fusion.6), channel_id=1, source_target_pairs={{0,2},{2,0},{4,6},{6,4},{8,10},{10,8},{12,14},{14,12},{16,18},{18,... | collective-permute-start | bytes 1179656 | tf_op jit(solution)/shard_map/ppermute | solution.py:456
  493.7 6.4 collective-permute-start.20
  501.3 23.3 %collective-permute-start.21 = (bf16[48,2048]{1,0:T(8,128)(2,1)S(1)}, bf16[48,2048]{1,0:T(8,128)(2,1)S(1)}, u32[]{:S(2)}, u32[]{:S(2)}) collective-permute-start(bf16[48,2048]{1,0:T(8,128)(2,1)S(1)} %dynamic-slice_bitcast_fusion.15), channel_id=1, source_target_pairs={{0,16},{2,18},{4,20},{6,22},{8,24},{10,26},{12,28},{14,30},{16,0},... | collective-permute-start | bytes 589832 | tf_op jit(solution)/shard_map/ppermute | solution.py:456
  504.8 19.8 %collective-permute-start.22 = (bf16[48,2048]{1,0:T(8,128)(2,1)S(1)}, bf16[48,2048]{1,0:T(8,128)(2,1)S(1)}, u32[]{:S(2)}, u32[]{:S(2)}) collective-permute-start(bf16[48,2048]{1,0:T(8,128)(2,1)S(1)} %dynamic-slice_bitcast_fusion.14), channel_id=1, source_target_pairs={{0,16},{2,18},{4,20},{6,22},{8,24},{10,26},{12,28},{14,30},{16,0},... | collective-permute-start | bytes 589832 | tf_op jit(solution)/shard_map/ppermute | solution.py:456
  505.0 19.6 %collective-permute-start.23 = (bf16[32,2048]{1,0:T(8,128)(2,1)S(1)}, bf16[32,2048]{1,0:T(8,128)(2,1)S(1)}, u32[]{:S(2)}, u32[]{:S(2)}) collective-permute-start(bf16[32,2048]{1,0:T(8,128)(2,1)S(1)} %dynamic-slice_bitcast_fusion.20), channel_id=1, source_target_pairs={{0,16},{2,18},{4,20},{6,22},{8,24},{10,26},{12,28},{14,30},{16,0},... | collective-permute-start | bytes 393224 | tf_op jit(solution)/shard_map/ppermute | solution.py:456
  514.4 10.4 %copy-start.7 = (f32[128,2048]{1,0:T(8,128)S(1)}, f32[128,2048]{1,0:T(8,128)}, u32[]{:S(2)}) copy-start(f32[128,2048]{1,0:T(8,128)} %copy-done.6) | copy-start | bytes 3145732
  514.4 10.4 %copy-start.45 = (f32[2048]{0:T(1024)S(1)}, f32[2048]{0:T(1024)}, u32[]{:S(2)}) copy-start(f32[2048]{0:T(1024)} %param.35) | copy-start | bytes 24580
  514.4 10.4 %copy-start.51 = (f32[128]{0:T(128)S(1)}, f32[128]{0:T(128)}, u32[]{:S(2)}) copy-start(f32[128]{0:T(128)} %copy-done.50) | copy-start | bytes 1540
  514.4 10.6 %copy-start.56 = (f32[128]{0:T(128)S(1)}, f32[128]{0:T(128)}, u32[]{:S(2)}) copy-start(f32[128]{0:T(128)} %copy-done.55) | copy-start | bytes 1540
  514.4 10.6 %copy-start.28 = (bf16[1,128,2048]{2,1,0:T(8,128)(2,1)S(1)}, bf16[1,128,2048]{2,1,0:T(8,128)(2,1)}, u32[]{:S(2)}) copy-start(bf16[1,128,2048]{2,1,0:T(8,128)(2,1)} %param.57) | copy-start | bytes 1572868
  529.9 17.3 %collective-permute-start.24 = (bf16[16,128,1024]{2,1,0:T(8,128)(2,1)}, bf16[16,128,1024]{2,1,0:T(8,128)(2,1)}, u32[]{:S(2)}, u32[]{:S(2)}) collective-permute-start(bf16[16,128,1024]{2,1,0:T(8,128)(2,1)} %bitcast.93), channel_id=1, source_target_pairs={{0,1},{1,0},{2,3},{3,2},{4,5},{5,4},{6,7},{7,6},{8,9},{9,8},{10,11... | collective-permute-start | bytes 12582920 | tf_op jit(solution)/shard_map/ppermute | solution.py:786
  532.5 14.0 %collective-permute-start.26 = (bf16[16,48,1024]{2,1,0:T(8,128)(2,1)S(1)}, bf16[16,48,1024]{2,1,0:T(8,128)(2,1)S(1)}, u32[]{:S(2)}, u32[]{:S(2)}) collective-permute-start(bf16[16,48,1024]{2,1,0:T(8,128)(2,1)S(1)} %constant_dynamic-slice_fusion.4), channel_id=1, source_target_pairs={{0,1},{1,0},{2,3},{3,2},{4,5},{5,4},{6,7},{7,6},{8,9},{9,8},{10,11... | collective-permute-start | bytes 4718600 | tf_op jit(solution)/shard_map/ppermute | solution.py:786
  534.6 39.1 %collective-permute-start.29 = (bf16[1024,2048]{1,0:T(8,128)(2,1)}, bf16[1024,2048]{1,0:T(8,128)(2,1)}, u32[]{:S(2)}, u32[]{:S(2)}) collective-permute-start(bf16[1024,2048]{1,0:T(8,128)(2,1)} %convolution_convert_fusion.4), channel_id=1, source_target_pairs={{0,1},{1,0},{2,3},{3,2},{4,5},{5,4},{6,7},{7,6},{8,9},{9,8},{10,11... | collective-permute-start | bytes 12582920 | tf_op jit(solution)/shard_map/ppermute | solution.py:751
  535.0 11.3 %collective-permute-start.25 = (bf16[16,16,1024]{2,1,0:T(8,128)(2,1)S(1)}, bf16[16,16,1024]{2,1,0:T(8,128)(2,1)S(1)}, u32[]{:S(2)}, u32[]{:S(2)}) collective-permute-start(bf16[16,16,1024]{2,1,0:T(8,128)(2,1)S(1)} %bitcast.634), channel_id=1, source_target_pairs={{0,1},{1,0},{2,3},{3,2},{4,5},{5,4},{6,7},{7,6},{8,9},{9,8},{10,11... | collective-permute-start | bytes 1572872 | tf_op jit(solution)/shard_map/ppermute | solution.py:786
  571.4 14.2 %collective-permute-start.27 = (bf16[2,2,2,64,512]{4,3,0,1,2:T(8,128)(2,1)S(1)}, bf16[2,2,2,64,512]{4,3,0,1,2:T(8,128)(2,1)S(1)}, u32[]{:S(2)}, u32[]{:S(2)}) collective-permute-start(bf16[2,2,2,64,512]{4,3,0,1,2:T(8,128)(2,1)S(1)} %bitcast.632), channel_id=1, source_target_pairs={{0,2},{2,0},{4,6},{6,4},{8,10},{10,8},{12,14},{14,12},{16,18},{18,... | collective-permute-start | bytes 1572872 | tf_op jit(solution)/shard_map/ppermute | solution.py:456
  573.5 13.8 %copy-start.25 = (bf16[1024,2048]{1,0:T(8,128)(2,1)S(1)}, bf16[1024,2048]{1,0:T(8,128)(2,1)}, u32[]{:S(2)}) copy-start(bf16[1024,2048]{1,0:T(8,128)(2,1)} %copy-done.24) | copy-start | bytes 12582916
  573.5 13.8 %collective-permute-start.28 = (bf16[2,2,2,64,512]{4,3,0,2,1:T(8,128)(2,1)S(1)}, bf16[2,2,2,64,512]{4,3,0,2,1:T(8,128)(2,1)S(1)}, u32[]{:S(2)}, u32[]{:S(2)}) collective-permute-start(bf16[2,2,2,64,512]{4,3,0,2,1:T(8,128)(2,1)S(1)} %bitcast.633), channel_id=1, source_target_pairs={{0,4},{2,6},{4,0},{6,2},{8,12},{10,14},{12,8},{14,10},{16,20},{18,... | collective-permute-start | bytes 1572872 | tf_op jit(solution)/shard_map/ppermute | solution.py:456
  587.3 8.6 %collective-permute-start.32 = (bf16[1024,2048]{1,0:T(8,128)(2,1)S(1)}, bf16[1024,2048]{1,0:T(8,128)(2,1)S(1)}, u32[]{:S(2)}, u32[]{:S(2)}) collective-permute-start(bf16[1024,2048]{1,0:T(8,128)(2,1)S(1)} %copy-done.25), channel_id=1, source_target_pairs={{0,1},{1,0},{2,3},{3,2},{4,5},{5,4},{6,7},{7,6},{8,9},{9,8},{10,11... | collective-permute-start | bytes 12582920 | tf_op jit(solution)/shard_map/ppermute | solution.py:751
  587.5 13.8 %collective-permute-start.30 = (bf16[2,2,64,512]{3,2,0,1:T(8,128)(2,1)S(1)}, bf16[2,2,64,512]{3,2,0,1:T(8,128)(2,1)S(1)}, u32[]{:S(2)}, u32[]{:S(2)}) collective-permute-start(bf16[2,2,64,512]{3,2,0,1:T(8,128)(2,1)S(1)} %dynamic-slice_bitcast_fusion.11), channel_id=1, source_target_pairs={{0,4},{2,6},{4,0},{6,2},{8,12},{10,14},{12,8},{14,10},{16,20},{18,... | collective-permute-start | bytes 786440 | tf_op jit(solution)/shard_map/ppermute | solution.py:456
  588.1 14.6 %collective-permute-start.31 = (bf16[2,2,64,512]{3,2,0,1:T(8,128)(2,1)S(1)}, bf16[2,2,64,512]{3,2,0,1:T(8,128)(2,1)S(1)}, u32[]{:S(2)}, u32[]{:S(2)}) collective-permute-start(bf16[2,2,64,512]{3,2,0,1:T(8,128)(2,1)S(1)} %dynamic-slice_bitcast_fusion.10), channel_id=1, source_target_pairs={{0,8},{2,10},{4,12},{6,14},{8,0},{10,2},{12,4},{14,6},{16,24},{18,... | collective-permute-start | bytes 786440 | tf_op jit(solution)/shard_map/ppermute | solution.py:456
  602.6 15.1 %collective-permute-start.35 = (bf16[1024,2048]{1,0:T(8,128)(2,1)}, bf16[1024,2048]{1,0:T(8,128)(2,1)}, u32[]{:S(2)}, u32[]{:S(2)}) collective-permute-start(bf16[1024,2048]{1,0:T(8,128)(2,1)} %convolution_convert_fusion.2), channel_id=1, source_target_pairs={{0,1},{1,0},{2,3},{3,2},{4,5},{5,4},{6,7},{7,6},{8,9},{9,8},{10,11... | collective-permute-start | bytes 12582920 | tf_op jit(solution)/shard_map/ppermute | solution.py:751
  610.0 13.1 %collective-permute-start.33 = (bf16[2,64,512]{2,1,0:T(8,128)(2,1)S(1)}, bf16[2,64,512]{2,1,0:T(8,128)(2,1)S(1)}, u32[]{:S(2)}, u32[]{:S(2)}) collective-permute-start(bf16[2,64,512]{2,1,0:T(8,128)(2,1)S(1)} %dynamic-slice_bitcast_fusion.19), channel_id=1, source_target_pairs={{0,8},{2,10},{4,12},{6,14},{8,0},{10,2},{12,4},{14,6},{16,24},{18,... | collective-permute-start | bytes 393224 | tf_op jit(solution)/shard_map/ppermute | solution.py:456
  615.9 17.1 %copy-start.3 = (bf16[1,128,2048]{2,1,0:T(8,128)(2,1)S(1)}, bf16[1,128,2048]{2,1,0:T(8,128)(2,1)}, u32[]{:S(2)}) copy-start(bf16[1,128,2048]{2,1,0:T(8,128)(2,1)} %param.32) | copy-start | bytes 1572868
  615.9 17.1 %copy-start.32 = (f32[2048]{0:T(1024)S(1)}, f32[2048]{0:T(1024)}, u32[]{:S(2)}) copy-start(f32[2048]{0:T(1024)} %param.34) | copy-start | bytes 24580
  615.9 17.1 %copy-start.47 = (f32[128]{0:T(128)S(1)}, f32[128]{0:T(128)}, u32[]{:S(2)}) copy-start(f32[128]{0:T(128)} %copy-done.46) | copy-start | bytes 1540
  615.9 7.2 collective-permute-start.34
  623.1 21.7 %copy-start.1 = (f32[1024,2048]{1,0:T(8,128)}, f32[1024,2048]{1,0:T(8,128)S(1)}, u32[]{:S(2)}) copy-start(f32[1024,2048]{1,0:T(8,128)S(1)} %convert_add_fusion) | copy-start | bytes 25165828
  623.2 32.8 %collective-permute-start.36 = (bf16[64,512]{1,0:T(8,128)(2,1)S(1)}, bf16[64,512]{1,0:T(8,128)(2,1)}, u32[]{:S(2)}, u32[]{:S(2)}) collective-permute-start(bf16[64,512]{1,0:T(8,128)(2,1)S(1)} %dynamic-slice_bitcast_fusion.23), channel_id=1, source_target_pairs={{0,16},{2,18},{4,20},{6,22},{8,24},{10,26},{12,28},{14,30},{16,0},... | collective-permute-start | bytes 196616 | tf_op jit(solution)/shard_map/ppermute | solution.py:456
  632.7 23.3 %collective-permute-start.37 = (bf16[64,512]{1,0:T(8,128)(2,1)}, bf16[64,512]{1,0:T(8,128)(2,1)}, u32[]{:S(2)}, u32[]{:S(2)}) collective-permute-start(bf16[64,512]{1,0:T(8,128)(2,1)} %dynamic-slice_bitcast_fusion.22), channel_id=1, source_target_pairs={{0,16},{2,18},{4,20},{6,22},{8,24},{10,26},{12,28},{14,30},{16,0},... | collective-permute-start | bytes 196616 | tf_op jit(solution)/shard_map/ppermute | solution.py:456
  782.5 10.9 %copy-start.22 = (bf16[256,2048]{1,0:T(8,128)(2,1)S(1)}, bf16[256,2048]{1,0:T(8,128)(2,1)}, u32[]{:S(2)}) copy-start(bf16[256,2048]{1,0:T(8,128)(2,1)} %param.50) | copy-start | bytes 3145732
  787.8 3.3 collective-permute-start.38
  (45 other events, 202.9 us)
Sparse Core Ops, SparseCore 0:
  102.9 146.3 all-gather.1
  602.9 184.8 reduce-scatter.1

commit v5 on v4

--- a/solution.py
+++ b/solution.py
@@ -263,7 +263,7 @@
         target[part] = total.astype(target.dtype)
 
 
-def scatter_kernel(terms_ref, out_ref, *refs):
+def scatter_kernel(first_ref, second_ref, out_ref, *refs):
     held, c_buf, a_buf, b_buf, z_buf = refs[:5]
     h_sem, c_send, c_recv, a_send, a_recv, b_send, b_recv, z_send, z_recv, o_send, o_recv = refs[5:]
     f, z, y, x, fx, fy, visits = place_of()
@@ -273,14 +273,23 @@
     base = pl.multiple_of(core * rows, 16)
     away = pl.multiple_of((1 - core) * rows, 16)
     part = rows // 2
+    middle = first_ref.shape[1] // 2
+    inputs = ((first_ref, 0, middle), (second_ref, middle, rows - middle))
+
+    def input_rows(i, k, which):
+        ref, _, count = inputs[i]
+        return ref.at[pl.ds(visits[k] * 4, 4), pl.ds(pl.multiple_of(which * count, 16), count)]
+
+    def came(i, k):
+        return c_buf.at[k, pl.ds(0, 4), pl.ds(inputs[i][1], inputs[i][2])]
+
     loads = []
     for k in range(LINE):
-        four = pl.ds(visits[k] * 4, 4)
-        copy = pltpu.make_async_copy(
-            terms_ref.at[four, pl.ds(base, rows)], held.at[four], h_sem.at[k]
-        )
-        copy.start()
-        loads.append(copy)
+        for i in range(2):
+            target = held.at[pl.ds(visits[k] * 4, 4), pl.ds(inputs[i][1], inputs[i][2])]
+            copy = pltpu.make_async_copy(input_rows(i, k, core), target, h_sem.at[k, i])
+            copy.start()
+            loads.append(copy)
     greet(f, z, fx, fy, True)
 
     def spots(p, v):
@@ -294,12 +303,21 @@
     sent = []
     near = ((fx, fy), (fy, fx))
     for k in range(LINE):
-        source = terms_ref.at[pl.ds(visits[k] * 4, 4), pl.ds(away, rows)]
-        sent.append(send(source, c_buf.at[k], c_send.at[k], c_recv.at[k], {"dp": 1 - core}))
+        for i in range(2):
+            sent.append(
+                send(
+                    input_rows(i, k, 1 - core),
+                    came(i, k),
+                    c_send.at[k, i],
+                    c_recv.at[k, i],
+                    {"dp": 1 - core},
+                )
+            )
 
     def start_a(k):
-        loads[k].wait()
-        arrived(c_buf.at[k], c_recv.at[k])
+        for i in range(2):
+            loads[2 * k + i].wait()
+            arrived(came(i, k), c_recv.at[k, i])
         for j in range(4):
             add_rows(held.at[visits[k] * 4 + j], c_buf.at[k, j])
         for j in range(2):
@@ -395,15 +413,17 @@
             pltpu.make_async_copy(b_buf.at[p, k], b_buf.at[p, k], z_send.at[p, k]).wait()
 
 
-def scatter_blocks(terms, number):
-    shards, rows, columns = terms.shape
+def scatter_blocks(first, second, number):
+    shards, columns = first.shape[0], first.shape[2]
+    rows = first.shape[1] + second.shape[1]
+    terms = first
     dma = pltpu.SemaphoreType.DMA
     own = rows // 2
     part = own // 2
-    return pl.pallas_call(
+    sums = pl.pallas_call(
         scatter_kernel,
         out_shape=jax.ShapeDtypeStruct((rows, columns), terms.dtype),
-        in_specs=[pl.BlockSpec(memory_space=pl.ANY)],
+        in_specs=[pl.BlockSpec(memory_space=pl.ANY)] * 2,
         out_specs=pl.BlockSpec(memory_space=pltpu.VMEM),
         scratch_shapes=[
             pltpu.VMEM((shards, own, columns), terms.dtype),
@@ -411,9 +431,9 @@
             pltpu.VMEM((2, LINE, 2, part, columns), terms.dtype),
             pltpu.VMEM((2, LINE, part, columns), terms.dtype),
             pltpu.VMEM((2, LINE + 1, part, columns), terms.dtype),
-            dma((LINE,)),
-            dma((LINE,)),
-            dma((LINE,)),
+            dma((LINE, 2)),
+            dma((LINE, 2)),
+            dma((LINE, 2)),
             dma((2, LINE, 2)),
             dma((2, LINE, 2)),
             dma((2, LINE)),
@@ -427,7 +447,10 @@
             collective_id=number, has_side_effects=True, vmem_limit_bytes=40 * 1024 * 1024
         ),
         name="scatter_blocks_%d" % number,
-    )(terms)
+    )(first, second)
+    sums = sums.reshape(2, own, columns)
+    middle = first.shape[1] // 2
+    return sums[:, :middle].reshape(-1, columns), sums[:, middle:].reshape(-1, columns)
 
 
 class HalvingSum:
@@ -617,7 +640,8 @@
         shards,
     )
     cot_own, key_value_weight = lax.optimization_barrier((cotangent[0], key_value_weight))
-    cot_all = lax.all_gather(cot_own, "fsdp", axis=0, tiled=True)
+    columns = width // 2
+    cot_first = lax.all_gather(cot_own[:, :columns], "fsdp", axis=0, tiled=True)
 
     normed_attn, pull_attn = jax.vjp(rms_norm, input_rows, gain_attn)
     attn_in = normed_attn.astype(bf16)
@@ -677,6 +701,9 @@
     normed_mlp, pull_mlp = jax.vjp(rms_norm, resid, gain_mlp)
     mlp_in = normed_mlp.astype(bf16)
     mlp_all = gather_rows(mlp_in, shards, 2)
+    mlp_all, cot_rest = lax.optimization_barrier((mlp_all, cot_own[:, columns:]))
+    cot_second = lax.all_gather(cot_rest, "fsdp", axis=0, tiled=True)
+    cot_all = jnp.concatenate([cot_first, cot_second], axis=1)
 
     first_unit = place * unit_rows
     gate_second = lax.dynamic_slice_in_dim(gate_factor_second, first_unit, unit_rows, 1)
@@ -697,15 +724,15 @@
 
     gate = right_product(mlp_all, gate_weight)
     up = right_product(mlp_all, up_weight)
-    hidden_full, pull_geglu = jax.vjp(geglu, gate, up)
-    hidden = hidden_full.astype(bf16)
+    hidden = geglu(gate, up).astype(bf16)
     edges = row_edges(tok_rows)
-    down_product, hidden, cot_late = lax.optimization_barrier(
-        (matrix_product(hidden, down_weight).astype(bf16), hidden, cot_all)
+    down_product, hidden, gate, up = lax.optimization_barrier(
+        (matrix_product(hidden, down_weight).astype(bf16), hidden, gate, up)
     )
     down_terms = HalvingSum(down_product, place, shards, edges)
     down_terms.start()
-    grad_hidden = right_product(cot_late, down_weight)
+    pull_geglu = jax.vjp(geglu, gate, up)[1]
+    grad_hidden = right_product(cot_all, down_weight)
     grad_gate_full, grad_up_full = pull_geglu(grad_hidden)
     grad_gate, grad_up = together(
         [down_terms], (grad_gate_full.astype(bf16), grad_up_full.astype(bf16))
@@ -768,8 +795,6 @@
     lora_query = matrix_product(attn_in, query_factor_first).astype(bf16)
     lora_key = matrix_product(attn_in, key_factor_first).astype(bf16)
     lora_value = matrix_product(attn_in, value_factor_first).astype(bf16)
-    columns = width // 2
-
     def half_of(values, which):
         return lax.dynamic_slice_in_dim(values, which * columns, columns, values.ndim - 1)
 
@@ -881,13 +906,13 @@
         ],
         axis=1,
     )
-    late = jnp.concatenate([query_terms.reshape(shards, per, width), late], axis=1)
+    query_terms = query_terms.reshape(shards, per, width)
     if shards == 4 * LINE:
-        late_sums = scatter_blocks(late, 4).astype(f32)
+        g_query_weight, late_sums = scatter_blocks(query_terms, late, 4)
     else:
-        late_sums = scatter_shared(late, core).astype(f32)
-    g_query_weight = late_sums[:per]
-    late_sums = late_sums[per:]
+        late_sums = scatter_shared(jnp.concatenate([query_terms, late], axis=1), core)
+        g_query_weight, late_sums = late_sums[:per], late_sums[per:]
+    g_query_weight, late_sums = g_query_weight.astype(f32), late_sums.astype(f32)
     g_query_out = late_sums[:few]
     pair = unpack_rows(late_sums[few : late_sums.shape[0] - few], 2 * head_size)
     g_key_weight = pair[:, :head_size]

time: 815 us -> 793 us (0.973); the launches traced: 802 us -> 792 us
  Pallas kernels: 317 us -> 293 us
  local copies, waits for them, and re-layouts: 49.5 us -> 69.5 us
    pallas_call x3, Pallas kernels: 222 us -> 197 us  [gather_blocks(): pl.pallas_call(functools.partial(gather_kernel, pieces, len(arrays), with...]
    unnamed x159 -> x180, local copies, waits for them, and re-layouts: 15.9 us -> 26.2 us
  transfers between devices with their start and end apart: 41 -> 42, of which waited for: 13 -> 15; matrix products, arithmetic and copies ran while one was open for 41% -> 42% of each run, Pallas kernels for 29% -> 26%
where the time goes in v5:
time: 793 us; the launch traced here: 792 us
  Pallas kernels  293 us (37%)
  matrix products  227 us (29%)
  other arithmetic  71.2 us (9%)
  starting transfers between devices  71.1 us (9%)
  local copies, waits for them, and re-layouts  69.5 us (9%)
  waiting for transfers between devices  43.8 us (6%)
  between operations  16.1 us (2%)
    pallas_call x3, Pallas kernels, gather_blocks(): pl.pallas_call(functools.partial(gather_kernel, pieces, len(arrays), with...  197 us
    pallas_call x1, Pallas kernels, scatter_blocks(): pl.pallas_call(scatter_kernel, out_shape=jax.ShapeDtypeStruct((rows, colu...  96 us
    dot_general x11, matrix products, right_product(): lax.dot_general(left, right, (((1,), (1,)), ((), ())), preferred_element_...  72 us
    ppermute x32, starting transfers between devices, start(): self.came.append(lax.ppermute(away, 'fsdp', pairs))  69.3 us
    dot_general x12, matrix products, matrix_product(): return jnp.dot(left, right, preferred_element_type=jnp.float32)  63.5 us
    dot_general x13, matrix products, left_matrix_product(): lax.dot_general(left, right, (((0,), (0,)), ((), ())), preferred_element_...  57.1 us
    ppermute x32, waiting for transfers between devices, start(): self.came.append(lax.ppermute(away, 'fsdp', pairs))  35 us
    unnamed x180, local copies, waits for them, and re-layouts  26.2 us
  transfers between devices with their start and end apart: 42, of which 15 were waited for; matrix products, arithmetic and copies ran while one was open for 42% of the time, Pallas kernels for 26%

profile of v5, /device:TPU:0, one launch (start us, length us, event | category | flops | bytes accessed | tf_op | source)
XLA Modules:
  0.0 791.8 jit_solution(14664286416979214876)
XLA Ops:
  10.2 2.3 fusion.73.refs_0_
  12.5 2.3 fusion.74.refs_1_
  14.8 88.0 %gather_blocks_1.1 = (bf16[16,2,64,2048]{3,2,1,0:T(8,128)(2,1)}, bf16[16,2,64,2048]{3,2,1,0:T(8,128)(2,1)}, bf16[16,2,64,512]{3,2,1,0:T(8,128)(2,1)}) custom-call(bf16[64,2048]{1,0:T(8,128)(2,1)} %fusion.73.refs_0_, bf16[64,2048]{1,0:T(8,128)(2,1)} %fusion.74.refs_1_, bf16[64,512]{1,0:T(8,128)(2,1)} %pad_maximum_fusion.12.refs_2_), custom_call_target="tpu_custom_call" | custom-call | tf_op jit(solution)/shard_map/gather_blocks_1/pallas_call | solution.py:227
  108.7 31.8 %gather_blocks_3.1 = bf16[16,128,512]{2,1,0:T(8,128)(2,1)} custom-call(bf16[128,512]{1,0:T(8,128)(2,1)} %pad_maximum_fusion.9.refs_0_), custom_call_target="tpu_custom_call" | custom-call | tf_op jit(solution)/shard_map/gather_blocks_3/pallas_call | solution.py:227
  140.5 2.6 fusion.227
  143.2 4.7 fusion.123
  157.5 2.2 while.38
  160.0 5.4 multiply_reduce_fusion.3
  167.3 76.7 %gather_blocks_2.1 = bf16[16,128,2048]{2,1,0:T(8,128)(2,1)} custom-call(bf16[128,2048]{1,0:T(8,128)(2,1)} %multiply_convert_fusion.1.refs_0_), custom_call_target="tpu_custom_call" | custom-call | tf_op jit(solution)/shard_map/gather_blocks_2/pallas_call | solution.py:227
  244.7 3.8 add_convert_fusion.3
  250.5 11.2 %fusion.236 = f32[2048,1024]{1,0:T(8,128)} fusion(bf16[2048,2048]{1,0:T(8,128)(2,1)S(1)} %bitcast.618, bf16[1024,2048]{1,0:T(8,128)(2,1)S(1)} %add_convert_fusion.3), kind=kOutput, calls=%fused_computation.479 | convolution fusion | flops 8589934592 | bytes 20971520 | tf_op jit(solution)/shard_map/dot_general | solution.py:26
  261.7 3.8 add_convert_fusion.2
  265.6 5.0 add_convert_fusion.1
  272.3 15.5 %fusion.62 = (bf16[2048,1024]{1,0:T(8,128)(2,1)}, f32[2048,1024]{1,0:T(8,128)}) fusion(f32[2048,1024]{1,0:T(8,128)} %fusion.236, bf16[2048,2048]{1,0:T(8,128)(2,1)S(1)} %bitcast.619, bf16[1024,2048]{1,0:T(8,128)(2,1)S(1)} %add_convert_fusion.2), kind=kOutput, calls=%fused_computation.82 | convolution fusion | flops 8610906112 | bytes 33554432 | tf_op jit(solution)/shard_map/dot_general | solution.py:26
  287.8 14.1 %convolution_convert_fusion = bf16[2048,2048]{1,0:T(8,128)(2,1)} fusion(bf16[2048,1024]{1,0:T(8,128)(2,1)} %get-tuple-element.307, bf16[1024,2048]{1,0:T(8,128)(2,1)} %add_convert_fusion.1), kind=kOutput, calls=%fused_computation.90 | convolution fusion | flops 8594128896 | bytes 16777216 | tf_op jit(solution)/shard_map/dot_general | solution.py:16
  301.9 5.4 fusion.225
  310.5 3.4 constant_dynamic-slice_fusion.12
  319.8 4.7 constant_dynamic-update-slice_fusion.10
  324.5 4.7 constant_dynamic-update-slice_fusion.9
  329.1 24.8 %multiply_convert_fusion = (bf16[2048,1024]{1,0:T(8,128)(2,1)}, bf16[2048,1024]{1,0:T(8,128)(2,1)}) fusion(f32[2048,1024]{1,0:T(8,128)} %fusion.236, f32[2048,1024]{1,0:T(8,128)} %get-tuple-element.281, bf16[2048,2048]{1,0:T(8,128)(2,1)} %constant_dynamic-update-slice_fusion.9, bf16[1024,2048]{1,0:T(8,128)(2,1)} %add_convert_fusion.1), kind=kOutput, calls=%fused_computation.86 | convolution fusion | flops 8640266240 | bytes 37748736 | tf_op jit(solution)/shard_map/dot_general | solution.py:26
  356.9 2.2 fusion.71
  363.2 11.7 %fusion.237 = f32[2048,2048]{1,0:T(8,128)} fusion(bf16[2048,1024]{1,0:T(8,128)(2,1)S(1)} %copy-done.69, bf16[1024,2048]{1,0:T(8,128)(2,1)S(1)} %copy-done.20), kind=kOutput, calls=%fused_computation.480 | convolution fusion | flops 8589934592 | bytes 25165824 | tf_op jit(solution)/shard_map/dot_general | solution.py:16
  381.5 12.1 %fusion.238 = f32[2048,2048]{1,0:T(8,128)} fusion(bf16[2048,1024]{1,0:T(8,128)(2,1)S(1)} %copy-done.68, bf16[1024,2048]{1,0:T(8,128)(2,1)S(1)} %copy-done.18), kind=kOutput, calls=%fused_computation.481 | convolution fusion | flops 8589934592 | bytes 25165824 | tf_op jit(solution)/shard_map/dot_general | solution.py:16
  393.7 11.5 %add_convert_fusion = bf16[2048,2048]{1,0:T(8,128)(2,1)S(1)} fusion(f32[2048,2048]{1,0:T(8,128)} %fusion.237, f32[2048,2048]{1,0:T(8,128)} %fusion.238), kind=kLoop, calls=%fused_computation.63 | loop fusion | flops 8388608 | bytes 41943040 | tf_op jit(solution)/shard_map/convert_element_type | solution.py:744
  406.6 4.7 collective-permute-start.9
  411.6 3.0 collective-permute-start.11
  418.8 12.4 %convolution_convert_fusion.4 = bf16[1024,2048]{1,0:T(8,128)(2,1)} fusion(bf16[2048,1024]{1,0:T(8,128)(2,1)} %get-tuple-element.298, bf16[2048,2048]{1,0:T(8,128)(2,1)S(1)} %bitcast.622), kind=kOutput, calls=%fused_computation.102 | convolution fusion | flops 8592031744 | bytes 16777216 | tf_op jit(solution)/shard_map/dot_general | solution.py:20
  432.9 11.3 %convolution_convert_fusion.3 = bf16[1024,2048]{1,0:T(8,128)(2,1)S(1)} fusion(bf16[2048,1024]{1,0:T(8,128)(2,1)} %get-tuple-element.299, bf16[2048,2048]{1,0:T(8,128)(2,1)S(1)} %bitcast.623), kind=kOutput, calls=%fused_computation.101 | convolution fusion | flops 8592031744 | bytes 16777216 | tf_op jit(solution)/shard_map/dot_general | solution.py:20
  444.2 12.4 %collective-permute-done.14 = bf16[2,2,2,32,2048]{4,3,0,1,2:T(8,128)(2,1)S(1)} collective-permute-done((bf16[2,2,2,32,2048]{4,3,0,1,2:T(8,128)(2,1)S(1)}, bf16[2,2,2,32,2048]{4,3,0,1,2:T(8,128)(2,1)S(1)}, u32[]{:S(2)}, u32[]{:S(2)}) %collective-permute-start.14) | collective-permute-done | bytes 1048608 | tf_op jit(solution)/shard_map/ppermute | solution.py:479
  462.7 11.0 %convolution_convert_fusion.2 = bf16[1024,2048]{1,0:T(8,128)(2,1)} fusion(bf16[2048,1024]{1,0:T(8,128)(2,1)S(1)} %copy-done.67, bf16[2048,2048]{1,0:T(8,128)(2,1)S(1)} %bitcast.638), kind=kOutput, calls=%fused_computation.100 | convolution fusion | flops 8592031744 | bytes 16777216 | tf_op jit(solution)/shard_map/dot_general | solution.py:20
  475.7 2.3 collective-permute-done.16
  481.8 3.6 convolution_convert_fusion.11
  488.0 3.1 collective-permute-start.21
  491.4 3.0 collective-permute-start.23
  494.4 2.4 convolution_convert_fusion.9
  497.2 3.6 convolution_convert_fusion.10
  500.9 2.3 maximum_maximum_fusion
  503.1 8.3 %collective-permute-done.23 = bf16[32,2048]{1,0:T(8,128)(2,1)S(1)} collective-permute-done((bf16[32,2048]{1,0:T(8,128)(2,1)S(1)}, bf16[32,2048]{1,0:T(8,128)(2,1)S(1)}, u32[]{:S(2)}, u32[]{:S(2)}) %collective-permute-start.23) | collective-permute-done | bytes 131104 | tf_op jit(solution)/shard_map/ppermute | solution.py:479
  513.5 3.3 convolution_convert_fusion.5
  524.0 6.4 convolution_convert_fusion.12
  530.4 2.7 collective-permute-done.25
  534.1 4.3 add.480
  538.4 5.5 pad_maximum_fusion.1
  547.1 9.2 %while.39 = (s32[]{:T(128)}, f32[8,128,256]{2,1,0:T(8,128)}, bf16[2048,512]{1,0:T(8,128)(2,1)}, s32[]{:T(128)}, s32[128]{0:T(128)S(1)}, /*index=5*/s32[2048]{0:T...) while((s32[]{:T(128)}, f32[8,128,256]{2,1,0:T(8,128)}, ...), condition=%wide.region_13.14_spmd.clone, body=%wide.region_12.13_spmd.clone.sunk | while | flops 1348665984 | bytes 20336396 | solution.py:850
  551.3 2.8 convolution_add_fusion.10
  560.6 9.1 %convert_add_fusion.2 = f32[1024,2048]{1,0:T(8,128)} fusion(bf16[1024,2048]{1,0:T(8,128)(2,1)} %collective-permute-done.29, bf16[1024,2048]{1,0:T(8,128)(2,1)} %convolution_convert_fusion.4), kind=kLoop, calls=%fused_computation.85 | loop fusion | flops 6291456 | bytes 16777216 | tf_op jit(solution)/shard_map/add | solution.py:778
  569.6 2.6 collective-permute-done.27
  574.7 9.5 %collective-permute-start.31 = (bf16[2,2,64,512]{3,2,0,1:T(8,128)(2,1)S(1)}, bf16[2,2,64,512]{3,2,0,1:T(8,128)(2,1)S(1)}, u32[]{:S(2)}, u32[]{:S(2)}) collective-permute-start(bf16[2,2,64,512]{3,2,0,1:T(8,128)(2,1)S(1)} %dynamic-slice_bitcast_fusion.10), channel_id=1, source_target_pairs={{0,8},{2,10},{4,12},{6,14},{8,0},{10,2},{12,4},{14,6},{16,24},{18,... | collective-permute-start | bytes 786440 | tf_op jit(solution)/shard_map/ppermute | solution.py:479
  584.2 5.3 convert_add_fusion.1
  592.6 5.6 fusion.85
  598.3 5.1 collective-permute-start.33
  604.5 5.4 convert_add_fusion
  610.0 16.7 %collective-permute-start.36 = (bf16[64,512]{1,0:T(8,128)(2,1)S(1)}, bf16[64,512]{1,0:T(8,128)(2,1)}, u32[]{:S(2)}, u32[]{:S(2)}) collective-permute-start(bf16[64,512]{1,0:T(8,128)(2,1)S(1)} %dynamic-slice_bitcast_fusion.23), channel_id=1, source_target_pairs={{0,16},{2,18},{4,20},{6,22},{8,24},{10,26},{12,28},{14,30},{16,0},... | collective-permute-start | bytes 196616 | tf_op jit(solution)/shard_map/ppermute | solution.py:479
  627.8 5.8 convolution_convert_fusion.1
  633.6 5.9 fusion.88
  639.4 2.5 fusion.63
  642.0 2.9 fusion.239
  644.9 3.3 convolution_convert_fusion.8
  648.2 2.6 copy.98
  653.5 3.4 fusion.100
  664.9 96.0 %scatter_blocks_4.1 = bf16[192,2048]{1,0:T(8,128)(2,1)S(1)} custom-call(bf16[16,128,2048]{2,1,0:T(8,128)(2,1)S(1)} %bitcast.598, bf16[16,64,2048]{2,1,0:T(8,128)(2,1)S(1)} %pad_maximum_fusion.2.second_ref), custom_call_target="tpu_custom_call" | custom-call | tf_op jit(solution)/shard_map/scatter_blocks_4/pallas_call | solution.py:423
  763.2 2.6 copy.99
  770.0 2.4 fusion.240
  773.8 5.1 reduce-scatter.2.cloned.1.call-done
  (444 shorter events, 128.7 us)
Async XLA Ops:
  7.2 237.4 %copy-start = (bf16[2048,256]{1,0:T(8,128)(2,1)S(1)}, bf16[2048,256]{1,0:T(8,128)(2,1)}, u32[]{:S(2)}) copy-start(bf16[2048,256]{1,0:T(8,128)(2,1)} %param.51) | copy-start | bytes 3145732
  7.2 95.6 %copy-start.33 = (bf16[1,128,2048]{2,1,0:T(8,128)(2,1)S(1)}, bf16[1,128,2048]{2,1,0:T(8,128)(2,1)}, u32[]{:S(2)}) copy-start(bf16[1,128,2048]{2,1,0:T(8,128)(2,1)} %param.57) | copy-start | bytes 1572868
  7.2 96.5 %copy-start.47 = (s32[1,2048]{1,0:T(1,128)S(1)}, s32[1,2048]{1,0:T(1,128)}, u32[]{:S(2)}) copy-start(s32[1,2048]{1,0:T(1,128)} %param.33) | copy-start | bytes 24580
  7.2 97.4 %copy-start.2 = (bf16[1,128,2048]{2,1,0:T(8,128)(2,1)S(1)}, bf16[1,128,2048]{2,1,0:T(8,128)(2,1)}, u32[]{:S(2)}) copy-start(bf16[1,128,2048]{2,1,0:T(8,128)(2,1)} %param.32) | copy-start | bytes 1572868
  7.3 97.7 %copy-start.38 = (f32[2048]{0:T(1024)S(1)}, f32[2048]{0:T(1024)}, u32[]{:S(2)}) copy-start(f32[2048]{0:T(1024)} %param.34) | copy-start | bytes 24580
  7.3 312.5 %all-gather.3.cloned.1.call-start = ((), (), s32[]{:S(2)}) async-start(), calls=%async_computation.1 | async-start | bytes 4456448 | tf_op jit(solution)/shard_map/all_gather | solution.py:644
  103.6 220.8 %all-gather.5.cloned.1.call-start = ((), (), s32[]{:S(2)}) async-start(), calls=%async_computation.2 | async-start | bytes 4456448 | tf_op jit(solution)/shard_map/all_gather | solution.py:705
  104.6 38.6 %copy-start.56 = (f32[128]{0:T(128)}, f32[128]{0:T(128)S(1)}, u32[]{:S(2)}) copy-start(f32[128]{0:T(128)S(1)} %get-tuple-element.571) | copy-start | bytes 1540
  104.7 38.5 %copy-start.62 = (f32[128]{0:T(128)}, f32[128]{0:T(128)S(1)}, u32[]{:S(2)}) copy-start(f32[128]{0:T(128)S(1)} %negate_power_fusion) | copy-start | bytes 1540
  104.9 38.3 %copy-start.54 = (f32[128]{0:T(128)}, f32[128]{0:T(128)S(1)}, u32[]{:S(2)}) copy-start(f32[128]{0:T(128)S(1)} %fusion.206) | copy-start | bytes 1540
  108.0 45.2 %copy-start.40 = (f32[128,128]{1,0:T(8,128)}, f32[128,128]{1,0:T(8,128)S(1)}, u32[]{:S(2)}) copy-start(f32[128,128]{1,0:T(8,128)S(1)} %get-tuple-element.642) | copy-start | bytes 196612
  165.4 78.7 %copy-start.63 = (f32[128]{0:T(128)}, f32[128]{0:T(128)S(1)}, u32[]{:S(2)}) copy-start(f32[128]{0:T(128)S(1)} %get-tuple-element.643) | copy-start | bytes 1540
  244.1 534.8 %reduce-scatter.2.cloned.1.call-start = ((), (), s32[]{:S(2)}) async-start(), calls=%async_computation.3 | async-start | bytes 6684672 | tf_op jit(solution)/shard_map/reduce_scatter | solution.py:518
  250.5 11.2 %copy-start.31 = (bf16[2048,256]{1,0:T(8,128)(2,1)S(1)}, bf16[2048,256]{1,0:T(8,128)(2,1)}, u32[]{:S(2)}) copy-start(bf16[2048,256]{1,0:T(8,128)(2,1)} %param.53) | copy-start | bytes 3145732
  310.0 43.9 %collective-permute-start = (bf16[2,2,2,48,2048]{4,3,0,1,2:T(8,128)(2,1)}, bf16[2,2,2,48,2048]{4,3,0,1,2:T(8,128)(2,1)}, u32[]{:S(2)}, u32[]{:S(2)}) collective-permute-start(bf16[2,2,2,48,2048]{4,3,0,1,2:T(8,128)(2,1)} %bitcast.536), channel_id=1, source_target_pairs={{0,2},{2,0},{4,6},{6,4},{8,10},{10,8},{12,14},{14,12},{16,18},{18,... | collective-permute-start | bytes 4718600 | tf_op jit(solution)/shard_map/ppermute | solution.py:479
  315.4 38.5 %collective-permute-start.1 = (bf16[2,2,2,48,2048]{4,3,0,2,1:T(8,128)(2,1)}, bf16[2,2,2,48,2048]{4,3,0,2,1:T(8,128)(2,1)}, u32[]{:S(2)}, u32[]{:S(2)}) collective-permute-start(bf16[2,2,2,48,2048]{4,3,0,2,1:T(8,128)(2,1)} %bitcast.535), channel_id=1, source_target_pairs={{0,4},{2,6},{4,0},{6,2},{8,12},{10,14},{12,8},{14,10},{16,20},{18,... | collective-permute-start | bytes 4718600 | tf_op jit(solution)/shard_map/ppermute | solution.py:479
  319.7 34.2 %collective-permute-start.2 = (bf16[2,2,2,32,2048]{4,3,0,1,2:T(8,128)(2,1)S(1)}, bf16[2,2,2,32,2048]{4,3,0,1,2:T(8,128)(2,1)S(1)}, u32[]{:S(2)}, u32[]{:S(2)}) collective-permute-start(bf16[2,2,2,32,2048]{4,3,0,1,2:T(8,128)(2,1)S(1)} %bitcast.642), channel_id=1, source_target_pairs={{0,8},{2,10},{4,12},{6,14},{8,0},{10,2},{12,4},{14,6},{16,24},{18,... | collective-permute-start | bytes 3145736 | tf_op jit(solution)/shard_map/ppermute | solution.py:479
  329.1 24.8 %copy-start.13 = (bf16[2,2,2,1,48,2048]{5,4,3,2,1,0:T(8,128)(2,1)S(1)}, bf16[2,2,2,1,48,2048]{5,4,3,2,1,0:T(8,128)(2,1)}, u32[]{:S(2)}) copy-start(bf16[2,2,2,1,48,2048]{5,4,3,2,1,0:T(8,128)(2,1)} %get-tuple-element.587) | copy-start | bytes 4718596
  356.2 18.7 %collective-permute-start.3 = (bf16[2,2,48,2048]{3,2,0,1:T(8,128)(2,1)S(1)}, bf16[2,2,48,2048]{3,2,0,1:T(8,128)(2,1)S(1)}, u32[]{:S(2)}, u32[]{:S(2)}) collective-permute-start(bf16[2,2,48,2048]{3,2,0,1:T(8,128)(2,1)S(1)} %dynamic-slice_bitcast_fusion.3), channel_id=1, source_target_pairs={{0,4},{2,6},{4,0},{6,2},{8,12},{10,14},{12,8},{14,10},{16,20},{18,... | collective-permute-start | bytes 2359304 | tf_op jit(solution)/shard_map/ppermute | solution.py:479
  359.1 17.4 %collective-permute-start.4 = (bf16[2,2,48,2048]{3,2,0,1:T(8,128)(2,1)S(1)}, bf16[2,2,48,2048]{3,2,0,1:T(8,128)(2,1)S(1)}, u32[]{:S(2)}, u32[]{:S(2)}) collective-permute-start(bf16[2,2,48,2048]{3,2,0,1:T(8,128)(2,1)S(1)} %dynamic-slice_bitcast_fusion.2), channel_id=1, source_target_pairs={{0,8},{2,10},{4,12},{6,14},{8,0},{10,2},{12,4},{14,6},{16,24},{18,... | collective-permute-start | bytes 2359304 | tf_op jit(solution)/shard_map/ppermute | solution.py:479
  361.6 13.2 %collective-permute-start.5 = (bf16[2,2,32,2048]{3,2,0,1:T(8,128)(2,1)S(1)}, bf16[2,2,32,2048]{3,2,0,1:T(8,128)(2,1)S(1)}, u32[]{:S(2)}, u32[]{:S(2)}) collective-permute-start(bf16[2,2,32,2048]{3,2,0,1:T(8,128)(2,1)S(1)} %dynamic-slice_bitcast_fusion.5), channel_id=1, source_target_pairs={{0,2},{2,0},{4,6},{6,4},{8,10},{10,8},{12,14},{14,12},{16,18},{18,... | collective-permute-start | bytes 1572872 | tf_op jit(solution)/shard_map/ppermute | solution.py:479
  376.8 28.3 %collective-permute-start.6 = (bf16[2,48,2048]{2,1,0:T(8,128)(2,1)S(1)}, bf16[2,48,2048]{2,1,0:T(8,128)(2,1)S(1)}, u32[]{:S(2)}, u32[]{:S(2)}) collective-permute-start(bf16[2,48,2048]{2,1,0:T(8,128)(2,1)S(1)} %dynamic-slice_bitcast_fusion.9), channel_id=1, source_target_pairs={{0,8},{2,10},{4,12},{6,14},{8,0},{10,2},{12,4},{14,6},{16,24},{18,... | collective-permute-start | bytes 1179656 | tf_op jit(solution)/shard_map/ppermute | solution.py:479
  379.2 26.0 %collective-permute-start.7 = (bf16[2,48,2048]{2,1,0:T(8,128)(2,1)S(1)}, bf16[2,48,2048]{2,1,0:T(8,128)(2,1)S(1)}, u32[]{:S(2)}, u32[]{:S(2)}) collective-permute-start(bf16[2,48,2048]{2,1,0:T(8,128)(2,1)S(1)} %dynamic-slice_bitcast_fusion.8), channel_id=1, source_target_pairs={{0,2},{2,0},{4,6},{6,4},{8,10},{10,8},{12,14},{14,12},{16,18},{18,... | collective-permute-start | bytes 1179656 | tf_op jit(solution)/shard_map/ppermute | solution.py:479
  380.9 24.2 %collective-permute-start.8 = (bf16[2,32,2048]{2,1,0:T(8,128)(2,1)S(1)}, bf16[2,32,2048]{2,1,0:T(8,128)(2,1)S(1)}, u32[]{:S(2)}, u32[]{:S(2)}) collective-permute-start(bf16[2,32,2048]{2,1,0:T(8,128)(2,1)S(1)} %dynamic-slice_bitcast_fusion.13), channel_id=1, source_target_pairs={{0,4},{2,6},{4,0},{6,2},{8,12},{10,14},{12,8},{14,10},{16,20},{18,... | collective-permute-start | bytes 786440 | tf_op jit(solution)/shard_map/ppermute | solution.py:479
  406.6 37.6 %collective-permute-start.9 = (bf16[48,2048]{1,0:T(8,128)(2,1)S(1)}, bf16[48,2048]{1,0:T(8,128)(2,1)S(1)}, u32[]{:S(2)}, u32[]{:S(2)}) collective-permute-start(bf16[48,2048]{1,0:T(8,128)(2,1)S(1)} %dynamic-slice_bitcast_fusion.17), channel_id=1, source_target_pairs={{0,16},{2,18},{4,20},{6,22},{8,24},{10,26},{12,28},{14,30},{16,0},... | collective-permute-start | bytes 589832 | tf_op jit(solution)/shard_map/ppermute | solution.py:479
  411.5 32.7 %collective-permute-start.10 = (bf16[48,2048]{1,0:T(8,128)(2,1)S(1)}, bf16[48,2048]{1,0:T(8,128)(2,1)S(1)}, u32[]{:S(2)}, u32[]{:S(2)}) collective-permute-start(bf16[48,2048]{1,0:T(8,128)(2,1)S(1)} %dynamic-slice_bitcast_fusion.16), channel_id=1, source_target_pairs={{0,16},{2,18},{4,20},{6,22},{8,24},{10,26},{12,28},{14,30},{16,0},... | collective-permute-start | bytes 589832 | tf_op jit(solution)/shard_map/ppermute | solution.py:479
  411.6 20.7 %collective-permute-start.11 = (bf16[32,2048]{1,0:T(8,128)(2,1)S(1)}, bf16[32,2048]{1,0:T(8,128)(2,1)S(1)}, u32[]{:S(2)}, u32[]{:S(2)}) collective-permute-start(bf16[32,2048]{1,0:T(8,128)(2,1)S(1)} %dynamic-slice_bitcast_fusion.21), channel_id=1, source_target_pairs={{0,16},{2,18},{4,20},{6,22},{8,24},{10,26},{12,28},{14,30},{16,0},... | collective-permute-start | bytes 393224 | tf_op jit(solution)/shard_map/ppermute | solution.py:479
  415.0 41.7 %collective-permute-start.12 = (bf16[2,2,2,48,2048]{4,3,0,1,2:T(8,128)(2,1)S(1)}, bf16[2,2,2,48,2048]{4,3,0,1,2:T(8,128)(2,1)S(1)}, u32[]{:S(2)}, u32[]{:S(2)}) collective-permute-start(bf16[2,2,2,48,2048]{4,3,0,1,2:T(8,128)(2,1)S(1)} %bitcast.640), channel_id=1, source_target_pairs={{0,2},{2,0},{4,6},{6,4},{8,10},{10,8},{12,14},{14,12},{16,18},{18,... | collective-permute-start | bytes 4718600 | tf_op jit(solution)/shard_map/ppermute | solution.py:479
  416.9 39.7 %collective-permute-start.13 = (bf16[2,2,2,48,2048]{4,3,0,2,1:T(8,128)(2,1)S(1)}, bf16[2,2,2,48,2048]{4,3,0,2,1:T(8,128)(2,1)S(1)}, u32[]{:S(2)}, u32[]{:S(2)}) collective-permute-start(bf16[2,2,2,48,2048]{4,3,0,2,1:T(8,128)(2,1)S(1)} %bitcast.641), channel_id=1, source_target_pairs={{0,4},{2,6},{4,0},{6,2},{8,12},{10,14},{12,8},{14,10},{16,20},{18,... | collective-permute-start | bytes 4718600 | tf_op jit(solution)/shard_map/ppermute | solution.py:479
  432.3 24.3 %collective-permute-start.14 = (bf16[2,2,2,32,2048]{4,3,0,1,2:T(8,128)(2,1)S(1)}, bf16[2,2,2,32,2048]{4,3,0,1,2:T(8,128)(2,1)S(1)}, u32[]{:S(2)}, u32[]{:S(2)}) collective-permute-start(bf16[2,2,2,32,2048]{4,3,0,1,2:T(8,128)(2,1)S(1)} %bitcast.643), channel_id=1, source_target_pairs={{0,8},{2,10},{4,12},{6,14},{8,0},{10,2},{12,4},{14,6},{16,24},{18,... | collective-permute-start | bytes 3145736 | tf_op jit(solution)/shard_map/ppermute | solution.py:479
  444.2 50.3 %copy-start.27 = (bf16[1024,2048]{1,0:T(8,128)(2,1)}, bf16[1024,2048]{1,0:T(8,128)(2,1)S(1)}, u32[]{:S(2)}) copy-start(bf16[1024,2048]{1,0:T(8,128)(2,1)S(1)} %convolution_convert_fusion.3) | copy-start | bytes 12582916
  457.4 18.3 %collective-permute-start.15 = (bf16[2,2,48,2048]{3,2,0,1:T(8,128)(2,1)S(1)}, bf16[2,2,48,2048]{3,2,0,1:T(8,128)(2,1)S(1)}, u32[]{:S(2)}, u32[]{:S(2)}) collective-permute-start(bf16[2,2,48,2048]{3,2,0,1:T(8,128)(2,1)S(1)} %dynamic-slice_bitcast_fusion.1), channel_id=1, source_target_pairs={{0,4},{2,6},{4,0},{6,2},{8,12},{10,14},{12,8},{14,10},{16,20},{18,... | collective-permute-start | bytes 2359304 | tf_op jit(solution)/shard_map/ppermute | solution.py:479
  460.0 18.0 %collective-permute-start.16 = (bf16[2,2,48,2048]{3,2,0,1:T(8,128)(2,1)S(1)}, bf16[2,2,48,2048]{3,2,0,1:T(8,128)(2,1)S(1)}, u32[]{:S(2)}, u32[]{:S(2)}) collective-permute-start(bf16[2,2,48,2048]{3,2,0,1:T(8,128)(2,1)S(1)} %dynamic-slice_bitcast_fusion), channel_id=1, source_target_pairs={{0,8},{2,10},{4,12},{6,14},{8,0},{10,2},{12,4},{14,6},{16,24},{18,... | collective-permute-start | bytes 2359304 | tf_op jit(solution)/shard_map/ppermute | solution.py:479
  460.8 13.1 %collective-permute-start.17 = (bf16[2,2,32,2048]{3,2,0,1:T(8,128)(2,1)S(1)}, bf16[2,2,32,2048]{3,2,0,1:T(8,128)(2,1)S(1)}, u32[]{:S(2)}, u32[]{:S(2)}) collective-permute-start(bf16[2,2,32,2048]{3,2,0,1:T(8,128)(2,1)S(1)} %dynamic-slice_bitcast_fusion.4), channel_id=1, source_target_pairs={{0,2},{2,0},{4,6},{6,4},{8,10},{10,8},{12,14},{14,12},{16,18},{18,... | collective-permute-start | bytes 1572872 | tf_op jit(solution)/shard_map/ppermute | solution.py:479
  478.3 8.8 %collective-permute-start.18 = (bf16[2,48,2048]{2,1,0:T(8,128)(2,1)S(1)}, bf16[2,48,2048]{2,1,0:T(8,128)(2,1)S(1)}, u32[]{:S(2)}, u32[]{:S(2)}) collective-permute-start(bf16[2,48,2048]{2,1,0:T(8,128)(2,1)S(1)} %dynamic-slice_bitcast_fusion.7), channel_id=1, source_target_pairs={{0,8},{2,10},{4,12},{6,14},{8,0},{10,2},{12,4},{14,6},{16,24},{18,... | collective-permute-start | bytes 1179656 | tf_op jit(solution)/shard_map/ppermute | solution.py:479
  479.2 8.7 %collective-permute-start.19 = (bf16[2,48,2048]{2,1,0:T(8,128)(2,1)S(1)}, bf16[2,48,2048]{2,1,0:T(8,128)(2,1)S(1)}, u32[]{:S(2)}, u32[]{:S(2)}) collective-permute-start(bf16[2,48,2048]{2,1,0:T(8,128)(2,1)S(1)} %dynamic-slice_bitcast_fusion.6), channel_id=1, source_target_pairs={{0,2},{2,0},{4,6},{6,4},{8,10},{10,8},{12,14},{14,12},{16,18},{18,... | collective-permute-start | bytes 1179656 | tf_op jit(solution)/shard_map/ppermute | solution.py:479
  480.6 6.4 collective-permute-start.20
  488.0 23.4 %collective-permute-start.21 = (bf16[48,2048]{1,0:T(8,128)(2,1)S(1)}, bf16[48,2048]{1,0:T(8,128)(2,1)S(1)}, u32[]{:S(2)}, u32[]{:S(2)}) collective-permute-start(bf16[48,2048]{1,0:T(8,128)(2,1)S(1)} %dynamic-slice_bitcast_fusion.15), channel_id=1, source_target_pairs={{0,16},{2,18},{4,20},{6,22},{8,24},{10,26},{12,28},{14,30},{16,0},... | collective-permute-start | bytes 589832 | tf_op jit(solution)/shard_map/ppermute | solution.py:479
  491.3 20.2 %collective-permute-start.22 = (bf16[48,2048]{1,0:T(8,128)(2,1)S(1)}, bf16[48,2048]{1,0:T(8,128)(2,1)S(1)}, u32[]{:S(2)}, u32[]{:S(2)}) collective-permute-start(bf16[48,2048]{1,0:T(8,128)(2,1)S(1)} %dynamic-slice_bitcast_fusion.14), channel_id=1, source_target_pairs={{0,16},{2,18},{4,20},{6,22},{8,24},{10,26},{12,28},{14,30},{16,0},... | collective-permute-start | bytes 589832 | tf_op jit(solution)/shard_map/ppermute | solution.py:479
  491.4 20.0 %collective-permute-start.23 = (bf16[32,2048]{1,0:T(8,128)(2,1)S(1)}, bf16[32,2048]{1,0:T(8,128)(2,1)S(1)}, u32[]{:S(2)}, u32[]{:S(2)}) collective-permute-start(bf16[32,2048]{1,0:T(8,128)(2,1)S(1)} %dynamic-slice_bitcast_fusion.20), channel_id=1, source_target_pairs={{0,16},{2,18},{4,20},{6,22},{8,24},{10,26},{12,28},{14,30},{16,0},... | collective-permute-start | bytes 393224 | tf_op jit(solution)/shard_map/ppermute | solution.py:479
  500.8 10.8 %copy-start.7 = (f32[128,2048]{1,0:T(8,128)S(1)}, f32[128,2048]{1,0:T(8,128)}, u32[]{:S(2)}) copy-start(f32[128,2048]{1,0:T(8,128)} %copy-done.6) | copy-start | bytes 3145732
  500.8 11.0 %copy-start.64 = (f32[128]{0:T(128)S(1)}, f32[128]{0:T(128)}, u32[]{:S(2)}) copy-start(f32[128]{0:T(128)} %copy-done.63) | copy-start | bytes 1540
  500.9 11.0 %copy-start.34 = (bf16[1,128,2048]{2,1,0:T(8,128)(2,1)S(1)}, bf16[1,128,2048]{2,1,0:T(8,128)(2,1)}, u32[]{:S(2)}) copy-start(bf16[1,128,2048]{2,1,0:T(8,128)(2,1)} %param.57) | copy-start | bytes 1572868
  516.8 17.3 %collective-permute-start.24 = (bf16[16,128,1024]{2,1,0:T(8,128)(2,1)}, bf16[16,128,1024]{2,1,0:T(8,128)(2,1)}, u32[]{:S(2)}, u32[]{:S(2)}) collective-permute-start(bf16[16,128,1024]{2,1,0:T(8,128)(2,1)} %bitcast.93), channel_id=1, source_target_pairs={{0,1},{1,0},{2,3},{3,2},{4,5},{5,4},{6,7},{7,6},{8,9},{9,8},{10,11... | collective-permute-start | bytes 12582920 | tf_op jit(solution)/shard_map/ppermute | solution.py:811
  519.3 14.0 %collective-permute-start.26 = (bf16[16,48,1024]{2,1,0:T(8,128)(2,1)S(1)}, bf16[16,48,1024]{2,1,0:T(8,128)(2,1)S(1)}, u32[]{:S(2)}, u32[]{:S(2)}) collective-permute-start(bf16[16,48,1024]{2,1,0:T(8,128)(2,1)S(1)} %constant_dynamic-slice_fusion.4), channel_id=1, source_target_pairs={{0,1},{1,0},{2,3},{3,2},{4,5},{5,4},{6,7},{7,6},{8,9},{9,8},{10,11... | collective-permute-start | bytes 4718600 | tf_op jit(solution)/shard_map/ppermute | solution.py:811
  521.4 39.1 %collective-permute-start.29 = (bf16[1024,2048]{1,0:T(8,128)(2,1)}, bf16[1024,2048]{1,0:T(8,128)(2,1)}, u32[]{:S(2)}, u32[]{:S(2)}) collective-permute-start(bf16[1024,2048]{1,0:T(8,128)(2,1)} %convolution_convert_fusion.4), channel_id=1, source_target_pairs={{0,1},{1,0},{2,3},{3,2},{4,5},{5,4},{6,7},{7,6},{8,9},{9,8},{10,11... | collective-permute-start | bytes 12582920 | tf_op jit(solution)/shard_map/ppermute | solution.py:778
  521.8 11.3 %collective-permute-start.25 = (bf16[16,16,1024]{2,1,0:T(8,128)(2,1)S(1)}, bf16[16,16,1024]{2,1,0:T(8,128)(2,1)S(1)}, u32[]{:S(2)}, u32[]{:S(2)}) collective-permute-start(bf16[16,16,1024]{2,1,0:T(8,128)(2,1)S(1)} %bitcast.647), channel_id=1, source_target_pairs={{0,1},{1,0},{2,3},{3,2},{4,5},{5,4},{6,7},{7,6},{8,9},{9,8},{10,11... | collective-permute-start | bytes 1572872 | tf_op jit(solution)/shard_map/ppermute | solution.py:811
  558.2 14.0 %collective-permute-start.27 = (bf16[2,2,2,64,512]{4,3,0,1,2:T(8,128)(2,1)S(1)}, bf16[2,2,2,64,512]{4,3,0,1,2:T(8,128)(2,1)S(1)}, u32[]{:S(2)}, u32[]{:S(2)}) collective-permute-start(bf16[2,2,2,64,512]{4,3,0,1,2:T(8,128)(2,1)S(1)} %bitcast.645), channel_id=1, source_target_pairs={{0,2},{2,0},{4,6},{6,4},{8,10},{10,8},{12,14},{14,12},{16,18},{18,... | collective-permute-start | bytes 1572872 | tf_op jit(solution)/shard_map/ppermute | solution.py:479
  559.6 13.8 %copy-start.28 = (bf16[1024,2048]{1,0:T(8,128)(2,1)S(1)}, bf16[1024,2048]{1,0:T(8,128)(2,1)}, u32[]{:S(2)}) copy-start(bf16[1024,2048]{1,0:T(8,128)(2,1)} %copy-done.27) | copy-start | bytes 12582916
  559.6 13.8 %collective-permute-start.28 = (bf16[2,2,2,64,512]{4,3,0,2,1:T(8,128)(2,1)S(1)}, bf16[2,2,2,64,512]{4,3,0,2,1:T(8,128)(2,1)S(1)}, u32[]{:S(2)}, u32[]{:S(2)}) collective-permute-start(bf16[2,2,2,64,512]{4,3,0,2,1:T(8,128)(2,1)S(1)} %bitcast.646), channel_id=1, source_target_pairs={{0,4},{2,6},{4,0},{6,2},{8,12},{10,14},{12,8},{14,10},{16,20},{18,... | collective-permute-start | bytes 1572872 | tf_op jit(solution)/shard_map/ppermute | solution.py:479
  573.4 10.8 %collective-permute-start.32 = (bf16[1024,2048]{1,0:T(8,128)(2,1)S(1)}, bf16[1024,2048]{1,0:T(8,128)(2,1)S(1)}, u32[]{:S(2)}, u32[]{:S(2)}) collective-permute-start(bf16[1024,2048]{1,0:T(8,128)(2,1)S(1)} %copy-done.28), channel_id=1, source_target_pairs={{0,1},{1,0},{2,3},{3,2},{4,5},{5,4},{6,7},{7,6},{8,9},{9,8},{10,11... | collective-permute-start | bytes 12582920 | tf_op jit(solution)/shard_map/ppermute | solution.py:778
  573.6 16.0 %collective-permute-start.30 = (bf16[2,2,64,512]{3,2,0,1:T(8,128)(2,1)S(1)}, bf16[2,2,64,512]{3,2,0,1:T(8,128)(2,1)S(1)}, u32[]{:S(2)}, u32[]{:S(2)}) collective-permute-start(bf16[2,2,64,512]{3,2,0,1:T(8,128)(2,1)S(1)} %dynamic-slice_bitcast_fusion.11), channel_id=1, source_target_pairs={{0,4},{2,6},{4,0},{6,2},{8,12},{10,14},{12,8},{14,10},{16,20},{18,... | collective-permute-start | bytes 786440 | tf_op jit(solution)/shard_map/ppermute | solution.py:479
  574.7 16.2 %collective-permute-start.31 = (bf16[2,2,64,512]{3,2,0,1:T(8,128)(2,1)S(1)}, bf16[2,2,64,512]{3,2,0,1:T(8,128)(2,1)S(1)}, u32[]{:S(2)}, u32[]{:S(2)}) collective-permute-start(bf16[2,2,64,512]{3,2,0,1:T(8,128)(2,1)S(1)} %dynamic-slice_bitcast_fusion.10), channel_id=1, source_target_pairs={{0,8},{2,10},{4,12},{6,14},{8,0},{10,2},{12,4},{14,6},{16,24},{18,... | collective-permute-start | bytes 786440 | tf_op jit(solution)/shard_map/ppermute | solution.py:479
  590.9 13.6 %collective-permute-start.35 = (bf16[1024,2048]{1,0:T(8,128)(2,1)}, bf16[1024,2048]{1,0:T(8,128)(2,1)}, u32[]{:S(2)}, u32[]{:S(2)}) collective-permute-start(bf16[1024,2048]{1,0:T(8,128)(2,1)} %convolution_convert_fusion.2), channel_id=1, source_target_pairs={{0,1},{1,0},{2,3},{3,2},{4,5},{5,4},{6,7},{7,6},{8,9},{9,8},{10,11... | collective-permute-start | bytes 12582920 | tf_op jit(solution)/shard_map/ppermute | solution.py:778
  598.3 11.6 %collective-permute-start.33 = (bf16[2,64,512]{2,1,0:T(8,128)(2,1)S(1)}, bf16[2,64,512]{2,1,0:T(8,128)(2,1)S(1)}, u32[]{:S(2)}, u32[]{:S(2)}) collective-permute-start(bf16[2,64,512]{2,1,0:T(8,128)(2,1)S(1)} %dynamic-slice_bitcast_fusion.19), channel_id=1, source_target_pairs={{0,8},{2,10},{4,12},{6,14},{8,0},{10,2},{12,4},{14,6},{16,24},{18,... | collective-permute-start | bytes 393224 | tf_op jit(solution)/shard_map/ppermute | solution.py:479
  603.6 24.2 %copy-start.3 = (bf16[1,128,2048]{2,1,0:T(8,128)(2,1)S(1)}, bf16[1,128,2048]{2,1,0:T(8,128)(2,1)}, u32[]{:S(2)}) copy-start(bf16[1,128,2048]{2,1,0:T(8,128)(2,1)} %param.32) | copy-start | bytes 1572868
  603.6 24.2 %copy-start.39 = (f32[2048]{0:T(1024)S(1)}, f32[2048]{0:T(1024)}, u32[]{:S(2)}) copy-start(f32[2048]{0:T(1024)} %param.34) | copy-start | bytes 24580
  603.6 24.2 %copy-start.55 = (f32[128]{0:T(128)S(1)}, f32[128]{0:T(128)}, u32[]{:S(2)}) copy-start(f32[128]{0:T(128)} %copy-done.54) | copy-start | bytes 1540
  603.6 6.3 collective-permute-start.34
  609.9 29.6 %copy-start.1 = (f32[1024,2048]{1,0:T(8,128)}, f32[1024,2048]{1,0:T(8,128)S(1)}, u32[]{:S(2)}) copy-start(f32[1024,2048]{1,0:T(8,128)S(1)} %convert_add_fusion) | copy-start | bytes 25165828
  610.0 40.8 %collective-permute-start.36 = (bf16[64,512]{1,0:T(8,128)(2,1)S(1)}, bf16[64,512]{1,0:T(8,128)(2,1)}, u32[]{:S(2)}, u32[]{:S(2)}) collective-permute-start(bf16[64,512]{1,0:T(8,128)(2,1)S(1)} %dynamic-slice_bitcast_fusion.23), channel_id=1, source_target_pairs={{0,16},{2,18},{4,20},{6,22},{8,24},{10,26},{12,28},{14,30},{16,0},... | collective-permute-start | bytes 196616 | tf_op jit(solution)/shard_map/ppermute | solution.py:479
  627.3 23.4 %collective-permute-start.37 = (bf16[64,512]{1,0:T(8,128)(2,1)}, bf16[64,512]{1,0:T(8,128)(2,1)}, u32[]{:S(2)}, u32[]{:S(2)}) collective-permute-start(bf16[64,512]{1,0:T(8,128)(2,1)} %dynamic-slice_bitcast_fusion.22), channel_id=1, source_target_pairs={{0,16},{2,18},{4,20},{6,22},{8,24},{10,26},{12,28},{14,30},{16,0},... | collective-permute-start | bytes 196616 | tf_op jit(solution)/shard_map/ppermute | solution.py:479
  768.3 11.7 %copy-start.45 = (f32[128,256]{1,0:T(8,128)}, f32[128,256]{1,0:T(8,128)S(1)}, u32[]{:S(2)}) copy-start(f32[128,256]{1,0:T(8,128)S(1)} %get-tuple-element.636) | copy-start | bytes 393220
  778.9 1.9 collective-permute-start.38
  (56 other events, 266.3 us)
Sparse Core Ops, SparseCore 0:
  103.8 83.3 all-gather.2
  244.2 77.8 all-gather.4
  591.1 187.7 reduce-scatter.1

commit v6 on v5

--- a/solution.py
+++ b/solution.py
@@ -539,10 +539,10 @@
 
 def gather_weights(query, output, key_value, shards):
     if shards == 4 * LINE:
-        rows = query.shape[0]
+        half = query.shape[0] // 2
         return gather_blocks(
             [query, output, key_value],
-            [[(rows, "y")], [(rows, "x")], [(rows // 2, "y"), (rows // 2, "x")]],
+            [[(half, "y"), (half, "x")]] * 3,
             True,
             1,
         )
@@ -555,8 +555,8 @@
 
 def gather_rows(own, shards, number):
     if shards == 4 * LINE:
-        half = own.shape[0] // 2
-        return gather_blocks([own], [[(half, "y"), (half, "x")]], False, number)[0]
+        fourth = own.shape[0] // 4
+        return gather_blocks([own], [[(fourth, "y"), (fourth, "x")] * 2], False, number)[0]
     return lax.all_gather(own, "fsdp", axis=0, tiled=True)
 
 

time: 793 us -> 788 us (level)
  transfers between devices with their start and end apart: 42 -> 42, of which waited for: 15 -> 13; matrix products, arithmetic and copies ran while one was open for 42% -> 43% of each run, Pallas kernels for 26% -> 26%
where the time goes in v6:
time: 788 us; the launch traced here: 779 us
  Pallas kernels  290 us (37%)
  matrix products  227 us (29%)
  other arithmetic  71.1 us (9%)
  local copies, waits for them, and re-layouts  68.5 us (9%)
  starting transfers between devices  65.5 us (8%)
  waiting for transfers between devices  40 us (5%)
  between operations  16.1 us (2%)
    pallas_call x3, Pallas kernels, gather_blocks(): pl.pallas_call(functools.partial(gather_kernel, pieces, len(arrays), with...  195 us
    pallas_call x1, Pallas kernels, scatter_blocks(): pl.pallas_call(scatter_kernel, out_shape=jax.ShapeDtypeStruct((rows, colu...  95.3 us
    dot_general x11, matrix products, right_product(): lax.dot_general(left, right, (((1,), (1,)), ((), ())), preferred_element_...  72 us
    ppermute x32, starting transfers between devices, start(): self.came.append(lax.ppermute(away, 'fsdp', pairs))  63.7 us
    dot_general x12, matrix products, matrix_product(): return jnp.dot(left, right, preferred_element_type=jnp.float32)  63.5 us
    dot_general x13, matrix products, left_matrix_product(): lax.dot_general(left, right, (((0,), (0,)), ((), ())), preferred_element_...  57.1 us
    ppermute x32, waiting for transfers between devices, start(): self.came.append(lax.ppermute(away, 'fsdp', pairs))  31.4 us
    unnamed x180, local copies, waits for them, and re-layouts  25.2 us
  transfers between devices with their start and end apart: 42, of which 13 were waited for; matrix products, arithmetic and copies ran while one was open for 43% of the time, Pallas kernels for 26%

profile of v6, /device:TPU:0, one launch (start us, length us, event | category | flops | bytes accessed | tf_op | source)
XLA Modules:
  0.0 779.0 jit_solution(11328620695322503471)
XLA Ops:
  10.2 2.3 fusion.73.refs_0_
  12.5 2.3 fusion.74.refs_1_
  14.8 88.6 %gather_blocks_1.1 = (bf16[16,2,64,2048]{3,2,1,0:T(8,128)(2,1)}, bf16[16,2,64,2048]{3,2,1,0:T(8,128)(2,1)}, bf16[16,2,64,512]{3,2,1,0:T(8,128)(2,1)}) custom-call(bf16[64,2048]{1,0:T(8,128)(2,1)} %fusion.73.refs_0_, bf16[64,2048]{1,0:T(8,128)(2,1)} %fusion.74.refs_1_, bf16[64,512]{1,0:T(8,128)(2,1)} %pad_maximum_fusion.12.refs_2_), custom_call_target="tpu_custom_call" | custom-call | tf_op jit(solution)/shard_map/gather_blocks_1/pallas_call | solution.py:227
  109.3 31.7 %gather_blocks_3.1 = bf16[16,128,512]{2,1,0:T(8,128)(2,1)} custom-call(bf16[128,512]{1,0:T(8,128)(2,1)} %pad_maximum_fusion.9.refs_0_), custom_call_target="tpu_custom_call" | custom-call | tf_op jit(solution)/shard_map/gather_blocks_3/pallas_call | solution.py:227
  141.0 2.6 fusion.227
  143.7 4.7 fusion.123
  160.4 5.4 multiply_reduce_fusion.3
  167.8 74.8 %gather_blocks_2.1 = bf16[16,128,2048]{2,1,0:T(8,128)(2,1)} custom-call(bf16[128,2048]{1,0:T(8,128)(2,1)} %multiply_convert_fusion.1.refs_0_), custom_call_target="tpu_custom_call" | custom-call | tf_op jit(solution)/shard_map/gather_blocks_2/pallas_call | solution.py:227
  243.1 3.8 add_convert_fusion.3
  248.9 11.2 %fusion.236 = f32[2048,1024]{1,0:T(8,128)} fusion(bf16[2048,2048]{1,0:T(8,128)(2,1)S(1)} %bitcast.618, bf16[1024,2048]{1,0:T(8,128)(2,1)S(1)} %add_convert_fusion.3), kind=kOutput, calls=%fused_computation.479 | convolution fusion | flops 8589934592 | bytes 20971520 | tf_op jit(solution)/shard_map/dot_general | solution.py:26
  260.1 3.8 add_convert_fusion.2
  264.0 5.1 add_convert_fusion.1
  270.6 15.5 %fusion.62 = (bf16[2048,1024]{1,0:T(8,128)(2,1)}, f32[2048,1024]{1,0:T(8,128)}) fusion(f32[2048,1024]{1,0:T(8,128)} %fusion.236, bf16[2048,2048]{1,0:T(8,128)(2,1)S(1)} %bitcast.619, bf16[1024,2048]{1,0:T(8,128)(2,1)S(1)} %add_convert_fusion.2), kind=kOutput, calls=%fused_computation.82 | convolution fusion | flops 8610906112 | bytes 33554432 | tf_op jit(solution)/shard_map/dot_general | solution.py:26
  286.1 14.1 %convolution_convert_fusion = bf16[2048,2048]{1,0:T(8,128)(2,1)} fusion(bf16[2048,1024]{1,0:T(8,128)(2,1)} %get-tuple-element.307, bf16[1024,2048]{1,0:T(8,128)(2,1)} %add_convert_fusion.1), kind=kOutput, calls=%fused_computation.90 | convolution fusion | flops 8594128896 | bytes 16777216 | tf_op jit(solution)/shard_map/dot_general | solution.py:16
  300.2 5.4 fusion.225
  309.5 3.4 constant_dynamic-slice_fusion.12
  318.3 4.7 constant_dynamic-update-slice_fusion.10
  322.9 4.7 constant_dynamic-update-slice_fusion.9
  327.6 24.8 %multiply_convert_fusion = (bf16[2048,1024]{1,0:T(8,128)(2,1)}, bf16[2048,1024]{1,0:T(8,128)(2,1)}) fusion(f32[2048,1024]{1,0:T(8,128)} %fusion.236, f32[2048,1024]{1,0:T(8,128)} %get-tuple-element.281, bf16[2048,2048]{1,0:T(8,128)(2,1)} %constant_dynamic-update-slice_fusion.9, bf16[1024,2048]{1,0:T(8,128)(2,1)} %add_convert_fusion.1), kind=kOutput, calls=%fused_computation.86 | convolution fusion | flops 8640266240 | bytes 37748736 | tf_op jit(solution)/shard_map/dot_general | solution.py:26
  361.5 11.7 %fusion.237 = f32[2048,2048]{1,0:T(8,128)} fusion(bf16[2048,1024]{1,0:T(8,128)(2,1)S(1)} %copy-done.69, bf16[1024,2048]{1,0:T(8,128)(2,1)S(1)} %copy-done.20), kind=kOutput, calls=%fused_computation.480 | convolution fusion | flops 8589934592 | bytes 25165824 | tf_op jit(solution)/shard_map/dot_general | solution.py:16
  373.2 2.3 collective-permute-done.4
  380.5 12.2 %fusion.238 = f32[2048,2048]{1,0:T(8,128)} fusion(bf16[2048,1024]{1,0:T(8,128)(2,1)S(1)} %copy-done.68, bf16[1024,2048]{1,0:T(8,128)(2,1)S(1)} %copy-done.18), kind=kOutput, calls=%fused_computation.481 | convolution fusion | flops 8589934592 | bytes 25165824 | tf_op jit(solution)/shard_map/dot_general | solution.py:16
  392.7 11.5 %add_convert_fusion = bf16[2048,2048]{1,0:T(8,128)(2,1)S(1)} fusion(f32[2048,2048]{1,0:T(8,128)} %fusion.237, f32[2048,2048]{1,0:T(8,128)} %fusion.238), kind=kLoop, calls=%fused_computation.63 | loop fusion | flops 8388608 | bytes 41943040 | tf_op jit(solution)/shard_map/convert_element_type | solution.py:744
  405.6 3.0 collective-permute-start.9
  408.9 3.0 collective-permute-start.11
  415.7 12.4 %convolution_convert_fusion.4 = bf16[1024,2048]{1,0:T(8,128)(2,1)} fusion(bf16[2048,1024]{1,0:T(8,128)(2,1)} %get-tuple-element.298, bf16[2048,2048]{1,0:T(8,128)(2,1)S(1)} %bitcast.622), kind=kOutput, calls=%fused_computation.102 | convolution fusion | flops 8592031744 | bytes 16777216 | tf_op jit(solution)/shard_map/dot_general | solution.py:20
  429.7 11.3 %convolution_convert_fusion.3 = bf16[1024,2048]{1,0:T(8,128)(2,1)S(1)} fusion(bf16[2048,1024]{1,0:T(8,128)(2,1)} %get-tuple-element.299, bf16[2048,2048]{1,0:T(8,128)(2,1)S(1)} %bitcast.623), kind=kOutput, calls=%fused_computation.101 | convolution fusion | flops 8592031744 | bytes 16777216 | tf_op jit(solution)/shard_map/dot_general | solution.py:20
  441.0 11.1 %collective-permute-done.14 = bf16[2,2,2,32,2048]{4,3,0,1,2:T(8,128)(2,1)S(1)} collective-permute-done((bf16[2,2,2,32,2048]{4,3,0,1,2:T(8,128)(2,1)S(1)}, bf16[2,2,2,32,2048]{4,3,0,1,2:T(8,128)(2,1)S(1)}, u32[]{:S(2)}, u32[]{:S(2)}) %collective-permute-start.14) | collective-permute-done | bytes 1048608 | tf_op jit(solution)/shard_map/ppermute | solution.py:479
  458.1 11.0 %convolution_convert_fusion.2 = bf16[1024,2048]{1,0:T(8,128)(2,1)} fusion(bf16[2048,1024]{1,0:T(8,128)(2,1)S(1)} %copy-done.67, bf16[2048,2048]{1,0:T(8,128)(2,1)S(1)} %bitcast.638), kind=kOutput, calls=%fused_computation.100 | convolution fusion | flops 8592031744 | bytes 16777216 | tf_op jit(solution)/shard_map/dot_general | solution.py:20
  470.6 2.3 collective-permute-done.16
  477.0 3.6 convolution_convert_fusion.11
  482.2 5.2 collective-permute-start.21
  487.8 3.0 collective-permute-start.23
  490.7 2.4 convolution_convert_fusion.9
  493.5 3.6 convolution_convert_fusion.10
  497.2 2.3 maximum_maximum_fusion
  499.5 8.4 %collective-permute-done.23 = bf16[32,2048]{1,0:T(8,128)(2,1)S(1)} collective-permute-done((bf16[32,2048]{1,0:T(8,128)(2,1)S(1)}, bf16[32,2048]{1,0:T(8,128)(2,1)S(1)}, u32[]{:S(2)}, u32[]{:S(2)}) %collective-permute-start.23) | collective-permute-done | bytes 131104 | tf_op jit(solution)/shard_map/ppermute | solution.py:479
  509.9 3.3 convolution_convert_fusion.5
  520.4 6.4 convolution_convert_fusion.12
  526.8 2.7 collective-permute-done.25
  530.5 4.3 add.480
  534.8 5.5 pad_maximum_fusion.1
  543.5 9.2 %while.39 = (s32[]{:T(128)}, f32[8,128,256]{2,1,0:T(8,128)}, bf16[2048,512]{1,0:T(8,128)(2,1)}, s32[]{:T(128)}, s32[128]{0:T(128)S(1)}, /*index=5*/s32[2048]{0:T...) while((s32[]{:T(128)}, f32[8,128,256]{2,1,0:T(8,128)}, ...), condition=%wide.region_13.14_spmd.clone, body=%wide.region_12.13_spmd.clone.sunk | while | flops 1348665984 | bytes 20336396 | solution.py:850
  547.7 2.8 convolution_add_fusion.10
  555.0 2.3 collective-permute-start.28
  557.3 8.8 %convert_add_fusion.2 = f32[1024,2048]{1,0:T(8,128)} fusion(bf16[1024,2048]{1,0:T(8,128)(2,1)} %collective-permute-done.29, bf16[1024,2048]{1,0:T(8,128)(2,1)} %convolution_convert_fusion.4), kind=kLoop, calls=%fused_computation.85 | loop fusion | flops 6291456 | bytes 16777216 | tf_op jit(solution)/shard_map/add | solution.py:778
  566.1 2.6 collective-permute-done.27
  571.4 7.7 collective-permute-start.31
  579.1 5.3 convert_add_fusion.1
  587.5 5.6 fusion.85
  593.2 5.7 collective-permute-start.33
  600.9 5.5 convert_add_fusion
  606.4 8.4 %collective-permute-start.36 = (bf16[64,512]{1,0:T(8,128)(2,1)S(1)}, bf16[64,512]{1,0:T(8,128)(2,1)}, u32[]{:S(2)}, u32[]{:S(2)}) collective-permute-start(bf16[64,512]{1,0:T(8,128)(2,1)S(1)} %dynamic-slice_bitcast_fusion.23), channel_id=1, source_target_pairs={{0,16},{2,18},{4,20},{6,22},{8,24},{10,26},{12,28},{14,30},{16,0},... | collective-permute-start | bytes 196616 | tf_op jit(solution)/shard_map/ppermute | solution.py:479
  615.8 5.8 convolution_convert_fusion.1
  621.6 5.9 fusion.88
  627.5 2.5 fusion.63
  630.0 2.9 fusion.239
  633.0 3.2 convolution_convert_fusion.8
  636.2 2.5 copy.98
  641.5 3.4 fusion.100
  653.0 95.3 %scatter_blocks_4.1 = bf16[192,2048]{1,0:T(8,128)(2,1)S(1)} custom-call(bf16[16,128,2048]{2,1,0:T(8,128)(2,1)S(1)} %bitcast.598, bf16[16,64,2048]{2,1,0:T(8,128)(2,1)S(1)} %pad_maximum_fusion.2.second_ref), custom_call_target="tpu_custom_call" | custom-call | tf_op jit(solution)/shard_map/scatter_blocks_4/pallas_call | solution.py:423
  750.6 2.6 copy.99
  757.4 2.4 fusion.240
  761.2 5.0 reduce-scatter.2.cloned.1.call-done
  (444 shorter events, 128.8 us)
Async XLA Ops:
  7.2 235.9 %copy-start = (bf16[2048,256]{1,0:T(8,128)(2,1)S(1)}, bf16[2048,256]{1,0:T(8,128)(2,1)}, u32[]{:S(2)}) copy-start(bf16[2048,256]{1,0:T(8,128)(2,1)} %param.51) | copy-start | bytes 3145732
  7.2 96.2 %copy-start.33 = (bf16[1,128,2048]{2,1,0:T(8,128)(2,1)S(1)}, bf16[1,128,2048]{2,1,0:T(8,128)(2,1)}, u32[]{:S(2)}) copy-start(bf16[1,128,2048]{2,1,0:T(8,128)(2,1)} %param.57) | copy-start | bytes 1572868
  7.2 97.1 %copy-start.47 = (s32[1,2048]{1,0:T(1,128)S(1)}, s32[1,2048]{1,0:T(1,128)}, u32[]{:S(2)}) copy-start(s32[1,2048]{1,0:T(1,128)} %param.33) | copy-start | bytes 24580
  7.2 98.1 %copy-start.2 = (bf16[1,128,2048]{2,1,0:T(8,128)(2,1)S(1)}, bf16[1,128,2048]{2,1,0:T(8,128)(2,1)}, u32[]{:S(2)}) copy-start(bf16[1,128,2048]{2,1,0:T(8,128)(2,1)} %param.32) | copy-start | bytes 1572868
  7.3 98.3 %copy-start.38 = (f32[2048]{0:T(1024)S(1)}, f32[2048]{0:T(1024)}, u32[]{:S(2)}) copy-start(f32[2048]{0:T(1024)} %param.34) | copy-start | bytes 24580
  7.3 311.0 %all-gather.3.cloned.1.call-start = ((), (), s32[]{:S(2)}) async-start(), calls=%async_computation.1 | async-start | bytes 4456448 | tf_op jit(solution)/shard_map/all_gather | solution.py:644
  104.3 218.6 %all-gather.5.cloned.1.call-start = ((), (), s32[]{:S(2)}) async-start(), calls=%async_computation.2 | async-start | bytes 4456448 | tf_op jit(solution)/shard_map/all_gather | solution.py:705
  105.2 38.4 %copy-start.56 = (f32[128]{0:T(128)}, f32[128]{0:T(128)S(1)}, u32[]{:S(2)}) copy-start(f32[128]{0:T(128)S(1)} %get-tuple-element.571) | copy-start | bytes 1540
  105.3 38.3 %copy-start.62 = (f32[128]{0:T(128)}, f32[128]{0:T(128)S(1)}, u32[]{:S(2)}) copy-start(f32[128]{0:T(128)S(1)} %negate_power_fusion) | copy-start | bytes 1540
  105.6 38.1 %copy-start.54 = (f32[128]{0:T(128)}, f32[128]{0:T(128)S(1)}, u32[]{:S(2)}) copy-start(f32[128]{0:T(128)S(1)} %fusion.206) | copy-start | bytes 1540
  108.6 45.0 %copy-start.40 = (f32[128,128]{1,0:T(8,128)}, f32[128,128]{1,0:T(8,128)S(1)}, u32[]{:S(2)}) copy-start(f32[128,128]{1,0:T(8,128)S(1)} %get-tuple-element.642) | copy-start | bytes 196612
  165.8 76.7 %copy-start.63 = (f32[128]{0:T(128)}, f32[128]{0:T(128)S(1)}, u32[]{:S(2)}) copy-start(f32[128]{0:T(128)S(1)} %get-tuple-element.643) | copy-start | bytes 1540
  242.6 523.6 %reduce-scatter.2.cloned.1.call-start = ((), (), s32[]{:S(2)}) async-start(), calls=%async_computation.3 | async-start | bytes 6684672 | tf_op jit(solution)/shard_map/reduce_scatter | solution.py:518
  248.9 11.2 %copy-start.31 = (bf16[2048,256]{1,0:T(8,128)(2,1)S(1)}, bf16[2048,256]{1,0:T(8,128)(2,1)}, u32[]{:S(2)}) copy-start(bf16[2048,256]{1,0:T(8,128)(2,1)} %param.53) | copy-start | bytes 3145732
  308.3 44.1 %collective-permute-start = (bf16[2,2,2,48,2048]{4,3,0,1,2:T(8,128)(2,1)}, bf16[2,2,2,48,2048]{4,3,0,1,2:T(8,128)(2,1)}, u32[]{:S(2)}, u32[]{:S(2)}) collective-permute-start(bf16[2,2,2,48,2048]{4,3,0,1,2:T(8,128)(2,1)} %bitcast.536), channel_id=1, source_target_pairs={{0,2},{2,0},{4,6},{6,4},{8,10},{10,8},{12,14},{14,12},{16,18},{18,... | collective-permute-start | bytes 4718600 | tf_op jit(solution)/shard_map/ppermute | solution.py:479
  314.3 38.1 %collective-permute-start.1 = (bf16[2,2,2,48,2048]{4,3,0,2,1:T(8,128)(2,1)}, bf16[2,2,2,48,2048]{4,3,0,2,1:T(8,128)(2,1)}, u32[]{:S(2)}, u32[]{:S(2)}) collective-permute-start(bf16[2,2,2,48,2048]{4,3,0,2,1:T(8,128)(2,1)} %bitcast.535), channel_id=1, source_target_pairs={{0,4},{2,6},{4,0},{6,2},{8,12},{10,14},{12,8},{14,10},{16,20},{18,... | collective-permute-start | bytes 4718600 | tf_op jit(solution)/shard_map/ppermute | solution.py:479
  318.1 34.2 %collective-permute-start.2 = (bf16[2,2,2,32,2048]{4,3,0,1,2:T(8,128)(2,1)S(1)}, bf16[2,2,2,32,2048]{4,3,0,1,2:T(8,128)(2,1)S(1)}, u32[]{:S(2)}, u32[]{:S(2)}) collective-permute-start(bf16[2,2,2,32,2048]{4,3,0,1,2:T(8,128)(2,1)S(1)} %bitcast.642), channel_id=1, source_target_pairs={{0,8},{2,10},{4,12},{6,14},{8,0},{10,2},{12,4},{14,6},{16,24},{18,... | collective-permute-start | bytes 3145736 | tf_op jit(solution)/shard_map/ppermute | solution.py:479
  327.6 24.8 %copy-start.13 = (bf16[2,2,2,1,48,2048]{5,4,3,2,1,0:T(8,128)(2,1)S(1)}, bf16[2,2,2,1,48,2048]{5,4,3,2,1,0:T(8,128)(2,1)}, u32[]{:S(2)}) copy-start(bf16[2,2,2,1,48,2048]{5,4,3,2,1,0:T(8,128)(2,1)} %get-tuple-element.587) | copy-start | bytes 4718596
  354.6 18.6 %collective-permute-start.3 = (bf16[2,2,48,2048]{3,2,0,1:T(8,128)(2,1)S(1)}, bf16[2,2,48,2048]{3,2,0,1:T(8,128)(2,1)S(1)}, u32[]{:S(2)}, u32[]{:S(2)}) collective-permute-start(bf16[2,2,48,2048]{3,2,0,1:T(8,128)(2,1)S(1)} %dynamic-slice_bitcast_fusion.3), channel_id=1, source_target_pairs={{0,4},{2,6},{4,0},{6,2},{8,12},{10,14},{12,8},{14,10},{16,20},{18,... | collective-permute-start | bytes 2359304 | tf_op jit(solution)/shard_map/ppermute | solution.py:479
  358.1 17.4 %collective-permute-start.4 = (bf16[2,2,48,2048]{3,2,0,1:T(8,128)(2,1)S(1)}, bf16[2,2,48,2048]{3,2,0,1:T(8,128)(2,1)S(1)}, u32[]{:S(2)}, u32[]{:S(2)}) collective-permute-start(bf16[2,2,48,2048]{3,2,0,1:T(8,128)(2,1)S(1)} %dynamic-slice_bitcast_fusion.2), channel_id=1, source_target_pairs={{0,8},{2,10},{4,12},{6,14},{8,0},{10,2},{12,4},{14,6},{16,24},{18,... | collective-permute-start | bytes 2359304 | tf_op jit(solution)/shard_map/ppermute | solution.py:479
  360.6 12.6 %collective-permute-start.5 = (bf16[2,2,32,2048]{3,2,0,1:T(8,128)(2,1)S(1)}, bf16[2,2,32,2048]{3,2,0,1:T(8,128)(2,1)S(1)}, u32[]{:S(2)}, u32[]{:S(2)}) collective-permute-start(bf16[2,2,32,2048]{3,2,0,1:T(8,128)(2,1)S(1)} %dynamic-slice_bitcast_fusion.5), channel_id=1, source_target_pairs={{0,2},{2,0},{4,6},{6,4},{8,10},{10,8},{12,14},{14,12},{16,18},{18,... | collective-permute-start | bytes 1572872 | tf_op jit(solution)/shard_map/ppermute | solution.py:479
  375.8 28.4 %collective-permute-start.6 = (bf16[2,48,2048]{2,1,0:T(8,128)(2,1)S(1)}, bf16[2,48,2048]{2,1,0:T(8,128)(2,1)S(1)}, u32[]{:S(2)}, u32[]{:S(2)}) collective-permute-start(bf16[2,48,2048]{2,1,0:T(8,128)(2,1)S(1)} %dynamic-slice_bitcast_fusion.9), channel_id=1, source_target_pairs={{0,8},{2,10},{4,12},{6,14},{8,0},{10,2},{12,4},{14,6},{16,24},{18,... | collective-permute-start | bytes 1179656 | tf_op jit(solution)/shard_map/ppermute | solution.py:479
  378.1 26.1 %collective-permute-start.7 = (bf16[2,48,2048]{2,1,0:T(8,128)(2,1)S(1)}, bf16[2,48,2048]{2,1,0:T(8,128)(2,1)S(1)}, u32[]{:S(2)}, u32[]{:S(2)}) collective-permute-start(bf16[2,48,2048]{2,1,0:T(8,128)(2,1)S(1)} %dynamic-slice_bitcast_fusion.8), channel_id=1, source_target_pairs={{0,2},{2,0},{4,6},{6,4},{8,10},{10,8},{12,14},{14,12},{16,18},{18,... | collective-permute-start | bytes 1179656 | tf_op jit(solution)/shard_map/ppermute | solution.py:479
  379.2 24.9 %collective-permute-start.8 = (bf16[2,32,2048]{2,1,0:T(8,128)(2,1)S(1)}, bf16[2,32,2048]{2,1,0:T(8,128)(2,1)S(1)}, u32[]{:S(2)}, u32[]{:S(2)}) collective-permute-start(bf16[2,32,2048]{2,1,0:T(8,128)(2,1)S(1)} %dynamic-slice_bitcast_fusion.13), channel_id=1, source_target_pairs={{0,4},{2,6},{4,0},{6,2},{8,12},{10,14},{12,8},{14,10},{16,20},{18,... | collective-permute-start | bytes 786440 | tf_op jit(solution)/shard_map/ppermute | solution.py:479
  405.6 35.4 %collective-permute-start.9 = (bf16[48,2048]{1,0:T(8,128)(2,1)S(1)}, bf16[48,2048]{1,0:T(8,128)(2,1)S(1)}, u32[]{:S(2)}, u32[]{:S(2)}) collective-permute-start(bf16[48,2048]{1,0:T(8,128)(2,1)S(1)} %dynamic-slice_bitcast_fusion.17), channel_id=1, source_target_pairs={{0,16},{2,18},{4,20},{6,22},{8,24},{10,26},{12,28},{14,30},{16,0},... | collective-permute-start | bytes 589832 | tf_op jit(solution)/shard_map/ppermute | solution.py:479
  408.7 32.3 %collective-permute-start.10 = (bf16[48,2048]{1,0:T(8,128)(2,1)S(1)}, bf16[48,2048]{1,0:T(8,128)(2,1)S(1)}, u32[]{:S(2)}, u32[]{:S(2)}) collective-permute-start(bf16[48,2048]{1,0:T(8,128)(2,1)S(1)} %dynamic-slice_bitcast_fusion.16), channel_id=1, source_target_pairs={{0,16},{2,18},{4,20},{6,22},{8,24},{10,26},{12,28},{14,30},{16,0},... | collective-permute-start | bytes 589832 | tf_op jit(solution)/shard_map/ppermute | solution.py:479
  408.9 19.5 %collective-permute-start.11 = (bf16[32,2048]{1,0:T(8,128)(2,1)S(1)}, bf16[32,2048]{1,0:T(8,128)(2,1)S(1)}, u32[]{:S(2)}, u32[]{:S(2)}) collective-permute-start(bf16[32,2048]{1,0:T(8,128)(2,1)S(1)} %dynamic-slice_bitcast_fusion.21), channel_id=1, source_target_pairs={{0,16},{2,18},{4,20},{6,22},{8,24},{10,26},{12,28},{14,30},{16,0},... | collective-permute-start | bytes 393224 | tf_op jit(solution)/shard_map/ppermute | solution.py:479
  412.2 40.0 %collective-permute-start.12 = (bf16[2,2,2,48,2048]{4,3,0,1,2:T(8,128)(2,1)S(1)}, bf16[2,2,2,48,2048]{4,3,0,1,2:T(8,128)(2,1)S(1)}, u32[]{:S(2)}, u32[]{:S(2)}) collective-permute-start(bf16[2,2,2,48,2048]{4,3,0,1,2:T(8,128)(2,1)S(1)} %bitcast.640), channel_id=1, source_target_pairs={{0,2},{2,0},{4,6},{6,4},{8,10},{10,8},{12,14},{14,12},{16,18},{18,... | collective-permute-start | bytes 4718600 | tf_op jit(solution)/shard_map/ppermute | solution.py:479
  413.7 38.5 %collective-permute-start.13 = (bf16[2,2,2,48,2048]{4,3,0,2,1:T(8,128)(2,1)S(1)}, bf16[2,2,2,48,2048]{4,3,0,2,1:T(8,128)(2,1)S(1)}, u32[]{:S(2)}, u32[]{:S(2)}) collective-permute-start(bf16[2,2,2,48,2048]{4,3,0,2,1:T(8,128)(2,1)S(1)} %bitcast.641), channel_id=1, source_target_pairs={{0,4},{2,6},{4,0},{6,2},{8,12},{10,14},{12,8},{14,10},{16,20},{18,... | collective-permute-start | bytes 4718600 | tf_op jit(solution)/shard_map/ppermute | solution.py:479
  428.4 23.8 %collective-permute-start.14 = (bf16[2,2,2,32,2048]{4,3,0,1,2:T(8,128)(2,1)S(1)}, bf16[2,2,2,32,2048]{4,3,0,1,2:T(8,128)(2,1)S(1)}, u32[]{:S(2)}, u32[]{:S(2)}) collective-permute-start(bf16[2,2,2,32,2048]{4,3,0,1,2:T(8,128)(2,1)S(1)} %bitcast.643), channel_id=1, source_target_pairs={{0,8},{2,10},{4,12},{6,14},{8,0},{10,2},{12,4},{14,6},{16,24},{18,... | collective-permute-start | bytes 3145736 | tf_op jit(solution)/shard_map/ppermute | solution.py:479
  441.0 49.7 %copy-start.27 = (bf16[1024,2048]{1,0:T(8,128)(2,1)}, bf16[1024,2048]{1,0:T(8,128)(2,1)S(1)}, u32[]{:S(2)}) copy-start(bf16[1024,2048]{1,0:T(8,128)(2,1)S(1)} %convolution_convert_fusion.3) | copy-start | bytes 12582916
  452.9 17.7 %collective-permute-start.15 = (bf16[2,2,48,2048]{3,2,0,1:T(8,128)(2,1)S(1)}, bf16[2,2,48,2048]{3,2,0,1:T(8,128)(2,1)S(1)}, u32[]{:S(2)}, u32[]{:S(2)}) collective-permute-start(bf16[2,2,48,2048]{3,2,0,1:T(8,128)(2,1)S(1)} %dynamic-slice_bitcast_fusion.1), channel_id=1, source_target_pairs={{0,4},{2,6},{4,0},{6,2},{8,12},{10,14},{12,8},{14,10},{16,20},{18,... | collective-permute-start | bytes 2359304 | tf_op jit(solution)/shard_map/ppermute | solution.py:479
  455.4 17.5 %collective-permute-start.16 = (bf16[2,2,48,2048]{3,2,0,1:T(8,128)(2,1)S(1)}, bf16[2,2,48,2048]{3,2,0,1:T(8,128)(2,1)S(1)}, u32[]{:S(2)}, u32[]{:S(2)}) collective-permute-start(bf16[2,2,48,2048]{3,2,0,1:T(8,128)(2,1)S(1)} %dynamic-slice_bitcast_fusion), channel_id=1, source_target_pairs={{0,8},{2,10},{4,12},{6,14},{8,0},{10,2},{12,4},{14,6},{16,24},{18,... | collective-permute-start | bytes 2359304 | tf_op jit(solution)/shard_map/ppermute | solution.py:479
  456.2 13.1 %collective-permute-start.17 = (bf16[2,2,32,2048]{3,2,0,1:T(8,128)(2,1)S(1)}, bf16[2,2,32,2048]{3,2,0,1:T(8,128)(2,1)S(1)}, u32[]{:S(2)}, u32[]{:S(2)}) collective-permute-start(bf16[2,2,32,2048]{3,2,0,1:T(8,128)(2,1)S(1)} %dynamic-slice_bitcast_fusion.4), channel_id=1, source_target_pairs={{0,2},{2,0},{4,6},{6,4},{8,10},{10,8},{12,14},{14,12},{16,18},{18,... | collective-permute-start | bytes 1572872 | tf_op jit(solution)/shard_map/ppermute | solution.py:479
  473.2 8.8 %collective-permute-start.18 = (bf16[2,48,2048]{2,1,0:T(8,128)(2,1)S(1)}, bf16[2,48,2048]{2,1,0:T(8,128)(2,1)S(1)}, u32[]{:S(2)}, u32[]{:S(2)}) collective-permute-start(bf16[2,48,2048]{2,1,0:T(8,128)(2,1)S(1)} %dynamic-slice_bitcast_fusion.7), channel_id=1, source_target_pairs={{0,8},{2,10},{4,12},{6,14},{8,0},{10,2},{12,4},{14,6},{16,24},{18,... | collective-permute-start | bytes 1179656 | tf_op jit(solution)/shard_map/ppermute | solution.py:479
  474.0 8.1 %collective-permute-start.19 = (bf16[2,48,2048]{2,1,0:T(8,128)(2,1)S(1)}, bf16[2,48,2048]{2,1,0:T(8,128)(2,1)S(1)}, u32[]{:S(2)}, u32[]{:S(2)}) collective-permute-start(bf16[2,48,2048]{2,1,0:T(8,128)(2,1)S(1)} %dynamic-slice_bitcast_fusion.6), channel_id=1, source_target_pairs={{0,2},{2,0},{4,6},{6,4},{8,10},{10,8},{12,14},{14,12},{16,18},{18,... | collective-permute-start | bytes 1179656 | tf_op jit(solution)/shard_map/ppermute | solution.py:479
  475.6 6.4 collective-permute-start.20
  482.2 25.6 %collective-permute-start.21 = (bf16[48,2048]{1,0:T(8,128)(2,1)S(1)}, bf16[48,2048]{1,0:T(8,128)(2,1)S(1)}, u32[]{:S(2)}, u32[]{:S(2)}) collective-permute-start(bf16[48,2048]{1,0:T(8,128)(2,1)S(1)} %dynamic-slice_bitcast_fusion.15), channel_id=1, source_target_pairs={{0,16},{2,18},{4,20},{6,22},{8,24},{10,26},{12,28},{14,30},{16,0},... | collective-permute-start | bytes 589832 | tf_op jit(solution)/shard_map/ppermute | solution.py:479
  487.6 20.3 %collective-permute-start.22 = (bf16[48,2048]{1,0:T(8,128)(2,1)S(1)}, bf16[48,2048]{1,0:T(8,128)(2,1)S(1)}, u32[]{:S(2)}, u32[]{:S(2)}) collective-permute-start(bf16[48,2048]{1,0:T(8,128)(2,1)S(1)} %dynamic-slice_bitcast_fusion.14), channel_id=1, source_target_pairs={{0,16},{2,18},{4,20},{6,22},{8,24},{10,26},{12,28},{14,30},{16,0},... | collective-permute-start | bytes 589832 | tf_op jit(solution)/shard_map/ppermute | solution.py:479
  487.8 20.1 %collective-permute-start.23 = (bf16[32,2048]{1,0:T(8,128)(2,1)S(1)}, bf16[32,2048]{1,0:T(8,128)(2,1)S(1)}, u32[]{:S(2)}, u32[]{:S(2)}) collective-permute-start(bf16[32,2048]{1,0:T(8,128)(2,1)S(1)} %dynamic-slice_bitcast_fusion.20), channel_id=1, source_target_pairs={{0,16},{2,18},{4,20},{6,22},{8,24},{10,26},{12,28},{14,30},{16,0},... | collective-permute-start | bytes 393224 | tf_op jit(solution)/shard_map/ppermute | solution.py:479
  497.1 10.9 %copy-start.7 = (f32[128,2048]{1,0:T(8,128)S(1)}, f32[128,2048]{1,0:T(8,128)}, u32[]{:S(2)}) copy-start(f32[128,2048]{1,0:T(8,128)} %copy-done.6) | copy-start | bytes 3145732
  497.2 11.1 %copy-start.64 = (f32[128]{0:T(128)S(1)}, f32[128]{0:T(128)}, u32[]{:S(2)}) copy-start(f32[128]{0:T(128)} %copy-done.63) | copy-start | bytes 1540
  497.2 11.1 %copy-start.34 = (bf16[1,128,2048]{2,1,0:T(8,128)(2,1)S(1)}, bf16[1,128,2048]{2,1,0:T(8,128)(2,1)}, u32[]{:S(2)}) copy-start(bf16[1,128,2048]{2,1,0:T(8,128)(2,1)} %param.57) | copy-start | bytes 1572868
  513.2 17.3 %collective-permute-start.24 = (bf16[16,128,1024]{2,1,0:T(8,128)(2,1)}, bf16[16,128,1024]{2,1,0:T(8,128)(2,1)}, u32[]{:S(2)}, u32[]{:S(2)}) collective-permute-start(bf16[16,128,1024]{2,1,0:T(8,128)(2,1)} %bitcast.93), channel_id=1, source_target_pairs={{0,1},{1,0},{2,3},{3,2},{4,5},{5,4},{6,7},{7,6},{8,9},{9,8},{10,11... | collective-permute-start | bytes 12582920 | tf_op jit(solution)/shard_map/ppermute | solution.py:811
  515.7 14.0 %collective-permute-start.26 = (bf16[16,48,1024]{2,1,0:T(8,128)(2,1)S(1)}, bf16[16,48,1024]{2,1,0:T(8,128)(2,1)S(1)}, u32[]{:S(2)}, u32[]{:S(2)}) collective-permute-start(bf16[16,48,1024]{2,1,0:T(8,128)(2,1)S(1)} %constant_dynamic-slice_fusion.4), channel_id=1, source_target_pairs={{0,1},{1,0},{2,3},{3,2},{4,5},{5,4},{6,7},{7,6},{8,9},{9,8},{10,11... | collective-permute-start | bytes 4718600 | tf_op jit(solution)/shard_map/ppermute | solution.py:811
  517.8 39.5 %collective-permute-start.29 = (bf16[1024,2048]{1,0:T(8,128)(2,1)}, bf16[1024,2048]{1,0:T(8,128)(2,1)}, u32[]{:S(2)}, u32[]{:S(2)}) collective-permute-start(bf16[1024,2048]{1,0:T(8,128)(2,1)} %convolution_convert_fusion.4), channel_id=1, source_target_pairs={{0,1},{1,0},{2,3},{3,2},{4,5},{5,4},{6,7},{7,6},{8,9},{9,8},{10,11... | collective-permute-start | bytes 12582920 | tf_op jit(solution)/shard_map/ppermute | solution.py:778
  518.2 11.3 %collective-permute-start.25 = (bf16[16,16,1024]{2,1,0:T(8,128)(2,1)S(1)}, bf16[16,16,1024]{2,1,0:T(8,128)(2,1)S(1)}, u32[]{:S(2)}, u32[]{:S(2)}) collective-permute-start(bf16[16,16,1024]{2,1,0:T(8,128)(2,1)S(1)} %bitcast.647), channel_id=1, source_target_pairs={{0,1},{1,0},{2,3},{3,2},{4,5},{5,4},{6,7},{7,6},{8,9},{9,8},{10,11... | collective-permute-start | bytes 1572872 | tf_op jit(solution)/shard_map/ppermute | solution.py:811
  554.6 14.0 %collective-permute-start.27 = (bf16[2,2,2,64,512]{4,3,0,1,2:T(8,128)(2,1)S(1)}, bf16[2,2,2,64,512]{4,3,0,1,2:T(8,128)(2,1)S(1)}, u32[]{:S(2)}, u32[]{:S(2)}) collective-permute-start(bf16[2,2,2,64,512]{4,3,0,1,2:T(8,128)(2,1)S(1)} %bitcast.645), channel_id=1, source_target_pairs={{0,2},{2,0},{4,6},{6,4},{8,10},{10,8},{12,14},{14,12},{16,18},{18,... | collective-permute-start | bytes 1572872 | tf_op jit(solution)/shard_map/ppermute | solution.py:479
  555.0 14.2 %copy-start.28 = (bf16[1024,2048]{1,0:T(8,128)(2,1)S(1)}, bf16[1024,2048]{1,0:T(8,128)(2,1)}, u32[]{:S(2)}) copy-start(bf16[1024,2048]{1,0:T(8,128)(2,1)} %copy-done.27) | copy-start | bytes 12582916
  555.0 14.2 %collective-permute-start.28 = (bf16[2,2,2,64,512]{4,3,0,2,1:T(8,128)(2,1)S(1)}, bf16[2,2,2,64,512]{4,3,0,2,1:T(8,128)(2,1)S(1)}, u32[]{:S(2)}, u32[]{:S(2)}) collective-permute-start(bf16[2,2,2,64,512]{4,3,0,2,1:T(8,128)(2,1)S(1)} %bitcast.646), channel_id=1, source_target_pairs={{0,4},{2,6},{4,0},{6,2},{8,12},{10,14},{12,8},{14,10},{16,20},{18,... | collective-permute-start | bytes 1572872 | tf_op jit(solution)/shard_map/ppermute | solution.py:479
  569.3 9.9 %collective-permute-start.32 = (bf16[1024,2048]{1,0:T(8,128)(2,1)S(1)}, bf16[1024,2048]{1,0:T(8,128)(2,1)S(1)}, u32[]{:S(2)}, u32[]{:S(2)}) collective-permute-start(bf16[1024,2048]{1,0:T(8,128)(2,1)S(1)} %copy-done.28), channel_id=1, source_target_pairs={{0,1},{1,0},{2,3},{3,2},{4,5},{5,4},{6,7},{7,6},{8,9},{9,8},{10,11... | collective-permute-start | bytes 12582920 | tf_op jit(solution)/shard_map/ppermute | solution.py:778
  569.4 15.0 %collective-permute-start.30 = (bf16[2,2,64,512]{3,2,0,1:T(8,128)(2,1)S(1)}, bf16[2,2,64,512]{3,2,0,1:T(8,128)(2,1)S(1)}, u32[]{:S(2)}, u32[]{:S(2)}) collective-permute-start(bf16[2,2,64,512]{3,2,0,1:T(8,128)(2,1)S(1)} %dynamic-slice_bitcast_fusion.11), channel_id=1, source_target_pairs={{0,4},{2,6},{4,0},{6,2},{8,12},{10,14},{12,8},{14,10},{16,20},{18,... | collective-permute-start | bytes 786440 | tf_op jit(solution)/shard_map/ppermute | solution.py:479
  571.4 14.4 %collective-permute-start.31 = (bf16[2,2,64,512]{3,2,0,1:T(8,128)(2,1)S(1)}, bf16[2,2,64,512]{3,2,0,1:T(8,128)(2,1)S(1)}, u32[]{:S(2)}, u32[]{:S(2)}) collective-permute-start(bf16[2,2,64,512]{3,2,0,1:T(8,128)(2,1)S(1)} %dynamic-slice_bitcast_fusion.10), channel_id=1, source_target_pairs={{0,8},{2,10},{4,12},{6,14},{8,0},{10,2},{12,4},{14,6},{16,24},{18,... | collective-permute-start | bytes 786440 | tf_op jit(solution)/shard_map/ppermute | solution.py:479
  585.8 15.0 %collective-permute-start.35 = (bf16[1024,2048]{1,0:T(8,128)(2,1)}, bf16[1024,2048]{1,0:T(8,128)(2,1)}, u32[]{:S(2)}, u32[]{:S(2)}) collective-permute-start(bf16[1024,2048]{1,0:T(8,128)(2,1)} %convolution_convert_fusion.2), channel_id=1, source_target_pairs={{0,1},{1,0},{2,3},{3,2},{4,5},{5,4},{6,7},{7,6},{8,9},{9,8},{10,11... | collective-permute-start | bytes 12582920 | tf_op jit(solution)/shard_map/ppermute | solution.py:778
  593.2 13.1 %collective-permute-start.33 = (bf16[2,64,512]{2,1,0:T(8,128)(2,1)S(1)}, bf16[2,64,512]{2,1,0:T(8,128)(2,1)S(1)}, u32[]{:S(2)}, u32[]{:S(2)}) collective-permute-start(bf16[2,64,512]{2,1,0:T(8,128)(2,1)S(1)} %dynamic-slice_bitcast_fusion.19), channel_id=1, source_target_pairs={{0,8},{2,10},{4,12},{6,14},{8,0},{10,2},{12,4},{14,6},{16,24},{18,... | collective-permute-start | bytes 393224 | tf_op jit(solution)/shard_map/ppermute | solution.py:479
  599.1 16.8 %copy-start.3 = (bf16[1,128,2048]{2,1,0:T(8,128)(2,1)S(1)}, bf16[1,128,2048]{2,1,0:T(8,128)(2,1)}, u32[]{:S(2)}) copy-start(bf16[1,128,2048]{2,1,0:T(8,128)(2,1)} %param.32) | copy-start | bytes 1572868
  599.1 16.8 %copy-start.39 = (f32[2048]{0:T(1024)S(1)}, f32[2048]{0:T(1024)}, u32[]{:S(2)}) copy-start(f32[2048]{0:T(1024)} %param.34) | copy-start | bytes 24580
  599.1 16.8 %copy-start.55 = (f32[128]{0:T(128)S(1)}, f32[128]{0:T(128)}, u32[]{:S(2)}) copy-start(f32[128]{0:T(128)} %copy-done.54) | copy-start | bytes 1540
  599.1 7.3 collective-permute-start.34
  606.3 21.2 %copy-start.1 = (f32[1024,2048]{1,0:T(8,128)}, f32[1024,2048]{1,0:T(8,128)S(1)}, u32[]{:S(2)}) copy-start(f32[1024,2048]{1,0:T(8,128)S(1)} %convert_add_fusion) | copy-start | bytes 25165828
  606.4 32.4 %collective-permute-start.36 = (bf16[64,512]{1,0:T(8,128)(2,1)S(1)}, bf16[64,512]{1,0:T(8,128)(2,1)}, u32[]{:S(2)}, u32[]{:S(2)}) collective-permute-start(bf16[64,512]{1,0:T(8,128)(2,1)S(1)} %dynamic-slice_bitcast_fusion.23), channel_id=1, source_target_pairs={{0,16},{2,18},{4,20},{6,22},{8,24},{10,26},{12,28},{14,30},{16,0},... | collective-permute-start | bytes 196616 | tf_op jit(solution)/shard_map/ppermute | solution.py:479
  615.5 23.3 %collective-permute-start.37 = (bf16[64,512]{1,0:T(8,128)(2,1)}, bf16[64,512]{1,0:T(8,128)(2,1)}, u32[]{:S(2)}, u32[]{:S(2)}) collective-permute-start(bf16[64,512]{1,0:T(8,128)(2,1)} %dynamic-slice_bitcast_fusion.22), channel_id=1, source_target_pairs={{0,16},{2,18},{4,20},{6,22},{8,24},{10,26},{12,28},{14,30},{16,0},... | collective-permute-start | bytes 196616 | tf_op jit(solution)/shard_map/ppermute | solution.py:479
  755.7 11.6 %copy-start.45 = (f32[128,256]{1,0:T(8,128)}, f32[128,256]{1,0:T(8,128)S(1)}, u32[]{:S(2)}) copy-start(f32[128,256]{1,0:T(8,128)S(1)} %get-tuple-element.636) | copy-start | bytes 393220
  766.2 1.9 collective-permute-start.38
  (56 other events, 268.0 us)
Sparse Core Ops, SparseCore 0:
  104.4 83.7 all-gather.2
  242.7 75.6 all-gather.4
  586.0 180.1 reduce-scatter.1
